TPU v7x, 512 devices: a whole 4x8x8 slice. The times are simulated.
512 devices in a mesh: blk: 8 (over z_lo, core), owner: 64 (over z_hi, x, y).
Axes of the slice: x: 4, y: 8, z: 8 (z_hi: 2, z_lo: 4; z = z_hi * 4 + z_lo), core: 2. Of those that a mesh axis runs over, the one named last changes fastest.
Arguments:
- tokens: bfloat16 [2048, 32, 1024], P(('owner', 'blk')), may hold values from -6 to 6
- w_qkv: bfloat16 [1024, 3, 1024], P(None, None, 'blk'), may hold values from -0.1875 to 0.1875
- w_out: bfloat16 [1024, 1024], P('blk'), may hold values from -0.5625 to 0.5625
- b_out: bfloat16 [1024], replicated, may hold values from -3 to 3
- gain1: bfloat16 [1024], replicated, may hold values from 0.5 to 1.5
- shift1: bfloat16 [1024], replicated, may hold values from -2 to 2
- w_up: bfloat16 [1024, 4096], P(None, 'blk'), may hold values from -0.1875 to 0.1875
- b_up: bfloat16 [4096], P('blk'), may hold values from -3 to 3
- w_down: bfloat16 [4096, 1024], P('blk'), may hold values from -0.09375 to 0.09375
- b_down: bfloat16 [1024], replicated, may hold values from -3 to 3
- gain2: bfloat16 [1024], replicated, may hold values from 0.5 to 1.5
- shift2: bfloat16 [1024], replicated, may hold values from -2 to 2
- root_cache: bfloat16 [2, 4, 1024, 1024], P(None, None, 'owner', 'blk'), may hold values from -90 to 90
- node_cache: bfloat16 [2, 128, 384, 1024], P(None, 'owner', None, 'blk'), may hold values from -90 to 90
- root_len: int32 [4], replicated, may hold values from 128 to 1024
- node_len: int32 [128], replicated, may hold values from 48 to 384
- node_parent: int32 [128], replicated, may hold values from 0 to 31, as said below
- node_place: int32 [128], replicated, may hold values from 0 to 127, as said below
- req_leaf: int32 [2048], P('owner'), may hold values from 32 to 127, as said below
Outputs:
- result: bfloat16 [2048, 32, 1024], P(('owner', 'blk'))
- new_caches: bfloat16 [2, 2048, 32, 1024], P(None, 'owner', None, 'blk')
Inputs may be any that keep to these rules, and one draw needn't show every extreme that they name: `node_parent`: entries below 32 are branch nodes and name their tenant; each other entry is a leaf and names its branch node; every branch node has exactly three leaves. `node_place`: a permutation of the pool slots; slot s lies on owner s // 2. `req_leaf`: always a leaf; the requests of one owner index lie below different branch nodes.
All inputs are finite; a program needn't handle non-finite values.
Results may differ from a plain program's by a relative error of at most 0.02.
Values may be sent and summed in bfloat16 or wider, within the bound.
No kernel may reach another device: no remote copies, remote signals or barrier semaphores. Data moves between devices by JAX's collectives and lax.ppermute only.
A program may use at most 128 MiB of HBM per device.

v0:
```python
import math

import jax
import jax.numpy as jnp
from jax import lax
from jax.sharding import PartitionSpec as P

HD = 64


norm_eps = 1e-05
masked_score = -1e30


def layer_norm(values, gain, shift):
    center = values - jnp.mean(values, axis=-1, keepdims=True)
    spread = jnp.mean(center * center, axis=-1, keepdims=True)
    return center * lax.rsqrt(spread + norm_eps) * gain.astype(jnp.float32) + shift.astype(
        jnp.float32
    )


def attend_own(queries, key_rows, value_rows, score_scale):
    scores = (
        jnp.einsum("rshe,rnhe->rshn", queries, key_rows, preferred_element_type=jnp.float32)
        * score_scale
    )
    peak = jnp.max(scores, axis=-1)
    weights = jnp.exp(scores - peak[..., None])
    weight_sum = jnp.sum(weights, axis=-1)
    mixed = jnp.einsum(
        "rshn,rnhe->rshe",
        weights.astype(jnp.bfloat16),
        value_rows,
        preferred_element_type=jnp.float32,
    )
    return (mixed / weight_sum[..., None], peak + jnp.log(weight_sum))


def on_device(
    tokens,
    w_qkv,
    w_out,
    b_out,
    gain1,
    shift1,
    w_up,
    b_up,
    w_down,
    b_down,
    gain2,
    shift2,
    root_cache,
    node_cache,
    root_len,
    node_len,
    node_parent,
    node_place,
    req_leaf,
):
    req_dev, suffix, model_width = tokens.shape
    head_cols = w_qkv.shape[2]
    local_heads = head_cols // HD
    own_rows = req_dev * suffix
    owners = lax.axis_size("owner")
    group_size = req_leaf.shape[0]
    score_scale = 1.0 / math.sqrt(HD)
    flat_qkv = w_qkv.reshape(model_width, 3 * head_cols)
    shard_rows = lax.all_gather(tokens, "blk", axis=0, tiled=True)
    row_count = shard_rows.shape[0]
    mixed = jnp.dot(
        shard_rows.reshape(row_count * suffix, model_width),
        flat_qkv,
        preferred_element_type=jnp.float32,
    )
    projected = mixed.astype(jnp.bfloat16).reshape(row_count, suffix, 3 * head_cols)
    queries = projected[:, :, :head_cols].reshape(group_size, suffix, local_heads, HD)
    keys_new = projected[:, :, head_cols : 2 * head_cols]
    values_new = projected[:, :, 2 * head_cols :]
    new_caches = jnp.stack([keys_new, values_new])
    branch = node_parent[req_leaf]
    tenant = node_parent[branch]
    root_limit = root_len[tenant]
    roots_all = lax.all_gather(root_cache, "owner", axis=2, tiled=True)
    root_rows = roots_all.shape[2]
    block_len = math.gcd(root_rows, 256)

    def root_block(block_index, state):
        peak, weight_sum, weighted = state
        offset = block_index * block_len
        key_rows = lax.dynamic_slice_in_dim(roots_all[0], offset, block_len, 1)
        value_rows = lax.dynamic_slice_in_dim(roots_all[1], offset, block_len, 1)
        key_block = jnp.take(key_rows, tenant, axis=0).reshape(
            group_size, block_len, local_heads, HD
        )
        value_block = jnp.take(value_rows, tenant, axis=0).reshape(
            group_size, block_len, local_heads, HD
        )
        positions = offset + jnp.arange(block_len, dtype=jnp.int32)
        in_range = (positions[None, :] < root_limit[:, None])[:, None, None, :]
        scores = (
            jnp.einsum("rshe,rnhe->rshn", queries, key_block, preferred_element_type=jnp.float32)
            * score_scale
        )
        scores = jnp.where(in_range, scores, masked_score)
        new_peak = jnp.maximum(peak, jnp.max(scores, axis=-1))
        weights = jnp.where(in_range, jnp.exp(scores - new_peak[..., None]), 0.0)
        factor = jnp.exp(peak - new_peak)
        weight_sum = weight_sum * factor + jnp.sum(weights, axis=-1)
        weighted = weighted * factor[..., None] + jnp.einsum(
            "rshn,rnhe->rshe",
            weights.astype(jnp.bfloat16),
            value_block,
            preferred_element_type=jnp.float32,
        )
        return (new_peak, weight_sum, weighted)

    start_state = (
        jnp.full((group_size, suffix, local_heads), masked_score, jnp.float32),
        jnp.zeros((group_size, suffix, local_heads), jnp.float32),
        jnp.zeros((group_size, suffix, local_heads, HD), jnp.float32),
    )
    root_peak, root_sum, root_weighted = lax.fori_loop(
        0, root_rows // block_len, root_block, start_state
    )
    root_out = root_weighted / root_sum[..., None]
    root_mass = root_peak + jnp.log(root_sum)
    slot_total = node_place.shape[0]
    slot_count = slot_total // owners
    node_max = node_cache.shape[2]
    slot_ids = jnp.arange(slot_total, dtype=jnp.int32)
    at_branch = slot_ids[:, None] == node_place[branch][None, :]
    at_leaf = slot_ids[:, None] == node_place[req_leaf][None, :]
    route = (at_branch | at_leaf).astype(jnp.bfloat16)
    outgoing = jnp.dot(
        route, queries.reshape(group_size, suffix * head_cols), preferred_element_type=jnp.float32
    )
    outgoing = outgoing.astype(jnp.bfloat16).reshape(owners, slot_count, suffix, head_cols)
    slot_len = jnp.sum(
        jnp.where(slot_ids[:, None] == node_place[None, :], node_len[None, :], 0), axis=1
    )
    my_owner = lax.axis_index("owner")
    local_len = lax.dynamic_slice_in_dim(slot_len, my_owner * slot_count, slot_count)
    cache_keys = node_cache[0].reshape(slot_count, node_max, local_heads, HD)
    cache_values = node_cache[1].reshape(slot_count, node_max, local_heads, HD)
    local_range = jnp.arange(node_max, dtype=jnp.int32)[None, :] < local_len[:, None]
    incoming = lax.all_to_all(outgoing, "owner", split_axis=0, concat_axis=0, tiled=True)
    sources, _, row_count, _ = incoming.shape
    block_width = 8
    blocks = incoming.reshape(
        sources // block_width, block_width, slot_count, row_count, local_heads, HD
    )

    def source_block(block_queries):
        scores = (
            jnp.einsum(
                "bkthe,knhe->bkthn", block_queries, cache_keys, preferred_element_type=jnp.float32
            )
            * score_scale
        )
        keep_rows = local_range[None, :, None, None, :]
        scores = jnp.where(keep_rows, scores, masked_score)
        peak = jnp.max(scores, axis=-1)
        weights = jnp.where(keep_rows, jnp.exp(scores - peak[..., None]), 0.0)
        weight_sum = jnp.sum(weights, axis=-1)
        mixed = jnp.einsum(
            "bkthn,knhe->bkthe",
            weights.astype(jnp.bfloat16),
            cache_values,
            preferred_element_type=jnp.float32,
        )
        mixed = mixed / weight_sum[..., None]
        return (
            mixed.reshape(block_width, slot_count, row_count, head_cols),
            peak + jnp.log(weight_sum),
        )

    mixed, log_mass = lax.map(source_block, blocks)
    mixed = mixed.reshape(sources, slot_count, row_count, head_cols)
    log_mass = log_mass.reshape(sources, slot_count, row_count, local_heads)
    back_out = lax.all_to_all(mixed, "owner", split_axis=0, concat_axis=0, tiled=True)
    back_mass = lax.all_to_all(log_mass, "owner", split_axis=0, concat_axis=0, tiled=True)
    back_flat = back_out.reshape(slot_total, suffix * head_cols)
    mass_flat = back_mass.reshape(slot_total, suffix * local_heads)

    def collect(selected):
        weights_sel = selected.astype(jnp.float32)
        gathered = jnp.einsum("gr,gf->rf", weights_sel, back_flat, precision=lax.Precision.HIGHEST)
        masses = jnp.einsum("gr,gf->rf", weights_sel, mass_flat, precision=lax.Precision.HIGHEST)
        return (
            gathered.reshape(group_size, suffix, local_heads, HD),
            masses.reshape(group_size, suffix, local_heads),
        )

    branch_out, branch_mass = collect(at_branch)
    leaf_out, leaf_mass = collect(at_leaf)
    own_out, own_mass = attend_own(
        queries,
        keys_new.reshape(group_size, suffix, local_heads, HD),
        values_new.reshape(group_size, suffix, local_heads, HD),
        score_scale,
    )
    set_outs = [root_out, branch_out, leaf_out, own_out]
    set_masses = [root_mass, branch_mass, leaf_mass, own_mass]
    highest = jnp.maximum(jnp.maximum(root_mass, branch_mass), jnp.maximum(leaf_mass, own_mass))
    mass_sum = (
        jnp.exp(root_mass - highest)
        + jnp.exp(branch_mass - highest)
        + jnp.exp(leaf_mass - highest)
        + jnp.exp(own_mass - highest)
    )
    total = highest + jnp.log(mass_sum)
    attn = set_outs[0] * jnp.exp(set_masses[0] - total)[..., None]
    for set_index in range(1, 4):
        attn = attn + set_outs[set_index] * jnp.exp(set_masses[set_index] - total)[..., None]
    attn = attn.astype(jnp.bfloat16).reshape(group_size, suffix, head_cols)
    attn_flat = attn.reshape(group_size * suffix, head_cols)
    head_sum = lax.psum_scatter(
        jnp.dot(attn_flat, w_out, preferred_element_type=jnp.float32).astype(jnp.bfloat16),
        "blk",
        scatter_dimension=0,
        tiled=True,
    ).astype(jnp.float32)
    first_norm = layer_norm(
        tokens.reshape(own_rows, model_width).astype(jnp.float32)
        + head_sum
        + b_out.astype(jnp.float32),
        gain1,
        shift1,
    ).astype(jnp.bfloat16)
    inner_act = jnp.dot(
        lax.all_gather(first_norm, "blk", axis=0, tiled=True),
        w_up,
        preferred_element_type=jnp.float32,
    ) + b_up.astype(jnp.float32)
    hidden = jax.nn.gelu(inner_act, approximate=False).astype(jnp.bfloat16)
    down_sum = lax.psum_scatter(
        jnp.dot(hidden, w_down, preferred_element_type=jnp.float32).astype(jnp.bfloat16),
        "blk",
        scatter_dimension=0,
        tiled=True,
    ).astype(jnp.float32)
    result = layer_norm(
        first_norm.astype(jnp.float32) + down_sum + b_down.astype(jnp.float32), gain2, shift2
    ).astype(jnp.bfloat16)
    return (result.reshape(req_dev, suffix, model_width), new_caches)


def solution(mesh):
    in_specs = (
        P(("owner", "blk"), None, None),
        P(None, None, "blk"),
        P("blk", None),
        P(),
        P(),
        P(),
        P(None, "blk"),
        P("blk"),
        P("blk", None),
        P(),
        P(),
        P(),
        P(None, None, "owner", "blk"),
        P(None, "owner", None, "blk"),
        P(),
        P(),
        P(),
        P(),
        P("owner"),
    )
    out_specs = (P(("owner", "blk"), None, None), P(None, "owner", None, "blk"))
    return jax.shard_map(
        on_device, mesh=mesh, in_specs=in_specs, out_specs=out_specs, check_vma=False
    )
```

profile of v0, /device:TPU:1, one launch (start us, length us, event | category | flops | bytes accessed | tf_op | source)
XLA Modules:
  0.0 545.7 jit_solution(3773147124506278843)
XLA Ops:
  13.0 44.2 %all-gather.6.cloned.1.call-done = bf16[32,32,1024]{2,1,0:T(8,128)(2,1)} async-done(((bf16[4,32,1024]{2,1,0:T(8,128)(2,1)}), bf16[32,32,1024]{2,1,0:T(8,128)(2,1)}) %all-gather.6.cloned.1.call-update) | async-done | bytes 2097168 | tf_op jit(solution)/shard_map/all_gather | solution.py:69
  57.1 2.9 convolution_convert_fusion.3
  62.8 13.8 %all-to-all-start = ((bf16[64,2,32,128]{3,2,1,0:T(8,128)(2,1)}), bf16[64,2,32,128]{3,2,1,0:T(8,128)(2,1)}, u32[]{:S(2)}, u32[]{:S(2)}) async-start(bf16[64,2,32,128]{3,2,1,0:T(8,128)(2,1)} %bitcast.57), calls=%async_computation | async-start | bytes 2097152 | tf_op jit(solution)/shard_map/all_to_all | solution.py:147
  79.8 2.6 fusion.115
  87.7 17.6 %all-to-all-done = bf16[64,2,32,128]{3,2,1,0:T(8,128)(2,1)} async-done(((bf16[64,2,32,128]{3,2,1,0:T(8,128)(2,1)}), bf16[64,2,32,128]{3,2,1,0:T(8,128)(2,1)}, u32[]{:S(2)}, u32[]{:S(2)}) %all-to-all-start) | async-done | bytes 1048608 | tf_op jit(solution)/shard_map/all_to_all | solution.py:147
  105.3 5.0 reshape.205
  110.3 39.3 %while.31 = (s32[]{:T(128)}, f32[8,8,2,32,128]{4,3,2,1,0:T(8,128)}, f32[8,8,2,32,2]{3,1,0,4,2:T(8,128)}, bf16[8,8,2,32,2,64]{5,4,3,2,1,0:T(2,128)(2,1)}, bf16[2,...) while((s32[]{:T(128)}, f32[8,8,2,32,128]{4,3,2,1,0:T(8,128)}, ...), condition=%wide.region_8.10_spmd.clone, body=%wide.region_5.9_spmd.clone.sunk | while | flops 104267520 | bytes 7389281 | solution.py:178
  151.4 7.8 %all-to-all-start.1 = ((f32[64,1,128]{2,1,0:T(1,128)}), f32[64,1,128]{2,1,0:T(1,128)S(1)}, u32[]{:S(2)}, u32[]{:S(2)}) async-start(f32[64,1,128]{2,1,0:T(1,128)} %reshape.304), calls=%async_computation.1 | async-start | bytes 65536 | tf_op jit(solution)/shard_map/all_to_all | solution.py:182
  162.2 10.3 %all-to-all-done.1 = f32[64,1,128]{2,1,0:T(1,128)S(1)} async-done(((f32[64,1,128]{2,1,0:T(1,128)}), f32[64,1,128]{2,1,0:T(1,128)S(1)}, u32[]{:S(2)}, u32[]{:S(2)}) %all-to-all-start.1) | async-done | bytes 32800 | tf_op jit(solution)/shard_map/all_to_all | solution.py:182
  173.1 5.6 %all-to-all-start.2 = ((f32[64,2,32,128]{3,2,1,0:T(8,128)}), f32[64,2,32,128]{3,2,1,0:T(8,128)}, u32[]{:S(2)}, u32[]{:S(2)}) async-start(f32[64,2,32,128]{3,2,1,0:T(8,128)} %bitcast.197), calls=%async_computation.2 | async-start | bytes 4194304 | tf_op jit(solution)/shard_map/all_to_all | solution.py:181
  178.9 87.7 %all-gather.4.cloned.1.call-done = bf16[2,4,1024,128]{3,2,1,0:T(8,128)(2,1)} async-done(((bf16[2,4,16,128]{3,2,1,0:T(8,128)(2,1)}), bf16[2,4,1024,128]{3,2,1,0:T(8,128)(2,1)}) %all-gather.4.cloned.1.call-update) | async-done | bytes 2097168 | tf_op jit(solution)/shard_map/all_gather | solution.py:84
  266.6 106.4 %while.32 = (s32[]{:T(128)}, f32[32,32,2]{1,2,0:T(2,128)S(1)}, f32[32,32,2]{1,2,0:T(2,128)S(1)}, f32[32,32,2,64]{3,1,2,0:T(8,128)}, s32[32]{0:T(128)S(1)}, /*ind...) while((s32[]{:T(128)}, f32[32,32,2]{1,2,0:T(2,128)S(1)}, ...), condition=%wide.region_3.5_spmd.clone, body=%wide.region_0.4_spmd.clone.sunk | while | flops 143543840 | bytes 50766020 | solution.py:123
  268.4 2.2 gather_fusion
  270.6 2.2 gather_fusion.1
  273.4 4.1 broadcast_select_fusion.4
  277.5 4.1 copy.240
  281.7 2.4 bitcast_reduce_fusion.5
  285.1 4.1 copy.241
  289.2 4.0 fusion.189
  294.9 2.2 gather_fusion
  297.1 2.2 gather_fusion.1
  300.0 4.1 broadcast_select_fusion.4
  304.0 4.1 copy.240
  308.2 2.4 bitcast_reduce_fusion.5
  311.6 4.1 copy.241
  315.7 4.0 fusion.189
  321.6 2.2 gather_fusion
  323.7 2.2 gather_fusion.1
  326.6 4.1 broadcast_select_fusion.4
  330.7 4.1 copy.240
  334.8 2.4 bitcast_reduce_fusion.5
  338.2 4.1 copy.241
  342.3 4.0 fusion.189
  348.2 2.2 gather_fusion
  350.4 2.2 gather_fusion.1
  353.2 4.1 broadcast_select_fusion.4
  357.3 4.1 copy.240
  361.5 2.4 bitcast_reduce_fusion.5
  364.8 4.1 copy.241
  369.0 4.0 fusion.189
  379.2 3.2 copy.232
  384.3 5.2 fusion.43
  389.6 4.0 fusion.46
  394.5 2.0 convolution_convert_fusion.2
  396.7 39.6 %reduce-scatter.3.cloned.1.call-done = bf16[128,1024]{1,0:T(8,128)(2,1)} async-done(((bf16[1024,1024]{1,0:T(8,128)(2,1)}), bf16[128,1024]{1,0:T(8,128)(2,1)}) %reduce-scatter.3.cloned.1.call-update) | async-done | bytes 262160 | tf_op jit(solution)/shard_map/reduce_scatter | solution.py:218
  440.5 42.2 %all-gather.8.cloned.1.call-done = bf16[1024,1024]{1,0:T(8,128)(2,1)} async-done(((bf16[128,1024]{1,0:T(8,128)(2,1)}), bf16[1024,1024]{1,0:T(8,128)(2,1)}) %all-gather.8.cloned.1.call-update) | async-done | bytes 2097168 | tf_op jit(solution)/shard_map/all_gather | solution.py:232
  482.8 9.0 %convolution_convert_fusion.1 = bf16[1024,1024]{1,0:T(8,128)(2,1)} fusion(bf16[512,1024]{1,0:T(8,128)(2,1)S(1)} %copy-done, bf16[1024,1024]{1,0:T(8,128)(2,1)} %all-gather.8.cloned.1.call-done, bf16[1024,512]{1,0:T(8,128)(2,1)S(1)} %copy-done.27, f32[512]{0:T(512)S(1)} %convert_element_type.89), kind=kOutput, calls=%fused_computation.81 | convolution fusion | flops 2183135232 | bytes 6293504 | tf_op jit(solution)/shard_map/dot_general | solution.py:238
  493.7 40.8 %reduce-scatter.5.cloned.1.call-done = bf16[128,1024]{1,0:T(8,128)(2,1)} async-done(((bf16[1024,1024]{1,0:T(8,128)(2,1)}), bf16[128,1024]{1,0:T(8,128)(2,1)}) %reduce-scatter.5.cloned.1.call-update) | async-done | bytes 262160 | tf_op jit(solution)/shard_map/reduce_scatter | solution.py:237
  (270 shorter events, 93.7 us)
Async XLA Ops:
  8.0 474.8 %copy-start = (bf16[512,1024]{1,0:T(8,128)(2,1)S(1)}, bf16[512,1024]{1,0:T(8,128)(2,1)}, u32[]{:S(2)}) copy-start(bf16[512,1024]{1,0:T(8,128)(2,1)} %param.33) | copy-start | bytes 3145732
  8.0 2.8 copy-start.1
  8.0 3.5 copy-start.2
  8.0 49.1 %all-gather.6.cloned.1.call-start = ((), (), s32[]{:S(2)}) async-start(), calls=%async_computation.6 | async-start | bytes 2359296 | tf_op jit(solution)/shard_map/all_gather | solution.py:69
  61.6 16.3 %copy-start.12 = (bf16[2,2,384,128]{3,2,1,0:T(8,128)(2,1)S(1)}, bf16[2,2,384,128]{3,2,1,0:T(8,128)(2,1)}, u32[]{:S(2)}) copy-start(bf16[2,2,384,128]{3,2,1,0:T(8,128)(2,1)} %param.38) | copy-start | bytes 1179652
  62.8 16.2 %copy-start.28 = (s32[128]{0:T(128)S(1)}, s32[128]{0:T(128)}, u32[]{:S(2)}) copy-start(s32[128]{0:T(128)} %param.40) | copy-start | bytes 1540
  62.8 16.3 %copy-start.17 = (s32[4]{0:T(128)S(1)}, s32[4]{0:T(128)}, u32[]{:S(2)}) copy-start(s32[4]{0:T(128)} %param.39) | copy-start | bytes 52
  62.8 42.5 %all-to-all-start = ((bf16[64,2,32,128]{3,2,1,0:T(8,128)(2,1)}), bf16[64,2,32,128]{3,2,1,0:T(8,128)(2,1)}, u32[]{:S(2)}, u32[]{:S(2)}) async-start(bf16[64,2,32,128]{3,2,1,0:T(8,128)(2,1)} %bitcast.57), calls=%async_computation | async-start | bytes 2097152 | tf_op jit(solution)/shard_map/all_to_all | solution.py:147
  76.6 190.0 %all-gather.4.cloned.1.call-start = ((), (), s32[]{:S(2)}) async-start(), calls=%async_computation.5 | async-start | bytes 2129920 | tf_op jit(solution)/shard_map/all_gather | solution.py:84
  82.7 5.1 copy-start.5
  84.8 1.5 copy-start.8
  87.7 22.6 %copy-start.14 = (bf16[1,2,384,128]{2,3,1,0:T(8,128)(2,1)S(1)}, bf16[1,2,384,128]{2,3,1,0:T(8,128)(2,1)}, u32[]{:S(2)}) copy-start(bf16[1,2,384,128]{2,3,1,0:T(8,128)(2,1)} %copy.135) | copy-start | bytes 589828
  151.4 21.0 %all-to-all-start.1 = ((f32[64,1,128]{2,1,0:T(1,128)}), f32[64,1,128]{2,1,0:T(1,128)S(1)}, u32[]{:S(2)}, u32[]{:S(2)}) async-start(f32[64,1,128]{2,1,0:T(1,128)} %reshape.304), calls=%async_computation.1 | async-start | bytes 65536 | tf_op jit(solution)/shard_map/all_to_all | solution.py:182
  172.5 0.6 copy-start.15
  173.1 206.2 %all-to-all-start.2 = ((f32[64,2,32,128]{3,2,1,0:T(8,128)}), f32[64,2,32,128]{3,2,1,0:T(8,128)}, u32[]{:S(2)}, u32[]{:S(2)}) async-start(f32[64,2,32,128]{3,2,1,0:T(8,128)} %bitcast.197), calls=%async_computation.2 | async-start | bytes 4194304 | tf_op jit(solution)/shard_map/all_to_all | solution.py:181
  178.7 257.7 %reduce-scatter.3.cloned.1.call-start = ((), (), s32[]{:S(2)}) async-start(), calls=%async_computation.7 | async-start | bytes 2359296 | tf_op jit(solution)/shard_map/reduce_scatter | solution.py:218
  266.6 1.8 copy-start.24
  270.6 2.8 copy-start.3
  289.2 4.0 copy-start.25
  293.1 1.8 copy-start.24
  297.1 2.8 copy-start.3
  315.7 4.1 copy-start.25
  319.8 1.8 copy-start.24
  323.7 2.8 copy-start.3
  342.3 4.1 copy-start.25
  346.4 1.8 copy-start.24
  350.4 2.8 copy-start.3
  368.9 4.1 copy-start.25
  384.3 5.3 copy-start.7
  384.3 5.3 copy-start.9
  384.3 5.3 copy-start.16
  389.6 4.9 copy-start.13
  394.5 2.1 copy-start.18
  394.5 2.2 copy-start.19
  394.5 2.2 copy-start.20
  394.5 41.8 %copy-start.6 = (bf16[4,32,1024]{2,1,0:T(8,128)(2,1)S(1)}, bf16[4,32,1024]{2,1,0:T(8,128)(2,1)}, u32[]{:S(2)}) copy-start(bf16[4,32,1024]{2,1,0:T(8,128)(2,1)} %param.25) | copy-start | bytes 786436
  396.5 44.0 %copy-start.26 = (bf16[512]{0:T(512)(128)(2,1)S(1)}, bf16[512]{0:T(512)(128)(2,1)}, u32[]{:S(2)}) copy-start(bf16[512]{0:T(512)(128)(2,1)} %param.32) | copy-start | bytes 3076
  396.5 86.3 %copy-start.27 = (bf16[1024,512]{1,0:T(8,128)(2,1)S(1)}, bf16[1024,512]{1,0:T(8,128)(2,1)}, u32[]{:S(2)}) copy-start(bf16[1024,512]{1,0:T(8,128)(2,1)} %param.31) | copy-start | bytes 3145732
  396.5 86.2 %all-gather.8.cloned.1.call-start = ((), (), s32[]{:S(2)}) async-start(), calls=%async_computation.8 | async-start | bytes 2359296 | tf_op jit(solution)/shard_map/all_gather | solution.py:232
  440.5 94.0 %reduce-scatter.5.cloned.1.call-start = ((), (), s32[]{:S(2)}) async-start(), calls=%async_computation.9 | async-start | bytes 2359296 | tf_op jit(solution)/shard_map/reduce_scatter | solution.py:237
  491.8 0.7 copy-start.21
  491.8 0.7 copy-start.22
  491.8 0.7 copy-start.23
  491.8 1.0 copy-start.10
  491.8 1.1 copy-start.11
  491.8 42.7 %copy-start.4 = (bf16[128,1024]{1,0:T(8,128)(2,1)S(1)}, bf16[128,1024]{1,0:T(8,128)(2,1)}, u32[]{:S(2)}) copy-start(bf16[128,1024]{1,0:T(8,128)(2,1)} %add_convert_fusion.1) | copy-start | bytes 786436
Sparse Core Ops, SparseCore 0:
  10.9 46.1 all-gather.5
  396.7 39.5 reduce-scatter.2
  440.6 42.1 all-gather.7
  492.0 42.4 reduce-scatter.4
Sparse Core Ops, SparseCore 1:
  81.4 185.2 all-gather.3
where the time goes:
time: 549 us; the launch traced here: 546 us
  waiting for transfers between devices  284 us (52%)
  local copies, waits for them, and re-layouts  110 us (20%)
  matrix products  61.6 us (11%)
  other arithmetic  46.7 us (9%)
  starting transfers between devices  27.5 us (5%)
  between operations  15.7 us (3%)
    all_gather x1, waiting for transfers between devices, on_device(): roots_all = lax.all_gather(root_cache, 'owner', axis=2, tiled=True)  87.7 us
    all_gather x1, waiting for transfers between devices, on_device(): shard_rows = lax.all_gather(tokens, 'blk', axis=0, tiled=True)  44.2 us
    all_gather x1, waiting for transfers between devices, on_device(): lax.all_gather(first_norm, 'blk', axis=0, tiled=True)  42.2 us
    reduce_scatter x1, waiting for transfers between devices, on_device(): lax.psum_scatter(jnp.dot(hidden, w_down, preferred_element_type=jnp.float...  40.8 us
    reduce_scatter x1, waiting for transfers between devices, on_device(): lax.psum_scatter(jnp.dot(attn_flat, w_out, preferred_element_type=jnp.flo...  39.6 us
    all_to_all x1, waiting for transfers between devices, on_device(): lax.all_to_all(outgoing, 'owner', split_axis=0, concat_axis=0, tiled=True)  17.6 us
    select_n x4, local copies, waits for them, and re-layouts, root_block(): jnp.take(value_rows, tenant, axis=0)  16.4 us
    select_n x4, local copies, waits for them, and re-layouts, root_block(): jnp.take(key_rows, tenant, axis=0)  16.4 us
  transfers between devices with their start and end apart: 8, of which 7 were waited for; matrix products, arithmetic and copies ran while one was open for 32% of the time, Pallas kernels for 0%

commit v1 on v0

v1 whole, which is shorter than its diff:
```python
import functools

import jax
import jax.numpy as jnp
from jax import lax
from jax.experimental import pallas as pl
from jax.experimental.pallas import tpu as pltpu
from jax.sharding import PartitionSpec as P

F32 = jnp.float32
BF16 = jnp.bfloat16
I32 = jnp.int32

HD = 64
LANES = 128
N_BLK = 8
NX, NY, NZ = 4, 8, 2
PEERS = NZ * NY
SLOTS = 2 * NX
CHUNK = 4
NEG = -1e30
EPS = 1e-05


def layer_norm(values, gain, shift):
    center = values - jnp.mean(values, axis=-1, keepdims=True)
    spread = jnp.mean(center * center, axis=-1, keepdims=True)
    return center * lax.rsqrt(spread + EPS) * gain.astype(F32) + shift.astype(F32)


def xor_pairs(count, bits):
    return [(i, i ^ bits) for i in range(count)]


def dot_nt(a, b):
    return lax.dot_general(a, b, (((1,), (1,)), ((), ())), preferred_element_type=F32)


def dot_nn(a, b):
    return lax.dot_general(a, b, (((1,), (0,)), ((), ())), preferred_element_type=F32)


def both_heads(q):
    lane = lax.broadcasted_iota(I32, q.shape, 1)
    zero = jnp.zeros_like(q)
    return jnp.concatenate([jnp.where(lane < HD, q, zero), jnp.where(lane < HD, zero, q)], axis=0)


def by_head(stacked):
    rows = stacked.shape[0] // 2
    lane = lax.broadcasted_iota(I32, (rows, LANES), 1)
    first = jnp.broadcast_to(stacked[:rows], (rows, LANES))
    second = jnp.broadcast_to(stacked[rows:], (rows, LANES))
    return jnp.where(lane < HD, first, second)


def route_kernel(pos, dst_b, dst_l, q_ref, out_ref):
    out_ref[...] = jnp.zeros_like(out_ref)

    def body(r, _):
        tile = q_ref[pos[r]]
        out_ref[dst_b[r]] = tile
        out_ref[dst_l[r]] = tile
        return 0

    lax.fori_loop(0, pos.shape[0], body, 0)


def route(pos, dst_b, dst_l, q):
    reqs, suf, _ = q.shape
    return pl.pallas_call(
        route_kernel,
        out_shape=jax.ShapeDtypeStruct((PEERS * SLOTS, suf, LANES), BF16),
        in_specs=[pl.BlockSpec(memory_space=pltpu.SMEM)] * 3
        + [pl.BlockSpec(memory_space=pltpu.VMEM)],
        out_specs=pl.BlockSpec(memory_space=pltpu.VMEM),
        cost_estimate=pl.CostEstimate(flops=0, bytes_accessed=3 << 20, transcendentals=0),
    )(pos, dst_b, dst_l, q)


def node_kernel(lens, q_ref, k_ref, v_ref, out_ref):
    slot = pl.program_id(0)
    peers, _, suf, _ = q_ref.shape
    group = 4
    rows = group * suf
    node_max = k_ref.shape[2]
    keys = k_ref[0, 0]
    values = v_ref[0, 0]
    keep = lax.broadcasted_iota(I32, (1, node_max), 1) < lens[slot]
    bias = jnp.where(keep, 0.0, NEG)
    lane = lax.broadcasted_iota(I32, (rows, LANES), 1) % HD

    @pl.when(slot == 0)
    def _():
        out_ref[:, SLOTS] = jnp.zeros((peers, suf, LANES), BF16)

    for g in range(peers // group):
        part = slice(g * group, (g + 1) * group)
        q = q_ref[part, slot].reshape(rows, LANES)
        scores = jnp.where(keep, dot_nt(both_heads(q), keys), NEG)
        peak = jnp.max(scores, axis=1, keepdims=True)
        weights = jnp.exp(scores - peak)
        total = jnp.sum(weights, axis=1, keepdims=True)
        mixed = by_head(dot_nn(weights.astype(BF16), values))
        out = mixed / by_head(total)
        out_ref[part, slot] = out.astype(BF16).reshape(group, suf, LANES)
        mass = by_head(peak + jnp.log(total))
        high = mass.astype(BF16)
        rest = mass - high.astype(F32)
        mid = rest.astype(BF16)
        low = (rest - mid.astype(F32)).astype(BF16)
        held = out_ref[part, SLOTS].reshape(rows, LANES)
        held = jnp.where(lane == 3 * slot, high, held)
        held = jnp.where(lane == 3 * slot + 1, mid, held)
        held = jnp.where(lane == 3 * slot + 2, low, held)
        out_ref[part, SLOTS] = held.reshape(group, suf, LANES)


def node_attention(lens, queries, caches):
    peers, slots, suf, _ = queries.shape
    node_max = caches.shape[3]
    return pl.pallas_call(
        node_kernel,
        out_shape=jax.ShapeDtypeStruct((peers, slots + 1, suf, LANES), BF16),
        grid_spec=pltpu.PrefetchScalarGridSpec(
            num_scalar_prefetch=1,
            grid=(slots,),
            in_specs=[
                pl.BlockSpec((peers, slots, suf, LANES), lambda s, n: (0, 0, 0, 0)),
                pl.BlockSpec(
                    (1, 1, pl.Squeezed(), node_max, LANES), lambda s, n: (s // 2, 0, s % 2, 0, 0)
                ),
                pl.BlockSpec(
                    (1, 1, pl.Squeezed(), node_max, LANES), lambda s, n: (s // 2, 1, s % 2, 0, 0)
                ),
            ],
            out_specs=pl.BlockSpec((peers, slots + 1, suf, LANES), lambda s, n: (0, 0, 0, 0)),
        ),
        compiler_params=pltpu.CompilerParams(vmem_limit_bytes=40 << 20),
        cost_estimate=pl.CostEstimate(
            flops=2 << 30, bytes_accessed=4 << 20, transcendentals=4 << 20
        ),
    )(lens, queries, caches, caches)


def root_kernel(
    used, members, valid, chunk_tenant, root_len, coords, q_ref, k_ref, v_ref, root_ref, out_ref, mass_ref
):
    suf = q_ref.shape[1]
    rows = CHUNK * suf
    root_rows = NY * NZ * NX * root_ref.shape[5]
    per = root_ref.shape[5]

    def body(c, _):
        tenant = chunk_tenant[c]
        where_ = [members[c * CHUNK + j] for j in range(CHUNK)]
        q = both_heads(jnp.concatenate([q_ref[w] for w in where_], axis=0))
        own_k = jnp.concatenate([k_ref[w] for w in where_], axis=0)
        own_v = jnp.concatenate([v_ref[w] for w in where_], axis=0)
        keys = root_ref[:, :, :, 0, tenant].reshape(root_rows, LANES)
        values = root_ref[:, :, :, 1, tenant].reshape(root_rows, LANES)
        n = lax.broadcasted_iota(I32, (1, root_rows), 1)
        row = n % per
        x = (n // per) % NX
        z = (n // (per * NX)) % NZ
        y = n // (per * NX * NZ)
        place = (((z ^ coords[0]) * NX + (x ^ coords[1])) * NY + y) * per + row
        scores = jnp.where(place < root_len[tenant], dot_nt(q, keys), NEG)
        own_row = (lax.broadcasted_iota(I32, (2 * rows, rows), 0) % rows) // suf
        own_col = lax.broadcasted_iota(I32, (2 * rows, rows), 1) // suf
        own = jnp.where(own_row == own_col, dot_nt(q, own_k), NEG)
        peak = jnp.maximum(
            jnp.max(scores, axis=1, keepdims=True), jnp.max(own, axis=1, keepdims=True)
        )
        weights = jnp.exp(scores - peak)
        own_weights = jnp.exp(own - peak)
        total = jnp.sum(weights, axis=1, keepdims=True) + jnp.sum(
            own_weights, axis=1, keepdims=True
        )
        mixed = dot_nn(weights.astype(BF16), values) + dot_nn(own_weights.astype(BF16), own_v)
        out = by_head(mixed) / by_head(total)
        mass = by_head(peak + jnp.log(total))
        for j in range(CHUNK):

            @pl.when(valid[c * CHUNK + j] > 0)
            def _(j=j):
                out_ref[where_[j]] = out[j * suf : (j + 1) * suf]
                mass_ref[where_[j]] = mass[j * suf : (j + 1) * suf]

        return 0

    lax.fori_loop(0, used[0], body, 0)


def root_attention(used, members, valid, chunk_tenant, root_len, coords, q, k, v, roots):
    reqs, suf, _ = q.shape
    shape = jax.ShapeDtypeStruct((reqs, suf, LANES), F32)
    vmem = pl.BlockSpec(memory_space=pltpu.VMEM)
    return pl.pallas_call(
        root_kernel,
        out_shape=(shape, shape),
        in_specs=[pl.BlockSpec(memory_space=pltpu.SMEM)] * 6 + [vmem] * 4,
        out_specs=(vmem, vmem),
        compiler_params=pltpu.CompilerParams(vmem_limit_bytes=40 << 20),
        cost_estimate=pl.CostEstimate(
            flops=4 << 30, bytes_accessed=4 << 20, transcendentals=4 << 20
        ),
    )(used, members, valid, chunk_tenant, root_len, coords, q, k, v, roots)


def merge_kernel(pos, dst_b, dst_l, back_ref, out_ref, mass_ref, send_ref, pick_ref):
    suf = out_ref.shape[1]
    reqs = out_ref.shape[0]
    per_block = reqs // N_BLK
    src = lax.broadcasted_iota(I32, (LANES, LANES), 0)
    dst = lax.broadcasted_iota(I32, (LANES, LANES), 1)
    for s in range(SLOTS):
        hit = (src // HD == dst // HD) & ((src % HD) // 3 == s)
        pick_ref[s] = jnp.where(hit, 1.0, 0.0).astype(BF16)

    def body(r, _):
        here = pos[r]
        outs = [out_ref[here]]
        masses = [mass_ref[here]]
        for table in (dst_b, dst_l):
            peer = table[r] // SLOTS
            slot = table[r] % SLOTS
            outs.append(back_ref[peer, slot].astype(F32))
            masses.append(dot_nn(back_ref[peer, SLOTS], pick_ref[slot]))
        top = jnp.maximum(jnp.maximum(masses[0], masses[1]), masses[2])
        parts = [jnp.exp(m - top) for m in masses]
        total = parts[0] + parts[1] + parts[2]
        attn = (parts[0] * outs[0] + parts[1] * outs[1] + parts[2] * outs[2]) / total
        attn = attn.astype(BF16)
        block = r // per_block
        core = block % 2
        for z in range(N_BLK // 2):
            send_ref[2 * z + core, block // 2, r % per_block] = attn
        return 0

    lax.fori_loop(0, reqs, body, 0)


def merge(pos, dst_b, dst_l, back, out, mass):
    reqs, suf, _ = out.shape
    vmem = pl.BlockSpec(memory_space=pltpu.VMEM)
    return pl.pallas_call(
        merge_kernel,
        out_shape=jax.ShapeDtypeStruct(
            (N_BLK, N_BLK // 2, reqs // N_BLK, suf, LANES), BF16
        ),
        in_specs=[pl.BlockSpec(memory_space=pltpu.SMEM)] * 3 + [vmem] * 3,
        out_specs=vmem,
        scratch_shapes=[pltpu.VMEM((SLOTS, LANES, LANES), BF16)],
        compiler_params=pltpu.CompilerParams(vmem_limit_bytes=30 << 20),
        cost_estimate=pl.CostEstimate(
            flops=1 << 27, bytes_accessed=4 << 20, transcendentals=1 << 20
        ),
    )(pos, dst_b, dst_l, back, out, mass)


def on_device(
    tokens,
    w_qkv,
    w_out,
    b_out,
    gain1,
    shift1,
    w_up,
    b_up,
    w_down,
    b_down,
    gain2,
    shift2,
    root_cache,
    node_cache,
    root_len,
    node_len,
    node_parent,
    node_place,
    req_leaf,
):
    req_dev, suf, width = tokens.shape
    cols = w_qkv.shape[2]
    own_rows = req_dev * suf
    reqs = req_leaf.shape[0]
    nodes = node_place.shape[0]
    node_max = node_cache.shape[2]
    tenants = root_cache.shape[1]
    root_per = root_cache.shape[2]
    blk = lax.axis_index("blk")
    owner = lax.axis_index("owner")
    my_z = owner // (NX * NY)
    my_x = (owner // NY) % NX
    my_y = owner % NY
    chip = blk // 2
    swap = xor_pairs(N_BLK, 1)
    n_own = N_BLK // 2

    tok = tokens.reshape(own_rows, width)
    half = [tok] + [lax.ppermute(tok, "blk", xor_pairs(N_BLK, 2 * k)) for k in range(1, n_own)]
    half = jnp.stack(half)
    other = lax.ppermute(half, "blk", swap)

    node_rows = node_cache.reshape(-1, LANES)
    root_rows = root_cache.reshape(-1, LANES)
    shard = jnp.concatenate([node_rows, root_rows], axis=0)
    n_owner = NX * NY * NZ
    shards = [shard] + [
        lax.ppermute(shard, "owner", xor_pairs(n_owner, k * NY)) for k in range(1, NX)
    ]
    caches = jnp.stack([s[: node_rows.shape[0]] for s in shards])
    caches = caches.reshape(NX, 2, 2, node_max, LANES)
    roots = jnp.stack([s[node_rows.shape[0] :] for s in shards])
    roots = jnp.stack([roots, lax.ppermute(roots, "owner", xor_pairs(n_owner, NX * NY))])
    y_groups = [[g * NY + y for y in range(NY)] for g in range(NZ * NX)]
    roots = lax.all_gather(roots, "owner", axis=0, tiled=False, axis_index_groups=y_groups)
    roots = roots.reshape(NY, NZ, NX, 2, tenants, root_per, LANES)

    w_out_all = lax.all_gather(w_out, "blk", axis=0, tiled=True)
    w_up_2 = lax.ppermute(w_up, "blk", swap)
    w_down_2 = lax.ppermute(w_down, "blk", swap)
    b_up_2 = lax.ppermute(b_up, "blk", swap)

    branch = node_parent[req_leaf]
    tenant = node_parent[branch]

    def slot_index(place):
        at = place // 2
        z, x, y = at // (NX * NY), (at // NY) % NX, at % NY
        return ((z * NY + y) * SLOTS + (x ^ my_x) * 2 + place % 2).astype(I32)

    dst_b = slot_index(node_place[branch])
    dst_l = slot_index(node_place[req_leaf])
    req_ids = jnp.arange(reqs, dtype=I32)
    rel = (req_ids // req_dev) ^ blk
    pos = ((rel % 2) * n_own + rel // 2) * req_dev + req_ids % req_dev
    local = jnp.arange(SLOTS, dtype=I32)
    local_slot = ((my_z * NX + ((local // 2) ^ my_x)) * NY + my_y) * 2 + local % 2
    lens = jnp.sum(jnp.where(local_slot[:, None] == node_place[None, :], node_len[None, :], 0), axis=1)
    same = tenant[:, None] == tenant[None, :]
    within = jnp.sum(jnp.where(same & (req_ids[None, :] < req_ids[:, None]), 1, 0), axis=1)
    tenant_ids = jnp.arange(tenants, dtype=I32)
    counts = jnp.sum(jnp.where(tenant_ids[:, None] == tenant[None, :], 1, 0), axis=1)
    chunks = (counts + CHUNK - 1) // CHUNK
    ends = jnp.sum(jnp.where(tenant_ids[None, :] <= tenant_ids[:, None], chunks[None, :], 0), axis=1)
    first = ends - chunks
    first_of = jnp.sum(jnp.where(tenant[:, None] == tenant_ids[None, :], first[None, :], 0), axis=1)
    place_in = first_of * CHUNK + within
    max_chunks = reqs // CHUNK + tenants - 1
    seats = jnp.arange(max_chunks * CHUNK, dtype=I32)
    seated = seats[:, None] == place_in[None, :]
    members = jnp.sum(jnp.where(seated, pos[None, :], 0), axis=1).astype(I32)
    valid = jnp.sum(jnp.where(seated, 1, 0), axis=1).astype(I32)
    chunk_ids = jnp.arange(max_chunks, dtype=I32)
    chunk_tenant = jnp.minimum(
        jnp.sum(jnp.where(chunk_ids[:, None] >= ends[None, :], 1, 0), axis=1), tenants - 1
    ).astype(I32)
    used = ends[-1:].astype(I32)
    coords = jnp.stack([my_z, my_x]).astype(I32)

    def project(which):
        w = w_qkv[:, which]
        out = jnp.concatenate(
            [jnp.dot(part.reshape(-1, width), w, preferred_element_type=F32) for part in (half, other)]
        )
        return out.astype(BF16).reshape(reqs, suf, cols)

    q = project(0) * jnp.asarray(HD**-0.5, BF16)
    outgoing = route(pos, dst_b, dst_l, q).reshape(PEERS, SLOTS, suf, cols)
    groups = [
        [(z * NX + x) * NY + y for z in range(NZ) for y in range(NY)] for x in range(NX)
    ]
    incoming = lax.all_to_all(
        outgoing, "owner", split_axis=0, concat_axis=0, axis_index_groups=groups, tiled=True
    )
    k_new = project(1)
    v_new = project(2)
    order = jnp.arange(N_BLK, dtype=I32) ^ blk
    order = (order % 2) * n_own + order // 2
    new_caches = jnp.stack([k_new, v_new]).reshape(2, N_BLK, req_dev, suf, cols)
    new_caches = jnp.take(new_caches, order, axis=1).reshape(2, reqs, suf, cols)

    answers = node_attention(lens, incoming, caches)
    back = lax.all_to_all(
        answers, "owner", split_axis=0, concat_axis=0, axis_index_groups=groups, tiled=True
    )
    out, mass = root_attention(
        used, members, valid, chunk_tenant, root_len, coords, q, k_new, v_new, roots
    )
    send = merge(pos, dst_b, dst_l, back, out, mass)
    half_rows = n_own * own_rows
    attn = lax.all_to_all(
        send.reshape(N_BLK, half_rows, cols), "blk", split_axis=0, concat_axis=0, tiled=True
    )
    attn = jnp.swapaxes(attn, 0, 1).reshape(half_rows, N_BLK * cols)
    residual = jnp.take(half, jnp.arange(n_own, dtype=I32) ^ chip, axis=0).reshape(half_rows, width)
    first_norm = layer_norm(
        residual.astype(F32)
        + jnp.dot(attn, w_out_all, preferred_element_type=F32)
        + b_out.astype(F32),
        gain1,
        shift1,
    ).astype(BF16)

    def feed(up, bias, down):
        inner = jnp.dot(first_norm, up, preferred_element_type=F32) + bias.astype(F32)
        hidden = jax.nn.gelu(inner, approximate=False).astype(BF16)
        return jnp.dot(hidden, down, preferred_element_type=F32)

    down = feed(w_up, b_up, w_down) + feed(w_up_2, b_up_2, w_down_2)
    down = down.astype(BF16).reshape(n_own, own_rows, width)

    def own_part(of_chip):
        return lax.dynamic_index_in_dim(down, of_chip, 0, keepdims=False)

    total = own_part(chip).astype(F32)
    for k in range(1, n_own):
        total = total + lax.ppermute(own_part(chip ^ k), "blk", xor_pairs(N_BLK, 2 * k)).astype(F32)
    own_norm = lax.dynamic_slice_in_dim(first_norm, chip * own_rows, own_rows, 0)
    result = layer_norm(
        own_norm.astype(F32) + total + b_down.astype(F32), gain2, shift2
    ).astype(BF16)
    return (result.reshape(req_dev, suf, width), new_caches)


def solution(mesh):
    in_specs = (
        P(("owner", "blk"), None, None),
        P(None, None, "blk"),
        P("blk", None),
        P(),
        P(),
        P(),
        P(None, "blk"),
        P("blk"),
        P("blk", None),
        P(),
        P(),
        P(),
        P(None, None, "owner", "blk"),
        P(None, "owner", None, "blk"),
        P(),
        P(),
        P(),
        P(),
        P("owner"),
    )
    out_specs = (P(("owner", "blk"), None, None), P(None, "owner", None, "blk"))
    return jax.shard_map(
        on_device, mesh=mesh, in_specs=in_specs, out_specs=out_specs, check_vma=False
    )
```

time: 549 us -> 284 us (0.52)
  waiting for transfers between devices: 284 us -> 101 us
  local copies, waits for them, and re-layouts: 110 us -> 9.94 us
  starting transfers between devices: 27.5 us -> 89.8 us
  matrix products: 61.6 us -> 20.4 us
  other arithmetic: 46.7 us -> 13 us
  Pallas kernels: 0 us -> 29.8 us
    all_gather x3 -> x2, waiting for transfers between devices: 174 us -> 0.02 us  [the longest x1 0.02 us: on_device(): lax.all_gather(roots, 'owner', axis=0, tiled=False, axis_index_groups=y_g...]
    reduce_scatter x2 -> x0, waiting for transfers between devices: 80.4 us -> none  [the longest x1 40.8 us: on_device(): lax.psum_scatter(jnp.dot(hidden, w_down, preferred_element_type=jnp.float...]
    ppermute x0 -> x14, starting transfers between devices: none -> 59.5 us  [the longest x1 13.5 us: on_device(): lax.ppermute(roots, 'owner', xor_pairs(n_owner, NX * NY))]
    dot_general x34 -> x9, matrix products: 61.6 us -> 20.4 us  [the longest x2 12.4 us: feed(): return jnp.dot(hidden, down, preferred_element_type=F32)]
    ppermute x0 -> x14, waiting for transfers between devices: none -> 40.5 us  [the longest x3 13.5 us: on_device(): lax.ppermute(shard, 'owner', xor_pairs(n_owner, k * NY))]
    select_n x8 -> x0, local copies, waits for them, and re-layouts: 32.8 us -> none  [the longest x4 16.4 us: root_block(): jnp.take(value_rows, tenant, axis=0)]
    all_to_all x3, waiting for transfers between devices: 27.9 us -> 59.4 us  [the longest x1 26.6 us: on_device(): lax.all_to_all(outgoing, 'owner', split_axis=0, concat_axis=0, axis_index...]
    pallas_call x0 -> x4, Pallas kernels: none -> 29.8 us  [the longest x1 12.9 us: node_attention(): pl.pallas_call(node_kernel, out_shape=jax.ShapeDtypeStruct((peers, slots...]
  transfers between devices with their start and end apart: 8 -> 19, of which waited for: 7 -> 11; matrix products, arithmetic and copies ran while one was open for 32% -> 10% of each run, Pallas kernels for 0% -> 11%
where the time goes in v1:
time: 284 us; the launch traced here: 279 us
  waiting for transfers between devices  101 us (36%)
  starting transfers between devices  89.8 us (32%)
  Pallas kernels  29.8 us (10%)
  matrix products  20.4 us (7%)
  between operations  14.9 us (5%)
  other arithmetic  13 us (5%)
  local copies, waits for them, and re-layouts  9.94 us (4%)
    all_to_all x1, waiting for transfers between devices, on_device(): lax.all_to_all(outgoing, 'owner', split_axis=0, concat_axis=0, axis_index...  26.6 us
    all_to_all x1, waiting for transfers between devices, on_device(): lax.all_to_all(send.reshape(N_BLK, half_rows, cols), 'blk', split_axis=0,...  16.6 us
    all_to_all x1, waiting for transfers between devices, on_device(): lax.all_to_all(answers, 'owner', split_axis=0, concat_axis=0, axis_index_...  16.2 us
    ppermute x3, waiting for transfers between devices, on_device(): lax.ppermute(shard, 'owner', xor_pairs(n_owner, k * NY))  13.5 us
    ppermute x1, starting transfers between devices, on_device(): lax.ppermute(roots, 'owner', xor_pairs(n_owner, NX * NY))  13.5 us
    pallas_call x1, Pallas kernels, node_attention(): pl.pallas_call(node_kernel, out_shape=jax.ShapeDtypeStruct((peers, slots...  12.9 us
    ppermute x3, starting transfers between devices, on_device(): lax.ppermute(tok, 'blk', xor_pairs(N_BLK, 2 * k))  12.9 us
    dot_general x2, matrix products, feed(): return jnp.dot(hidden, down, preferred_element_type=F32)  12.4 us
  transfers between devices with their start and end apart: 19, of which 11 were waited for; matrix products, arithmetic and copies ran while one was open for 10% of the time, Pallas kernels for 11%

profile of v1, /device:TPU:1, one launch (start us, length us, event | category | flops | bytes accessed | tf_op | source)
XLA Modules:
  0.0 278.6 jit_solution(4228680570680910536)
XLA Ops:
  7.2 1.1 pad_maximum_fusion.3
  8.3 5.2 %collective-permute-start.6 = (bf16[1664,128]{1,0:T(8,128)(2,1)S(1)}, bf16[1664,128]{1,0:T(8,128)(2,1)S(1)}, u32[]{:S(2)}, u32[]{:S(2)}) collective-permute-start(bf16[1664,128]{1,0:T(8,128)(2,1)S(1)} %pad_maximum_fusion.3), channel_id=1, source_target_pairs={{0,24},{1,25},{2,26},{3,27},{4,28},{5,29},{6,30},{7,31},{8,16},{9,... | collective-permute-start | bytes 1277960 | tf_op jit(solution)/shard_map/ppermute | solution.py:310
  13.6 2.4 collective-permute-start.5
  16.0 2.0 collective-permute-start.4
  18.0 8.9 %collective-permute-done.6 = bf16[1664,128]{1,0:T(8,128)(2,1)S(1)} collective-permute-done((bf16[1664,128]{1,0:T(8,128)(2,1)S(1)}, bf16[1664,128]{1,0:T(8,128)(2,1)S(1)}, u32[]{:S(2)}, u32[]{:S(2)}) %collective-permute-start.6) | collective-permute-done | bytes 426016 | tf_op jit(solution)/shard_map/ppermute | solution.py:310
  26.9 4.6 %collective-permute-done.4 = bf16[1664,128]{1,0:T(8,128)(2,1)S(1)} collective-permute-done((bf16[1664,128]{1,0:T(8,128)(2,1)S(1)}, bf16[1664,128]{1,0:T(8,128)(2,1)S(1)}, u32[]{:S(2)}, u32[]{:S(2)}) %collective-permute-start.4) | collective-permute-done | bytes 426016 | tf_op jit(solution)/shard_map/ppermute | solution.py:310
  31.5 0.8 fusion.193
  32.3 13.5 %collective-permute-start.7 = (bf16[4,128,128]{2,1,0:T(8,128)(2,1)S(1)}, bf16[4,128,128]{2,1,0:T(8,128)(2,1)S(1)}, u32[]{:S(2)}, u32[]{:S(2)}) collective-permute-start(bf16[4,128,128]{2,1,0:T(8,128)(2,1)S(1)} %get-tuple-element.14), channel_id=1, source_target_pairs={{0,32},{1,33},{2,34},{3,35},{4,36},{5,37},{6,38},{7,39},{8,40},{9,... | collective-permute-start | bytes 393224 | tf_op jit(solution)/shard_map/ppermute | solution.py:315
  45.8 2.4 collective-permute-done.7
  49.0 3.1 %collective-permute-start = (bf16[128,1024]{1,0:T(8,128)(2,1)S(1)}, bf16[128,1024]{1,0:T(8,128)(2,1)S(1)}, u32[]{:S(2)}, u32[]{:S(2)}) collective-permute-start(bf16[128,1024]{1,0:T(8,128)(2,1)S(1)} %bitcast.113), channel_id=1, source_target_pairs={{0,128},{64,192},{128,0},{192,64},{256,384},{320,448},{384,256},{4... | collective-permute-start | bytes 786440 | tf_op jit(solution)/shard_map/ppermute | solution.py:301
  52.1 6.6 %collective-permute-start.1 = (bf16[128,1024]{1,0:T(8,128)(2,1)S(1)}, bf16[128,1024]{1,0:T(8,128)(2,1)S(1)}, u32[]{:S(2)}, u32[]{:S(2)}) collective-permute-start(bf16[128,1024]{1,0:T(8,128)(2,1)S(1)} %bitcast.114), channel_id=1, source_target_pairs={{0,256},{64,320},{128,384},{192,448},{256,0},{320,64},{384,128},{4... | collective-permute-start | bytes 786440 | tf_op jit(solution)/shard_map/ppermute | solution.py:301
  58.8 3.1 %collective-permute-start.2 = (bf16[128,1024]{1,0:T(8,128)(2,1)S(1)}, bf16[128,1024]{1,0:T(8,128)(2,1)S(1)}, u32[]{:S(2)}, u32[]{:S(2)}) collective-permute-start(bf16[128,1024]{1,0:T(8,128)(2,1)S(1)} %bitcast.115), channel_id=1, source_target_pairs={{0,384},{64,448},{128,256},{192,320},{256,128},{320,192},{384,0},{... | collective-permute-start | bytes 786440 | tf_op jit(solution)/shard_map/ppermute | solution.py:301
  62.5 2.4 collective-permute-done.1
  64.9 9.5 %collective-permute-done.2 = bf16[128,1024]{1,0:T(8,128)(2,1)S(1)} collective-permute-done((bf16[128,1024]{1,0:T(8,128)(2,1)S(1)}, bf16[128,1024]{1,0:T(8,128)(2,1)S(1)}, u32[]{:S(2)}, u32[]{:S(2)}) %collective-permute-start.2) | collective-permute-done | bytes 262176 | tf_op jit(solution)/shard_map/ppermute | solution.py:301
  74.6 7.8 %collective-permute-start.3 = (bf16[4,128,1024]{2,1,0:T(8,128)(2,1)S(1)}, bf16[4,128,1024]{2,1,0:T(8,128)(2,1)S(1)}, u32[]{:S(2)}, u32[]{:S(2)}) collective-permute-start(bf16[4,128,1024]{2,1,0:T(8,128)(2,1)S(1)} %pad_maximum_fusion.1), channel_id=1, source_target_pairs={{0,64},{64,0},{128,192},{192,128},{256,320},{320,256},{384,448},{4... | collective-permute-start | bytes 3145736 | tf_op jit(solution)/shard_map/ppermute | solution.py:303
  86.6 0.8 maximum_multiply_fusion
  87.3 2.5 shard_map.194
  89.8 11.7 %all-to-all-start = ((bf16[16,8,32,128]{3,2,1,0:T(8,128)(2,1)}), bf16[16,8,32,128]{3,2,1,0:T(8,128)(2,1)S(1)}, u32[]{:S(2)}, u32[]{:S(2)}) async-start(bf16[16,8,32,128]{3,2,1,0:T(8,128)(2,1)} %bitcast.102), calls=%async_computation | async-start | bytes 2097152 | tf_op jit(solution)/shard_map/all_to_all | solution.py:374
  104.1 26.6 %all-to-all-done.q_ref = bf16[16,8,32,128]{3,2,1,0:T(8,128)(2,1)S(1)} async-done(((bf16[16,8,32,128]{3,2,1,0:T(8,128)(2,1)}), bf16[16,8,32,128]{3,2,1,0:T(8,128)(2,1)S(1)}, u32[]{:S(2)}, u32[]{:S(2)}) %all-to-all-start) | async-done | bytes 1048608 | tf_op jit(solution)/shard_map/all_to_all | solution.py:374
  130.7 12.9 %shard_map.195 = bf16[16,9,32,128]{3,2,1,0:T(8,128)(2,1)} custom-call(s32[8]{0:T(128)S(1)} %select_reduce_fusion.3.lens, bf16[16,8,32,128]{3,2,1,0:T(8,128)(2,1)S(1)} %all-to-all-done.q_ref, bf16[4,2,2,384,128]{4,3,2,1,0:T(8,128)(2,1)S(1)} %pad_maximum_fusion.k_ref.v_ref, bf16[4,2,2,384,128]{4,3,2,1,0:T(8,128)(2,1)S(1)} %pad_maximum_fusion.k_ref.v_ref), custom_call_target="tpu_custom_call" | custom-call | flops 2147483648 | bytes 4194304 | tf_op jit(solution)/shard_map/pallas_call | solution.py:122
  143.6 9.6 %all-to-all-start.1 = ((bf16[16,9,32,128]{3,2,1,0:T(8,128)(2,1)}), bf16[16,9,32,128]{3,2,1,0:T(8,128)(2,1)S(1)}, u32[]{:S(2)}, u32[]{:S(2)}) async-start(bf16[16,9,32,128]{3,2,1,0:T(8,128)(2,1)} %shard_map.195), calls=%async_computation.1 | async-start | bytes 2359296 | tf_op jit(solution)/shard_map/all_to_all | solution.py:385
  154.1 1.4 fusion.93
  155.5 1.4 fusion.89
  157.9 1.6 copy-done.7
  159.5 8.7 %shard_map.196 = (f32[32,32,128]{2,1,0:T(8,128)S(1)}, f32[32,32,128]{2,1,0:T(8,128)S(1)}) custom-call(s32[1]{0:T(128)} %slice.34.used, s32[44]{0:T(128)S(1)} %get-tuple-element.7.members, s32[44]{0:T(128)S(1)} %get-tuple-element.6.valid, s32[11]{0:T(128)S(1)} %broadcast_minimum_fusion.chunk_tenant, s32[4]{0:T(128)S(1)} %copy-done.8, ...), custom_call_target="tpu_custom_call" | custom-call | flops 4294967296 | bytes 4194304 | tf_op jit(solution)/shard_map/pallas_call | solution.py:199
  168.2 0.8 copy-done.2
  169.0 16.2 %all-to-all-done.1.back_ref = bf16[16,9,32,128]{3,2,1,0:T(8,128)(2,1)S(1)} async-done(((bf16[16,9,32,128]{3,2,1,0:T(8,128)(2,1)}), bf16[16,9,32,128]{3,2,1,0:T(8,128)(2,1)S(1)}, u32[]{:S(2)}, u32[]{:S(2)}) %all-to-all-start.1) | async-done | bytes 1179680 | tf_op jit(solution)/shard_map/all_to_all | solution.py:385
  185.2 1.0 copy-done.3
  186.3 5.8 %shard_map.197 = bf16[8,4,4,32,128]{4,3,2,1,0:T(8,128)(2,1)S(1)} custom-call(s32[32]{0:T(128)S(1)} %copy-done.4, s32[32]{0:T(128)S(1)} %copy-done.6, s32[32]{0:T(128)S(1)} %copy-done.5, bf16[16,9,32,128]{3,2,1,0:T(8,128)(2,1)S(1)} %all-to-all-done.1.back_ref, f32[32,32,128]{2,1,0:T(8,128)S(1)} %get-tuple-element.4.out_ref, f32[32,32,128]{2,1,0:T(8,128)S(1)} %copy-done.3), custom_call_target="tpu_custom_call" | custom-call | flops 134217728 | bytes 4194304 | tf_op jit(solution)/shard_map/pallas_call | solution.py:247
  192.1 1.3 copy.26
  193.4 9.0 %all-to-all-start.2 = ((bf16[8,512,128]{1,2,0:T(8,128)(2,1)}), bf16[8,512,128]{1,2,0:T(8,128)(2,1)}, u32[]{:S(2)}, u32[]{:S(2)}) async-start(bf16[8,512,128]{1,2,0:T(8,128)(2,1)} %copy.26), calls=%async_computation.2 | async-start | bytes 2097152 | tf_op jit(solution)/shard_map/all_to_all | solution.py:393
  202.4 1.9 collective-permute-start.10
  204.3 2.4 collective-permute-start.8
  206.8 2.1 collective-permute-start.9
  210.4 1.2 bitcast_select_fusion
  211.6 16.6 %all-to-all-done.2 = bf16[8,512,128]{1,2,0:T(8,128)(2,1)} async-done(((bf16[8,512,128]{1,2,0:T(8,128)(2,1)}), bf16[8,512,128]{1,2,0:T(8,128)(2,1)}, u32[]{:S(2)}, u32[]{:S(2)}) %all-to-all-start.2) | async-done | bytes 1048608 | tf_op jit(solution)/shard_map/all_to_all | solution.py:393
  228.3 3.5 %fusion.196 = (f32[512]{0:T(512)S(1)}, f32[512,1024]{1,0:T(8,128)S(1)}) fusion(f32[1024]{0:T(1024)S(1)} %convert_element_type.104, bf16[512,1024]{0,1:T(8,128)(2,1)} %bitcast.36, bf16[1024,1024]{1,0:T(8,128)(2,1)} %all-gather.4.cloned.1.call-done, bf16[512,1024]{1,0:T(8,128)(2,1)} %bitcast_select_fusion), kind=kOutput, calls=%fused_computation.342 | convolution fusion | flops 1075838464 | bytes 6297600 | tf_op jit(solution)/shard_map/dot_general | solution.py:400
  232.2 1.4 add_convert_fusion.1
  233.6 6.7 %fusion.20 = f32[512,1024]{1,0:T(8,128)} fusion(bf16[512,1024]{1,0:T(8,128)(2,1)} %param.27, bf16[512,1024]{1,0:T(8,128)(2,1)} %add_convert_fusion.1, bf16[1024,512]{1,0:T(8,128)(2,1)} %param.25, f32[512]{0:T(512)S(1)} %convert_element_type.109), kind=kOutput, calls=%fused_computation.55 | convolution fusion | flops 1091043328 | bytes 5244928 | tf_op jit(solution)/shard_map/dot_general | solution.py:409
  240.3 5.7 %add_convert_fusion = bf16[512,1024]{1,0:T(8,128)(2,1)S(1)} fusion(f32[512,1024]{1,0:T(8,128)} %fusion.20, bf16[512,1024]{1,0:T(8,128)(2,1)} %collective-permute-done.10, bf16[512,1024]{1,0:T(8,128)(2,1)S(1)} %copy-done.13, bf16[1024,512]{1,0:T(8,128)(2,1)} %collective-permute-done.8, f32[512]{0:T(512)S(1)} %convert_element_type.111), kind=kOutput, calls=%fused_computation.6 | convolution fusion | flops 1092091904 | bytes 6293504 | tf_op jit(solution)/shard_map/dot_general | solution.py:409
  246.1 1.9 collective-permute-start.11
  248.0 3.6 %collective-permute-start.12 = (bf16[128,1024]{1,0:T(8,128)(2,1)S(1)}, bf16[128,1024]{1,0:T(8,128)(2,1)}, u32[]{:S(2)}, u32[]{:S(2)}) collective-permute-start(bf16[128,1024]{1,0:T(8,128)(2,1)S(1)} %get-tuple-element.12), channel_id=1, source_target_pairs={{0,256},{64,320},{128,384},{192,448},{256,0},{320,64},{384,128},{4... | collective-permute-start | bytes 786440 | tf_op jit(solution)/shard_map/ppermute | solution.py:419
  251.6 3.8 %collective-permute-start.13 = (bf16[128,1024]{1,0:T(8,128)(2,1)S(1)}, bf16[128,1024]{1,0:T(8,128)(2,1)}, u32[]{:S(2)}, u32[]{:S(2)}) collective-permute-start(bf16[128,1024]{1,0:T(8,128)(2,1)S(1)} %get-tuple-element.11), channel_id=1, source_target_pairs={{0,384},{64,448},{128,256},{192,320},{256,128},{320,192},{384,0},{... | collective-permute-start | bytes 786440 | tf_op jit(solution)/shard_map/ppermute | solution.py:419
  256.1 0.9 broadcast_select_fusion
  257.0 0.8 collective-permute-done.11
  257.8 11.3 %collective-permute-done.12 = bf16[128,1024]{1,0:T(8,128)(2,1)} collective-permute-done((bf16[128,1024]{1,0:T(8,128)(2,1)S(1)}, bf16[128,1024]{1,0:T(8,128)(2,1)}, u32[]{:S(2)}, u32[]{:S(2)}) %collective-permute-start.12) | collective-permute-done | bytes 262176 | tf_op jit(solution)/shard_map/ppermute | solution.py:419
  269.2 1.5 fusion.194
  270.9 0.9 add_convert_fusion.2
  (145 shorter events, 12.7 us)
Async XLA Ops:
  7.2 75.3 %copy-start = (s32[128]{0:T(128)S(1)}, s32[128]{0:T(128)}, u32[]{:S(2)}) copy-start(s32[128]{0:T(128)} %param.35) | copy-start | bytes 1540
  7.2 41.8 %copy-start.20 = (bf16[4,32,1024]{2,1,0:T(8,128)(2,1)S(1)}, bf16[4,32,1024]{2,1,0:T(8,128)(2,1)}, u32[]{:S(2)}) copy-start(bf16[4,32,1024]{2,1,0:T(8,128)(2,1)} %param.19) | copy-start | bytes 786436
  7.2 54.7 %copy-start.28 = (s32[32]{0:T(128)S(1)}, s32[32]{0:T(128)}, u32[]{:S(2)}) copy-start(s32[32]{0:T(128)} %param.37) | copy-start | bytes 388
  7.2 150.7 %all-gather.6.cloned.1.call-start = ((), (), s32[]{:S(2)}) async-start(), calls=%async_computation.4 | async-start | bytes 2359296 | tf_op jit(solution)/shard_map/all_gather | solution.py:317
  8.3 74.8 %copy-start.9 = (s32[128]{0:T(128)S(1)}, s32[128]{0:T(128)}, u32[]{:S(2)}) copy-start(s32[128]{0:T(128)} %param.36) | copy-start | bytes 1540
  8.3 18.6 %collective-permute-start.6 = (bf16[1664,128]{1,0:T(8,128)(2,1)S(1)}, bf16[1664,128]{1,0:T(8,128)(2,1)S(1)}, u32[]{:S(2)}, u32[]{:S(2)}) collective-permute-start(bf16[1664,128]{1,0:T(8,128)(2,1)S(1)} %pad_maximum_fusion.3), channel_id=1, source_target_pairs={{0,24},{1,25},{2,26},{3,27},{4,28},{5,29},{6,30},{7,31},{8,16},{9,... | collective-permute-start | bytes 1277960 | tf_op jit(solution)/shard_map/ppermute | solution.py:310
  13.6 13.3 %collective-permute-start.5 = (bf16[1664,128]{1,0:T(8,128)(2,1)S(1)}, bf16[1664,128]{1,0:T(8,128)(2,1)S(1)}, u32[]{:S(2)}, u32[]{:S(2)}) collective-permute-start(bf16[1664,128]{1,0:T(8,128)(2,1)S(1)} %pad_maximum_fusion.3), channel_id=1, source_target_pairs={{0,16},{1,17},{2,18},{3,19},{4,20},{5,21},{6,22},{7,23},{8,24},{9,... | collective-permute-start | bytes 1277960 | tf_op jit(solution)/shard_map/ppermute | solution.py:310
  16.0 15.5 %collective-permute-start.4 = (bf16[1664,128]{1,0:T(8,128)(2,1)S(1)}, bf16[1664,128]{1,0:T(8,128)(2,1)S(1)}, u32[]{:S(2)}, u32[]{:S(2)}) collective-permute-start(bf16[1664,128]{1,0:T(8,128)(2,1)S(1)} %pad_maximum_fusion.3), channel_id=1, source_target_pairs={{0,8},{1,9},{2,10},{3,11},{4,12},{5,13},{6,14},{7,15},{8,0},{9,1},... | collective-permute-start | bytes 1277960 | tf_op jit(solution)/shard_map/ppermute | solution.py:310
  26.9 47.6 %copy-start.16 = (bf16[1664,128]{1,0:T(8,128)(2,1)}, bf16[1664,128]{1,0:T(8,128)(2,1)S(1)}, u32[]{:S(2)}) copy-start(bf16[1664,128]{1,0:T(8,128)(2,1)S(1)} %collective-permute-done.5) | copy-start | bytes 1277956
  31.5 43.0 %copy-start.18 = (bf16[1664,128]{1,0:T(8,128)(2,1)}, bf16[1664,128]{1,0:T(8,128)(2,1)S(1)}, u32[]{:S(2)}) copy-start(bf16[1664,128]{1,0:T(8,128)(2,1)S(1)} %collective-permute-done.4) | copy-start | bytes 1277956
  32.3 15.9 %collective-permute-start.7 = (bf16[4,128,128]{2,1,0:T(8,128)(2,1)S(1)}, bf16[4,128,128]{2,1,0:T(8,128)(2,1)S(1)}, u32[]{:S(2)}, u32[]{:S(2)}) collective-permute-start(bf16[4,128,128]{2,1,0:T(8,128)(2,1)S(1)} %get-tuple-element.14), channel_id=1, source_target_pairs={{0,32},{1,33},{2,34},{3,35},{4,36},{5,37},{6,38},{7,39},{8,40},{9,... | collective-permute-start | bytes 393224 | tf_op jit(solution)/shard_map/ppermute | solution.py:315
  49.0 36.7 %copy-start.32 = (bf16[1024,3,128]{2,0,1:T(8,128)(2,1)S(1)}, bf16[1024,3,128]{2,0,1:T(8,128)(2,1)}, u32[]{:S(2)}) copy-start(bf16[1024,3,128]{2,0,1:T(8,128)(2,1)} %param.20) | copy-start | bytes 2359300
  49.0 13.5 %collective-permute-start = (bf16[128,1024]{1,0:T(8,128)(2,1)S(1)}, bf16[128,1024]{1,0:T(8,128)(2,1)S(1)}, u32[]{:S(2)}, u32[]{:S(2)}) collective-permute-start(bf16[128,1024]{1,0:T(8,128)(2,1)S(1)} %bitcast.113), channel_id=1, source_target_pairs={{0,128},{64,192},{128,0},{192,64},{256,384},{320,448},{384,256},{4... | collective-permute-start | bytes 786440 | tf_op jit(solution)/shard_map/ppermute | solution.py:301
  52.1 12.8 %collective-permute-start.1 = (bf16[128,1024]{1,0:T(8,128)(2,1)S(1)}, bf16[128,1024]{1,0:T(8,128)(2,1)S(1)}, u32[]{:S(2)}, u32[]{:S(2)}) collective-permute-start(bf16[128,1024]{1,0:T(8,128)(2,1)S(1)} %bitcast.114), channel_id=1, source_target_pairs={{0,256},{64,320},{128,384},{192,448},{256,0},{320,64},{384,128},{4... | collective-permute-start | bytes 786440 | tf_op jit(solution)/shard_map/ppermute | solution.py:301
  58.8 15.7 %collective-permute-start.2 = (bf16[128,1024]{1,0:T(8,128)(2,1)S(1)}, bf16[128,1024]{1,0:T(8,128)(2,1)S(1)}, u32[]{:S(2)}, u32[]{:S(2)}) collective-permute-start(bf16[128,1024]{1,0:T(8,128)(2,1)S(1)} %bitcast.115), channel_id=1, source_target_pairs={{0,384},{64,448},{128,256},{192,320},{256,128},{320,192},{384,0},{... | collective-permute-start | bytes 786440 | tf_op jit(solution)/shard_map/ppermute | solution.py:301
  74.6 12.0 %copy-start.10 = (bf16[4,128,1024]{2,1,0:T(8,128)(2,1)}, bf16[4,128,1024]{2,1,0:T(8,128)(2,1)S(1)}, u32[]{:S(2)}) copy-start(bf16[4,128,1024]{2,1,0:T(8,128)(2,1)S(1)} %pad_maximum_fusion.1) | copy-start | bytes 3145732
  74.6 11.5 %collective-permute-start.3 = (bf16[4,128,1024]{2,1,0:T(8,128)(2,1)S(1)}, bf16[4,128,1024]{2,1,0:T(8,128)(2,1)S(1)}, u32[]{:S(2)}, u32[]{:S(2)}) collective-permute-start(bf16[4,128,1024]{2,1,0:T(8,128)(2,1)S(1)} %pad_maximum_fusion.1), channel_id=1, source_target_pairs={{0,64},{64,0},{128,192},{192,128},{256,320},{320,256},{384,448},{4... | collective-permute-start | bytes 3145736 | tf_op jit(solution)/shard_map/ppermute | solution.py:303
  86.1 3.7 %copy-start.30 = (bf16[4,128,1024]{2,1,0:T(8,128)(2,1)}, bf16[4,128,1024]{2,1,0:T(8,128)(2,1)S(1)}, u32[]{:S(2)}) copy-start(bf16[4,128,1024]{2,1,0:T(8,128)(2,1)S(1)} %collective-permute-done.3) | copy-start | bytes 3145732
  87.3 16.2 %copy-start.29 = (s32[128]{0:T(128)S(1)}, s32[128]{0:T(128)}, u32[]{:S(2)}) copy-start(s32[128]{0:T(128)} %param.34) | copy-start | bytes 1540
  87.3 16.4 %copy-start.19 = (bf16[1664,128]{1,0:T(8,128)(2,1)S(1)}, bf16[1664,128]{1,0:T(8,128)(2,1)}, u32[]{:S(2)}) copy-start(bf16[1664,128]{1,0:T(8,128)(2,1)} %copy-done.18) | copy-start | bytes 1277956
  89.8 14.0 %copy-start.17 = (bf16[1664,128]{1,0:T(8,128)(2,1)S(1)}, bf16[1664,128]{1,0:T(8,128)(2,1)}, u32[]{:S(2)}) copy-start(bf16[1664,128]{1,0:T(8,128)(2,1)} %copy-done.16) | copy-start | bytes 1277956
  89.8 40.9 %all-to-all-start = ((bf16[16,8,32,128]{3,2,1,0:T(8,128)(2,1)}), bf16[16,8,32,128]{3,2,1,0:T(8,128)(2,1)S(1)}, u32[]{:S(2)}, u32[]{:S(2)}) async-start(bf16[16,8,32,128]{3,2,1,0:T(8,128)(2,1)} %bitcast.102), calls=%async_computation | async-start | bytes 2097152 | tf_op jit(solution)/shard_map/all_to_all | solution.py:374
  101.5 2.4 copy-start.14
  101.5 110.1 %all-gather.4.cloned.1.call-start = ((), (), s32[]{:S(2)}) async-start(), calls=%async_computation.3 | async-start | bytes 2359296 | tf_op jit(solution)/shard_map/all_gather | solution.py:320
  143.6 10.4 %copy-start.4 = (s32[32]{0:T(128)S(1)}, s32[32]{0:T(128)}, u32[]{:S(2)}) copy-start(s32[32]{0:T(128)} %get-tuple-element.18.pos) | copy-start | bytes 388
  143.6 10.5 %copy-start.11 = (bf16[4,128,1024]{2,1,0:T(8,128)(2,1)S(1)}, bf16[4,128,1024]{2,1,0:T(8,128)(2,1)}, u32[]{:S(2)}) copy-start(bf16[4,128,1024]{2,1,0:T(8,128)(2,1)} %copy-done.10) | copy-start | bytes 3145732
  143.6 41.7 %all-to-all-start.1 = ((bf16[16,9,32,128]{3,2,1,0:T(8,128)(2,1)}), bf16[16,9,32,128]{3,2,1,0:T(8,128)(2,1)S(1)}, u32[]{:S(2)}, u32[]{:S(2)}) async-start(bf16[16,9,32,128]{3,2,1,0:T(8,128)(2,1)} %shard_map.195), calls=%async_computation.1 | async-start | bytes 2359296 | tf_op jit(solution)/shard_map/all_to_all | solution.py:385
  153.2 3.7 %copy-start.31 = (bf16[4,128,1024]{2,1,0:T(8,128)(2,1)S(1)}, bf16[4,128,1024]{2,1,0:T(8,128)(2,1)}, u32[]{:S(2)}) copy-start(bf16[4,128,1024]{2,1,0:T(8,128)(2,1)} %copy-done.30) | copy-start | bytes 3145732
  153.2 3.7 %copy-start.33 = (bf16[1024,3,128]{2,0,1:T(8,128)(2,1)S(1)}, bf16[1024,3,128]{2,0,1:T(8,128)(2,1)}, u32[]{:S(2)}) copy-start(bf16[1024,3,128]{2,0,1:T(8,128)(2,1)} %param.20) | copy-start | bytes 2359300
  159.5 25.7 %copy-start.5 = (s32[32]{0:T(128)S(1)}, s32[32]{0:T(128)}, u32[]{:S(2)}) copy-start(s32[32]{0:T(128)} %fusion.109.dst_l) | copy-start | bytes 388
  159.5 25.7 %copy-start.6 = (s32[32]{0:T(128)S(1)}, s32[32]{0:T(128)}, u32[]{:S(2)}) copy-start(s32[32]{0:T(128)} %fusion.107.dst_b) | copy-start | bytes 388
  192.1 14.7 %copy-start.27 = (bf16[512]{0:T(512)(128)(2,1)S(1)}, bf16[512]{0:T(512)(128)(2,1)}, u32[]{:S(2)}) copy-start(bf16[512]{0:T(512)(128)(2,1)} %param.26) | copy-start | bytes 3076
  192.1 16.9 %copy-start.21 = (bf16[1024]{0:T(1024)(128)(2,1)S(1)}, bf16[1024]{0:T(1024)(128)(2,1)}, u32[]{:S(2)}) copy-start(bf16[1024]{0:T(1024)(128)(2,1)} %param.22) | copy-start | bytes 6148
  192.1 16.9 %copy-start.22 = (bf16[1024]{0:T(1024)(128)(2,1)S(1)}, bf16[1024]{0:T(1024)(128)(2,1)}, u32[]{:S(2)}) copy-start(bf16[1024]{0:T(1024)(128)(2,1)} %param.23) | copy-start | bytes 6148
  192.1 17.0 %copy-start.23 = (bf16[1024]{0:T(1024)(128)(2,1)S(1)}, bf16[1024]{0:T(1024)(128)(2,1)}, u32[]{:S(2)}) copy-start(bf16[1024]{0:T(1024)(128)(2,1)} %param.24) | copy-start | bytes 6148
  192.1 17.0 %copy-start.24 = (bf16[1024]{0:T(1024)(128)(2,1)S(1)}, bf16[1024]{0:T(1024)(128)(2,1)}, u32[]{:S(2)}) copy-start(bf16[1024]{0:T(1024)(128)(2,1)} %param.28) | copy-start | bytes 6148
  192.1 17.0 %copy-start.25 = (bf16[1024]{0:T(1024)(128)(2,1)S(1)}, bf16[1024]{0:T(1024)(128)(2,1)}, u32[]{:S(2)}) copy-start(bf16[1024]{0:T(1024)(128)(2,1)} %param.29) | copy-start | bytes 6148
  192.1 17.1 %copy-start.26 = (bf16[1024]{0:T(1024)(128)(2,1)S(1)}, bf16[1024]{0:T(1024)(128)(2,1)}, u32[]{:S(2)}) copy-start(bf16[1024]{0:T(1024)(128)(2,1)} %param.30) | copy-start | bytes 6148
  193.4 16.4 %copy-start.12 = (bf16[4,128,1024]{2,1,0:T(8,128)(2,1)S(1)}, bf16[4,128,1024]{2,1,0:T(8,128)(2,1)}, u32[]{:S(2)}) copy-start(bf16[4,128,1024]{2,1,0:T(8,128)(2,1)} %copy-done.10) | copy-start | bytes 3145732
  193.4 34.8 %all-to-all-start.2 = ((bf16[8,512,128]{1,2,0:T(8,128)(2,1)}), bf16[8,512,128]{1,2,0:T(8,128)(2,1)}, u32[]{:S(2)}, u32[]{:S(2)}) async-start(bf16[8,512,128]{1,2,0:T(8,128)(2,1)} %copy.26), calls=%async_computation.2 | async-start | bytes 2097152 | tf_op jit(solution)/shard_map/all_to_all | solution.py:393
  202.4 37.9 %collective-permute-start.10 = (bf16[512,1024]{1,0:T(8,128)(2,1)}, bf16[512,1024]{1,0:T(8,128)(2,1)}, u32[]{:S(2)}, u32[]{:S(2)}) collective-permute-start(bf16[512,1024]{1,0:T(8,128)(2,1)} %param.27), channel_id=1, source_target_pairs={{0,64},{64,0},{128,192},{192,128},{256,320},{320,256},{384,448},{4... | collective-permute-start | bytes 3145736 | tf_op jit(solution)/shard_map/ppermute | solution.py:322
  204.3 35.9 %collective-permute-start.8 = (bf16[1024,512]{1,0:T(8,128)(2,1)}, bf16[1024,512]{1,0:T(8,128)(2,1)}, u32[]{:S(2)}, u32[]{:S(2)}) collective-permute-start(bf16[1024,512]{1,0:T(8,128)(2,1)} %param.25), channel_id=1, source_target_pairs={{0,64},{64,0},{128,192},{192,128},{256,320},{320,256},{384,448},{4... | collective-permute-start | bytes 3145736 | tf_op jit(solution)/shard_map/ppermute | solution.py:321
  206.8 3.0 %collective-permute-start.9 = (bf16[512]{0:T(512)(128)(2,1)S(1)}, bf16[512]{0:T(512)(128)(2,1)S(1)}, u32[]{:S(2)}, u32[]{:S(2)}) collective-permute-start(bf16[512]{0:T(512)(128)(2,1)S(1)} %copy-done.27), channel_id=1, source_target_pairs={{0,64},{64,0},{128,192},{192,128},{256,320},{320,256},{384,448},{4... | collective-permute-start | bytes 3080 | tf_op jit(solution)/shard_map/ppermute | solution.py:323
  233.6 6.7 %copy-start.13 = (bf16[512,1024]{1,0:T(8,128)(2,1)S(1)}, bf16[512,1024]{1,0:T(8,128)(2,1)}, u32[]{:S(2)}) copy-start(bf16[512,1024]{1,0:T(8,128)(2,1)} %add_convert_fusion.1) | copy-start | bytes 3145732
  246.0 9.4 %copy-start.15 = (bf16[512,1024]{1,0:T(8,128)(2,1)}, bf16[512,1024]{1,0:T(8,128)(2,1)S(1)}, u32[]{:S(2)}) copy-start(bf16[512,1024]{1,0:T(8,128)(2,1)S(1)} %add_convert_fusion) | copy-start | bytes 3145732
  246.1 11.8 %collective-permute-start.11 = (bf16[128,1024]{1,0:T(8,128)(2,1)S(1)}, bf16[128,1024]{1,0:T(8,128)(2,1)}, u32[]{:S(2)}, u32[]{:S(2)}) collective-permute-start(bf16[128,1024]{1,0:T(8,128)(2,1)S(1)} %get-tuple-element.10), channel_id=1, source_target_pairs={{0,128},{64,192},{128,0},{192,64},{256,384},{320,448},{384,256},{4... | collective-permute-start | bytes 786440 | tf_op jit(solution)/shard_map/ppermute | solution.py:419
  248.0 21.2 %collective-permute-start.12 = (bf16[128,1024]{1,0:T(8,128)(2,1)S(1)}, bf16[128,1024]{1,0:T(8,128)(2,1)}, u32[]{:S(2)}, u32[]{:S(2)}) collective-permute-start(bf16[128,1024]{1,0:T(8,128)(2,1)S(1)} %get-tuple-element.12), channel_id=1, source_target_pairs={{0,256},{64,320},{128,384},{192,448},{256,0},{320,64},{384,128},{4... | collective-permute-start | bytes 786440 | tf_op jit(solution)/shard_map/ppermute | solution.py:419
  251.6 17.6 %collective-permute-start.13 = (bf16[128,1024]{1,0:T(8,128)(2,1)S(1)}, bf16[128,1024]{1,0:T(8,128)(2,1)}, u32[]{:S(2)}, u32[]{:S(2)}) collective-permute-start(bf16[128,1024]{1,0:T(8,128)(2,1)S(1)} %get-tuple-element.11), channel_id=1, source_target_pairs={{0,384},{64,448},{128,256},{192,320},{256,128},{320,192},{384,0},{... | collective-permute-start | bytes 786440 | tf_op jit(solution)/shard_map/ppermute | solution.py:419
  (5 other events, 5.4 us)
Sparse Core Ops, SparseCore 0:
  49.1 45.4 all-gather.5
  104.4 48.5 all-gather.3

commit v2 on v1

--- a/solution.py
+++ b/solution.py
@@ -15,8 +15,9 @@
 LANES = 128
 N_BLK = 8
 NX, NY, NZ = 4, 8, 2
-PEERS = NZ * NY
-SLOTS = 2 * NX
+PEERS = NX * NY
+SLOTS = 2 * NZ
+HALF = 16
 CHUNK = 4
 NEG = -1e30
 EPS = 1e-05
@@ -81,60 +82,70 @@
 def node_kernel(lens, q_ref, k_ref, v_ref, out_ref):
     slot = pl.program_id(0)
     peers, _, suf, _ = q_ref.shape
-    group = 4
+    group = 8
     rows = group * suf
     node_max = k_ref.shape[2]
-    keys = k_ref[0, 0]
-    values = v_ref[0, 0]
+    keys = both_heads(k_ref[0, 0])
+    values = both_heads(v_ref[0, 0])
     keep = lax.broadcasted_iota(I32, (1, node_max), 1) < lens[slot]
-    bias = jnp.where(keep, 0.0, NEG)
-    lane = lax.broadcasted_iota(I32, (rows, LANES), 1) % HD
+    lane = lax.broadcasted_iota(I32, (group, HALF, LANES), 2)
+    piece = lane % (HD // 2) - 3 * slot
 
     @pl.when(slot == 0)
     def _():
-        out_ref[:, SLOTS] = jnp.zeros((peers, suf, LANES), BF16)
+        out_ref[:, 2 * SLOTS] = jnp.zeros((peers, HALF, LANES), BF16)
 
     for g in range(peers // group):
         part = slice(g * group, (g + 1) * group)
         q = q_ref[part, slot].reshape(rows, LANES)
-        scores = jnp.where(keep, dot_nt(both_heads(q), keys), NEG)
-        peak = jnp.max(scores, axis=1, keepdims=True)
-        weights = jnp.exp(scores - peak)
-        total = jnp.sum(weights, axis=1, keepdims=True)
-        mixed = by_head(dot_nn(weights.astype(BF16), values))
-        out = mixed / by_head(total)
-        out_ref[part, slot] = out.astype(BF16).reshape(group, suf, LANES)
-        mass = by_head(peak + jnp.log(total))
-        high = mass.astype(BF16)
-        rest = mass - high.astype(F32)
-        mid = rest.astype(BF16)
-        low = (rest - mid.astype(F32)).astype(BF16)
-        held = out_ref[part, SLOTS].reshape(rows, LANES)
-        held = jnp.where(lane == 3 * slot, high, held)
-        held = jnp.where(lane == 3 * slot + 1, mid, held)
-        held = jnp.where(lane == 3 * slot + 2, low, held)
-        out_ref[part, SLOTS] = held.reshape(group, suf, LANES)
+        scores = dot_nt(q, keys)
+        weights, totals, masses = [], [], []
+        for h in range(2):
+            own = jnp.where(keep, scores[:, h * node_max : (h + 1) * node_max], NEG)
+            peak = jnp.max(own, axis=1, keepdims=True)
+            weight = jnp.exp(own - peak)
+            total = jnp.sum(weight, axis=1, keepdims=True)
+            weights.append(weight.astype(BF16))
+            totals.append(total)
+            masses.append(peak + jnp.log(total))
+        mixed = dot_nn(jnp.concatenate(weights, axis=1), values)
+        total = by_head(jnp.concatenate(totals, axis=0))
+        mass = by_head(jnp.concatenate(masses, axis=0))
+        out = (mixed / total).astype(BF16).reshape(group, 2, HALF, LANES)
+        out_ref[part, 2 * slot] = out[:, 0]
+        out_ref[part, 2 * slot + 1] = out[:, 1]
+        mass = mass.reshape(group, 2, HALF, LANES)
+        mass = jnp.where(lane % HD < HD // 2, mass[:, 0], mass[:, 1])
+        high = mass.astype(BF16).astype(F32)
+        rest = mass - high
+        mid = rest.astype(BF16).astype(F32)
+        sent = jnp.where(piece == 0, high, jnp.where(piece == 1, mid, rest - mid))
+        held = out_ref[part, 2 * SLOTS].astype(F32)
+        held = jnp.where((piece >= 0) & (piece < 3), sent, held)
+        out_ref[part, 2 * SLOTS] = held.astype(BF16)
 
 
 def node_attention(lens, queries, caches):
     peers, slots, suf, _ = queries.shape
     node_max = caches.shape[3]
+
+    def cache_spec(which):
+        return pl.BlockSpec(
+            (1, 1, pl.Squeezed(), node_max, LANES), lambda s, n: (s // 2, which, s % 2, 0, 0)
+        )
+
     return pl.pallas_call(
         node_kernel,
-        out_shape=jax.ShapeDtypeStruct((peers, slots + 1, suf, LANES), BF16),
+        out_shape=jax.ShapeDtypeStruct((peers, 2 * slots + 1, HALF, LANES), BF16),
         grid_spec=pltpu.PrefetchScalarGridSpec(
             num_scalar_prefetch=1,
             grid=(slots,),
             in_specs=[
                 pl.BlockSpec((peers, slots, suf, LANES), lambda s, n: (0, 0, 0, 0)),
-                pl.BlockSpec(
-                    (1, 1, pl.Squeezed(), node_max, LANES), lambda s, n: (s // 2, 0, s % 2, 0, 0)
-                ),
-                pl.BlockSpec(
-                    (1, 1, pl.Squeezed(), node_max, LANES), lambda s, n: (s // 2, 1, s % 2, 0, 0)
-                ),
+                cache_spec(0),
+                cache_spec(1),
             ],
-            out_specs=pl.BlockSpec((peers, slots + 1, suf, LANES), lambda s, n: (0, 0, 0, 0)),
+            out_specs=pl.BlockSpec((peers, 2 * slots + 1, HALF, LANES), lambda s, n: (0, 0, 0, 0)),
         ),
         compiler_params=pltpu.CompilerParams(vmem_limit_bytes=40 << 20),
         cost_estimate=pl.CostEstimate(
@@ -161,8 +172,8 @@
         values = root_ref[:, :, :, 1, tenant].reshape(root_rows, LANES)
         n = lax.broadcasted_iota(I32, (1, root_rows), 1)
         row = n % per
-        x = (n // per) % NX
-        z = (n // (per * NX)) % NZ
+        z = (n // per) % NZ
+        x = (n // (per * NZ)) % NX
         y = n // (per * NX * NZ)
         place = (((z ^ coords[0]) * NX + (x ^ coords[1])) * NY + y) * per + row
         scores = jnp.where(place < root_len[tenant], dot_nt(q, keys), NEG)
@@ -208,15 +219,18 @@
     )(used, members, valid, chunk_tenant, root_len, coords, q, k, v, roots)
 
 
-def merge_kernel(pos, dst_b, dst_l, back_ref, out_ref, mass_ref, send_ref, pick_ref):
-    suf = out_ref.shape[1]
-    reqs = out_ref.shape[0]
+def merge_kernel(pos, dst_b, dst_l, back_ref, out_ref, mass_ref, send_ref, node_mass):
+    reqs, suf, _ = out_ref.shape
     per_block = reqs // N_BLK
     src = lax.broadcasted_iota(I32, (LANES, LANES), 0)
     dst = lax.broadcasted_iota(I32, (LANES, LANES), 1)
+    packed = back_ref[:, 2 * SLOTS].reshape(PEERS * HALF, LANES)
     for s in range(SLOTS):
-        hit = (src // HD == dst // HD) & ((src % HD) // 3 == s)
-        pick_ref[s] = jnp.where(hit, 1.0, 0.0).astype(BF16)
+        for g in range(2):
+            hit = (src // HD == dst // HD) & ((src % HD) // (HD // 2) == g)
+            hit = hit & ((src % (HD // 2)) // 3 == s)
+            pick = jnp.where(hit, 1.0, 0.0).astype(BF16)
+            node_mass[:, s, g] = dot_nn(packed, pick).reshape(PEERS, HALF, LANES)
 
     def body(r, _):
         here = pos[r]
@@ -225,20 +239,19 @@
         for table in (dst_b, dst_l):
             peer = table[r] // SLOTS
             slot = table[r] % SLOTS
-            outs.append(back_ref[peer, slot].astype(F32))
-            masses.append(dot_nn(back_ref[peer, SLOTS], pick_ref[slot]))
+            outs.append(back_ref[peer, pl.ds(2 * slot, 2)].astype(F32).reshape(suf, LANES))
+            masses.append(node_mass[peer, slot].reshape(suf, LANES))
         top = jnp.maximum(jnp.maximum(masses[0], masses[1]), masses[2])
         parts = [jnp.exp(m - top) for m in masses]
         total = parts[0] + parts[1] + parts[2]
         attn = (parts[0] * outs[0] + parts[1] * outs[1] + parts[2] * outs[2]) / total
         attn = attn.astype(BF16)
         block = r // per_block
-        core = block % 2
-        for z in range(N_BLK // 2):
-            send_ref[2 * z + core, block // 2, r % per_block] = attn
+        send_ref[block, 0, r % per_block] = attn
+        send_ref[(block + N_BLK // 2) % N_BLK, 1, r % per_block] = attn
         return 0
 
-    lax.fori_loop(0, reqs, body, 0)
+    lax.fori_loop(0, reqs, body, 0, unroll=2)
 
 
 def merge(pos, dst_b, dst_l, back, out, mass):
@@ -246,17 +259,62 @@
     vmem = pl.BlockSpec(memory_space=pltpu.VMEM)
     return pl.pallas_call(
         merge_kernel,
-        out_shape=jax.ShapeDtypeStruct(
-            (N_BLK, N_BLK // 2, reqs // N_BLK, suf, LANES), BF16
-        ),
+        out_shape=jax.ShapeDtypeStruct((N_BLK, 2, reqs // N_BLK, suf, LANES), BF16),
         in_specs=[pl.BlockSpec(memory_space=pltpu.SMEM)] * 3 + [vmem] * 3,
         out_specs=vmem,
-        scratch_shapes=[pltpu.VMEM((SLOTS, LANES, LANES), BF16)],
+        scratch_shapes=[pltpu.VMEM((PEERS, SLOTS, 2, HALF, LANES), F32)],
         compiler_params=pltpu.CompilerParams(vmem_limit_bytes=30 << 20),
         cost_estimate=pl.CostEstimate(
             flops=1 << 27, bytes_accessed=4 << 20, transcendentals=1 << 20
         ),
     )(pos, dst_b, dst_l, back, out, mass)
+
+
+def rows_norm(values, gain, shift):
+    center = values - jnp.mean(values, axis=1, keepdims=True)
+    spread = jnp.mean(center * center, axis=1, keepdims=True)
+    return center * lax.rsqrt(spread + EPS) * gain + shift
+
+
+def feed_kernel(attn_ref, w_out_ref, tok_a, tok_b, vec_ref, w0, w1, w2, w3, norm_ref, own_ref, far_ref):
+    rows = tok_a.shape[0]
+    width = tok_a.shape[1]
+    attn = jnp.concatenate([attn_ref[h] for h in range(N_BLK)], axis=1)
+    tok = jnp.concatenate([tok_a[...], tok_b[...]], axis=0).astype(F32)
+    vec = vec_ref[...].astype(F32)
+    mixed = tok + dot_nn(attn, w_out_ref[...]) + vec[0:1]
+    norm = rows_norm(mixed, vec[1:2], vec[2:3]).astype(BF16)
+    norm_ref[...] = norm[:rows]
+    total = jnp.zeros((2 * rows, width), F32)
+    units = w0.shape[1]
+    for w in (w0, w1, w2, w3):
+        inner = dot_nn(norm, w[:width]) + w[width + 2 * units : width + 2 * units + 16].astype(F32)[0:1]
+        hidden = (0.5 * inner * (1.0 + lax.erf(inner * (0.5**0.5)))).astype(BF16)
+        down = [
+            dot_nn(hidden, w[width + i * units : width + (i + 1) * units]) for i in range(width // units)
+        ]
+        total = total + jnp.concatenate(down, axis=1)
+    own_ref[...] = total[:rows]
+    far_ref[...] = total[rows:].astype(BF16)
+
+
+def feed_forward(attn, w_out, tok_a, tok_b, vectors, packs):
+    rows, width = tok_a.shape
+    vmem = pl.BlockSpec(memory_space=pltpu.VMEM)
+    return pl.pallas_call(
+        feed_kernel,
+        out_shape=(
+            jax.ShapeDtypeStruct((rows, width), BF16),
+            jax.ShapeDtypeStruct((rows, width), F32),
+            jax.ShapeDtypeStruct((rows, width), BF16),
+        ),
+        in_specs=[vmem] * 9,
+        out_specs=(vmem, vmem, vmem),
+        compiler_params=pltpu.CompilerParams(vmem_limit_bytes=48 << 20),
+        cost_estimate=pl.CostEstimate(
+            flops=3 << 30, bytes_accessed=12 << 20, transcendentals=1 << 20
+        ),
+    )(attn, w_out, tok_a, tok_b, vectors, *packs)
 
 
 def on_device(
@@ -293,34 +351,46 @@
     my_z = owner // (NX * NY)
     my_x = (owner // NY) % NX
     my_y = owner % NY
-    chip = blk // 2
     swap = xor_pairs(N_BLK, 1)
     n_own = N_BLK // 2
 
+    def zero_after(value):
+        flat = value.reshape(-1, value.shape[-1])
+        return jnp.minimum(jnp.abs(flat[:1, :1]), 0)
+
     tok = tokens.reshape(own_rows, width)
     half = [tok] + [lax.ppermute(tok, "blk", xor_pairs(N_BLK, 2 * k)) for k in range(1, n_own)]
+    tok_far = half[2]
+    first_come, last_come = half[1], half[3]
     half = jnp.stack(half)
     other = lax.ppermute(half, "blk", swap)
 
-    node_rows = node_cache.reshape(-1, LANES)
-    root_rows = root_cache.reshape(-1, LANES)
-    shard = jnp.concatenate([node_rows, root_rows], axis=0)
     n_owner = NX * NY * NZ
-    shards = [shard] + [
-        lax.ppermute(shard, "owner", xor_pairs(n_owner, k * NY)) for k in range(1, NX)
-    ]
-    caches = jnp.stack([s[: node_rows.shape[0]] for s in shards])
-    caches = caches.reshape(NX, 2, 2, node_max, LANES)
-    roots = jnp.stack([s[node_rows.shape[0] :] for s in shards])
+    roots = root_cache.reshape(-1, LANES) + zero_after(first_come)
     roots = jnp.stack([roots, lax.ppermute(roots, "owner", xor_pairs(n_owner, NX * NY))])
+    roots = jnp.stack(
+        [roots] + [lax.ppermute(roots, "owner", xor_pairs(n_owner, k * NY)) for k in range(1, NX)]
+    )
     y_groups = [[g * NY + y for y in range(NY)] for g in range(NZ * NX)]
     roots = lax.all_gather(roots, "owner", axis=0, tiled=False, axis_index_groups=y_groups)
-    roots = roots.reshape(NY, NZ, NX, 2, tenants, root_per, LANES)
-
-    w_out_all = lax.all_gather(w_out, "blk", axis=0, tiled=True)
-    w_up_2 = lax.ppermute(w_up, "blk", swap)
-    w_down_2 = lax.ppermute(w_down, "blk", swap)
-    b_up_2 = lax.ppermute(b_up, "blk", swap)
+    roots = roots.reshape(NY, NX, NZ, 2, tenants, root_per, LANES)
+
+    node_rows = node_cache.reshape(-1, LANES) + zero_after(last_come)
+    node_far = lax.ppermute(node_rows, "owner", xor_pairs(n_owner, NX * NY))
+    caches = jnp.stack([node_rows, node_far]).reshape(NZ, 2, 2, node_max, LANES)
+
+    w_out_all = lax.all_gather(w_out + zero_after(last_come), "blk", axis=0, tiled=True)
+    units = w_up.shape[1]
+    pack = jnp.concatenate(
+        [w_up]
+        + [w_down[:, i * units : (i + 1) * units] for i in range(width // units)]
+        + [jnp.broadcast_to(b_up[None, :], (16, units))],
+        axis=0,
+    )
+    pack_side = lax.ppermute(pack, "blk", swap)
+    pack_next = lax.ppermute(pack + zero_after(node_far), "blk", xor_pairs(N_BLK, 2))
+    pack_last = lax.ppermute(pack_next, "blk", swap)
+    packs = [pack, pack_side, pack_next, pack_last]
 
     branch = node_parent[req_leaf]
     tenant = node_parent[branch]
@@ -328,7 +398,7 @@
     def slot_index(place):
         at = place // 2
         z, x, y = at // (NX * NY), (at // NY) % NX, at % NY
-        return ((z * NY + y) * SLOTS + (x ^ my_x) * 2 + place % 2).astype(I32)
+        return ((x * NY + y) * SLOTS + (z ^ my_z) * 2 + place % 2).astype(I32)
 
     dst_b = slot_index(node_place[branch])
     dst_l = slot_index(node_place[req_leaf])
@@ -336,7 +406,7 @@
     rel = (req_ids // req_dev) ^ blk
     pos = ((rel % 2) * n_own + rel // 2) * req_dev + req_ids % req_dev
     local = jnp.arange(SLOTS, dtype=I32)
-    local_slot = ((my_z * NX + ((local // 2) ^ my_x)) * NY + my_y) * 2 + local % 2
+    local_slot = ((((local // 2) ^ my_z) * NX + my_x) * NY + my_y) * 2 + local % 2
     lens = jnp.sum(jnp.where(local_slot[:, None] == node_place[None, :], node_len[None, :], 0), axis=1)
     same = tenant[:, None] == tenant[None, :]
     within = jnp.sum(jnp.where(same & (req_ids[None, :] < req_ids[:, None]), 1, 0), axis=1)
@@ -368,9 +438,7 @@
 
     q = project(0) * jnp.asarray(HD**-0.5, BF16)
     outgoing = route(pos, dst_b, dst_l, q).reshape(PEERS, SLOTS, suf, cols)
-    groups = [
-        [(z * NX + x) * NY + y for z in range(NZ) for y in range(NY)] for x in range(NX)
-    ]
+    groups = [[z * PEERS + p for p in range(PEERS)] for z in range(NZ)]
     incoming = lax.all_to_all(
         outgoing, "owner", split_axis=0, concat_axis=0, axis_index_groups=groups, tiled=True
     )
@@ -389,35 +457,12 @@
         used, members, valid, chunk_tenant, root_len, coords, q, k_new, v_new, roots
     )
     send = merge(pos, dst_b, dst_l, back, out, mass)
-    half_rows = n_own * own_rows
     attn = lax.all_to_all(
-        send.reshape(N_BLK, half_rows, cols), "blk", split_axis=0, concat_axis=0, tiled=True
-    )
-    attn = jnp.swapaxes(attn, 0, 1).reshape(half_rows, N_BLK * cols)
-    residual = jnp.take(half, jnp.arange(n_own, dtype=I32) ^ chip, axis=0).reshape(half_rows, width)
-    first_norm = layer_norm(
-        residual.astype(F32)
-        + jnp.dot(attn, w_out_all, preferred_element_type=F32)
-        + b_out.astype(F32),
-        gain1,
-        shift1,
-    ).astype(BF16)
-
-    def feed(up, bias, down):
-        inner = jnp.dot(first_norm, up, preferred_element_type=F32) + bias.astype(F32)
-        hidden = jax.nn.gelu(inner, approximate=False).astype(BF16)
-        return jnp.dot(hidden, down, preferred_element_type=F32)
-
-    down = feed(w_up, b_up, w_down) + feed(w_up_2, b_up_2, w_down_2)
-    down = down.astype(BF16).reshape(n_own, own_rows, width)
-
-    def own_part(of_chip):
-        return lax.dynamic_index_in_dim(down, of_chip, 0, keepdims=False)
-
-    total = own_part(chip).astype(F32)
-    for k in range(1, n_own):
-        total = total + lax.ppermute(own_part(chip ^ k), "blk", xor_pairs(N_BLK, 2 * k)).astype(F32)
-    own_norm = lax.dynamic_slice_in_dim(first_norm, chip * own_rows, own_rows, 0)
+        send.reshape(N_BLK, 2 * own_rows, cols), "blk", split_axis=0, concat_axis=0, tiled=True
+    )
+    vectors = jnp.stack([b_out, gain1, shift1])
+    own_norm, down, down_far = feed_forward(attn, w_out_all, tok, tok_far, vectors, packs)
+    total = down + lax.ppermute(down_far, "blk", xor_pairs(N_BLK, N_BLK // 2)).astype(F32)
     result = layer_norm(
         own_norm.astype(F32) + total + b_down.astype(F32), gain2, shift2
     ).astype(BF16)

time: 284 us -> 248 us (0.87); the launches traced: 279 us -> 247 us
  starting transfers between devices: 89.8 us -> 72.5 us
  matrix products: 20.4 us -> 6.64 us
  waiting for transfers between devices: 101 us -> 88.7 us
  Pallas kernels: 29.8 us -> 35.4 us
  local copies, waits for them, and re-layouts: 9.94 us -> 13.6 us
    ppermute x9 -> x8, waiting for transfers between devices: 26.1 us -> 64.8 us  [the longest x1 30.3 us: on_device(): lax.ppermute(pack + zero_after(node_far), 'blk', xor_pairs(N_BLK, 2))]
    all_to_all x1, waiting for transfers between devices: 26.6 us -> 4.62 us  [on_device(): lax.all_to_all(outgoing, 'owner', split_axis=0, concat_axis=0, axis_index...]
    all_to_all x1, waiting for transfers between devices: 16.2 us -> 0.01 us  [on_device(): lax.all_to_all(answers, 'owner', split_axis=0, concat_axis=0, axis_index_...]
    dot_general x3 -> x0, matrix products: 15.9 us -> none  [the longest x2 12.4 us: feed(): return jnp.dot(hidden, down, preferred_element_type=F32)]
    ppermute x3, waiting for transfers between devices: 12 us -> 0.01 us  [on_device(): lax.ppermute(tok, 'blk', xor_pairs(N_BLK, 2 * k))]
    pallas_call x2 -> x3, Pallas kernels: 18.7 us -> 24.2 us  [the longest x1 14.1 us: node_attention(): pl.pallas_call(node_kernel, out_shape=jax.ShapeDtypeStruct((peers, 2 * sl...]
    add x4 -> x8, other arithmetic: 1.08 us -> 5.91 us  [the longest x1 2.28 us: on_device(): pack + zero_after(node_far)]
    ppermute x1, starting transfers between devices: 13.5 us -> 8.68 us  [on_device(): lax.ppermute(roots, 'owner', xor_pairs(n_owner, NX * NY))]
  transfers between devices with their start and end apart: 19 -> 18, of which waited for: 11 -> 8; matrix products, arithmetic and copies ran while one was open for 10% -> 10% of each run, Pallas kernels for 11% -> 11%
where the time goes in v2:
time: 248 us; the launch traced here: 247 us
  waiting for transfers between devices  88.7 us (36%)
  starting transfers between devices  72.5 us (29%)
  Pallas kernels  35.4 us (14%)
  between operations  16.7 us (7%)
  local copies, waits for them, and re-layouts  13.6 us (5%)
  other arithmetic  13.2 us (5%)
  matrix products  6.64 us (3%)
    ppermute x1, waiting for transfers between devices, on_device(): lax.ppermute(pack + zero_after(node_far), 'blk', xor_pairs(N_BLK, 2))  30.3 us
    ppermute x1, waiting for transfers between devices, on_device(): node_far = lax.ppermute(node_rows, 'owner', xor_pairs(n_owner, NX * NY))  18.4 us
    pallas_call x1, Pallas kernels, node_attention(): pl.pallas_call(node_kernel, out_shape=jax.ShapeDtypeStruct((peers, 2 * sl...  14.1 us
    all_to_all x1, waiting for transfers between devices, on_device(): lax.all_to_all(send.reshape(N_BLK, 2 * own_rows, cols), 'blk', split_axis...  14.1 us
    ppermute x3, starting transfers between devices, on_device(): lax.ppermute(tok, 'blk', xor_pairs(N_BLK, 2 * k))  12.7 us
    ppermute x1, waiting for transfers between devices, on_device(): lax.ppermute(down_far, 'blk', xor_pairs(N_BLK, N_BLK // 2)).astype(F32)  12.1 us
    ppermute x3, starting transfers between devices, on_device(): lax.ppermute(roots, 'owner', xor_pairs(n_owner, k * NY))  9.58 us
    pallas_call x1, Pallas kernels, root_attention(): pl.pallas_call(root_kernel, out_shape=(shape, shape), in_specs=[pl.BlockS...  8.71 us
  transfers between devices with their start and end apart: 18, of which 8 were waited for; matrix products, arithmetic and copies ran while one was open for 10% of the time, Pallas kernels for 11%

profile of v2, /device:TPU:1, one launch (start us, length us, event | category | flops | bytes accessed | tf_op | source)
XLA Modules:
  0.0 246.6 jit_solution(10314975026908484396)
XLA Ops:
  7.2 5.0 %collective-permute-start = (bf16[128,1024]{1,0:T(8,128)(2,1)}, bf16[128,1024]{1,0:T(8,128)(2,1)S(1)}, u32[]{:S(2)}, u32[]{:S(2)}) collective-permute-start(bf16[128,1024]{1,0:T(8,128)(2,1)} %bitcast.68), channel_id=1, source_target_pairs={{0,128},{64,192},{128,0},{192,64},{256,384},{320,448},{384,256},{4... | collective-permute-start | bytes 786440 | tf_op jit(solution)/shard_map/ppermute | solution.py:362
  12.2 5.8 %collective-permute-start.1 = (bf16[128,1024]{1,0:T(8,128)(2,1)}, bf16[128,1024]{1,0:T(8,128)(2,1)S(1)}, u32[]{:S(2)}, u32[]{:S(2)}) collective-permute-start(bf16[128,1024]{1,0:T(8,128)(2,1)} %bitcast.69), channel_id=1, source_target_pairs={{0,256},{64,320},{128,384},{192,448},{256,0},{320,64},{384,128},{4... | collective-permute-start | bytes 786440 | tf_op jit(solution)/shard_map/ppermute | solution.py:362
  18.0 1.9 collective-permute-start.2
  20.6 0.7 gather_fusion
  21.3 0.7 gather_fusion.3
  23.2 0.8 broadcast_add_fusion.3
  24.0 8.7 %collective-permute-start.5 = (bf16[128,128]{1,0:T(8,128)(2,1)S(1)}, bf16[128,128]{1,0:T(8,128)(2,1)S(1)}, u32[]{:S(2)}, u32[]{:S(2)}) collective-permute-start(bf16[128,128]{1,0:T(8,128)(2,1)S(1)} %bitcast.86), channel_id=1, source_target_pairs={{0,32},{1,33},{2,34},{3,35},{4,36},{5,37},{6,38},{7,39},{8,40},{9,... | collective-permute-start | bytes 98312 | tf_op jit(solution)/shard_map/ppermute | solution.py:370
  32.9 5.1 %collective-permute-done.5 = bf16[128,128]{1,0:T(8,128)(2,1)S(1)} collective-permute-done((bf16[128,128]{1,0:T(8,128)(2,1)S(1)}, bf16[128,128]{1,0:T(8,128)(2,1)S(1)}, u32[]{:S(2)}, u32[]{:S(2)}) %collective-permute-start.5) | collective-permute-done | bytes 32800 | tf_op jit(solution)/shard_map/ppermute | solution.py:370
  38.0 3.1 %collective-permute-start.6 = (bf16[2,128,128]{2,1,0:T(8,128)(2,1)S(1)}, bf16[2,128,128]{2,1,0:T(8,128)(2,1)S(1)}, u32[]{:S(2)}, u32[]{:S(2)}) collective-permute-start(bf16[2,128,128]{2,1,0:T(8,128)(2,1)S(1)} %get-tuple-element.21), channel_id=1, source_target_pairs={{0,8},{1,9},{2,10},{3,11},{4,12},{5,13},{6,14},{7,15},{8,0},{9,1},... | collective-permute-start | bytes 196616 | tf_op jit(solution)/shard_map/ppermute | solution.py:372
  41.1 4.4 %collective-permute-start.7 = (bf16[2,128,128]{2,1,0:T(8,128)(2,1)S(1)}, bf16[2,128,128]{2,1,0:T(8,128)(2,1)S(1)}, u32[]{:S(2)}, u32[]{:S(2)}) collective-permute-start(bf16[2,128,128]{2,1,0:T(8,128)(2,1)S(1)} %get-tuple-element.21), channel_id=1, source_target_pairs={{0,16},{1,17},{2,18},{3,19},{4,20},{5,21},{6,22},{7,23},{8,24},{9,... | collective-permute-start | bytes 196616 | tf_op jit(solution)/shard_map/ppermute | solution.py:372
  45.5 2.1 collective-permute-start.8
  48.3 3.5 %collective-permute-done.8 = bf16[2,128,128]{2,1,0:T(8,128)(2,1)S(1)} collective-permute-done((bf16[2,128,128]{2,1,0:T(8,128)(2,1)S(1)}, bf16[2,128,128]{2,1,0:T(8,128)(2,1)S(1)}, u32[]{:S(2)}, u32[]{:S(2)}) %collective-permute-start.8) | collective-permute-done | bytes 65568 | tf_op jit(solution)/shard_map/ppermute | solution.py:372
  51.7 0.7 pad_maximum_fusion.4
  52.7 5.5 %collective-permute-start.3 = (bf16[4,128,1024]{2,1,0:T(8,128)(2,1)S(1)}, bf16[4,128,1024]{2,1,0:T(8,128)(2,1)S(1)}, u32[]{:S(2)}, u32[]{:S(2)}) collective-permute-start(bf16[4,128,1024]{2,1,0:T(8,128)(2,1)S(1)} %pad_maximum_fusion.1), channel_id=1, source_target_pairs={{0,64},{64,0},{128,192},{192,128},{256,320},{320,256},{384,448},{4... | collective-permute-start | bytes 3145736 | tf_op jit(solution)/shard_map/ppermute | solution.py:366
  58.3 0.7 gather_fusion.1
  59.0 0.7 gather_fusion.2
  62.1 1.4 convolution_convert_fusion.1
  63.6 1.6 convolution_convert_fusion
  65.2 0.8 maximum_multiply_fusion
  65.9 2.5 %shard_map.194 = bf16[128,32,128]{2,1,0:T(8,128)(2,1)} custom-call(s32[32]{0:T(128)} %get-tuple-element.24.pos, s32[32]{0:T(128)} %get-tuple-element.22.dst_b, s32[32]{0:T(128)} %get-tuple-element.23.dst_l, bf16[32,32,128]{2,1,0:T(8,128)(2,1)} %bitcast.62), custom_call_target="tpu_custom_call" | custom-call | bytes 3145728 | tf_op jit(solution)/shard_map/pallas_call | solution.py:72
  68.4 7.4 %all-to-all-start = ((bf16[32,4,32,128]{3,2,1,0:T(8,128)(2,1)}), bf16[32,4,32,128]{3,2,1,0:T(8,128)(2,1)S(1)}, u32[]{:S(2)}, u32[]{:S(2)}) async-start(bf16[32,4,32,128]{3,2,1,0:T(8,128)(2,1)} %bitcast.75), calls=%async_computation | async-start | bytes 2097152 | tf_op jit(solution)/shard_map/all_to_all | solution.py:442
  75.9 5.0 %collective-permute-start.4 = (bf16[1536,128]{1,0:T(8,128)(2,1)S(1)}, bf16[1536,128]{1,0:T(8,128)(2,1)S(1)}, u32[]{:S(2)}, u32[]{:S(2)}) collective-permute-start(bf16[1536,128]{1,0:T(8,128)(2,1)S(1)} %bitcast.82), channel_id=1, source_target_pairs={{0,32},{1,33},{2,34},{3,35},{4,36},{5,37},{6,38},{7,39},{8,40},{9,... | collective-permute-start | bytes 1179656 | tf_op jit(solution)/shard_map/ppermute | solution.py:379
  80.9 1.3 fusion.44
  82.2 18.4 %collective-permute-done.4 = bf16[1536,128]{1,0:T(8,128)(2,1)S(1)} collective-permute-done((bf16[1536,128]{1,0:T(8,128)(2,1)S(1)}, bf16[1536,128]{1,0:T(8,128)(2,1)S(1)}, u32[]{:S(2)}, u32[]{:S(2)}) %collective-permute-start.4) | collective-permute-done | bytes 393248 | tf_op jit(solution)/shard_map/ppermute | solution.py:379
  101.7 2.3 broadcast_add_fusion
  104.0 1.9 collective-permute-start.10
  106.2 1.7 broadcast_add_fusion.2
  108.0 4.6 %all-to-all-done.q_ref = bf16[32,4,32,128]{3,2,1,0:T(8,128)(2,1)S(1)} async-done(((bf16[32,4,32,128]{3,2,1,0:T(8,128)(2,1)}), bf16[32,4,32,128]{3,2,1,0:T(8,128)(2,1)S(1)}, u32[]{:S(2)}, u32[]{:S(2)}) %all-to-all-start) | async-done | bytes 1048608 | tf_op jit(solution)/shard_map/all_to_all | solution.py:442
  112.6 14.1 %shard_map.195 = bf16[32,9,16,128]{3,2,1,0:T(8,128)(2,1)} custom-call(s32[4]{0:T(128)S(1)} %select_reduce_fusion.7.lens, bf16[32,4,32,128]{3,2,1,0:T(8,128)(2,1)S(1)} %all-to-all-done.q_ref, bf16[2,2,2,384,128]{4,3,2,1,0:T(8,128)(2,1)S(1)} %pad_maximum_fusion.2.k_ref.v_ref, bf16[2,2,2,384,128]{4,3,2,1,0:T(8,128)(2,1)S(1)} %pad_maximum_fusion.2.k_ref.v_ref), custom_call_target="tpu_custom_call" | custom-call | flops 2147483648 | bytes 4194304 | tf_op jit(solution)/shard_map/pallas_call | solution.py:137
  126.7 7.8 %all-to-all-start.1 = ((bf16[32,9,16,128]{3,2,1,0:T(8,128)(2,1)}), bf16[32,9,16,128]{3,2,1,0:T(8,128)(2,1)S(1)}, u32[]{:S(2)}, u32[]{:S(2)}) async-start(bf16[32,9,16,128]{3,2,1,0:T(8,128)(2,1)} %shard_map.195), calls=%async_computation.1 | async-start | bytes 2359296 | tf_op jit(solution)/shard_map/all_to_all | solution.py:453
  135.8 0.7 select_reduce_fusion
  137.1 1.4 fusion.6
  138.5 2.6 %collective-permute-start.9 = (bf16[2064,512]{1,0:T(8,128)(2,1)}, bf16[2064,512]{1,0:T(8,128)(2,1)}, u32[]{:S(2)}, u32[]{:S(2)}) collective-permute-start(bf16[2064,512]{1,0:T(8,128)(2,1)} %get-tuple-element.17.w0), channel_id=1, source_target_pairs={{0,64},{64,0},{128,192},{192,128},{256,320},{320,256},{384,448},{4... | collective-permute-start | bytes 6340616 | tf_op jit(solution)/shard_map/ppermute | solution.py:390
  141.1 30.3 %collective-permute-done.10.w2 = bf16[2064,512]{1,0:T(8,128)(2,1)} collective-permute-done((bf16[2064,512]{1,0:T(8,128)(2,1)}, bf16[2064,512]{1,0:T(8,128)(2,1)}, u32[]{:S(2)}, u32[]{:S(2)}) %collective-permute-start.10) | collective-permute-done | bytes 2113568 | tf_op jit(solution)/shard_map/ppermute | solution.py:391
  171.4 4.7 %collective-permute-start.11 = (bf16[2064,512]{1,0:T(8,128)(2,1)}, bf16[2064,512]{1,0:T(8,128)(2,1)}, u32[]{:S(2)}, u32[]{:S(2)}) collective-permute-start(bf16[2064,512]{1,0:T(8,128)(2,1)} %collective-permute-done.10.w2), channel_id=1, source_target_pairs={{0,64},{64,0},{128,192},{192,128},{256,320},{320,256},{384,448},{4... | collective-permute-start | bytes 6340616 | tf_op jit(solution)/shard_map/ppermute | solution.py:392
  176.1 1.4 fusion.2
  179.1 0.7 copy-done.7
  179.8 1.6 copy-done.8
  183.2 8.7 %shard_map.196 = (f32[32,32,128]{2,1,0:T(8,128)S(1)}, f32[32,32,128]{2,1,0:T(8,128)S(1)}) custom-call(s32[1]{0:T(128)} %slice.30.used, s32[44]{0:T(128)S(1)} %copy-done.7, s32[44]{0:T(128)S(1)} %copy-done.6, s32[11]{0:T(128)S(1)} %copy-done.12, s32[4]{0:T(128)S(1)} %copy-done.10, s32[2]{0:T(128)S(1)} %copy-done.11, bf16[32,32,128]{2,1,0:T(8,128)(2,1)S(1)} %bitcast.63, ...), custom_call_target="tpu_custom_call" | custom-call | flops 4294967296 | bytes 4194304 | tf_op jit(solution)/shard_map/pallas_call | solution.py:210
  192.1 2.8 %shard_map.197 = bf16[8,2,4,32,128]{4,3,2,1,0:T(8,128)(2,1)} custom-call(s32[32]{0:T(128)S(1)} %copy-done.3, s32[32]{0:T(128)S(1)} %copy-done.4, s32[32]{0:T(128)S(1)} %copy-done.5, bf16[32,9,16,128]{3,2,1,0:T(8,128)(2,1)S(1)} %all-to-all-done.1.back_ref, f32[32,32,128]{2,1,0:T(8,128)S(1)} %get-tuple-element.7.out_ref, ...), custom_call_target="tpu_custom_call" | custom-call | flops 134217728 | bytes 4194304 | tf_op jit(solution)/shard_map/pallas_call | solution.py:260
  194.9 4.7 %all-to-all-start.2 = ((bf16[8,256,128]{2,1,0:T(8,128)(2,1)}), bf16[8,256,128]{2,1,0:T(8,128)(2,1)S(1)}, u32[]{:S(2)}, u32[]{:S(2)}) async-start(bf16[8,256,128]{2,1,0:T(8,128)(2,1)} %bitcast.31), calls=%async_computation.2 | async-start | bytes 1048576 | tf_op jit(solution)/shard_map/all_to_all | solution.py:460
  200.0 14.1 %all-to-all-done.2.attn_ref = bf16[8,256,128]{2,1,0:T(8,128)(2,1)S(1)} async-done(((bf16[8,256,128]{2,1,0:T(8,128)(2,1)}), bf16[8,256,128]{2,1,0:T(8,128)(2,1)S(1)}, u32[]{:S(2)}, u32[]{:S(2)}) %all-to-all-start.2) | async-done | bytes 524320 | tf_op jit(solution)/shard_map/all_to_all | solution.py:460
  214.1 1.6 copy-done.9
  215.7 7.2 %shard_map.198 = (bf16[128,1024]{1,0:T(8,128)(2,1)S(1)}, f32[128,1024]{1,0:T(8,128)S(1)}, bf16[128,1024]{1,0:T(8,128)(2,1)S(1)}) custom-call(bf16[8,256,128]{2,1,0:T(8,128)(2,1)S(1)} %all-to-all-done.2.attn_ref, bf16[1024,1024]{1,0:T(8,128)(2,1)S(1)} %copy-done.9, bf16[128,1024]{1,0:T(8,128)(2,1)S(1)} %bitcast.72, ...), custom_call_target="tpu_custom_call" | custom-call | flops 3221225472 | bytes 12582912 | tf_op jit(solution)/shard_map/pallas_call | solution.py:304
  222.8 1.9 collective-permute-start.12
  225.5 0.9 broadcast_select_fusion
  226.4 12.1 %collective-permute-done.12 = bf16[128,1024]{1,0:T(8,128)(2,1)S(1)} collective-permute-done((bf16[128,1024]{1,0:T(8,128)(2,1)S(1)}, bf16[128,1024]{1,0:T(8,128)(2,1)S(1)}, u32[]{:S(2)}, u32[]{:S(2)}) %collective-permute-start.12) | collective-permute-done | bytes 262176 | tf_op jit(solution)/shard_map/ppermute | solution.py:465
  238.9 0.9 add_convert_fusion
  (120 shorter events, 11.7 us)
Async XLA Ops:
  7.2 13.5 %copy-start = (s32[128]{0:T(128)S(1)}, s32[128]{0:T(128)}, u32[]{:S(2)}) copy-start(s32[128]{0:T(128)} %param.35) | copy-start | bytes 1540
  7.2 45.3 %copy-start.2 = (bf16[4,32,1024]{2,1,0:T(8,128)(2,1)S(1)}, bf16[4,32,1024]{2,1,0:T(8,128)(2,1)}, u32[]{:S(2)}) copy-start(bf16[4,32,1024]{2,1,0:T(8,128)(2,1)} %param.19) | copy-start | bytes 786436
  7.2 171.3 %all-gather.6.cloned.1.call-start = ((), (), s32[]{:S(2)}) async-start(), calls=%async_computation.4 | async-start | bytes 2359296 | tf_op jit(solution)/shard_map/all_gather | solution.py:375
  7.2 14.8 %collective-permute-start = (bf16[128,1024]{1,0:T(8,128)(2,1)}, bf16[128,1024]{1,0:T(8,128)(2,1)S(1)}, u32[]{:S(2)}, u32[]{:S(2)}) collective-permute-start(bf16[128,1024]{1,0:T(8,128)(2,1)} %bitcast.68), channel_id=1, source_target_pairs={{0,128},{64,192},{128,0},{192,64},{256,384},{320,448},{384,256},{4... | collective-permute-start | bytes 786440 | tf_op jit(solution)/shard_map/ppermute | solution.py:362
  12.2 40.3 %collective-permute-start.1 = (bf16[128,1024]{1,0:T(8,128)(2,1)}, bf16[128,1024]{1,0:T(8,128)(2,1)S(1)}, u32[]{:S(2)}, u32[]{:S(2)}) collective-permute-start(bf16[128,1024]{1,0:T(8,128)(2,1)} %bitcast.69), channel_id=1, source_target_pairs={{0,256},{64,320},{128,384},{192,448},{256,0},{320,64},{384,128},{4... | collective-permute-start | bytes 786440 | tf_op jit(solution)/shard_map/ppermute | solution.py:362
  18.0 34.5 %collective-permute-start.2 = (bf16[128,1024]{1,0:T(8,128)(2,1)}, bf16[128,1024]{1,0:T(8,128)(2,1)S(1)}, u32[]{:S(2)}, u32[]{:S(2)}) collective-permute-start(bf16[128,1024]{1,0:T(8,128)(2,1)} %bitcast.70), channel_id=1, source_target_pairs={{0,384},{64,448},{128,256},{192,320},{256,128},{320,192},{384,0},{... | collective-permute-start | bytes 786440 | tf_op jit(solution)/shard_map/ppermute | solution.py:362
  20.6 37.7 %copy-start.13 = (s32[128]{0:T(128)S(1)}, s32[128]{0:T(128)}, u32[]{:S(2)}) copy-start(s32[128]{0:T(128)} %param.36) | copy-start | bytes 1540
  24.0 14.0 %collective-permute-start.5 = (bf16[128,128]{1,0:T(8,128)(2,1)S(1)}, bf16[128,128]{1,0:T(8,128)(2,1)S(1)}, u32[]{:S(2)}, u32[]{:S(2)}) collective-permute-start(bf16[128,128]{1,0:T(8,128)(2,1)S(1)} %bitcast.86), channel_id=1, source_target_pairs={{0,32},{1,33},{2,34},{3,35},{4,36},{5,37},{6,38},{7,39},{8,40},{9,... | collective-permute-start | bytes 98312 | tf_op jit(solution)/shard_map/ppermute | solution.py:370
  38.0 9.7 %collective-permute-start.6 = (bf16[2,128,128]{2,1,0:T(8,128)(2,1)S(1)}, bf16[2,128,128]{2,1,0:T(8,128)(2,1)S(1)}, u32[]{:S(2)}, u32[]{:S(2)}) collective-permute-start(bf16[2,128,128]{2,1,0:T(8,128)(2,1)S(1)} %get-tuple-element.21), channel_id=1, source_target_pairs={{0,8},{1,9},{2,10},{3,11},{4,12},{5,13},{6,14},{7,15},{8,0},{9,1},... | collective-permute-start | bytes 196616 | tf_op jit(solution)/shard_map/ppermute | solution.py:372
  41.1 7.1 %collective-permute-start.7 = (bf16[2,128,128]{2,1,0:T(8,128)(2,1)S(1)}, bf16[2,128,128]{2,1,0:T(8,128)(2,1)S(1)}, u32[]{:S(2)}, u32[]{:S(2)}) collective-permute-start(bf16[2,128,128]{2,1,0:T(8,128)(2,1)S(1)} %get-tuple-element.21), channel_id=1, source_target_pairs={{0,16},{1,17},{2,18},{3,19},{4,20},{5,21},{6,22},{7,23},{8,24},{9,... | collective-permute-start | bytes 196616 | tf_op jit(solution)/shard_map/ppermute | solution.py:372
  45.5 6.2 %collective-permute-start.8 = (bf16[2,128,128]{2,1,0:T(8,128)(2,1)S(1)}, bf16[2,128,128]{2,1,0:T(8,128)(2,1)S(1)}, u32[]{:S(2)}, u32[]{:S(2)}) collective-permute-start(bf16[2,128,128]{2,1,0:T(8,128)(2,1)S(1)} %get-tuple-element.21), channel_id=1, source_target_pairs={{0,24},{1,25},{2,26},{3,27},{4,28},{5,29},{6,30},{7,31},{8,16},{9,... | collective-permute-start | bytes 196616 | tf_op jit(solution)/shard_map/ppermute | solution.py:372
  52.7 10.9 %copy-start.16 = (bf16[4,128,1024]{2,1,0:T(8,128)(2,1)}, bf16[4,128,1024]{2,1,0:T(8,128)(2,1)S(1)}, u32[]{:S(2)}) copy-start(bf16[4,128,1024]{2,1,0:T(8,128)(2,1)S(1)} %pad_maximum_fusion.1) | copy-start | bytes 3145732
  52.7 10.8 %collective-permute-start.3 = (bf16[4,128,1024]{2,1,0:T(8,128)(2,1)S(1)}, bf16[4,128,1024]{2,1,0:T(8,128)(2,1)S(1)}, u32[]{:S(2)}, u32[]{:S(2)}) collective-permute-start(bf16[4,128,1024]{2,1,0:T(8,128)(2,1)S(1)} %pad_maximum_fusion.1), channel_id=1, source_target_pairs={{0,64},{64,0},{128,192},{192,128},{256,320},{320,256},{384,448},{4... | collective-permute-start | bytes 3145736 | tf_op jit(solution)/shard_map/ppermute | solution.py:366
  63.5 4.9 %copy-start.26 = (bf16[4,128,1024]{2,1,0:T(8,128)(2,1)}, bf16[4,128,1024]{2,1,0:T(8,128)(2,1)S(1)}, u32[]{:S(2)}) copy-start(bf16[4,128,1024]{2,1,0:T(8,128)(2,1)S(1)} %collective-permute-done.3) | copy-start | bytes 3145732
  65.2 10.7 %copy-start.14 = (bf16[2,2,384,128]{3,2,1,0:T(8,128)(2,1)S(1)}, bf16[2,2,384,128]{3,2,1,0:T(8,128)(2,1)}, u32[]{:S(2)}) copy-start(bf16[2,2,384,128]{3,2,1,0:T(8,128)(2,1)} %param.32) | copy-start | bytes 1179652
  68.4 33.2 %copy-start.24 = (bf16[512]{0:T(512)(128)(2,1)S(1)}, bf16[512]{0:T(512)(128)(2,1)}, u32[]{:S(2)}) copy-start(bf16[512]{0:T(512)(128)(2,1)} %param.26) | copy-start | bytes 3076
  68.4 33.3 %copy-start.15 = (bf16[1024,512]{1,0:T(8,128)(2,1)S(1)}, bf16[1024,512]{1,0:T(8,128)(2,1)}, u32[]{:S(2)}) copy-start(bf16[1024,512]{1,0:T(8,128)(2,1)} %param.25) | copy-start | bytes 3145732
  68.4 44.2 %all-to-all-start = ((bf16[32,4,32,128]{3,2,1,0:T(8,128)(2,1)}), bf16[32,4,32,128]{3,2,1,0:T(8,128)(2,1)S(1)}, u32[]{:S(2)}, u32[]{:S(2)}) async-start(bf16[32,4,32,128]{3,2,1,0:T(8,128)(2,1)} %bitcast.75), calls=%async_computation | async-start | bytes 2097152 | tf_op jit(solution)/shard_map/all_to_all | solution.py:442
  75.8 124.2 %all-gather.4.cloned.1.call-start = ((), (), s32[]{:S(2)}) async-start(), calls=%async_computation.3 | async-start | bytes 2359296 | tf_op jit(solution)/shard_map/all_gather | solution.py:382
  75.9 24.7 %collective-permute-start.4 = (bf16[1536,128]{1,0:T(8,128)(2,1)S(1)}, bf16[1536,128]{1,0:T(8,128)(2,1)S(1)}, u32[]{:S(2)}, u32[]{:S(2)}) collective-permute-start(bf16[1536,128]{1,0:T(8,128)(2,1)S(1)} %bitcast.82), channel_id=1, source_target_pairs={{0,32},{1,33},{2,34},{3,35},{4,36},{5,37},{6,38},{7,39},{8,40},{9,... | collective-permute-start | bytes 1179656 | tf_op jit(solution)/shard_map/ppermute | solution.py:379
  101.7 4.3 %copy-start.25 = (s32[128]{0:T(128)S(1)}, s32[128]{0:T(128)}, u32[]{:S(2)}) copy-start(s32[128]{0:T(128)} %param.34) | copy-start | bytes 1540
  104.0 67.4 %collective-permute-start.10 = (bf16[2064,512]{1,0:T(8,128)(2,1)}, bf16[2064,512]{1,0:T(8,128)(2,1)}, u32[]{:S(2)}, u32[]{:S(2)}) collective-permute-start(bf16[2064,512]{1,0:T(8,128)(2,1)} %get-tuple-element.16), channel_id=1, source_target_pairs={{0,128},{64,192},{128,0},{192,64},{256,384},{320,448},{384,256},{4... | collective-permute-start | bytes 6340616 | tf_op jit(solution)/shard_map/ppermute | solution.py:391
  126.7 9.1 %copy-start.3 = (s32[32]{0:T(128)S(1)}, s32[32]{0:T(128)}, u32[]{:S(2)}) copy-start(s32[32]{0:T(128)} %get-tuple-element.24.pos) | copy-start | bytes 388
  126.7 10.3 %copy-start.17 = (bf16[4,128,1024]{2,1,0:T(8,128)(2,1)S(1)}, bf16[4,128,1024]{2,1,0:T(8,128)(2,1)}, u32[]{:S(2)}) copy-start(bf16[4,128,1024]{2,1,0:T(8,128)(2,1)} %copy-done.16) | copy-start | bytes 3145732
  126.7 65.3 %all-to-all-start.1 = ((bf16[32,9,16,128]{3,2,1,0:T(8,128)(2,1)}), bf16[32,9,16,128]{3,2,1,0:T(8,128)(2,1)S(1)}, u32[]{:S(2)}, u32[]{:S(2)}) async-start(bf16[32,9,16,128]{3,2,1,0:T(8,128)(2,1)} %shard_map.195), calls=%async_computation.1 | async-start | bytes 2359296 | tf_op jit(solution)/shard_map/all_to_all | solution.py:453
  134.5 42.9 %copy-start.27 = (bf16[4,128,1024]{2,1,0:T(8,128)(2,1)S(1)}, bf16[4,128,1024]{2,1,0:T(8,128)(2,1)}, u32[]{:S(2)}) copy-start(bf16[4,128,1024]{2,1,0:T(8,128)(2,1)} %copy-done.26) | copy-start | bytes 3145732
  134.5 42.9 %copy-start.28 = (bf16[1024,3,128]{2,0,1:T(8,128)(2,1)S(1)}, bf16[1024,3,128]{2,0,1:T(8,128)(2,1)}, u32[]{:S(2)}) copy-start(bf16[1024,3,128]{2,0,1:T(8,128)(2,1)} %param.20) | copy-start | bytes 2359300
  138.5 61.5 %collective-permute-start.9 = (bf16[2064,512]{1,0:T(8,128)(2,1)}, bf16[2064,512]{1,0:T(8,128)(2,1)}, u32[]{:S(2)}, u32[]{:S(2)}) collective-permute-start(bf16[2064,512]{1,0:T(8,128)(2,1)} %get-tuple-element.17.w0), channel_id=1, source_target_pairs={{0,64},{64,0},{128,192},{192,128},{256,320},{320,256},{384,448},{4... | collective-permute-start | bytes 6340616 | tf_op jit(solution)/shard_map/ppermute | solution.py:390
  171.4 28.6 %collective-permute-start.11 = (bf16[2064,512]{1,0:T(8,128)(2,1)}, bf16[2064,512]{1,0:T(8,128)(2,1)}, u32[]{:S(2)}, u32[]{:S(2)}) collective-permute-start(bf16[2064,512]{1,0:T(8,128)(2,1)} %collective-permute-done.10.w2), channel_id=1, source_target_pairs={{0,64},{64,0},{128,192},{192,128},{256,320},{320,256},{384,448},{4... | collective-permute-start | bytes 6340616 | tf_op jit(solution)/shard_map/ppermute | solution.py:392
  177.5 1.0 copy-start.1
  178.5 0.6 copy-start.6
  179.1 0.7 copy-start.7
  179.8 1.6 copy-start.8
  181.4 0.7 copy-start.10
  182.0 0.6 copy-start.11
  182.6 0.6 copy-start.12
  183.2 8.8 %copy-start.4 = (s32[32]{0:T(128)S(1)}, s32[32]{0:T(128)}, u32[]{:S(2)}) copy-start(s32[32]{0:T(128)} %get-tuple-element.22.dst_b) | copy-start | bytes 388
  183.2 8.8 %copy-start.5 = (s32[32]{0:T(128)S(1)}, s32[32]{0:T(128)}, u32[]{:S(2)}) copy-start(s32[32]{0:T(128)} %get-tuple-element.23.dst_l) | copy-start | bytes 388
  192.0 7.6 %copy-start.18 = (bf16[1024]{0:T(1024)(128)(2,1)S(1)}, bf16[1024]{0:T(1024)(128)(2,1)}, u32[]{:S(2)}) copy-start(bf16[1024]{0:T(1024)(128)(2,1)} %param.22) | copy-start | bytes 6148
  192.0 7.6 %copy-start.19 = (bf16[1024]{0:T(1024)(128)(2,1)S(1)}, bf16[1024]{0:T(1024)(128)(2,1)}, u32[]{:S(2)}) copy-start(bf16[1024]{0:T(1024)(128)(2,1)} %param.23) | copy-start | bytes 6148
  192.0 7.6 %copy-start.20 = (bf16[1024]{0:T(1024)(128)(2,1)S(1)}, bf16[1024]{0:T(1024)(128)(2,1)}, u32[]{:S(2)}) copy-start(bf16[1024]{0:T(1024)(128)(2,1)} %param.24) | copy-start | bytes 6148
  192.0 7.6 %copy-start.21 = (bf16[1024]{0:T(1024)(128)(2,1)S(1)}, bf16[1024]{0:T(1024)(128)(2,1)}, u32[]{:S(2)}) copy-start(bf16[1024]{0:T(1024)(128)(2,1)} %param.28) | copy-start | bytes 6148
  192.0 7.6 %copy-start.22 = (bf16[1024]{0:T(1024)(128)(2,1)S(1)}, bf16[1024]{0:T(1024)(128)(2,1)}, u32[]{:S(2)}) copy-start(bf16[1024]{0:T(1024)(128)(2,1)} %param.29) | copy-start | bytes 6148
  192.0 7.7 %copy-start.23 = (bf16[1024]{0:T(1024)(128)(2,1)S(1)}, bf16[1024]{0:T(1024)(128)(2,1)}, u32[]{:S(2)}) copy-start(bf16[1024]{0:T(1024)(128)(2,1)} %param.30) | copy-start | bytes 6148
  194.9 19.2 %all-to-all-start.2 = ((bf16[8,256,128]{2,1,0:T(8,128)(2,1)}), bf16[8,256,128]{2,1,0:T(8,128)(2,1)S(1)}, u32[]{:S(2)}, u32[]{:S(2)}) async-start(bf16[8,256,128]{2,1,0:T(8,128)(2,1)} %bitcast.31), calls=%async_computation.2 | async-start | bytes 1048576 | tf_op jit(solution)/shard_map/all_to_all | solution.py:460
  214.1 1.6 copy-start.9
  222.8 15.7 %collective-permute-start.12 = (bf16[128,1024]{1,0:T(8,128)(2,1)S(1)}, bf16[128,1024]{1,0:T(8,128)(2,1)S(1)}, u32[]{:S(2)}, u32[]{:S(2)}) collective-permute-start(bf16[128,1024]{1,0:T(8,128)(2,1)S(1)} %get-tuple-element.11), channel_id=1, source_target_pairs={{0,256},{64,320},{128,384},{192,448},{256,0},{320,64},{384,128},{4... | collective-permute-start | bytes 786440 | tf_op jit(solution)/shard_map/ppermute | solution.py:465
Sparse Core Ops, SparseCore 0:
  52.6 60.5 all-gather.5
  115.2 56.7 all-gather.3

commit v3 on v2

--- a/solution.py
+++ b/solution.py
@@ -55,8 +55,18 @@
     return jnp.where(lane < HD, first, second)
 
 
-def route_kernel(pos, dst_b, dst_l, q_ref, out_ref):
+def query_kernel(pos, dst_b, dst_l, half_ref, near_ref, other_ref, w_ref, after_ref, q_ref, out_ref):
+    del after_ref
+    reqs, suf, cols = q_ref.shape
     out_ref[...] = jnp.zeros_like(out_ref)
+    weights = w_ref[...]
+    at = 0
+    for ref in (half_ref, near_ref, other_ref):
+        rows = ref[...].reshape(-1, ref.shape[-1])
+        q = dot_nn(rows, weights).astype(BF16).astype(F32) * HD**-0.5
+        count = rows.shape[0] // suf
+        q_ref[at : at + count] = q.astype(BF16).reshape(count, suf, cols)
+        at += count
 
     def body(r, _):
         tile = q_ref[pos[r]]
@@ -64,22 +74,57 @@
         out_ref[dst_l[r]] = tile
         return 0
 
-    lax.fori_loop(0, pos.shape[0], body, 0)
-
-
-def route(pos, dst_b, dst_l, q):
-    reqs, suf, _ = q.shape
+    lax.fori_loop(0, reqs, body, 0, unroll=2)
+
+
+def query_and_route(pos, dst_b, dst_l, half, near, other, w, suf, after):
+    reqs = pos.shape[0]
+    vmem = pl.BlockSpec(memory_space=pltpu.VMEM)
     return pl.pallas_call(
-        route_kernel,
-        out_shape=jax.ShapeDtypeStruct((PEERS * SLOTS, suf, LANES), BF16),
+        query_kernel,
+        out_shape=(
+            jax.ShapeDtypeStruct((reqs, suf, LANES), BF16),
+            jax.ShapeDtypeStruct((PEERS * SLOTS, suf, LANES), BF16),
+        ),
         in_specs=[pl.BlockSpec(memory_space=pltpu.SMEM)] * 3
-        + [pl.BlockSpec(memory_space=pltpu.VMEM)],
-        out_specs=pl.BlockSpec(memory_space=pltpu.VMEM),
-        cost_estimate=pl.CostEstimate(flops=0, bytes_accessed=3 << 20, transcendentals=0),
-    )(pos, dst_b, dst_l, q)
-
-
-def node_kernel(lens, q_ref, k_ref, v_ref, out_ref):
+        + [vmem] * 4
+        + [pl.BlockSpec(memory_space=pl.ANY)],
+        out_specs=(vmem, vmem),
+        compiler_params=pltpu.CompilerParams(vmem_limit_bytes=24 << 20),
+        cost_estimate=pl.CostEstimate(flops=1 << 28, bytes_accessed=4 << 20, transcendentals=0),
+    )(pos, dst_b, dst_l, half, near, other, w, after)
+
+
+def pack_kernel(up_ref, down_ref, bias_ref, after_ref, out_ref):
+    del after_ref
+    width = up_ref.shape[0]
+    units = out_ref.shape[2]
+    for j in range(2):
+        own = slice(j * units, (j + 1) * units)
+        out_ref[j, :width] = up_ref[:, own]
+        for i in range(width // units):
+            out_ref[j, width + i * units : width + (i + 1) * units] = down_ref[
+                own, i * units : (i + 1) * units
+            ]
+        bias = jnp.broadcast_to(bias_ref[:, own].astype(F32), (16, units))
+        out_ref[j, 2 * width :] = bias.astype(BF16)
+
+
+def pack_weights(up, down, bias, after):
+    width, units = up.shape
+    vmem = pl.BlockSpec(memory_space=pltpu.VMEM)
+    return pl.pallas_call(
+        pack_kernel,
+        out_shape=jax.ShapeDtypeStruct((2, 2 * width + 16, units // 2), BF16),
+        in_specs=[vmem] * 3 + [pl.BlockSpec(memory_space=pl.ANY)],
+        out_specs=vmem,
+        compiler_params=pltpu.CompilerParams(vmem_limit_bytes=16 << 20),
+        cost_estimate=pl.CostEstimate(flops=0, bytes_accessed=4 << 20, transcendentals=0),
+    )(up, down, bias.reshape(1, units), after)
+
+
+def node_kernel(lens, q_ref, k_ref, v_ref, after_ref, out_ref):
+    del after_ref
     slot = pl.program_id(0)
     peers, _, suf, _ = q_ref.shape
     group = 8
@@ -125,7 +170,7 @@
         out_ref[part, 2 * SLOTS] = held.astype(BF16)
 
 
-def node_attention(lens, queries, caches):
+def node_attention(lens, queries, caches, after):
     peers, slots, suf, _ = queries.shape
     node_max = caches.shape[3]
 
@@ -144,6 +189,7 @@
                 pl.BlockSpec((peers, slots, suf, LANES), lambda s, n: (0, 0, 0, 0)),
                 cache_spec(0),
                 cache_spec(1),
+                pl.BlockSpec(memory_space=pl.ANY),
             ],
             out_specs=pl.BlockSpec((peers, 2 * slots + 1, HALF, LANES), lambda s, n: (0, 0, 0, 0)),
         ),
@@ -151,7 +197,7 @@
         cost_estimate=pl.CostEstimate(
             flops=2 << 30, bytes_accessed=4 << 20, transcendentals=4 << 20
         ),
-    )(lens, queries, caches, caches)
+    )(lens, queries, caches, caches, after)
 
 
 def root_kernel(
@@ -173,8 +219,8 @@
         n = lax.broadcasted_iota(I32, (1, root_rows), 1)
         row = n % per
         z = (n // per) % NZ
-        x = (n // (per * NZ)) % NX
-        y = n // (per * NX * NZ)
+        y = (n // (per * NZ)) % NY
+        x = n // (per * NY * NZ)
         place = (((z ^ coords[0]) * NX + (x ^ coords[1])) * NY + y) * per + row
         scores = jnp.where(place < root_len[tenant], dot_nt(q, keys), NEG)
         own_row = (lax.broadcasted_iota(I32, (2 * rows, rows), 0) % rows) // suf
@@ -286,12 +332,14 @@
     norm = rows_norm(mixed, vec[1:2], vec[2:3]).astype(BF16)
     norm_ref[...] = norm[:rows]
     total = jnp.zeros((2 * rows, width), F32)
-    units = w0.shape[1]
-    for w in (w0, w1, w2, w3):
-        inner = dot_nn(norm, w[:width]) + w[width + 2 * units : width + 2 * units + 16].astype(F32)[0:1]
+    units = w0.shape[-1]
+    for w in [ref.at[i] for ref in (w0, w1, w2, w3) for i in range(2)]:
+        bias = w[width + units * (width // units) :].astype(F32)[0:1]
+        inner = dot_nn(norm, w[:width]) + bias
         hidden = (0.5 * inner * (1.0 + lax.erf(inner * (0.5**0.5)))).astype(BF16)
         down = [
-            dot_nn(hidden, w[width + i * units : width + (i + 1) * units]) for i in range(width // units)
+            dot_nn(hidden, w[width + i * units : width + (i + 1) * units])
+            for i in range(width // units)
         ]
         total = total + jnp.concatenate(down, axis=1)
     own_ref[...] = total[:rows]
@@ -308,7 +356,7 @@
             jax.ShapeDtypeStruct((rows, width), F32),
             jax.ShapeDtypeStruct((rows, width), BF16),
         ),
-        in_specs=[vmem] * 9,
+        in_specs=[vmem] * (5 + len(packs)),
         out_specs=(vmem, vmem, vmem),
         compiler_params=pltpu.CompilerParams(vmem_limit_bytes=48 << 20),
         cost_estimate=pl.CostEstimate(
@@ -359,38 +407,45 @@
         return jnp.minimum(jnp.abs(flat[:1, :1]), 0)
 
     tok = tokens.reshape(own_rows, width)
-    half = [tok] + [lax.ppermute(tok, "blk", xor_pairs(N_BLK, 2 * k)) for k in range(1, n_own)]
-    tok_far = half[2]
-    first_come, last_come = half[1], half[3]
-    half = jnp.stack(half)
-    other = lax.ppermute(half, "blk", swap)
+    near = lax.ppermute(tok, "blk", swap)
+    half = [lax.ppermute(tok, "blk", xor_pairs(N_BLK, 2 * k)) for k in range(1, n_own)]
+    tok_far, last_come = half[1], half[2]
 
     n_owner = NX * NY * NZ
-    roots = root_cache.reshape(-1, LANES) + zero_after(first_come)
+    roots = root_cache.reshape(-1, LANES) + zero_after(near)
     roots = jnp.stack([roots, lax.ppermute(roots, "owner", xor_pairs(n_owner, NX * NY))])
+    y_groups = [[g * NY + y for y in range(NY)] for g in range(NZ * NX)]
+    roots_y = lax.all_gather(roots, "owner", axis=0, tiled=False, axis_index_groups=y_groups)
+    other = lax.ppermute(jnp.stack(half) + zero_after(roots_y), "blk", swap)
+    half = jnp.stack([tok] + half)
     roots = jnp.stack(
-        [roots] + [lax.ppermute(roots, "owner", xor_pairs(n_owner, k * NY)) for k in range(1, NX)]
-    )
-    y_groups = [[g * NY + y for y in range(NY)] for g in range(NZ * NX)]
-    roots = lax.all_gather(roots, "owner", axis=0, tiled=False, axis_index_groups=y_groups)
-    roots = roots.reshape(NY, NX, NZ, 2, tenants, root_per, LANES)
+        [roots_y]
+        + [lax.ppermute(roots_y, "owner", xor_pairs(n_owner, k * NY)) for k in range(1, NX)]
+    )
+    roots = roots.reshape(NX, NY, NZ, 2, tenants, root_per, LANES)
 
     node_rows = node_cache.reshape(-1, LANES) + zero_after(last_come)
     node_far = lax.ppermute(node_rows, "owner", xor_pairs(n_owner, NX * NY))
     caches = jnp.stack([node_rows, node_far]).reshape(NZ, 2, 2, node_max, LANES)
 
     w_out_all = lax.all_gather(w_out + zero_after(last_come), "blk", axis=0, tiled=True)
-    units = w_up.shape[1]
-    pack = jnp.concatenate(
-        [w_up]
-        + [w_down[:, i * units : (i + 1) * units] for i in range(width // units)]
-        + [jnp.broadcast_to(b_up[None, :], (16, units))],
-        axis=0,
-    )
-    pack_side = lax.ppermute(pack, "blk", swap)
-    pack_next = lax.ppermute(pack + zero_after(node_far), "blk", xor_pairs(N_BLK, 2))
+    packs = pack_weights(w_up, w_down, b_up, last_come)
+    pack_side = lax.ppermute(packs, "blk", swap)
+    z_chips = NZ * n_own
+
+    def to_neighbour(step):
+        pairs = []
+        for dev in range(n_owner * N_BLK):
+            b, own = dev // n_owner, dev % n_owner
+            z = (own // PEERS * n_own + b // 2 + step) % z_chips
+            pairs.append((dev, (z % n_own * 2 + b % 2) * n_owner + z // n_own * PEERS + own % PEERS))
+        part = ((blk // 2 + step + n_own) % n_own) // (n_own // 2)
+        sent = lax.dynamic_index_in_dim(packs, part, 0, keepdims=False) + zero_after(node_far)
+        return lax.ppermute(sent, ("blk", "owner"), pairs)
+
+    pack_next = jnp.stack([to_neighbour(1), to_neighbour(-1)])
     pack_last = lax.ppermute(pack_next, "blk", swap)
-    packs = [pack, pack_side, pack_next, pack_last]
+    packs = [packs, pack_side, pack_next, pack_last]
 
     branch = node_parent[req_leaf]
     tenant = node_parent[branch]
@@ -429,15 +484,19 @@
     used = ends[-1:].astype(I32)
     coords = jnp.stack([my_z, my_x]).astype(I32)
 
+    q, outgoing = query_and_route(pos, dst_b, dst_l, half, near, other, w_qkv[:, 0], suf, roots_y)
+    outgoing = outgoing.reshape(PEERS, SLOTS, suf, cols)
+
     def project(which):
         w = w_qkv[:, which]
         out = jnp.concatenate(
-            [jnp.dot(part.reshape(-1, width), w, preferred_element_type=F32) for part in (half, other)]
+            [
+                jnp.dot(part.reshape(-1, width), w, preferred_element_type=F32)
+                for part in (half, near, other)
+            ]
         )
         return out.astype(BF16).reshape(reqs, suf, cols)
 
-    q = project(0) * jnp.asarray(HD**-0.5, BF16)
-    outgoing = route(pos, dst_b, dst_l, q).reshape(PEERS, SLOTS, suf, cols)
     groups = [[z * PEERS + p for p in range(PEERS)] for z in range(NZ)]
     incoming = lax.all_to_all(
         outgoing, "owner", split_axis=0, concat_axis=0, axis_index_groups=groups, tiled=True
@@ -449,7 +508,7 @@
     new_caches = jnp.stack([k_new, v_new]).reshape(2, N_BLK, req_dev, suf, cols)
     new_caches = jnp.take(new_caches, order, axis=1).reshape(2, reqs, suf, cols)
 
-    answers = node_attention(lens, incoming, caches)
+    answers = node_attention(lens, incoming, caches, roots)
     back = lax.all_to_all(
         answers, "owner", split_axis=0, concat_axis=0, axis_index_groups=groups, tiled=True
     )

time: 248 us -> 253 us (1.020)
  waiting for transfers between devices: 88.7 us -> 42.3 us
  blocking collectives: 0 us -> 20.4 us
  starting transfers between devices: 72.5 us -> 90.3 us
  local copies, waits for them, and re-layouts: 13.6 us -> 23.9 us
  other arithmetic: 13.2 us -> 16.2 us
    ppermute x6 -> x8, waiting for transfers between devices: 34.3 us -> 7.87 us  [the longest x3 7.31 us: on_device(): lax.ppermute(roots_y, 'owner', xor_pairs(n_owner, k * NY))]
    all_gather x0 -> x1, blocking collectives: none -> 20.4 us  [on_device(): lax.all_gather(roots, 'owner', axis=0, tiled=False, axis_index_groups=y_g...]
    ppermute x1, waiting for transfers between devices: 18.4 us -> 0.01 us  [on_device(): node_far = lax.ppermute(node_rows, 'owner', xor_pairs(n_owner, NX * NY))]
    ppermute x6 -> x8, starting transfers between devices: 19.6 us -> 36.9 us  [the longest x2 10.2 us: to_neighbour(): return lax.ppermute(sent, ('blk', 'owner'), pairs)]
    unnamed x58 -> x86, local copies, waits for them, and re-layouts: 6.44 us -> 15.9 us
    all_to_all x1, waiting for transfers between devices: 0.01 us -> 6.97 us  [on_device(): lax.all_to_all(answers, 'owner', split_axis=0, concat_axis=0, axis_index_...]
    another operation x3 -> x4, other arithmetic: 0.88 us -> 6.32 us  [the longest x1 3.24 us: on_device(): pack_next = jnp.stack([to_neighbour(1), to_neighbour(-1)])]
    all_to_all x1, waiting for transfers between devices: 4.62 us -> 0.01 us  [on_device(): lax.all_to_all(outgoing, 'owner', split_axis=0, concat_axis=0, axis_index...]
  transfers between devices with their start and end apart: 18 -> 19, of which waited for: 8 -> 6; matrix products, arithmetic and copies ran while one was open for 10% -> 11% of each run, Pallas kernels for 11% -> 10%
where the time goes in v3:
time: 253 us; the launch traced here: 251 us
  starting transfers between devices  90.3 us (36%)
  waiting for transfers between devices  42.3 us (17%)
  Pallas kernels  34.6 us (14%)
  local copies, waits for them, and re-layouts  23.9 us (9%)
  blocking collectives  20.4 us (8%)
  between operations  17.6 us (7%)
  other arithmetic  16.2 us (6%)
  matrix products  5.96 us (2%)
    all_gather x1, blocking collectives, on_device(): lax.all_gather(roots, 'owner', axis=0, tiled=False, axis_index_groups=y_g...  20.4 us
    unnamed x86, local copies, waits for them, and re-layouts  15.9 us
    pallas_call x1, Pallas kernels, node_attention(): pl.pallas_call(node_kernel, out_shape=jax.ShapeDtypeStruct((peers, 2 * sl...  14.4 us
    all_to_all x1, waiting for transfers between devices, on_device(): lax.all_to_all(send.reshape(N_BLK, 2 * own_rows, cols), 'blk', split_axis...  14.1 us
    ppermute x3, starting transfers between devices, on_device(): lax.ppermute(tok, 'blk', xor_pairs(N_BLK, 2 * k))  12.7 us
    ppermute x1, waiting for transfers between devices, on_device(): lax.ppermute(down_far, 'blk', xor_pairs(N_BLK, N_BLK // 2)).astype(F32)  12.1 us
    ppermute x2, starting transfers between devices, to_neighbour(): return lax.ppermute(sent, ('blk', 'owner'), pairs)  10.2 us
    ppermute x3, starting transfers between devices, on_device(): lax.ppermute(roots_y, 'owner', xor_pairs(n_owner, k * NY))  8.97 us
  transfers between devices with their start and end apart: 19, of which 6 were waited for; matrix products, arithmetic and copies ran while one was open for 11% of the time, Pallas kernels for 10%

profile of v3, /device:TPU:1, one launch (start us, length us, event | category | flops | bytes accessed | tf_op | source)
XLA Modules:
  0.0 251.4 jit_solution(1430965158466270782)
XLA Ops:
  7.2 8.6 %collective-permute-start.2 = (bf16[128,1024]{1,0:T(8,128)(2,1)}, bf16[128,1024]{1,0:T(8,128)(2,1)S(1)}, u32[]{:S(2)}, u32[]{:S(2)}) collective-permute-start(bf16[128,1024]{1,0:T(8,128)(2,1)} %bitcast.88), channel_id=1, source_target_pairs={{0,384},{64,448},{128,256},{192,320},{256,128},{320,192},{384,0},{... | collective-permute-start | bytes 786440 | tf_op jit(solution)/shard_map/ppermute | solution.py:411
  15.8 1.9 collective-permute-start.1
  17.7 2.2 collective-permute-start
  19.9 6.3 %collective-permute-start.3 = (bf16[128,1024]{1,0:T(8,128)(2,1)}, bf16[128,1024]{1,0:T(8,128)(2,1)S(1)}, u32[]{:S(2)}, u32[]{:S(2)}) collective-permute-start(bf16[128,1024]{1,0:T(8,128)(2,1)} %bitcast.91), channel_id=1, source_target_pairs={{0,64},{64,0},{128,192},{192,128},{256,320},{320,256},{384,448},{4... | collective-permute-start | bytes 786440 | tf_op jit(solution)/shard_map/ppermute | solution.py:410
  28.7 1.4 gather_fusion.1
  32.4 5.3 %collective-permute-start.4 = (bf16[128,128]{1,0:T(8,128)(2,1)S(1)}, bf16[128,128]{1,0:T(8,128)(2,1)S(1)}, u32[]{:S(2)}, u32[]{:S(2)}) collective-permute-start(bf16[128,128]{1,0:T(8,128)(2,1)S(1)} %bitcast.101), channel_id=1, source_target_pairs={{0,32},{1,33},{2,34},{3,35},{4,36},{5,37},{6,38},{7,39},{8,40},{9,... | collective-permute-start | bytes 98312 | tf_op jit(solution)/shard_map/ppermute | solution.py:416
  39.8 1.3 collective-permute-done.4
  41.1 20.4 %all-gather = bf16[16,128,128]{2,1,0:T(8,128)(2,1)S(1)} all-gather(bf16[2,128,128]{2,1,0:T(8,128)(2,1)S(1)} %pad_maximum_fusion.5), channel_id=2, replica_groups={{0,1,2,3,4,5,6,7},{8,9,10,11,12,13,14,15},{16,17,18,19,20,21,22,23},{24..., dimensions={0}, use_global_device_ids=true | all-gather | bytes 589824 | tf_op jit(solution)/shard_map/all_gather | solution.py:418
  62.9 8.8 %collective-permute-start.5 = (bf16[3,128,1024]{2,1,0:T(8,128)(2,1)S(1)}, bf16[3,128,1024]{2,1,0:T(8,128)(2,1)S(1)}, u32[]{:S(2)}, u32[]{:S(2)}) collective-permute-start(bf16[3,128,1024]{2,1,0:T(8,128)(2,1)S(1)} %maximum_add_fusion), channel_id=1, source_target_pairs={{0,64},{64,0},{128,192},{192,128},{256,320},{320,256},{384,448},{4... | collective-permute-start | bytes 2359304 | tf_op jit(solution)/shard_map/ppermute | solution.py:419
  71.9 1.0 slice_bitcast_fusion.w_ref
  73.6 2.4 shard_map.194
  76.0 1.0 copy-done.2
  76.9 8.1 %all-to-all-start = ((bf16[32,4,32,128]{3,2,1,0:T(8,128)(2,1)}), bf16[32,4,32,128]{3,2,1,0:T(8,128)(2,1)}, u32[]{:S(2)}, u32[]{:S(2)}) async-start(bf16[32,4,32,128]{3,2,1,0:T(8,128)(2,1)} %bitcast.15), calls=%async_computation | async-start | bytes 2097152 | tf_op jit(solution)/shard_map/all_to_all | solution.py:501
  86.4 6.4 %collective-permute-start.6 = (bf16[1536,128]{1,0:T(8,128)(2,1)S(1)}, bf16[1536,128]{1,0:T(8,128)(2,1)S(1)}, u32[]{:S(2)}, u32[]{:S(2)}) collective-permute-start(bf16[1536,128]{1,0:T(8,128)(2,1)S(1)} %bitcast.99), channel_id=1, source_target_pairs={{0,32},{1,33},{2,34},{3,35},{4,36},{5,37},{6,38},{7,39},{8,40},{9,... | collective-permute-start | bytes 1179656 | tf_op jit(solution)/shard_map/ppermute | solution.py:428
  92.9 1.2 copy-done.14
  94.1 1.2 copy-done.15
  96.3 2.0 fusion.10
  98.4 4.3 %collective-permute-start.9 = (bf16[8,2,128,128]{3,2,1,0:T(8,128)(2,1)S(1)}, bf16[8,2,128,128]{3,2,1,0:T(8,128)(2,1)}, u32[]{:S(2)}, u32[]{:S(2)}) collective-permute-start(bf16[8,2,128,128]{3,2,1,0:T(8,128)(2,1)S(1)} %bitcast.71), channel_id=1, source_target_pairs={{0,24},{1,25},{2,26},{3,27},{4,28},{5,29},{6,30},{7,31},{8,16},{9,... | collective-permute-start | bytes 1572872 | tf_op jit(solution)/shard_map/ppermute | solution.py:423
  102.7 2.4 collective-permute-start.8
  105.1 2.2 collective-permute-start.7
  109.4 1.5 add_bitcast_fusion.1
  110.9 6.5 %collective-permute-start.12 = (bf16[2064,256]{1,0:T(8,128)(2,1)}, bf16[2064,256]{1,0:T(8,128)(2,1)}, u32[]{:S(2)}, u32[]{:S(2)}) collective-permute-start(bf16[2064,256]{1,0:T(8,128)(2,1)} %get-tuple-element.21), channel_id=1, source_target_pairs={{0,416},{1,417},{2,418},{3,419},{4,420},{5,421},{6,422},{7,423},{8... | collective-permute-start | bytes 3170312 | tf_op jit(solution)/shard_map/ppermute | solution.py:444
  117.5 3.7 %collective-permute-start.11 = (bf16[2064,256]{1,0:T(8,128)(2,1)}, bf16[2064,256]{1,0:T(8,128)(2,1)}, u32[]{:S(2)}, u32[]{:S(2)}) collective-permute-start(bf16[2064,256]{1,0:T(8,128)(2,1)} %get-tuple-element.20), channel_id=1, source_target_pairs={{0,128},{1,129},{2,130},{3,131},{4,132},{5,133},{6,134},{7,135},{8... | collective-permute-start | bytes 3170312 | tf_op jit(solution)/shard_map/ppermute | solution.py:444
  121.9 1.2 pad_maximum_fusion.3.k_ref.v_ref
  123.1 7.3 %collective-permute-done.9 = bf16[8,2,128,128]{3,2,1,0:T(8,128)(2,1)} collective-permute-done((bf16[8,2,128,128]{3,2,1,0:T(8,128)(2,1)S(1)}, bf16[8,2,128,128]{3,2,1,0:T(8,128)(2,1)}, u32[]{:S(2)}, u32[]{:S(2)}) %collective-permute-start.9) | collective-permute-done | bytes 524320 | tf_op jit(solution)/shard_map/ppermute | solution.py:423
  130.4 2.6 %collective-permute-start.10 = (bf16[2,2064,256]{2,1,0:T(8,128)(2,1)S(1)}, bf16[2,2064,256]{2,1,0:T(8,128)(2,1)}, u32[]{:S(2)}, u32[]{:S(2)}) collective-permute-start(bf16[2,2064,256]{2,1,0:T(8,128)(2,1)S(1)} %shard_map.198.w0), channel_id=1, source_target_pairs={{0,64},{64,0},{128,192},{192,128},{256,320},{320,256},{384,448},{4... | collective-permute-start | bytes 6340616 | tf_op jit(solution)/shard_map/ppermute | solution.py:433
  133.0 2.9 %pad_maximum_fusion.1.after_ref.root_ref = bf16[4,8,2,2,4,16,128]{6,5,4,3,2,1,0:T(8,128)(2,1)} fusion(bf16[1,8,2,2,4,16,128]{6,5,4,3,2,1,0:T(8,128)(2,1)} %bitcast.23, bf16[1,8,2,2,4,16,128]{6,5,4,3,2,1,0:T(8,128)(2,1)} %bitcast.22, bf16[1,8,2,2,4,16,128]{6,5,4,3,2,1,0:T(8,128)(2,1)} %bitcast.21, bf16[1,8,2,2,4,16,128]{6,5,4,3,2,1,0:T(8,128)(2,1)S(1)} %bitcast.74), kind=kLoop, calls=%fused_computation.6 | loop fusion | flops 3145728 | bytes 4194304 | tf_op jit(solution)/shard_map/stack | solution.py:421
  136.0 1.7 copy-done.6
  137.6 14.4 %shard_map.195 = bf16[32,9,16,128]{3,2,1,0:T(8,128)(2,1)S(1)} custom-call(s32[4]{0:T(128)S(1)} %select_reduce_fusion.7.lens, bf16[32,4,32,128]{3,2,1,0:T(8,128)(2,1)} %all-to-all-done.q_ref, bf16[2,2,2,384,128]{4,3,2,1,0:T(8,128)(2,1)S(1)} %pad_maximum_fusion.3.k_ref.v_ref, bf16[2,2,2,384,128]{4,3,2,1,0:T(8,128)(2,1)S(1)} %pad_maximum_fusion.3.k_ref.v_ref, ...), custom_call_target="tpu_custom_call" | custom-call | flops 2147483648 | bytes 4194304 | tf_op jit(solution)/shard_map/pallas_call | solution.py:182
  152.0 1.0 copy-done.9
  153.0 7.7 %all-to-all-start.1 = ((bf16[32,9,16,128]{3,2,1,0:T(8,128)(2,1)}), bf16[32,9,16,128]{3,2,1,0:T(8,128)(2,1)S(1)}, u32[]{:S(2)}, u32[]{:S(2)}) async-start(bf16[32,9,16,128]{3,2,1,0:T(8,128)(2,1)} %copy-done.9), calls=%async_computation.1 | async-start | bytes 2359296 | tf_op jit(solution)/shard_map/all_to_all | solution.py:512
  160.7 1.2 fusion.8
  162.0 1.7 fusion.4
  163.8 3.2 %pad_maximum_fusion.w2 = bf16[2,2064,256]{2,1,0:T(8,128)(2,1)} fusion(bf16[1,2064,256]{2,1,0:T(8,128)(2,1)} %bitcast.37, bf16[1,2064,256]{2,1,0:T(8,128)(2,1)} %bitcast.35), kind=kLoop, calls=%fused_computation.5 | loop fusion | flops 1056768 | bytes 4227072 | tf_op jit(solution)/shard_map/stack | solution.py:446
  167.0 2.4 collective-permute-start.13
  170.8 8.7 %shard_map.196 = (f32[32,32,128]{2,1,0:T(8,128)S(1)}, f32[32,32,128]{2,1,0:T(8,128)S(1)}) custom-call(s32[1]{0:T(128)} %slice.30.used, s32[44]{0:T(128)S(1)} %get-tuple-element.17.members, s32[44]{0:T(128)S(1)} %get-tuple-element.16.valid, s32[11]{0:T(128)S(1)} %broadcast_minimum_fusion.chunk_tenant, s32[4]{0:T(128)S(1)} %copy-done.29, ...), custom_call_target="tpu_custom_call" | custom-call | flops 4294967296 | bytes 4194304 | tf_op jit(solution)/shard_map/pallas_call | solution.py:256
  181.8 7.0 %all-to-all-done.1.back_ref = bf16[32,9,16,128]{3,2,1,0:T(8,128)(2,1)S(1)} async-done(((bf16[32,9,16,128]{3,2,1,0:T(8,128)(2,1)}), bf16[32,9,16,128]{3,2,1,0:T(8,128)(2,1)S(1)}, u32[]{:S(2)}, u32[]{:S(2)}) %all-to-all-start.1) | async-done | bytes 1179680 | tf_op jit(solution)/shard_map/all_to_all | solution.py:512
  188.7 1.0 copy-done.21
  189.8 1.0 copy-done.23
  190.8 2.1 shard_map.197
  193.7 8.9 %all-to-all-start.2 = ((bf16[8,256,128]{2,1,0:T(8,128)(2,1)}), bf16[8,256,128]{2,1,0:T(8,128)(2,1)S(1)}, u32[]{:S(2)}, u32[]{:S(2)}) async-start(bf16[8,256,128]{2,1,0:T(8,128)(2,1)} %bitcast.79), calls=%async_computation.2 | async-start | bytes 1048576 | tf_op jit(solution)/shard_map/all_to_all | solution.py:519
  203.0 14.1 %all-to-all-done.2.attn_ref = bf16[8,256,128]{2,1,0:T(8,128)(2,1)S(1)} async-done(((bf16[8,256,128]{2,1,0:T(8,128)(2,1)}), bf16[8,256,128]{2,1,0:T(8,128)(2,1)S(1)}, u32[]{:S(2)}, u32[]{:S(2)}) %all-to-all-start.2) | async-done | bytes 524320 | tf_op jit(solution)/shard_map/all_to_all | solution.py:519
  217.1 0.9 copy-done.17
  218.0 0.9 copy-done.25
  219.0 1.6 copy-done.26
  220.6 7.0 %shard_map.199 = (bf16[128,1024]{1,0:T(8,128)(2,1)S(1)}, f32[128,1024]{1,0:T(8,128)S(1)}, bf16[128,1024]{1,0:T(8,128)(2,1)S(1)}) custom-call(bf16[8,256,128]{2,1,0:T(8,128)(2,1)S(1)} %all-to-all-done.2.attn_ref, bf16[1024,1024]{1,0:T(8,128)(2,1)S(1)} %copy-done.26, bf16[128,1024]{1,0:T(8,128)(2,1)S(1)} %bitcast.93, bf16[128,1024]{1,0:T(8,128)(2,1)S(1)} %copy-done.17, ...), custom_call_target="tpu_custom_call" | custom-call | flops 3221225472 | bytes 12582912 | tf_op jit(solution)/shard_map/pallas_call | solution.py:352
  227.6 1.9 collective-permute-start.14
  231.2 12.1 %collective-permute-done.14 = bf16[128,1024]{1,0:T(8,128)(2,1)S(1)} collective-permute-done((bf16[128,1024]{1,0:T(8,128)(2,1)S(1)}, bf16[128,1024]{1,0:T(8,128)(2,1)S(1)}, u32[]{:S(2)}, u32[]{:S(2)}) %collective-permute-start.14) | collective-permute-done | bytes 262176 | tf_op jit(solution)/shard_map/ppermute | solution.py:524
  (154 shorter events, 19.1 us)
Async XLA Ops:
  7.2 19.8 %copy-start = (s32[128]{0:T(128)S(1)}, s32[128]{0:T(128)}, u32[]{:S(2)}) copy-start(s32[128]{0:T(128)} %param.35) | copy-start | bytes 1540
  7.2 31.3 %copy-start.30 = (s32[128]{0:T(128)S(1)}, s32[128]{0:T(128)}, u32[]{:S(2)}) copy-start(s32[128]{0:T(128)} %param.36) | copy-start | bytes 1540
  7.2 32.6 %copy-start.42 = (bf16[512]{0:T(512)(128)(2,1)S(1)}, bf16[512]{0:T(512)(128)(2,1)}, u32[]{:S(2)}) copy-start(bf16[512]{0:T(512)(128)(2,1)} %param.26) | copy-start | bytes 3076
  7.2 55.5 %collective-permute-start.2 = (bf16[128,1024]{1,0:T(8,128)(2,1)}, bf16[128,1024]{1,0:T(8,128)(2,1)S(1)}, u32[]{:S(2)}, u32[]{:S(2)}) collective-permute-start(bf16[128,1024]{1,0:T(8,128)(2,1)} %bitcast.88), channel_id=1, source_target_pairs={{0,384},{64,448},{128,256},{192,320},{256,128},{320,192},{384,0},{... | collective-permute-start | bytes 786440 | tf_op jit(solution)/shard_map/ppermute | solution.py:411
  15.8 47.0 %collective-permute-start.1 = (bf16[128,1024]{1,0:T(8,128)(2,1)}, bf16[128,1024]{1,0:T(8,128)(2,1)S(1)}, u32[]{:S(2)}, u32[]{:S(2)}) collective-permute-start(bf16[128,1024]{1,0:T(8,128)(2,1)} %bitcast.89), channel_id=1, source_target_pairs={{0,256},{64,320},{128,384},{192,448},{256,0},{320,64},{384,128},{4... | collective-permute-start | bytes 786440 | tf_op jit(solution)/shard_map/ppermute | solution.py:411
  17.7 45.0 %collective-permute-start = (bf16[128,1024]{1,0:T(8,128)(2,1)}, bf16[128,1024]{1,0:T(8,128)(2,1)S(1)}, u32[]{:S(2)}, u32[]{:S(2)}) collective-permute-start(bf16[128,1024]{1,0:T(8,128)(2,1)} %bitcast.90), channel_id=1, source_target_pairs={{0,128},{64,192},{128,0},{192,64},{256,384},{320,448},{384,256},{4... | collective-permute-start | bytes 786440 | tf_op jit(solution)/shard_map/ppermute | solution.py:411
  19.9 10.5 %collective-permute-start.3 = (bf16[128,1024]{1,0:T(8,128)(2,1)}, bf16[128,1024]{1,0:T(8,128)(2,1)S(1)}, u32[]{:S(2)}, u32[]{:S(2)}) collective-permute-start(bf16[128,1024]{1,0:T(8,128)(2,1)} %bitcast.91), channel_id=1, source_target_pairs={{0,64},{64,0},{128,192},{192,128},{256,320},{320,256},{384,448},{4... | collective-permute-start | bytes 786440 | tf_op jit(solution)/shard_map/ppermute | solution.py:410
  28.4 44.5 %copy-start.24 = (bf16[4,32,1024]{2,1,0:T(8,128)(2,1)S(1)}, bf16[4,32,1024]{2,1,0:T(8,128)(2,1)}, u32[]{:S(2)}) copy-start(bf16[4,32,1024]{2,1,0:T(8,128)(2,1)} %param.19) | copy-start | bytes 786436
  30.4 43.2 %copy-start.4 = (bf16[128,1024]{1,0:T(8,128)(2,1)}, bf16[128,1024]{1,0:T(8,128)(2,1)S(1)}, u32[]{:S(2)}) copy-start(bf16[128,1024]{1,0:T(8,128)(2,1)S(1)} %collective-permute-done.3.near_ref) | copy-start | bytes 786436
  32.4 8.7 %collective-permute-start.4 = (bf16[128,128]{1,0:T(8,128)(2,1)S(1)}, bf16[128,128]{1,0:T(8,128)(2,1)S(1)}, u32[]{:S(2)}, u32[]{:S(2)}) collective-permute-start(bf16[128,128]{1,0:T(8,128)(2,1)S(1)} %bitcast.101), channel_id=1, source_target_pairs={{0,32},{1,33},{2,34},{3,35},{4,36},{5,37},{6,38},{7,39},{8,40},{9,... | collective-permute-start | bytes 98312 | tf_op jit(solution)/shard_map/ppermute | solution.py:416
  62.8 10.3 %copy-start.16 = (bf16[128,1024]{1,0:T(8,128)(2,1)}, bf16[128,1024]{1,0:T(8,128)(2,1)S(1)}, u32[]{:S(2)}) copy-start(bf16[128,1024]{1,0:T(8,128)(2,1)S(1)} %collective-permute-done.1.tok_b) | copy-start | bytes 786436
  62.9 10.7 %collective-permute-start.5 = (bf16[3,128,1024]{2,1,0:T(8,128)(2,1)S(1)}, bf16[3,128,1024]{2,1,0:T(8,128)(2,1)S(1)}, u32[]{:S(2)}, u32[]{:S(2)}) collective-permute-start(bf16[3,128,1024]{2,1,0:T(8,128)(2,1)S(1)} %maximum_add_fusion), channel_id=1, source_target_pairs={{0,64},{64,0},{128,192},{192,128},{256,320},{320,256},{384,448},{4... | collective-permute-start | bytes 2359304 | tf_op jit(solution)/shard_map/ppermute | solution.py:419
  73.6 3.4 %copy-start.18 = (bf16[3,128,1024]{2,1,0:T(8,128)(2,1)}, bf16[3,128,1024]{2,1,0:T(8,128)(2,1)S(1)}, u32[]{:S(2)}) copy-start(bf16[3,128,1024]{2,1,0:T(8,128)(2,1)S(1)} %collective-permute-done.5.other_ref) | copy-start | bytes 2359300
  73.6 12.8 %copy-start.31 = (bf16[2,2,384,128]{3,2,1,0:T(8,128)(2,1)S(1)}, bf16[2,2,384,128]{3,2,1,0:T(8,128)(2,1)}, u32[]{:S(2)}) copy-start(bf16[2,2,384,128]{3,2,1,0:T(8,128)(2,1)} %param.32) | copy-start | bytes 1179652
  76.9 9.5 %copy-start.27 = (bf16[32,32,128]{2,1,0:T(8,128)(2,1)}, bf16[32,32,128]{2,1,0:T(8,128)(2,1)S(1)}, u32[]{:S(2)}) copy-start(bf16[32,32,128]{2,1,0:T(8,128)(2,1)S(1)} %get-tuple-element.10.q_ref) | copy-start | bytes 786436
  76.9 59.0 %all-to-all-start = ((bf16[32,4,32,128]{3,2,1,0:T(8,128)(2,1)}), bf16[32,4,32,128]{3,2,1,0:T(8,128)(2,1)}, u32[]{:S(2)}, u32[]{:S(2)}) async-start(bf16[32,4,32,128]{3,2,1,0:T(8,128)(2,1)} %bitcast.15), calls=%async_computation | async-start | bytes 2097152 | tf_op jit(solution)/shard_map/all_to_all | solution.py:501
  85.0 118.0 %all-gather.3.cloned.1.call-start = ((), (), s32[]{:S(2)}) async-start(), calls=%async_computation.3 | async-start | bytes 2359296 | tf_op jit(solution)/shard_map/all_gather | solution.py:431
  86.4 9.9 %copy-start.3 = (bf16[4,128,1024]{2,1,0:T(8,128)(2,1)S(1)}, bf16[4,128,1024]{2,1,0:T(8,128)(2,1)}, u32[]{:S(2)}) copy-start(bf16[4,128,1024]{2,1,0:T(8,128)(2,1)} %copy-done.2) | copy-start | bytes 3145732
  86.4 21.0 %collective-permute-start.6 = (bf16[1536,128]{1,0:T(8,128)(2,1)S(1)}, bf16[1536,128]{1,0:T(8,128)(2,1)S(1)}, u32[]{:S(2)}, u32[]{:S(2)}) collective-permute-start(bf16[1536,128]{1,0:T(8,128)(2,1)S(1)} %bitcast.99), channel_id=1, source_target_pairs={{0,32},{1,33},{2,34},{3,35},{4,36},{5,37},{6,38},{7,39},{8,40},{9,... | collective-permute-start | bytes 1179656 | tf_op jit(solution)/shard_map/ppermute | solution.py:428
  95.5 35.0 %copy-start.1 = (bf16[2,2064,256]{2,1,0:T(8,128)(2,1)}, bf16[2,2064,256]{2,1,0:T(8,128)(2,1)S(1)}, u32[]{:S(2)}) copy-start(bf16[2,2064,256]{2,1,0:T(8,128)(2,1)S(1)} %shard_map.198.w0) | copy-start | bytes 6340612
  98.4 32.1 %collective-permute-start.9 = (bf16[8,2,128,128]{3,2,1,0:T(8,128)(2,1)S(1)}, bf16[8,2,128,128]{3,2,1,0:T(8,128)(2,1)}, u32[]{:S(2)}, u32[]{:S(2)}) collective-permute-start(bf16[8,2,128,128]{3,2,1,0:T(8,128)(2,1)S(1)} %bitcast.71), channel_id=1, source_target_pairs={{0,24},{1,25},{2,26},{3,27},{4,28},{5,29},{6,30},{7,31},{8,16},{9,... | collective-permute-start | bytes 1572872 | tf_op jit(solution)/shard_map/ppermute | solution.py:423
  102.7 30.3 %collective-permute-start.8 = (bf16[8,2,128,128]{3,2,1,0:T(8,128)(2,1)S(1)}, bf16[8,2,128,128]{3,2,1,0:T(8,128)(2,1)}, u32[]{:S(2)}, u32[]{:S(2)}) collective-permute-start(bf16[8,2,128,128]{3,2,1,0:T(8,128)(2,1)S(1)} %bitcast.72), channel_id=1, source_target_pairs={{0,16},{1,17},{2,18},{3,19},{4,20},{5,21},{6,22},{7,23},{8,24},{9,... | collective-permute-start | bytes 1572872 | tf_op jit(solution)/shard_map/ppermute | solution.py:423
  105.1 27.9 %collective-permute-start.7 = (bf16[8,2,128,128]{3,2,1,0:T(8,128)(2,1)S(1)}, bf16[8,2,128,128]{3,2,1,0:T(8,128)(2,1)}, u32[]{:S(2)}, u32[]{:S(2)}) collective-permute-start(bf16[8,2,128,128]{3,2,1,0:T(8,128)(2,1)S(1)} %bitcast.73), channel_id=1, source_target_pairs={{0,8},{1,9},{2,10},{3,11},{4,12},{5,13},{6,14},{7,15},{8,0},{9,1},... | collective-permute-start | bytes 1572872 | tf_op jit(solution)/shard_map/ppermute | solution.py:423
  109.4 11.8 %copy-start.34 = (bf16[128,1024]{1,0:T(8,128)(2,1)S(1)}, bf16[128,1024]{1,0:T(8,128)(2,1)}, u32[]{:S(2)}) copy-start(bf16[128,1024]{1,0:T(8,128)(2,1)} %param.21) | copy-start | bytes 786436
  110.9 52.8 %collective-permute-start.12 = (bf16[2064,256]{1,0:T(8,128)(2,1)}, bf16[2064,256]{1,0:T(8,128)(2,1)}, u32[]{:S(2)}, u32[]{:S(2)}) collective-permute-start(bf16[2064,256]{1,0:T(8,128)(2,1)} %get-tuple-element.21), channel_id=1, source_target_pairs={{0,416},{1,417},{2,418},{3,419},{4,420},{5,421},{6,422},{7,423},{8... | collective-permute-start | bytes 3170312 | tf_op jit(solution)/shard_map/ppermute | solution.py:444
  117.5 46.3 %collective-permute-start.11 = (bf16[2064,256]{1,0:T(8,128)(2,1)}, bf16[2064,256]{1,0:T(8,128)(2,1)}, u32[]{:S(2)}, u32[]{:S(2)}) collective-permute-start(bf16[2064,256]{1,0:T(8,128)(2,1)} %get-tuple-element.20), channel_id=1, source_target_pairs={{0,128},{1,129},{2,130},{3,131},{4,132},{5,133},{6,134},{7,135},{8... | collective-permute-start | bytes 3170312 | tf_op jit(solution)/shard_map/ppermute | solution.py:444
  130.4 72.5 %collective-permute-start.10 = (bf16[2,2064,256]{2,1,0:T(8,128)(2,1)S(1)}, bf16[2,2064,256]{2,1,0:T(8,128)(2,1)}, u32[]{:S(2)}, u32[]{:S(2)}) collective-permute-start(bf16[2,2064,256]{2,1,0:T(8,128)(2,1)S(1)} %shard_map.198.w0), channel_id=1, source_target_pairs={{0,64},{64,0},{128,192},{192,128},{256,320},{320,256},{384,448},{4... | collective-permute-start | bytes 6340616 | tf_op jit(solution)/shard_map/ppermute | solution.py:433
  136.0 1.7 copy-start.6
  153.0 35.7 %all-to-all-start.1 = ((bf16[32,9,16,128]{3,2,1,0:T(8,128)(2,1)}), bf16[32,9,16,128]{3,2,1,0:T(8,128)(2,1)S(1)}, u32[]{:S(2)}, u32[]{:S(2)}) async-start(bf16[32,9,16,128]{3,2,1,0:T(8,128)(2,1)} %copy-done.9), calls=%async_computation.1 | async-start | bytes 2359296 | tf_op jit(solution)/shard_map/all_to_all | solution.py:512
  163.7 5.7 %copy-start.5 = (bf16[128,1024]{1,0:T(8,128)(2,1)S(1)}, bf16[128,1024]{1,0:T(8,128)(2,1)}, u32[]{:S(2)}) copy-start(bf16[128,1024]{1,0:T(8,128)(2,1)} %copy-done.4) | copy-start | bytes 786436
  163.7 5.7 %copy-start.32 = (bf16[1024,3,128]{2,0,1:T(8,128)(2,1)S(1)}, bf16[1024,3,128]{2,0,1:T(8,128)(2,1)}, u32[]{:S(2)}) copy-start(bf16[1024,3,128]{2,0,1:T(8,128)(2,1)} %param.20) | copy-start | bytes 2359300
  163.8 5.9 %copy-start.19 = (bf16[3,128,1024]{2,1,0:T(8,128)(2,1)S(1)}, bf16[3,128,1024]{2,1,0:T(8,128)(2,1)}, u32[]{:S(2)}) copy-start(bf16[3,128,1024]{2,1,0:T(8,128)(2,1)} %copy-done.18) | copy-start | bytes 2359300
  163.8 6.3 %copy-start.35 = (bf16[512,128]{1,0:T(8,128)(2,1)S(1)}, bf16[512,128]{1,0:T(8,128)(2,1)}, u32[]{:S(2)}) copy-start(bf16[512,128]{1,0:T(8,128)(2,1)} %fusion.10) | copy-start | bytes 393220
  167.0 3.7 %copy-start.7 = (bf16[4,8,2,2,4,16,128]{6,5,4,3,2,1,0:T(8,128)(2,1)S(1)}, bf16[4,8,2,2,4,16,128]{6,5,4,3,2,1,0:T(8,128)(2,1)}, u32[]{:S(2)}) copy-start(bf16[4,8,2,2,4,16,128]{6,5,4,3,2,1,0:T(8,128)(2,1)} %pad_maximum_fusion.1.after_ref.root_ref) | copy-start | bytes 6291460
  167.0 3.7 %copy-start.28 = (bf16[32,32,128]{2,1,0:T(8,128)(2,1)S(1)}, bf16[32,32,128]{2,1,0:T(8,128)(2,1)}, u32[]{:S(2)}) copy-start(bf16[32,32,128]{2,1,0:T(8,128)(2,1)} %copy-done.27) | copy-start | bytes 786436
  167.0 3.7 %copy-start.29 = (s32[4]{0:T(128)S(1)}, s32[4]{0:T(128)}, u32[]{:S(2)}) copy-start(s32[4]{0:T(128)} %root_len.1) | copy-start | bytes 52
  167.0 35.9 %collective-permute-start.13 = (bf16[2,2064,256]{2,1,0:T(8,128)(2,1)}, bf16[2,2064,256]{2,1,0:T(8,128)(2,1)}, u32[]{:S(2)}, u32[]{:S(2)}) collective-permute-start(bf16[2,2064,256]{2,1,0:T(8,128)(2,1)} %pad_maximum_fusion.w2), channel_id=1, source_target_pairs={{0,64},{64,0},{128,192},{192,128},{256,320},{320,256},{384,448},{4... | collective-permute-start | bytes 6340616 | tf_op jit(solution)/shard_map/ppermute | solution.py:447
  170.7 31.8 %copy-start.37 = (bf16[1024]{0:T(1024)(128)(2,1)S(1)}, bf16[1024]{0:T(1024)(128)(2,1)}, u32[]{:S(2)}) copy-start(bf16[1024]{0:T(1024)(128)(2,1)} %param.24) | copy-start | bytes 6148
  170.8 31.8 %copy-start.38 = (bf16[1024]{0:T(1024)(128)(2,1)S(1)}, bf16[1024]{0:T(1024)(128)(2,1)}, u32[]{:S(2)}) copy-start(bf16[1024]{0:T(1024)(128)(2,1)} %param.23) | copy-start | bytes 6148
  170.8 31.9 %copy-start.39 = (bf16[1024]{0:T(1024)(128)(2,1)S(1)}, bf16[1024]{0:T(1024)(128)(2,1)}, u32[]{:S(2)}) copy-start(bf16[1024]{0:T(1024)(128)(2,1)} %param.22) | copy-start | bytes 6148
  170.8 31.9 %copy-start.40 = (bf16[1024]{0:T(1024)(128)(2,1)S(1)}, bf16[1024]{0:T(1024)(128)(2,1)}, u32[]{:S(2)}) copy-start(bf16[1024]{0:T(1024)(128)(2,1)} %param.30) | copy-start | bytes 6148
  170.8 31.9 %copy-start.41 = (bf16[1024]{0:T(1024)(128)(2,1)S(1)}, bf16[1024]{0:T(1024)(128)(2,1)}, u32[]{:S(2)}) copy-start(bf16[1024]{0:T(1024)(128)(2,1)} %param.29) | copy-start | bytes 6148
  181.8 20.8 %copy-start.36 = (bf16[1024]{0:T(1024)(128)(2,1)S(1)}, bf16[1024]{0:T(1024)(128)(2,1)}, u32[]{:S(2)}) copy-start(bf16[1024]{0:T(1024)(128)(2,1)} %param.28) | copy-start | bytes 6148
  193.7 23.4 %all-to-all-start.2 = ((bf16[8,256,128]{2,1,0:T(8,128)(2,1)}), bf16[8,256,128]{2,1,0:T(8,128)(2,1)S(1)}, u32[]{:S(2)}, u32[]{:S(2)}) async-start(bf16[8,256,128]{2,1,0:T(8,128)(2,1)} %bitcast.79), calls=%async_computation.2 | async-start | bytes 1048576 | tf_op jit(solution)/shard_map/all_to_all | solution.py:519
  202.9 26.6 %copy-start.11 = (bf16[1024,128]{1,0:T(8,128)(2,1)S(1)}, bf16[1024,128]{1,0:T(8,128)(2,1)}, u32[]{:S(2)}) copy-start(bf16[1024,128]{1,0:T(8,128)(2,1)} %copy-done.10) | copy-start | bytes 786436
  202.9 26.6 %copy-start.13 = (bf16[1024,128]{1,0:T(8,128)(2,1)S(1)}, bf16[1024,128]{1,0:T(8,128)(2,1)}, u32[]{:S(2)}) copy-start(bf16[1024,128]{1,0:T(8,128)(2,1)} %copy-done.12) | copy-start | bytes 786436
  219.0 1.6 copy-start.26
  227.6 15.7 %collective-permute-start.14 = (bf16[128,1024]{1,0:T(8,128)(2,1)S(1)}, bf16[128,1024]{1,0:T(8,128)(2,1)S(1)}, u32[]{:S(2)}, u32[]{:S(2)}) collective-permute-start(bf16[128,1024]{1,0:T(8,128)(2,1)S(1)} %get-tuple-element.15), channel_id=1, source_target_pairs={{0,256},{64,320},{128,384},{192,448},{256,0},{320,64},{384,128},{4... | collective-permute-start | bytes 786440 | tf_op jit(solution)/shard_map/ppermute | solution.py:524
  (14 other events, 12.9 us)
Sparse Core Ops, SparseCore 0:
  122.1 45.0 all-gather.2

commit v4 on v3

--- a/solution.py
+++ b/solution.py
@@ -53,6 +53,92 @@
     first = jnp.broadcast_to(stacked[:rows], (rows, LANES))
     second = jnp.broadcast_to(stacked[rows:], (rows, LANES))
     return jnp.where(lane < HD, first, second)
+
+
+def table_kernel(
+    coords, leaf_of, parent, place, length, dst_b, dst_l, pos, lens, members, valid, chunk_tenant, used, tenant_of, count
+):
+    my_z, my_x, my_y, blk = (coords[i] for i in range(4))
+    reqs = leaf_of.shape[0]
+    req_dev = reqs // N_BLK
+    tenants = count.shape[0]
+
+    def slot_index(slot):
+        owner = slot // 2
+        return (owner % PEERS) * SLOTS + ((owner // PEERS) ^ my_z) * 2 + slot % 2
+
+    for t in range(tenants):
+        count[t] = 0
+
+    def first_pass(r, _):
+        leaf = leaf_of[r]
+        branch = parent[leaf]
+        tenant = parent[branch]
+        dst_b[r] = slot_index(place[branch])
+        dst_l[r] = slot_index(place[leaf])
+        rel = (r // req_dev) ^ blk
+        pos[r] = ((rel % 2) * (N_BLK // 2) + rel // 2) * req_dev + r % req_dev
+        tenant_of[r] = tenant
+        count[tenant] = count[tenant] + 1
+        return 0
+
+    lax.fori_loop(0, reqs, first_pass, 0)
+
+    def clear(i, _):
+        members[i] = 0
+        valid[i] = 0
+        return 0
+
+    lax.fori_loop(0, members.shape[0], clear, 0)
+    end = 0
+    for t in range(tenants):
+        chunks = (count[t] + CHUNK - 1) // CHUNK
+
+        def name(c, _, t=t):
+            chunk_tenant[c] = t
+            return 0
+
+        lax.fori_loop(end, end + chunks, name, 0)
+        count[t] = end * CHUNK
+        end = end + chunks
+    used[0] = end
+
+    def second_pass(r, _):
+        tenant = tenant_of[r]
+        seat = count[tenant]
+        count[tenant] = seat + 1
+        members[seat] = pos[r]
+        valid[seat] = 1
+        return 0
+
+    lax.fori_loop(0, reqs, second_pass, 0)
+
+    def node(n, _):
+        slot = place[n]
+        owner = slot // 2
+
+        @pl.when(owner % PEERS == my_x * NY + my_y)
+        def _():
+            lens[((owner // PEERS) ^ my_z) * 2 + slot % 2] = length[n]
+
+        return 0
+
+    lax.fori_loop(0, place.shape[0], node, 0)
+
+
+def make_tables(coords, leaf_of, parent, place, length, tenants):
+    reqs = leaf_of.shape[0]
+    max_chunks = reqs // CHUNK + tenants - 1
+    smem = pl.BlockSpec(memory_space=pltpu.SMEM)
+    sizes = (reqs, reqs, reqs, SLOTS, max_chunks * CHUNK, max_chunks * CHUNK, max_chunks, 1)
+    return pl.pallas_call(
+        table_kernel,
+        out_shape=tuple(jax.ShapeDtypeStruct((n,), I32) for n in sizes),
+        in_specs=[smem] * 5,
+        out_specs=(smem,) * len(sizes),
+        scratch_shapes=[pltpu.SMEM((reqs,), I32), pltpu.SMEM((tenants,), I32)],
+        cost_estimate=pl.CostEstimate(flops=1 << 20, bytes_accessed=1 << 12, transcendentals=0),
+    )(coords, leaf_of, parent, place, length)
 
 
 def query_kernel(pos, dst_b, dst_l, half_ref, near_ref, other_ref, w_ref, after_ref, q_ref, out_ref):
@@ -221,7 +307,7 @@
         z = (n // per) % NZ
         y = (n // (per * NZ)) % NY
         x = n // (per * NY * NZ)
-        place = (((z ^ coords[0]) * NX + (x ^ coords[1])) * NY + y) * per + row
+        place = (((z ^ coords[0]) * NX + x) * NY + y) * per + row
         scores = jnp.where(place < root_len[tenant], dot_nt(q, keys), NEG)
         own_row = (lax.broadcasted_iota(I32, (2 * rows, rows), 0) % rows) // suf
         own_col = lax.broadcasted_iota(I32, (2 * rows, rows), 1) // suf
@@ -322,7 +408,7 @@
     return center * lax.rsqrt(spread + EPS) * gain + shift
 
 
-def feed_kernel(attn_ref, w_out_ref, tok_a, tok_b, vec_ref, w0, w1, w2, w3, norm_ref, own_ref, far_ref):
+def feed_kernel(attn_ref, w_out_ref, tok_a, tok_b, vec_ref, w0, w1, w2, w3, w4, w5, norm_ref, own_ref, far_ref):
     rows = tok_a.shape[0]
     width = tok_a.shape[1]
     attn = jnp.concatenate([attn_ref[h] for h in range(N_BLK)], axis=1)
@@ -333,7 +419,7 @@
     norm_ref[...] = norm[:rows]
     total = jnp.zeros((2 * rows, width), F32)
     units = w0.shape[-1]
-    for w in [ref.at[i] for ref in (w0, w1, w2, w3) for i in range(2)]:
+    for w in [ref.at[i] for ref in (w0, w1) for i in range(2)] + [w2, w3, w4, w5]:
         bias = w[width + units * (width // units) :].astype(F32)[0:1]
         inner = dot_nn(norm, w[:width]) + bias
         hidden = (0.5 * inner * (1.0 + lax.erf(inner * (0.5**0.5)))).astype(BF16)
@@ -390,7 +476,6 @@
     cols = w_qkv.shape[2]
     own_rows = req_dev * suf
     reqs = req_leaf.shape[0]
-    nodes = node_place.shape[0]
     node_max = node_cache.shape[2]
     tenants = root_cache.shape[1]
     root_per = root_cache.shape[2]
@@ -406,22 +491,25 @@
         flat = value.reshape(-1, value.shape[-1])
         return jnp.minimum(jnp.abs(flat[:1, :1]), 0)
 
+    coords = jnp.stack([my_z, my_x, my_y, blk]).astype(I32)
+    dst_b, dst_l, pos, lens, members, valid, chunk_tenant, used = make_tables(
+        coords, req_leaf, node_parent, node_place, node_len, tenants
+    )
+
     tok = tokens.reshape(own_rows, width)
     near = lax.ppermute(tok, "blk", swap)
     half = [lax.ppermute(tok, "blk", xor_pairs(N_BLK, 2 * k)) for k in range(1, n_own)]
     tok_far, last_come = half[1], half[2]
 
     n_owner = NX * NY * NZ
-    roots = root_cache.reshape(-1, LANES) + zero_after(near)
+    roots = root_cache.reshape(-1, LANES)
     roots = jnp.stack([roots, lax.ppermute(roots, "owner", xor_pairs(n_owner, NX * NY))])
-    y_groups = [[g * NY + y for y in range(NY)] for g in range(NZ * NX)]
-    roots_y = lax.all_gather(roots, "owner", axis=0, tiled=False, axis_index_groups=y_groups)
-    other = lax.ppermute(jnp.stack(half) + zero_after(roots_y), "blk", swap)
+    for came in half + [near, jnp.broadcast_to(pos[None, :1], (1, 1)).astype(BF16)]:
+        roots = roots + zero_after(came)
+    groups = [[z * PEERS + p for p in range(PEERS)] for z in range(NZ)]
+    roots = lax.all_gather(roots, "owner", axis=0, tiled=False, axis_index_groups=groups)
+    other = lax.ppermute(jnp.stack(half), "blk", swap)
     half = jnp.stack([tok] + half)
-    roots = jnp.stack(
-        [roots_y]
-        + [lax.ppermute(roots_y, "owner", xor_pairs(n_owner, k * NY)) for k in range(1, NX)]
-    )
     roots = roots.reshape(NX, NY, NZ, 2, tenants, root_per, LANES)
 
     node_rows = node_cache.reshape(-1, LANES) + zero_after(last_come)
@@ -431,60 +519,8 @@
     w_out_all = lax.all_gather(w_out + zero_after(last_come), "blk", axis=0, tiled=True)
     packs = pack_weights(w_up, w_down, b_up, last_come)
     pack_side = lax.ppermute(packs, "blk", swap)
-    z_chips = NZ * n_own
-
-    def to_neighbour(step):
-        pairs = []
-        for dev in range(n_owner * N_BLK):
-            b, own = dev // n_owner, dev % n_owner
-            z = (own // PEERS * n_own + b // 2 + step) % z_chips
-            pairs.append((dev, (z % n_own * 2 + b % 2) * n_owner + z // n_own * PEERS + own % PEERS))
-        part = ((blk // 2 + step + n_own) % n_own) // (n_own // 2)
-        sent = lax.dynamic_index_in_dim(packs, part, 0, keepdims=False) + zero_after(node_far)
-        return lax.ppermute(sent, ("blk", "owner"), pairs)
-
-    pack_next = jnp.stack([to_neighbour(1), to_neighbour(-1)])
-    pack_last = lax.ppermute(pack_next, "blk", swap)
-    packs = [packs, pack_side, pack_next, pack_last]
-
-    branch = node_parent[req_leaf]
-    tenant = node_parent[branch]
-
-    def slot_index(place):
-        at = place // 2
-        z, x, y = at // (NX * NY), (at // NY) % NX, at % NY
-        return ((x * NY + y) * SLOTS + (z ^ my_z) * 2 + place % 2).astype(I32)
-
-    dst_b = slot_index(node_place[branch])
-    dst_l = slot_index(node_place[req_leaf])
-    req_ids = jnp.arange(reqs, dtype=I32)
-    rel = (req_ids // req_dev) ^ blk
-    pos = ((rel % 2) * n_own + rel // 2) * req_dev + req_ids % req_dev
-    local = jnp.arange(SLOTS, dtype=I32)
-    local_slot = ((((local // 2) ^ my_z) * NX + my_x) * NY + my_y) * 2 + local % 2
-    lens = jnp.sum(jnp.where(local_slot[:, None] == node_place[None, :], node_len[None, :], 0), axis=1)
-    same = tenant[:, None] == tenant[None, :]
-    within = jnp.sum(jnp.where(same & (req_ids[None, :] < req_ids[:, None]), 1, 0), axis=1)
-    tenant_ids = jnp.arange(tenants, dtype=I32)
-    counts = jnp.sum(jnp.where(tenant_ids[:, None] == tenant[None, :], 1, 0), axis=1)
-    chunks = (counts + CHUNK - 1) // CHUNK
-    ends = jnp.sum(jnp.where(tenant_ids[None, :] <= tenant_ids[:, None], chunks[None, :], 0), axis=1)
-    first = ends - chunks
-    first_of = jnp.sum(jnp.where(tenant[:, None] == tenant_ids[None, :], first[None, :], 0), axis=1)
-    place_in = first_of * CHUNK + within
-    max_chunks = reqs // CHUNK + tenants - 1
-    seats = jnp.arange(max_chunks * CHUNK, dtype=I32)
-    seated = seats[:, None] == place_in[None, :]
-    members = jnp.sum(jnp.where(seated, pos[None, :], 0), axis=1).astype(I32)
-    valid = jnp.sum(jnp.where(seated, 1, 0), axis=1).astype(I32)
-    chunk_ids = jnp.arange(max_chunks, dtype=I32)
-    chunk_tenant = jnp.minimum(
-        jnp.sum(jnp.where(chunk_ids[:, None] >= ends[None, :], 1, 0), axis=1), tenants - 1
-    ).astype(I32)
-    used = ends[-1:].astype(I32)
-    coords = jnp.stack([my_z, my_x]).astype(I32)
-
-    q, outgoing = query_and_route(pos, dst_b, dst_l, half, near, other, w_qkv[:, 0], suf, roots_y)
+
+    q, outgoing = query_and_route(pos, dst_b, dst_l, half, near, other, w_qkv[:, 0], suf, last_come)
     outgoing = outgoing.reshape(PEERS, SLOTS, suf, cols)
 
     def project(which):
@@ -497,7 +533,6 @@
         )
         return out.astype(BF16).reshape(reqs, suf, cols)
 
-    groups = [[z * PEERS + p for p in range(PEERS)] for z in range(NZ)]
     incoming = lax.all_to_all(
         outgoing, "owner", split_axis=0, concat_axis=0, axis_index_groups=groups, tiled=True
     )
@@ -508,7 +543,22 @@
     new_caches = jnp.stack([k_new, v_new]).reshape(2, N_BLK, req_dev, suf, cols)
     new_caches = jnp.take(new_caches, order, axis=1).reshape(2, reqs, suf, cols)
 
-    answers = node_attention(lens, incoming, caches, roots)
+    answers = node_attention(lens, incoming, caches, packs)
+    z_chips = NZ * n_own
+
+    def to_neighbour(step):
+        pairs = []
+        for dev in range(n_owner * N_BLK):
+            b, own = dev // n_owner, dev % n_owner
+            z = (own // PEERS * n_own + b // 2 + step) % z_chips
+            pairs.append((dev, (z % n_own * 2 + b % 2) * n_owner + z // n_own * PEERS + own % PEERS))
+        part = ((blk // 2 + step + n_own) % n_own) // (n_own // 2)
+        sent = lax.dynamic_index_in_dim(packs, part, 0, keepdims=False) + zero_after(answers)
+        return lax.ppermute(sent, ("blk", "owner"), pairs)
+
+    pack_next = [to_neighbour(1), to_neighbour(-1)]
+    pack_last = [lax.ppermute(part, "blk", swap) for part in pack_next]
+    parts = [packs, pack_side] + pack_next + pack_last
     back = lax.all_to_all(
         answers, "owner", split_axis=0, concat_axis=0, axis_index_groups=groups, tiled=True
     )
@@ -520,7 +570,7 @@
         send.reshape(N_BLK, 2 * own_rows, cols), "blk", split_axis=0, concat_axis=0, tiled=True
     )
     vectors = jnp.stack([b_out, gain1, shift1])
-    own_norm, down, down_far = feed_forward(attn, w_out_all, tok, tok_far, vectors, packs)
+    own_norm, down, down_far = feed_forward(attn, w_out_all, tok, tok_far, vectors, parts)
     total = down + lax.ppermute(down_far, "blk", xor_pairs(N_BLK, N_BLK // 2)).astype(F32)
     result = layer_norm(
         own_norm.astype(F32) + total + b_down.astype(F32), gain2, shift2

time: 253 us -> 230 us (0.909)
  blocking collectives: 20.4 us -> 0 us
  waiting for transfers between devices: 42.3 us -> 59.5 us
  starting transfers between devices: 90.3 us -> 76 us
  Pallas kernels: 34.6 us -> 42.2 us
  other arithmetic: 16.2 us -> 8.61 us
  local copies, waits for them, and re-layouts: 23.9 us -> 20.3 us
    all_gather x1 -> x0, blocking collectives: 20.4 us -> none  [on_device(): lax.all_gather(roots, 'owner', axis=0, tiled=False, axis_index_groups=y_g...]
    ppermute x2, waiting for transfers between devices: 0.01 us -> 18.6 us  [to_neighbour(): return lax.ppermute(sent, ('blk', 'owner'), pairs)]
    ppermute x1, waiting for transfers between devices: 0.01 us -> 12.2 us  [on_device(): node_far = lax.ppermute(node_rows, 'owner', xor_pairs(n_owner, NX * NY))]
    ppermute x5 -> x3, starting transfers between devices: 20.1 us -> 8.26 us  [the longest x2 5.5 us: on_device(): pack_last = [lax.ppermute(part, 'blk', swap) for part in pack_next]]
    all_to_all x1, waiting for transfers between devices: 6.97 us -> 0.01 us  [on_device(): lax.all_to_all(answers, 'owner', split_axis=0, concat_axis=0, axis_index_...]
    ppermute x5 -> x3, waiting for transfers between devices: 7.86 us -> 1.66 us  [the longest x1 1.65 us: on_device(): other = lax.ppermute(jnp.stack(half), 'blk', swap)]
    pallas_call x0 -> x1, Pallas kernels: none -> 6.2 us  [make_tables(): pl.pallas_call(table_kernel, out_shape=tuple((jax.ShapeDtypeStruct((n,),...]
    another operation x4 -> x3, other arithmetic: 6.26 us -> 1.27 us  [the longest x1 0.6 us: on_device(): coords = jnp.stack([my_z, my_x, my_y, blk]).astype(I32)]
  transfers between devices with their start and end apart: 19 -> 18, of which waited for: 6 -> 7; matrix products, arithmetic and copies ran while one was open for 11% -> 6% of each run, Pallas kernels for 10% -> 15%
where the time goes in v4:
time: 230 us; the launch traced here: 229 us
  starting transfers between devices  76 us (33%)
  waiting for transfers between devices  59.5 us (26%)
  Pallas kernels  42.2 us (18%)
  local copies, waits for them, and re-layouts  20.3 us (9%)
  between operations  18.3 us (8%)
  other arithmetic  8.61 us (4%)
  matrix products  3.97 us (2%)
    ppermute x2, waiting for transfers between devices, to_neighbour(): return lax.ppermute(sent, ('blk', 'owner'), pairs)  18.6 us
    ppermute x3, starting transfers between devices, on_device(): lax.ppermute(tok, 'blk', xor_pairs(N_BLK, 2 * k))  15.6 us
    unnamed x88, local copies, waits for them, and re-layouts  15.3 us
    pallas_call x1, Pallas kernels, node_attention(): pl.pallas_call(node_kernel, out_shape=jax.ShapeDtypeStruct((peers, 2 * sl...  14.3 us
    all_to_all x1, waiting for transfers between devices, on_device(): lax.all_to_all(send.reshape(N_BLK, 2 * own_rows, cols), 'blk', split_axis...  12.7 us
    ppermute x1, waiting for transfers between devices, on_device(): lax.ppermute(down_far, 'blk', xor_pairs(N_BLK, N_BLK // 2)).astype(F32)  12.6 us
    ppermute x1, waiting for transfers between devices, on_device(): node_far = lax.ppermute(node_rows, 'owner', xor_pairs(n_owner, NX * NY))  12.2 us
    all_to_all x1, starting transfers between devices, on_device(): lax.all_to_all(outgoing, 'owner', split_axis=0, concat_axis=0, axis_index...  9.95 us
  transfers between devices with their start and end apart: 18, of which 7 were waited for; matrix products, arithmetic and copies ran while one was open for 6% of the time, Pallas kernels for 15%

profile of v4, /device:TPU:1, one launch (start us, length us, event | category | flops | bytes accessed | tf_op | source)
XLA Modules:
  0.0 229.0 jit_solution(17197666251233697306)
XLA Ops:
  7.2 8.6 %collective-permute-start.2 = (bf16[128,1024]{1,0:T(8,128)(2,1)}, bf16[128,1024]{1,0:T(8,128)(2,1)S(1)}, u32[]{:S(2)}, u32[]{:S(2)}) collective-permute-start(bf16[128,1024]{1,0:T(8,128)(2,1)} %bitcast.78), channel_id=1, source_target_pairs={{0,384},{64,448},{128,256},{192,320},{256,128},{320,192},{384,0},{... | collective-permute-start | bytes 786440 | tf_op jit(solution)/shard_map/ppermute | solution.py:501
  15.8 2.9 %collective-permute-start.3 = (bf16[128,1024]{1,0:T(8,128)(2,1)}, bf16[128,1024]{1,0:T(8,128)(2,1)S(1)}, u32[]{:S(2)}, u32[]{:S(2)}) collective-permute-start(bf16[128,1024]{1,0:T(8,128)(2,1)} %bitcast.79), channel_id=1, source_target_pairs={{0,64},{64,0},{128,192},{192,128},{256,320},{320,256},{384,448},{4... | collective-permute-start | bytes 786440 | tf_op jit(solution)/shard_map/ppermute | solution.py:500
  18.7 1.9 collective-permute-start.1
  20.6 5.1 %collective-permute-start = (bf16[128,1024]{1,0:T(8,128)(2,1)}, bf16[128,1024]{1,0:T(8,128)(2,1)S(1)}, u32[]{:S(2)}, u32[]{:S(2)}) collective-permute-start(bf16[128,1024]{1,0:T(8,128)(2,1)} %bitcast.81), channel_id=1, source_target_pairs={{0,128},{64,192},{128,0},{192,64},{256,384},{320,448},{384,256},{4... | collective-permute-start | bytes 786440 | tf_op jit(solution)/shard_map/ppermute | solution.py:501
  25.7 5.3 %collective-permute-start.6 = (bf16[128,128]{1,0:T(8,128)(2,1)}, bf16[128,128]{1,0:T(8,128)(2,1)S(1)}, u32[]{:S(2)}, u32[]{:S(2)}) collective-permute-start(bf16[128,128]{1,0:T(8,128)(2,1)} %bitcast.90), channel_id=1, source_target_pairs={{0,32},{1,33},{2,34},{3,35},{4,36},{5,37},{6,38},{7,39},{8,40},{9,... | collective-permute-start | bytes 98312 | tf_op jit(solution)/shard_map/ppermute | solution.py:506
  31.6 6.2 %shard_map.194 = (s32[32]{0:T(128)}, s32[32]{0:T(128)}, s32[32]{0:T(128)}, s32[4]{0:T(128)}, s32[44]{0:T(128)}, /*index=5*/s32[44]{0:T(128)}, s32[11]{0:T(128)}, s32[1]{0:T(128)}) custom-call(s32[4]{0:T(128)} %pad_add_fusion.coords, s32[32]{0:T(128)} %leaf_of.1, s32[128]{0:T(128)} %parent.1, s32[128]{0:T(128)} %place.1, s32[128]{0:T(128)} %length.1), custom_call_target="tpu_custom_call" | custom-call | flops 1048576 | bytes 4096 | tf_op jit(solution)/shard_map/pallas_call | solution.py:134
  43.4 1.4 fusion.21
  45.0 2.8 %collective-permute-start.4 = (bf16[3,128,1024]{2,1,0:T(8,128)(2,1)S(1)}, bf16[3,128,1024]{2,1,0:T(8,128)(2,1)S(1)}, u32[]{:S(2)}, u32[]{:S(2)}) collective-permute-start(bf16[3,128,1024]{2,1,0:T(8,128)(2,1)S(1)} %pad_maximum_fusion.1), channel_id=1, source_target_pairs={{0,64},{64,0},{128,192},{192,128},{256,320},{320,256},{384,448},{4... | collective-permute-start | bytes 2359304 | tf_op jit(solution)/shard_map/ppermute | solution.py:511
  48.0 1.7 collective-permute-done.4.other_ref
  49.6 2.4 %shard_map.195 = (bf16[32,32,128]{2,1,0:T(8,128)(2,1)S(1)}, bf16[128,32,128]{2,1,0:T(8,128)(2,1)}) custom-call(s32[32]{0:T(128)S(1)} %copy-done.22, s32[32]{0:T(128)S(1)} %copy-done.18, s32[32]{0:T(128)S(1)} %copy-done.20, bf16[4,128,1024]{2,1,0:T(8,128)(2,1)S(1)} %pad_maximum_fusion.half_ref, bf16[128,1024]{1,0:T(8,128)(2,1)S(1)} %collective-permute-done.3.near_ref, ...), custom_call_target="tpu_custom_call" | custom-call | flops 268435456 | bytes 4194304 | tf_op jit(solution)/shard_map/pallas_call | solution.py:169
  52.1 9.9 %all-to-all-start = ((bf16[32,4,32,128]{3,2,1,0:T(8,128)(2,1)}), bf16[32,4,32,128]{3,2,1,0:T(8,128)(2,1)}, u32[]{:S(2)}, u32[]{:S(2)}) async-start(bf16[32,4,32,128]{3,2,1,0:T(8,128)(2,1)} %bitcast.10), calls=%async_computation | async-start | bytes 2097152 | tf_op jit(solution)/shard_map/all_to_all | solution.py:536
  62.2 0.8 broadcast_add_fusion
  63.0 7.0 %collective-permute-start.5 = (bf16[1536,128]{1,0:T(8,128)(2,1)}, bf16[1536,128]{1,0:T(8,128)(2,1)}, u32[]{:S(2)}, u32[]{:S(2)}) collective-permute-start(bf16[1536,128]{1,0:T(8,128)(2,1)} %bitcast.13), channel_id=1, source_target_pairs={{0,32},{1,33},{2,34},{3,35},{4,36},{5,37},{6,38},{7,39},{8,40},{9,... | collective-permute-start | bytes 1179656 | tf_op jit(solution)/shard_map/ppermute | solution.py:516
  70.9 1.1 fusion.10
  72.6 2.8 %collective-permute-start.7 = (bf16[2,2064,256]{2,1,0:T(8,128)(2,1)S(1)}, bf16[2,2064,256]{2,1,0:T(8,128)(2,1)}, u32[]{:S(2)}, u32[]{:S(2)}) collective-permute-start(bf16[2,2064,256]{2,1,0:T(8,128)(2,1)S(1)} %shard_map.196.after_ref.w0), channel_id=1, source_target_pairs={{0,64},{64,0},{128,192},{192,128},{256,320},{320,256},{384,448},{4... | collective-permute-start | bytes 6340616 | tf_op jit(solution)/shard_map/ppermute | solution.py:521
  75.5 12.2 %collective-permute-done.5 = bf16[1536,128]{1,0:T(8,128)(2,1)} collective-permute-done((bf16[1536,128]{1,0:T(8,128)(2,1)}, bf16[1536,128]{1,0:T(8,128)(2,1)}, u32[]{:S(2)}, u32[]{:S(2)}) %collective-permute-start.5) | collective-permute-done | bytes 393248 | tf_op jit(solution)/shard_map/ppermute | solution.py:516
  87.7 1.1 pad_maximum_fusion.2.k_ref.v_ref
  88.7 0.9 all-to-all-done.q_ref
  89.6 14.3 %shard_map.197 = bf16[32,9,16,128]{3,2,1,0:T(8,128)(2,1)S(1)} custom-call(s32[4]{0:T(128)S(1)} %copy-done.32, bf16[32,4,32,128]{3,2,1,0:T(8,128)(2,1)} %all-to-all-done.q_ref, bf16[2,2,2,384,128]{4,3,2,1,0:T(8,128)(2,1)S(1)} %pad_maximum_fusion.2.k_ref.v_ref, bf16[2,2,2,384,128]{4,3,2,1,0:T(8,128)(2,1)S(1)} %pad_maximum_fusion.2.k_ref.v_ref, ...), custom_call_target="tpu_custom_call" | custom-call | flops 2147483648 | bytes 4194304 | tf_op jit(solution)/shard_map/pallas_call | solution.py:268
  104.0 1.0 copy-done.3
  105.0 8.3 %all-to-all-start.1 = ((bf16[32,9,16,128]{3,2,1,0:T(8,128)(2,1)}), bf16[32,9,16,128]{3,2,1,0:T(8,128)(2,1)S(1)}, u32[]{:S(2)}, u32[]{:S(2)}) async-start(bf16[32,9,16,128]{3,2,1,0:T(8,128)(2,1)} %copy-done.3), calls=%async_computation.1 | async-start | bytes 2359296 | tf_op jit(solution)/shard_map/all_to_all | solution.py:562
  113.2 1.7 fusion.4
  115.0 1.2 slice.46
  117.0 2.4 %collective-permute-start.8 = (bf16[2064,256]{1,0:T(8,128)(2,1)S(1)}, bf16[2064,256]{1,0:T(8,128)(2,1)}, u32[]{:S(2)}, u32[]{:S(2)}) collective-permute-start(bf16[2064,256]{1,0:T(8,128)(2,1)S(1)} %get-tuple-element.35), channel_id=1, source_target_pairs={{0,128},{1,129},{2,130},{3,131},{4,132},{5,133},{6,134},{7,135},{8... | collective-permute-start | bytes 3170312 | tf_op jit(solution)/shard_map/ppermute | solution.py:557
  119.5 5.8 %collective-permute-start.9 = (bf16[2064,256]{1,0:T(8,128)(2,1)S(1)}, bf16[2064,256]{1,0:T(8,128)(2,1)}, u32[]{:S(2)}, u32[]{:S(2)}) collective-permute-start(bf16[2064,256]{1,0:T(8,128)(2,1)S(1)} %get-tuple-element.34), channel_id=1, source_target_pairs={{0,416},{1,417},{2,418},{3,419},{4,420},{5,421},{6,422},{7,423},{8... | collective-permute-start | bytes 3170312 | tf_op jit(solution)/shard_map/ppermute | solution.py:557
  126.5 0.7 maximum_convert_fusion.1
  127.2 18.6 %collective-permute-done.8.w2 = bf16[2064,256]{1,0:T(8,128)(2,1)} collective-permute-done((bf16[2064,256]{1,0:T(8,128)(2,1)S(1)}, bf16[2064,256]{1,0:T(8,128)(2,1)}, u32[]{:S(2)}, u32[]{:S(2)}) %collective-permute-start.8) | collective-permute-done | bytes 1056800 | tf_op jit(solution)/shard_map/ppermute | solution.py:557
  145.9 3.6 %collective-permute-start.10 = (bf16[2064,256]{1,0:T(8,128)(2,1)}, bf16[2064,256]{1,0:T(8,128)(2,1)}, u32[]{:S(2)}, u32[]{:S(2)}) collective-permute-start(bf16[2064,256]{1,0:T(8,128)(2,1)} %collective-permute-done.8.w2), channel_id=1, source_target_pairs={{0,64},{64,0},{128,192},{192,128},{256,320},{320,256},{384,448},{4... | collective-permute-start | bytes 3170312 | tf_op jit(solution)/shard_map/ppermute | solution.py:560
  149.5 1.9 collective-permute-start.11
  151.4 0.9 copy-done.4
  153.0 1.6 copy-done.25
  154.6 0.9 copy-done.27
  158.0 9.6 %shard_map.198 = (f32[32,32,128]{2,1,0:T(8,128)S(1)}, f32[32,32,128]{2,1,0:T(8,128)S(1)}) custom-call(s32[1]{0:T(128)} %get-tuple-element.22.used, s32[44]{0:T(128)S(1)} %copy-done.29, s32[44]{0:T(128)S(1)} %copy-done.30, s32[11]{0:T(128)S(1)} %copy-done.31, s32[4]{0:T(128)S(1)} %copy-done.28, s32[4]{0:T(128)S(1)} %copy-done.24, ...), custom_call_target="tpu_custom_call" | custom-call | flops 4294967296 | bytes 4194304 | tf_op jit(solution)/shard_map/pallas_call | solution.py:342
  167.6 0.8 copy-done.12
  168.4 0.8 copy-done.14
  169.1 1.0 copy-done.13
  170.2 1.0 copy-done.15
  173.1 2.1 shard_map.199
  175.1 0.8 copy-done.2
  175.9 5.7 %all-to-all-start.2 = ((bf16[8,256,128]{2,1,0:T(8,128)(2,1)}), bf16[8,256,128]{2,1,0:T(8,128)(2,1)S(1)}, u32[]{:S(2)}, u32[]{:S(2)}) async-start(bf16[8,256,128]{2,1,0:T(8,128)(2,1)} %bitcast.68), calls=%async_computation.2 | async-start | bytes 1048576 | tf_op jit(solution)/shard_map/all_to_all | solution.py:569
  182.7 0.8 all-gather.5.cloned.1.call-done.w_out_ref
  183.5 12.7 %all-to-all-done.2.attn_ref = bf16[8,256,128]{2,1,0:T(8,128)(2,1)S(1)} async-done(((bf16[8,256,128]{2,1,0:T(8,128)(2,1)}), bf16[8,256,128]{2,1,0:T(8,128)(2,1)S(1)}, u32[]{:S(2)}, u32[]{:S(2)}) %all-to-all-start.2) | async-done | bytes 524320 | tf_op jit(solution)/shard_map/all_to_all | solution.py:569
  196.1 0.9 copy-done.17
  197.1 7.5 %shard_map.200 = (bf16[128,1024]{1,0:T(8,128)(2,1)S(1)}, f32[128,1024]{1,0:T(8,128)S(1)}, bf16[128,1024]{1,0:T(8,128)(2,1)S(1)}) custom-call(bf16[8,256,128]{2,1,0:T(8,128)(2,1)S(1)} %all-to-all-done.2.attn_ref, bf16[1024,1024]{1,0:T(8,128)(2,1)} %all-gather.5.cloned.1.call-done.w_out_ref, bf16[128,1024]{1,0:T(8,128)(2,1)S(1)} %bitcast.83, ...), custom_call_target="tpu_custom_call" | custom-call | flops 3221225472 | bytes 12582912 | tf_op jit(solution)/shard_map/pallas_call | solution.py:438
  204.6 1.9 collective-permute-start.12
  207.3 0.9 broadcast_select_fusion
  208.2 12.6 %collective-permute-done.12 = bf16[128,1024]{1,0:T(8,128)(2,1)S(1)} collective-permute-done((bf16[128,1024]{1,0:T(8,128)(2,1)S(1)}, bf16[128,1024]{1,0:T(8,128)(2,1)S(1)}, u32[]{:S(2)}, u32[]{:S(2)}) %collective-permute-start.12) | collective-permute-done | bytes 262176 | tf_op jit(solution)/shard_map/ppermute | solution.py:574
  221.3 0.9 add_convert_fusion
  (131 shorter events, 13.6 us)
Async XLA Ops:
  7.2 40.6 %copy-start.34 = (bf16[1024,3,128]{2,0,1:T(8,128)(2,1)S(1)}, bf16[1024,3,128]{2,0,1:T(8,128)(2,1)}, u32[]{:S(2)}) copy-start(bf16[1024,3,128]{2,0,1:T(8,128)(2,1)} %param.20) | copy-start | bytes 2359300
  7.2 144.2 %all-gather.3.cloned.1.call-start = ((), (), s32[]{:S(2)}) async-start(), calls=%async_computation.3 | async-start | bytes 2162688 | tf_op jit(solution)/shard_map/all_gather | solution.py:510
  7.2 31.3 %collective-permute-start.2 = (bf16[128,1024]{1,0:T(8,128)(2,1)}, bf16[128,1024]{1,0:T(8,128)(2,1)S(1)}, u32[]{:S(2)}, u32[]{:S(2)}) collective-permute-start(bf16[128,1024]{1,0:T(8,128)(2,1)} %bitcast.78), channel_id=1, source_target_pairs={{0,384},{64,448},{128,256},{192,320},{256,128},{320,192},{384,0},{... | collective-permute-start | bytes 786440 | tf_op jit(solution)/shard_map/ppermute | solution.py:501
  15.8 23.9 %collective-permute-start.3 = (bf16[128,1024]{1,0:T(8,128)(2,1)}, bf16[128,1024]{1,0:T(8,128)(2,1)S(1)}, u32[]{:S(2)}, u32[]{:S(2)}) collective-permute-start(bf16[128,1024]{1,0:T(8,128)(2,1)} %bitcast.79), channel_id=1, source_target_pairs={{0,64},{64,0},{128,192},{192,128},{256,320},{320,256},{384,448},{4... | collective-permute-start | bytes 786440 | tf_op jit(solution)/shard_map/ppermute | solution.py:500
  18.7 22.2 %collective-permute-start.1 = (bf16[128,1024]{1,0:T(8,128)(2,1)}, bf16[128,1024]{1,0:T(8,128)(2,1)S(1)}, u32[]{:S(2)}, u32[]{:S(2)}) collective-permute-start(bf16[128,1024]{1,0:T(8,128)(2,1)} %bitcast.80), channel_id=1, source_target_pairs={{0,256},{64,320},{128,384},{192,448},{256,0},{320,64},{384,128},{4... | collective-permute-start | bytes 786440 | tf_op jit(solution)/shard_map/ppermute | solution.py:501
  20.6 21.5 %collective-permute-start = (bf16[128,1024]{1,0:T(8,128)(2,1)}, bf16[128,1024]{1,0:T(8,128)(2,1)S(1)}, u32[]{:S(2)}, u32[]{:S(2)}) collective-permute-start(bf16[128,1024]{1,0:T(8,128)(2,1)} %bitcast.81), channel_id=1, source_target_pairs={{0,128},{64,192},{128,0},{192,64},{256,384},{320,448},{384,256},{4... | collective-permute-start | bytes 786440 | tf_op jit(solution)/shard_map/ppermute | solution.py:501
  25.7 17.7 %collective-permute-start.6 = (bf16[128,128]{1,0:T(8,128)(2,1)}, bf16[128,128]{1,0:T(8,128)(2,1)S(1)}, u32[]{:S(2)}, u32[]{:S(2)}) collective-permute-start(bf16[128,128]{1,0:T(8,128)(2,1)} %bitcast.90), channel_id=1, source_target_pairs={{0,32},{1,33},{2,34},{3,35},{4,36},{5,37},{6,38},{7,39},{8,40},{9,... | collective-permute-start | bytes 98312 | tf_op jit(solution)/shard_map/ppermute | solution.py:506
  40.9 6.9 %copy-start.8 = (bf16[128,1024]{1,0:T(8,128)(2,1)}, bf16[128,1024]{1,0:T(8,128)(2,1)S(1)}, u32[]{:S(2)}) copy-start(bf16[128,1024]{1,0:T(8,128)(2,1)S(1)} %collective-permute-done.1.tok_b) | copy-start | bytes 786436
  44.9 3.0 %copy-start.16 = (bf16[4,32,1024]{2,1,0:T(8,128)(2,1)S(1)}, bf16[4,32,1024]{2,1,0:T(8,128)(2,1)}, u32[]{:S(2)}) copy-start(bf16[4,32,1024]{2,1,0:T(8,128)(2,1)} %param.19) | copy-start | bytes 786436
  45.0 4.7 %collective-permute-start.4 = (bf16[3,128,1024]{2,1,0:T(8,128)(2,1)S(1)}, bf16[3,128,1024]{2,1,0:T(8,128)(2,1)S(1)}, u32[]{:S(2)}, u32[]{:S(2)}) collective-permute-start(bf16[3,128,1024]{2,1,0:T(8,128)(2,1)S(1)} %pad_maximum_fusion.1), channel_id=1, source_target_pairs={{0,64},{64,0},{128,192},{192,128},{256,320},{320,256},{384,448},{4... | collective-permute-start | bytes 2359304 | tf_op jit(solution)/shard_map/ppermute | solution.py:511
  47.8 1.9 copy-start.18
  47.8 1.9 copy-start.20
  47.8 1.8 copy-start.22
  48.0 22.9 %copy-start.1 = (bf16[4,128,1024]{2,1,0:T(8,128)(2,1)}, bf16[4,128,1024]{2,1,0:T(8,128)(2,1)S(1)}, u32[]{:S(2)}) copy-start(bf16[4,128,1024]{2,1,0:T(8,128)(2,1)S(1)} %pad_maximum_fusion.half_ref) | copy-start | bytes 3145732
  49.6 2.5 %copy-start.10 = (bf16[3,128,1024]{2,1,0:T(8,128)(2,1)}, bf16[3,128,1024]{2,1,0:T(8,128)(2,1)S(1)}, u32[]{:S(2)}) copy-start(bf16[3,128,1024]{2,1,0:T(8,128)(2,1)S(1)} %collective-permute-done.4.other_ref) | copy-start | bytes 2359300
  52.1 10.0 %copy-start.26 = (bf16[32,32,128]{2,1,0:T(8,128)(2,1)}, bf16[32,32,128]{2,1,0:T(8,128)(2,1)S(1)}, u32[]{:S(2)}) copy-start(bf16[32,32,128]{2,1,0:T(8,128)(2,1)S(1)} %get-tuple-element.26.q_ref) | copy-start | bytes 786436
  52.1 10.1 %copy-start.43 = (bf16[512]{0:T(512)(128)(2,1)S(1)}, bf16[512]{0:T(512)(128)(2,1)}, u32[]{:S(2)}) copy-start(bf16[512]{0:T(512)(128)(2,1)} %param.26) | copy-start | bytes 3076
  52.1 10.2 %copy-start.33 = (bf16[2,2,384,128]{3,2,1,0:T(8,128)(2,1)S(1)}, bf16[2,2,384,128]{3,2,1,0:T(8,128)(2,1)}, u32[]{:S(2)}) copy-start(bf16[2,2,384,128]{3,2,1,0:T(8,128)(2,1)} %param.32) | copy-start | bytes 1179652
  52.1 18.0 %copy-start.36 = (bf16[128,1024]{1,0:T(8,128)(2,1)S(1)}, bf16[128,1024]{1,0:T(8,128)(2,1)}, u32[]{:S(2)}) copy-start(bf16[128,1024]{1,0:T(8,128)(2,1)} %param.21) | copy-start | bytes 786436
  52.1 37.5 %all-to-all-start = ((bf16[32,4,32,128]{3,2,1,0:T(8,128)(2,1)}), bf16[32,4,32,128]{3,2,1,0:T(8,128)(2,1)}, u32[]{:S(2)}, u32[]{:S(2)}) async-start(bf16[32,4,32,128]{3,2,1,0:T(8,128)(2,1)} %bitcast.10), calls=%async_computation | async-start | bytes 2097152 | tf_op jit(solution)/shard_map/all_to_all | solution.py:536
  62.1 121.4 %all-gather.5.cloned.1.call-start = ((), (), s32[]{:S(2)}) async-start(), calls=%async_computation.4 | async-start | bytes 2359296 | tf_op jit(solution)/shard_map/all_gather | solution.py:519
  63.0 24.6 %collective-permute-start.5 = (bf16[1536,128]{1,0:T(8,128)(2,1)}, bf16[1536,128]{1,0:T(8,128)(2,1)}, u32[]{:S(2)}, u32[]{:S(2)}) collective-permute-start(bf16[1536,128]{1,0:T(8,128)(2,1)} %bitcast.13), channel_id=1, source_target_pairs={{0,32},{1,33},{2,34},{3,35},{4,36},{5,37},{6,38},{7,39},{8,40},{9,... | collective-permute-start | bytes 1179656 | tf_op jit(solution)/shard_map/ppermute | solution.py:516
  70.8 1.2 copy-start.6
  70.8 1.6 copy-start.7
  72.6 44.2 %copy-start = (bf16[2,2064,256]{2,1,0:T(8,128)(2,1)}, bf16[2,2064,256]{2,1,0:T(8,128)(2,1)S(1)}, u32[]{:S(2)}) copy-start(bf16[2,2064,256]{2,1,0:T(8,128)(2,1)S(1)} %shard_map.196.after_ref.w0) | copy-start | bytes 6340612
  72.6 17.0 %copy-start.32 = (s32[4]{0:T(128)S(1)}, s32[4]{0:T(128)}, u32[]{:S(2)}) copy-start(s32[4]{0:T(128)} %get-tuple-element.20.lens) | copy-start | bytes 52
  72.6 110.1 %collective-permute-start.7 = (bf16[2,2064,256]{2,1,0:T(8,128)(2,1)S(1)}, bf16[2,2064,256]{2,1,0:T(8,128)(2,1)}, u32[]{:S(2)}, u32[]{:S(2)}) collective-permute-start(bf16[2,2064,256]{2,1,0:T(8,128)(2,1)S(1)} %shard_map.196.after_ref.w0), channel_id=1, source_target_pairs={{0,64},{64,0},{128,192},{192,128},{256,320},{320,256},{384,448},{4... | collective-permute-start | bytes 6340616 | tf_op jit(solution)/shard_map/ppermute | solution.py:521
  104.0 1.0 copy-start.3
  105.0 64.2 %all-to-all-start.1 = ((bf16[32,9,16,128]{3,2,1,0:T(8,128)(2,1)}), bf16[32,9,16,128]{3,2,1,0:T(8,128)(2,1)S(1)}, u32[]{:S(2)}, u32[]{:S(2)}) async-start(bf16[32,9,16,128]{3,2,1,0:T(8,128)(2,1)} %copy-done.3), calls=%async_computation.1 | async-start | bytes 2359296 | tf_op jit(solution)/shard_map/all_to_all | solution.py:562
  116.8 8.4 %copy-start.35 = (bf16[1024,3,128]{2,0,1:T(8,128)(2,1)S(1)}, bf16[1024,3,128]{2,0,1:T(8,128)(2,1)}, u32[]{:S(2)}) copy-start(bf16[1024,3,128]{2,0,1:T(8,128)(2,1)} %param.20) | copy-start | bytes 2359300
  117.0 8.7 %copy-start.11 = (bf16[3,128,1024]{2,1,0:T(8,128)(2,1)S(1)}, bf16[3,128,1024]{2,1,0:T(8,128)(2,1)}, u32[]{:S(2)}) copy-start(bf16[3,128,1024]{2,1,0:T(8,128)(2,1)} %copy-done.10) | copy-start | bytes 2359300
  117.0 28.9 %collective-permute-start.8 = (bf16[2064,256]{1,0:T(8,128)(2,1)S(1)}, bf16[2064,256]{1,0:T(8,128)(2,1)}, u32[]{:S(2)}, u32[]{:S(2)}) collective-permute-start(bf16[2064,256]{1,0:T(8,128)(2,1)S(1)} %get-tuple-element.35), channel_id=1, source_target_pairs={{0,128},{1,129},{2,130},{3,131},{4,132},{5,133},{6,134},{7,135},{8... | collective-permute-start | bytes 3170312 | tf_op jit(solution)/shard_map/ppermute | solution.py:557
  119.4 6.7 %copy-start.37 = (bf16[512,128]{1,0:T(8,128)(2,1)S(1)}, bf16[512,128]{1,0:T(8,128)(2,1)}, u32[]{:S(2)}) copy-start(bf16[512,128]{1,0:T(8,128)(2,1)} %fusion.10) | copy-start | bytes 393220
  119.5 30.0 %collective-permute-start.9 = (bf16[2064,256]{1,0:T(8,128)(2,1)S(1)}, bf16[2064,256]{1,0:T(8,128)(2,1)}, u32[]{:S(2)}, u32[]{:S(2)}) collective-permute-start(bf16[2064,256]{1,0:T(8,128)(2,1)S(1)} %get-tuple-element.34), channel_id=1, source_target_pairs={{0,416},{1,417},{2,418},{3,419},{4,420},{5,421},{6,422},{7,423},{8... | collective-permute-start | bytes 3170312 | tf_op jit(solution)/shard_map/ppermute | solution.py:557
  145.9 37.6 %collective-permute-start.10 = (bf16[2064,256]{1,0:T(8,128)(2,1)}, bf16[2064,256]{1,0:T(8,128)(2,1)}, u32[]{:S(2)}, u32[]{:S(2)}) collective-permute-start(bf16[2064,256]{1,0:T(8,128)(2,1)} %collective-permute-done.8.w2), channel_id=1, source_target_pairs={{0,64},{64,0},{128,192},{192,128},{256,320},{320,256},{384,448},{4... | collective-permute-start | bytes 3170312 | tf_op jit(solution)/shard_map/ppermute | solution.py:560
  149.5 34.0 %collective-permute-start.11 = (bf16[2064,256]{1,0:T(8,128)(2,1)}, bf16[2064,256]{1,0:T(8,128)(2,1)}, u32[]{:S(2)}, u32[]{:S(2)}) collective-permute-start(bf16[2064,256]{1,0:T(8,128)(2,1)} %collective-permute-done.9.w3), channel_id=1, source_target_pairs={{0,64},{64,0},{128,192},{192,128},{256,320},{320,256},{384,448},{4... | collective-permute-start | bytes 3170312 | tf_op jit(solution)/shard_map/ppermute | solution.py:560
  153.0 1.6 copy-start.25
  169.1 1.0 copy-start.13
  170.2 1.0 copy-start.15
  175.9 6.4 %copy-start.38 = (bf16[1024]{0:T(1024)(128)(2,1)S(1)}, bf16[1024]{0:T(1024)(128)(2,1)}, u32[]{:S(2)}) copy-start(bf16[1024]{0:T(1024)(128)(2,1)} %param.23) | copy-start | bytes 6148
  175.9 6.4 %copy-start.39 = (bf16[1024]{0:T(1024)(128)(2,1)S(1)}, bf16[1024]{0:T(1024)(128)(2,1)}, u32[]{:S(2)}) copy-start(bf16[1024]{0:T(1024)(128)(2,1)} %param.24) | copy-start | bytes 6148
  175.9 6.5 %copy-start.40 = (bf16[1024]{0:T(1024)(128)(2,1)S(1)}, bf16[1024]{0:T(1024)(128)(2,1)}, u32[]{:S(2)}) copy-start(bf16[1024]{0:T(1024)(128)(2,1)} %param.28) | copy-start | bytes 6148
  175.9 6.5 %copy-start.41 = (bf16[1024]{0:T(1024)(128)(2,1)S(1)}, bf16[1024]{0:T(1024)(128)(2,1)}, u32[]{:S(2)}) copy-start(bf16[1024]{0:T(1024)(128)(2,1)} %param.29) | copy-start | bytes 6148
  175.9 6.5 %copy-start.42 = (bf16[1024]{0:T(1024)(128)(2,1)S(1)}, bf16[1024]{0:T(1024)(128)(2,1)}, u32[]{:S(2)}) copy-start(bf16[1024]{0:T(1024)(128)(2,1)} %param.30) | copy-start | bytes 6148
  175.9 20.2 %copy-start.9 = (bf16[128,1024]{1,0:T(8,128)(2,1)S(1)}, bf16[128,1024]{1,0:T(8,128)(2,1)}, u32[]{:S(2)}) copy-start(bf16[128,1024]{1,0:T(8,128)(2,1)} %copy-done.8) | copy-start | bytes 786436
  175.9 20.2 %all-to-all-start.2 = ((bf16[8,256,128]{2,1,0:T(8,128)(2,1)}), bf16[8,256,128]{2,1,0:T(8,128)(2,1)S(1)}, u32[]{:S(2)}, u32[]{:S(2)}) async-start(bf16[8,256,128]{2,1,0:T(8,128)(2,1)} %bitcast.68), calls=%async_computation.2 | async-start | bytes 1048576 | tf_op jit(solution)/shard_map/all_to_all | solution.py:569
  182.7 23.9 %copy-start.5 = (bf16[1024,128]{1,0:T(8,128)(2,1)S(1)}, bf16[1024,128]{1,0:T(8,128)(2,1)}, u32[]{:S(2)}) copy-start(bf16[1024,128]{1,0:T(8,128)(2,1)} %maximum_convert_fusion.1) | copy-start | bytes 786436
  204.6 16.2 %collective-permute-start.12 = (bf16[128,1024]{1,0:T(8,128)(2,1)S(1)}, bf16[128,1024]{1,0:T(8,128)(2,1)S(1)}, u32[]{:S(2)}, u32[]{:S(2)}) collective-permute-start(bf16[128,1024]{1,0:T(8,128)(2,1)S(1)} %get-tuple-element.31), channel_id=1, source_target_pairs={{0,256},{64,320},{128,384},{192,448},{256,0},{320,64},{384,128},{4... | collective-permute-start | bytes 786440 | tf_op jit(solution)/shard_map/ppermute | solution.py:574
  (14 other events, 10.1 us)
Sparse Core Ops, SparseCore 0:
  45.0 94.8 all-gather.2
  141.9 41.5 all-gather.4

commit v5 on v4

--- a/solution.py
+++ b/solution.py
@@ -209,81 +209,69 @@
     )(up, down, bias.reshape(1, units), after)
 
 
-def node_kernel(lens, q_ref, k_ref, v_ref, after_ref, out_ref):
+def node_kernel(lens, q_ref, cache_ref, after_ref, out_ref):
     del after_ref
-    slot = pl.program_id(0)
-    peers, _, suf, _ = q_ref.shape
-    group = 8
+    peers, slots, suf, _ = q_ref.shape
+    group = 4
     rows = group * suf
-    node_max = k_ref.shape[2]
-    keys = both_heads(k_ref[0, 0])
-    values = both_heads(v_ref[0, 0])
-    keep = lax.broadcasted_iota(I32, (1, node_max), 1) < lens[slot]
-    lane = lax.broadcasted_iota(I32, (group, HALF, LANES), 2)
-    piece = lane % (HD // 2) - 3 * slot
-
-    @pl.when(slot == 0)
-    def _():
-        out_ref[:, 2 * SLOTS] = jnp.zeros((peers, HALF, LANES), BF16)
-
-    for g in range(peers // group):
-        part = slice(g * group, (g + 1) * group)
-        q = q_ref[part, slot].reshape(rows, LANES)
-        scores = dot_nt(q, keys)
-        weights, totals, masses = [], [], []
-        for h in range(2):
-            own = jnp.where(keep, scores[:, h * node_max : (h + 1) * node_max], NEG)
-            peak = jnp.max(own, axis=1, keepdims=True)
-            weight = jnp.exp(own - peak)
-            total = jnp.sum(weight, axis=1, keepdims=True)
-            weights.append(weight.astype(BF16))
-            totals.append(total)
-            masses.append(peak + jnp.log(total))
-        mixed = dot_nn(jnp.concatenate(weights, axis=1), values)
-        total = by_head(jnp.concatenate(totals, axis=0))
-        mass = by_head(jnp.concatenate(masses, axis=0))
-        out = (mixed / total).astype(BF16).reshape(group, 2, HALF, LANES)
-        out_ref[part, 2 * slot] = out[:, 0]
-        out_ref[part, 2 * slot + 1] = out[:, 1]
-        mass = mass.reshape(group, 2, HALF, LANES)
-        mass = jnp.where(lane % HD < HD // 2, mass[:, 0], mass[:, 1])
-        high = mass.astype(BF16).astype(F32)
-        rest = mass - high
-        mid = rest.astype(BF16).astype(F32)
-        sent = jnp.where(piece == 0, high, jnp.where(piece == 1, mid, rest - mid))
-        held = out_ref[part, 2 * SLOTS].astype(F32)
-        held = jnp.where((piece >= 0) & (piece < 3), sent, held)
-        out_ref[part, 2 * SLOTS] = held.astype(BF16)
+    node_max = cache_ref.shape[3]
+    out_ref[:, 2 * SLOTS] = jnp.zeros((peers, HALF, LANES), BF16)
+
+    def one_slot(slot, _):
+        keys = both_heads(cache_ref[slot // 2, 0, slot % 2])
+        values = cache_ref[slot // 2, 1, slot % 2]
+        values = jnp.concatenate([both_heads(values), both_heads(jnp.ones_like(values))], axis=1)
+        keep = lax.broadcasted_iota(I32, (1, node_max), 1) < lens[slot]
+        lane = lax.broadcasted_iota(I32, (group, HALF, LANES), 2)
+        piece = lane % (HD // 2) - 3 * slot
+        for g in range(peers // group):
+            part = slice(g * group, (g + 1) * group)
+            q = q_ref[part, slot].reshape(rows, LANES)
+            scores = dot_nt(q, keys)
+            weights, peaks = [], []
+            for h in range(2):
+                own = jnp.where(keep, scores[:, h * node_max : (h + 1) * node_max], NEG)
+                peak = jnp.max(own, axis=1, keepdims=True)
+                weights.append(jnp.exp(own - peak).astype(BF16))
+                peaks.append(peak)
+            mixed = dot_nn(jnp.concatenate(weights, axis=1), values)
+            total = mixed[:, LANES:]
+            mass = by_head(jnp.concatenate(peaks, axis=0)) + jnp.log(total)
+            out = (mixed[:, :LANES] / total).astype(BF16).reshape(group, 2, HALF, LANES)
+            out_ref[part, 2 * slot] = out[:, 0]
+            out_ref[part, 2 * slot + 1] = out[:, 1]
+            mass = mass.reshape(group, 2, HALF, LANES)
+            mass = jnp.where(lane % HD < HD // 2, mass[:, 0], mass[:, 1])
+            high = mass.astype(BF16).astype(F32)
+            rest = mass - high
+            mid = rest.astype(BF16).astype(F32)
+            sent = jnp.where(piece == 0, high, jnp.where(piece == 1, mid, rest - mid))
+            held = out_ref[part, 2 * SLOTS].astype(F32)
+            held = jnp.where((piece >= 0) & (piece < 3), sent, held)
+            out_ref[part, 2 * SLOTS] = held.astype(BF16)
+        return 0
+
+    lax.fori_loop(0, slots, one_slot, 0)
 
 
 def node_attention(lens, queries, caches, after):
     peers, slots, suf, _ = queries.shape
-    node_max = caches.shape[3]
-
-    def cache_spec(which):
-        return pl.BlockSpec(
-            (1, 1, pl.Squeezed(), node_max, LANES), lambda s, n: (s // 2, which, s % 2, 0, 0)
-        )
-
+    vmem = pl.BlockSpec(memory_space=pltpu.VMEM)
     return pl.pallas_call(
         node_kernel,
         out_shape=jax.ShapeDtypeStruct((peers, 2 * slots + 1, HALF, LANES), BF16),
-        grid_spec=pltpu.PrefetchScalarGridSpec(
-            num_scalar_prefetch=1,
-            grid=(slots,),
-            in_specs=[
-                pl.BlockSpec((peers, slots, suf, LANES), lambda s, n: (0, 0, 0, 0)),
-                cache_spec(0),
-                cache_spec(1),
-                pl.BlockSpec(memory_space=pl.ANY),
-            ],
-            out_specs=pl.BlockSpec((peers, 2 * slots + 1, HALF, LANES), lambda s, n: (0, 0, 0, 0)),
-        ),
-        compiler_params=pltpu.CompilerParams(vmem_limit_bytes=40 << 20),
+        in_specs=[
+            pl.BlockSpec(memory_space=pltpu.SMEM),
+            vmem,
+            vmem,
+            pl.BlockSpec(memory_space=pl.ANY),
+        ],
+        out_specs=vmem,
+        compiler_params=pltpu.CompilerParams(vmem_limit_bytes=24 << 20),
         cost_estimate=pl.CostEstimate(
             flops=2 << 30, bytes_accessed=4 << 20, transcendentals=4 << 20
         ),
-    )(lens, queries, caches, caches, after)
+    )(lens, queries, caches, after)
 
 
 def root_kernel(
@@ -304,10 +292,11 @@
         values = root_ref[:, :, :, 1, tenant].reshape(root_rows, LANES)
         n = lax.broadcasted_iota(I32, (1, root_rows), 1)
         row = n % per
-        z = (n // per) % NZ
-        y = (n // (per * NZ)) % NY
-        x = n // (per * NY * NZ)
-        place = (((z ^ coords[0]) * NX + x) * NY + y) * per + row
+        z = ((n // per) % NZ) ^ coords[0]
+        x_side = (n // (per * NZ)) % 2
+        y = (n // (per * NZ * 2)) % NY
+        x = (n // (per * NZ * 2 * NY) * 2 + coords[1]) ^ x_side
+        place = ((z * NX + x) * NY + y) * per + row
         scores = jnp.where(place < root_len[tenant], dot_nt(q, keys), NEG)
         own_row = (lax.broadcasted_iota(I32, (2 * rows, rows), 0) % rows) // suf
         own_col = lax.broadcasted_iota(I32, (2 * rows, rows), 1) // suf
@@ -504,13 +493,18 @@
     n_owner = NX * NY * NZ
     roots = root_cache.reshape(-1, LANES)
     roots = jnp.stack([roots, lax.ppermute(roots, "owner", xor_pairs(n_owner, NX * NY))])
-    for came in half + [near, jnp.broadcast_to(pos[None, :1], (1, 1)).astype(BF16)]:
-        roots = roots + zero_after(came)
-    groups = [[z * PEERS + p for p in range(PEERS)] for z in range(NZ)]
+    roots = jnp.stack([roots, lax.ppermute(roots, "owner", xor_pairs(n_owner, NY))])
+    roots = roots + zero_after(last_come)
+    groups = [
+        [(z * NX + parity + 2 * i) * NY + y for i in range(NX // 2) for y in range(NY)]
+        for z in range(NZ)
+        for parity in range(2)
+    ]
     roots = lax.all_gather(roots, "owner", axis=0, tiled=False, axis_index_groups=groups)
-    other = lax.ppermute(jnp.stack(half), "blk", swap)
+    planned = zero_after(jnp.broadcast_to(pos[None, :1], (1, 1)).astype(BF16))
+    other = lax.ppermute(jnp.stack(half) + planned, "blk", swap)
     half = jnp.stack([tok] + half)
-    roots = roots.reshape(NX, NY, NZ, 2, tenants, root_per, LANES)
+    roots = roots.reshape(NX // 2 * NY, 2, NZ, 2, tenants, root_per, LANES)
 
     node_rows = node_cache.reshape(-1, LANES) + zero_after(last_come)
     node_far = lax.ppermute(node_rows, "owner", xor_pairs(n_owner, NX * NY))
@@ -533,6 +527,7 @@
         )
         return out.astype(BF16).reshape(reqs, suf, cols)
 
+    groups = [[z * PEERS + p for p in range(PEERS)] for z in range(NZ)]
     incoming = lax.all_to_all(
         outgoing, "owner", split_axis=0, concat_axis=0, axis_index_groups=groups, tiled=True
     )
@@ -562,8 +557,9 @@
     back = lax.all_to_all(
         answers, "owner", split_axis=0, concat_axis=0, axis_index_groups=groups, tiled=True
     )
+    parity = jnp.stack([my_z, my_x % 2]).astype(I32)
     out, mass = root_attention(
-        used, members, valid, chunk_tenant, root_len, coords, q, k_new, v_new, roots
+        used, members, valid, chunk_tenant, root_len, parity, q, k_new, v_new, roots
     )
     send = merge(pos, dst_b, dst_l, back, out, mass)
     attn = lax.all_to_all(

time: 230 us -> 231 us (level)
  waiting for transfers between devices: 59.5 us -> 68.9 us
  Pallas kernels: 42.2 us -> 36 us
    pallas_call x1, Pallas kernels: 14.3 us -> 8.14 us  [node_attention(): pl.pallas_call(node_kernel, out_shape=jax.ShapeDtypeStruct((peers, 2 * sl...]
    ppermute x1, waiting for transfers between devices: 0.01 us -> 4.93 us  [on_device(): lax.ppermute(roots, 'owner', xor_pairs(n_owner, NX * NY))]
    ppermute x1 -> x2, starting transfers between devices: 2.76 us -> 7.6 us  [the longest x1 4.35 us: on_device(): other = lax.ppermute(jnp.stack(half) + planned, 'blk', swap)]
    ppermute x1, waiting for transfers between devices: 12.2 us -> 15.9 us  [on_device(): node_far = lax.ppermute(node_rows, 'owner', xor_pairs(n_owner, NX * NY))]
    ppermute x1, starting transfers between devices: 5.26 us -> 7.94 us  [on_device(): lax.ppermute(roots, 'owner', xor_pairs(n_owner, NX * NY))]
    ppermute x1, starting transfers between devices: 7.03 us -> 4.57 us  [on_device(): node_far = lax.ppermute(node_rows, 'owner', xor_pairs(n_owner, NX * NY))]
  transfers between devices with their start and end apart: 18 -> 19, of which waited for: 7 -> 8; matrix products, arithmetic and copies ran while one was open for 6% -> 6% of each run, Pallas kernels for 15% -> 12%
where the time goes in v5:
time: 231 us; the launch traced here: 230 us
  starting transfers between devices  76.2 us (33%)
  waiting for transfers between devices  68.9 us (30%)
  Pallas kernels  36 us (16%)
  local copies, waits for them, and re-layouts  18.8 us (8%)
  between operations  16.4 us (7%)
  other arithmetic  9.32 us (4%)
  matrix products  3.99 us (2%)
    ppermute x2, waiting for transfers between devices, to_neighbour(): return lax.ppermute(sent, ('blk', 'owner'), pairs)  18.6 us
    ppermute x1, waiting for transfers between devices, on_device(): node_far = lax.ppermute(node_rows, 'owner', xor_pairs(n_owner, NX * NY))  15.9 us
    unnamed x88, local copies, waits for them, and re-layouts  15.5 us
    ppermute x3, starting transfers between devices, on_device(): lax.ppermute(tok, 'blk', xor_pairs(N_BLK, 2 * k))  14.1 us
    all_to_all x1, waiting for transfers between devices, on_device(): lax.all_to_all(send.reshape(N_BLK, 2 * own_rows, cols), 'blk', split_axis...  13.4 us
    ppermute x1, waiting for transfers between devices, on_device(): lax.ppermute(down_far, 'blk', xor_pairs(N_BLK, N_BLK // 2)).astype(F32)  12.1 us
    all_to_all x1, starting transfers between devices, on_device(): lax.all_to_all(outgoing, 'owner', split_axis=0, concat_axis=0, axis_index...  9.95 us
    pallas_call x1, Pallas kernels, root_attention(): pl.pallas_call(root_kernel, out_shape=(shape, shape), in_specs=[pl.BlockS...  9.53 us
  transfers between devices with their start and end apart: 19, of which 8 were waited for; matrix products, arithmetic and copies ran while one was open for 6% of the time, Pallas kernels for 12%

profile of v5, /device:TPU:1, one launch (start us, length us, event | category | flops | bytes accessed | tf_op | source)
XLA Modules:
  0.0 229.6 jit_solution(7629973097592987549)
XLA Ops:
  7.2 8.4 %collective-permute-start.2 = (bf16[128,1024]{1,0:T(8,128)(2,1)}, bf16[128,1024]{1,0:T(8,128)(2,1)S(1)}, u32[]{:S(2)}, u32[]{:S(2)}) collective-permute-start(bf16[128,1024]{1,0:T(8,128)(2,1)} %bitcast.79), channel_id=1, source_target_pairs={{0,384},{64,448},{128,256},{192,320},{256,128},{320,192},{384,0},{... | collective-permute-start | bytes 786440 | tf_op jit(solution)/shard_map/ppermute | solution.py:490
  15.7 7.9 %collective-permute-start.6 = (bf16[128,128]{1,0:T(8,128)(2,1)}, bf16[128,128]{1,0:T(8,128)(2,1)S(1)}, u32[]{:S(2)}, u32[]{:S(2)}) collective-permute-start(bf16[128,128]{1,0:T(8,128)(2,1)} %bitcast.92), channel_id=1, source_target_pairs={{0,32},{1,33},{2,34},{3,35},{4,36},{5,37},{6,38},{7,39},{8,40},{9,... | collective-permute-start | bytes 98312 | tf_op jit(solution)/shard_map/ppermute | solution.py:495
  23.6 4.9 %collective-permute-done.6 = bf16[128,128]{1,0:T(8,128)(2,1)S(1)} collective-permute-done((bf16[128,128]{1,0:T(8,128)(2,1)}, bf16[128,128]{1,0:T(8,128)(2,1)S(1)}, u32[]{:S(2)}, u32[]{:S(2)}) %collective-permute-start.6) | collective-permute-done | bytes 32800 | tf_op jit(solution)/shard_map/ppermute | solution.py:495
  28.5 0.8 fusion.23
  29.3 3.3 %collective-permute-start.7 = (bf16[2,128,128]{2,1,0:T(8,128)(2,1)S(1)}, bf16[2,128,128]{2,1,0:T(8,128)(2,1)S(1)}, u32[]{:S(2)}, u32[]{:S(2)}) collective-permute-start(bf16[2,128,128]{2,1,0:T(8,128)(2,1)S(1)} %get-tuple-element.37), channel_id=1, source_target_pairs={{0,8},{1,9},{2,10},{3,11},{4,12},{5,13},{6,14},{7,15},{8,0},{9,1},... | collective-permute-start | bytes 196616 | tf_op jit(solution)/shard_map/ppermute | solution.py:496
  35.2 1.9 collective-permute-start.1
  37.1 3.8 %collective-permute-start = (bf16[128,1024]{1,0:T(8,128)(2,1)}, bf16[128,1024]{1,0:T(8,128)(2,1)S(1)}, u32[]{:S(2)}, u32[]{:S(2)}) collective-permute-start(bf16[128,1024]{1,0:T(8,128)(2,1)} %bitcast.81), channel_id=1, source_target_pairs={{0,128},{64,192},{128,0},{192,64},{256,384},{320,448},{384,256},{4... | collective-permute-start | bytes 786440 | tf_op jit(solution)/shard_map/ppermute | solution.py:490
  41.5 6.2 %shard_map.194 = (s32[32]{0:T(128)}, s32[32]{0:T(128)}, s32[32]{0:T(128)}, s32[4]{0:T(128)}, s32[44]{0:T(128)}, /*index=5*/s32[44]{0:T(128)}, s32[11]{0:T(128)}, s32[1]{0:T(128)}) custom-call(s32[4]{0:T(128)} %pad_add_fusion.coords, s32[32]{0:T(128)} %leaf_of.1, s32[128]{0:T(128)} %parent.1, s32[128]{0:T(128)} %place.1, s32[128]{0:T(128)} %length.1), custom_call_target="tpu_custom_call" | custom-call | flops 1048576 | bytes 4096 | tf_op jit(solution)/shard_map/pallas_call | solution.py:134
  48.4 2.0 collective-permute-done.1.tok_b
  50.5 4.3 %collective-permute-start.4 = (bf16[3,128,1024]{2,1,0:T(8,128)(2,1)S(1)}, bf16[3,128,1024]{2,1,0:T(8,128)(2,1)S(1)}, u32[]{:S(2)}, u32[]{:S(2)}) collective-permute-start(bf16[3,128,1024]{2,1,0:T(8,128)(2,1)S(1)} %maximum_add_fusion), channel_id=1, source_target_pairs={{0,64},{64,0},{128,192},{192,128},{256,320},{320,256},{384,448},{4... | collective-permute-start | bytes 2359304 | tf_op jit(solution)/shard_map/ppermute | solution.py:505
  54.8 1.9 collective-permute-start.3
  57.0 1.3 collective-permute-done.3.near_ref
  58.3 2.4 %shard_map.195 = (bf16[32,32,128]{2,1,0:T(8,128)(2,1)S(1)}, bf16[128,32,128]{2,1,0:T(8,128)(2,1)}) custom-call(s32[32]{0:T(128)S(1)} %copy-done.22, s32[32]{0:T(128)S(1)} %copy-done.18, s32[32]{0:T(128)S(1)} %copy-done.20, bf16[4,128,1024]{2,1,0:T(8,128)(2,1)S(1)} %pad_maximum_fusion.half_ref, bf16[128,1024]{1,0:T(8,128)(2,1)S(1)} %collective-permute-done.3.near_ref, ...), custom_call_target="tpu_custom_call" | custom-call | flops 268435456 | bytes 4194304 | tf_op jit(solution)/shard_map/pallas_call | solution.py:169
  60.8 9.9 %all-to-all-start = ((bf16[32,4,32,128]{3,2,1,0:T(8,128)(2,1)}), bf16[32,4,32,128]{3,2,1,0:T(8,128)(2,1)}, u32[]{:S(2)}, u32[]{:S(2)}) async-start(bf16[32,4,32,128]{3,2,1,0:T(8,128)(2,1)} %bitcast.11), calls=%async_computation | async-start | bytes 2097152 | tf_op jit(solution)/shard_map/all_to_all | solution.py:531
  71.6 0.8 broadcast_add_fusion
  72.4 4.6 %collective-permute-start.5 = (bf16[1536,128]{1,0:T(8,128)(2,1)}, bf16[1536,128]{1,0:T(8,128)(2,1)}, u32[]{:S(2)}, u32[]{:S(2)}) collective-permute-start(bf16[1536,128]{1,0:T(8,128)(2,1)} %bitcast.14), channel_id=1, source_target_pairs={{0,32},{1,33},{2,34},{3,35},{4,36},{5,37},{6,38},{7,39},{8,40},{9,... | collective-permute-start | bytes 1179656 | tf_op jit(solution)/shard_map/ppermute | solution.py:510
  77.7 1.1 fusion.10
  79.5 2.6 %collective-permute-start.8 = (bf16[2,2064,256]{2,1,0:T(8,128)(2,1)S(1)}, bf16[2,2064,256]{2,1,0:T(8,128)(2,1)}, u32[]{:S(2)}, u32[]{:S(2)}) collective-permute-start(bf16[2,2064,256]{2,1,0:T(8,128)(2,1)S(1)} %shard_map.196.after_ref.w0), channel_id=1, source_target_pairs={{0,64},{64,0},{128,192},{192,128},{256,320},{320,256},{384,448},{4... | collective-permute-start | bytes 6340616 | tf_op jit(solution)/shard_map/ppermute | solution.py:515
  82.1 15.9 %collective-permute-done.5 = bf16[1536,128]{1,0:T(8,128)(2,1)} collective-permute-done((bf16[1536,128]{1,0:T(8,128)(2,1)}, bf16[1536,128]{1,0:T(8,128)(2,1)}, u32[]{:S(2)}, u32[]{:S(2)}) %collective-permute-start.5) | collective-permute-done | bytes 393248 | tf_op jit(solution)/shard_map/ppermute | solution.py:510
  98.0 1.1 pad_maximum_fusion.1.cache_ref
  99.1 8.1 %shard_map.197 = bf16[32,9,16,128]{3,2,1,0:T(8,128)(2,1)S(1)} custom-call(s32[4]{0:T(128)S(1)} %copy-done.32, bf16[32,4,32,128]{3,2,1,0:T(8,128)(2,1)} %all-to-all-done.q_ref, bf16[2,2,2,384,128]{4,3,2,1,0:T(8,128)(2,1)S(1)} %pad_maximum_fusion.1.cache_ref, bf16[2,2064,256]{2,1,0:T(8,128)(2,1)S(1)} %shard_map.196.after_ref.w0), custom_call_target="tpu_custom_call" | custom-call | flops 2147483648 | bytes 4194304 | tf_op jit(solution)/shard_map/pallas_call | solution.py:260
  107.2 1.0 copy-done.3
  108.2 9.1 %all-to-all-start.1 = ((bf16[32,9,16,128]{3,2,1,0:T(8,128)(2,1)}), bf16[32,9,16,128]{3,2,1,0:T(8,128)(2,1)S(1)}, u32[]{:S(2)}, u32[]{:S(2)}) async-start(bf16[32,9,16,128]{3,2,1,0:T(8,128)(2,1)} %copy-done.3), calls=%async_computation.1 | async-start | bytes 2359296 | tf_op jit(solution)/shard_map/all_to_all | solution.py:557
  117.4 1.7 fusion.4
  119.1 1.2 slice.31
  121.1 2.1 collective-permute-start.9
  123.2 4.7 %collective-permute-start.10 = (bf16[2064,256]{1,0:T(8,128)(2,1)S(1)}, bf16[2064,256]{1,0:T(8,128)(2,1)}, u32[]{:S(2)}, u32[]{:S(2)}) collective-permute-start(bf16[2064,256]{1,0:T(8,128)(2,1)S(1)} %get-tuple-element.34), channel_id=1, source_target_pairs={{0,416},{1,417},{2,418},{3,419},{4,420},{5,421},{6,422},{7,423},{8... | collective-permute-start | bytes 3170312 | tf_op jit(solution)/shard_map/ppermute | solution.py:552
  129.9 18.6 %collective-permute-done.9.w2 = bf16[2064,256]{1,0:T(8,128)(2,1)} collective-permute-done((bf16[2064,256]{1,0:T(8,128)(2,1)S(1)}, bf16[2064,256]{1,0:T(8,128)(2,1)}, u32[]{:S(2)}, u32[]{:S(2)}) %collective-permute-start.9) | collective-permute-done | bytes 1056800 | tf_op jit(solution)/shard_map/ppermute | solution.py:552
  148.5 3.6 %collective-permute-start.11 = (bf16[2064,256]{1,0:T(8,128)(2,1)}, bf16[2064,256]{1,0:T(8,128)(2,1)}, u32[]{:S(2)}, u32[]{:S(2)}) collective-permute-start(bf16[2064,256]{1,0:T(8,128)(2,1)} %collective-permute-done.9.w2), channel_id=1, source_target_pairs={{0,64},{64,0},{128,192},{192,128},{256,320},{320,256},{384,448},{4... | collective-permute-start | bytes 3170312 | tf_op jit(solution)/shard_map/ppermute | solution.py:555
  152.1 1.9 collective-permute-start.12
  154.1 0.9 copy-done.4
  155.0 1.6 copy-done.24
  156.7 0.9 copy-done.26
  160.9 9.5 %shard_map.198 = (f32[32,32,128]{2,1,0:T(8,128)S(1)}, f32[32,32,128]{2,1,0:T(8,128)S(1)}) custom-call(s32[1]{0:T(128)} %get-tuple-element.22.used, s32[44]{0:T(128)S(1)} %copy-done.29, s32[44]{0:T(128)S(1)} %copy-done.30, s32[11]{0:T(128)S(1)} %copy-done.31, s32[4]{0:T(128)S(1)} %copy-done.27, s32[2]{0:T(128)S(1)} %copy-done.28, ...), custom_call_target="tpu_custom_call" | custom-call | flops 4294967296 | bytes 4194304 | tf_op jit(solution)/shard_map/pallas_call | solution.py:331
  170.4 0.8 copy-done.12
  171.2 0.8 copy-done.14
  172.0 1.0 copy-done.13
  173.1 1.0 copy-done.15
  175.9 2.1 shard_map.199
  178.0 0.8 copy-done.2
  178.8 4.0 %all-to-all-start.2 = ((bf16[8,256,128]{2,1,0:T(8,128)(2,1)}), bf16[8,256,128]{2,1,0:T(8,128)(2,1)S(1)}, u32[]{:S(2)}, u32[]{:S(2)}) async-start(bf16[8,256,128]{2,1,0:T(8,128)(2,1)} %bitcast.69), calls=%async_computation.2 | async-start | bytes 1048576 | tf_op jit(solution)/shard_map/all_to_all | solution.py:565
  183.9 13.4 %all-to-all-done.2.attn_ref = bf16[8,256,128]{2,1,0:T(8,128)(2,1)S(1)} async-done(((bf16[8,256,128]{2,1,0:T(8,128)(2,1)}), bf16[8,256,128]{2,1,0:T(8,128)(2,1)S(1)}, u32[]{:S(2)}, u32[]{:S(2)}) %all-to-all-start.2) | async-done | bytes 524320 | tf_op jit(solution)/shard_map/all_to_all | solution.py:565
  197.3 0.9 copy-done.17
  198.3 7.5 %shard_map.200 = (bf16[128,1024]{1,0:T(8,128)(2,1)S(1)}, f32[128,1024]{1,0:T(8,128)S(1)}, bf16[128,1024]{1,0:T(8,128)(2,1)S(1)}) custom-call(bf16[8,256,128]{2,1,0:T(8,128)(2,1)S(1)} %all-to-all-done.2.attn_ref, bf16[1024,1024]{1,0:T(8,128)(2,1)} %all-gather.5.cloned.1.call-done.w_out_ref, bf16[128,1024]{1,0:T(8,128)(2,1)S(1)} %bitcast.84, ...), custom_call_target="tpu_custom_call" | custom-call | flops 3221225472 | bytes 12582912 | tf_op jit(solution)/shard_map/pallas_call | solution.py:427
  205.8 1.9 collective-permute-start.13
  208.5 0.9 broadcast_select_fusion
  209.4 12.1 %collective-permute-done.13 = bf16[128,1024]{1,0:T(8,128)(2,1)S(1)} collective-permute-done((bf16[128,1024]{1,0:T(8,128)(2,1)S(1)}, bf16[128,1024]{1,0:T(8,128)(2,1)S(1)}, u32[]{:S(2)}, u32[]{:S(2)}) %collective-permute-start.13) | collective-permute-done | bytes 262176 | tf_op jit(solution)/shard_map/ppermute | solution.py:570
  221.9 0.9 add_convert_fusion
  (132 shorter events, 14.8 us)
Async XLA Ops:
  7.2 146.9 %all-gather.3.cloned.1.call-start = ((), (), s32[]{:S(2)}) async-start(), calls=%async_computation.3 | async-start | bytes 2228224 | tf_op jit(solution)/shard_map/all_gather | solution.py:503
  7.2 25.4 %collective-permute-start.2 = (bf16[128,1024]{1,0:T(8,128)(2,1)}, bf16[128,1024]{1,0:T(8,128)(2,1)S(1)}, u32[]{:S(2)}, u32[]{:S(2)}) collective-permute-start(bf16[128,1024]{1,0:T(8,128)(2,1)} %bitcast.79), channel_id=1, source_target_pairs={{0,384},{64,448},{128,256},{192,320},{256,128},{320,192},{384,0},{... | collective-permute-start | bytes 786440 | tf_op jit(solution)/shard_map/ppermute | solution.py:490
  15.7 12.9 %collective-permute-start.6 = (bf16[128,128]{1,0:T(8,128)(2,1)}, bf16[128,128]{1,0:T(8,128)(2,1)S(1)}, u32[]{:S(2)}, u32[]{:S(2)}) collective-permute-start(bf16[128,128]{1,0:T(8,128)(2,1)} %bitcast.92), channel_id=1, source_target_pairs={{0,32},{1,33},{2,34},{3,35},{4,36},{5,37},{6,38},{7,39},{8,40},{9,... | collective-permute-start | bytes 98312 | tf_op jit(solution)/shard_map/ppermute | solution.py:495
  29.3 25.5 %copy-start.16 = (bf16[4,32,1024]{2,1,0:T(8,128)(2,1)S(1)}, bf16[4,32,1024]{2,1,0:T(8,128)(2,1)}, u32[]{:S(2)}) copy-start(bf16[4,32,1024]{2,1,0:T(8,128)(2,1)} %param.19) | copy-start | bytes 786436
  29.3 27.4 %copy-start.34 = (bf16[1024,3,128]{2,0,1:T(8,128)(2,1)S(1)}, bf16[1024,3,128]{2,0,1:T(8,128)(2,1)}, u32[]{:S(2)}) copy-start(bf16[1024,3,128]{2,0,1:T(8,128)(2,1)} %param.20) | copy-start | bytes 2359300
  29.3 5.1 %collective-permute-start.7 = (bf16[2,128,128]{2,1,0:T(8,128)(2,1)S(1)}, bf16[2,128,128]{2,1,0:T(8,128)(2,1)S(1)}, u32[]{:S(2)}, u32[]{:S(2)}) collective-permute-start(bf16[2,128,128]{2,1,0:T(8,128)(2,1)S(1)} %get-tuple-element.37), channel_id=1, source_target_pairs={{0,8},{1,9},{2,10},{3,11},{4,12},{5,13},{6,14},{7,15},{8,0},{9,1},... | collective-permute-start | bytes 196616 | tf_op jit(solution)/shard_map/ppermute | solution.py:496
  35.2 15.2 %collective-permute-start.1 = (bf16[128,1024]{1,0:T(8,128)(2,1)}, bf16[128,1024]{1,0:T(8,128)(2,1)S(1)}, u32[]{:S(2)}, u32[]{:S(2)}) collective-permute-start(bf16[128,1024]{1,0:T(8,128)(2,1)} %bitcast.80), channel_id=1, source_target_pairs={{0,256},{64,320},{128,384},{192,448},{256,0},{320,64},{384,128},{4... | collective-permute-start | bytes 786440 | tf_op jit(solution)/shard_map/ppermute | solution.py:490
  37.1 13.3 %collective-permute-start = (bf16[128,1024]{1,0:T(8,128)(2,1)}, bf16[128,1024]{1,0:T(8,128)(2,1)S(1)}, u32[]{:S(2)}, u32[]{:S(2)}) collective-permute-start(bf16[128,1024]{1,0:T(8,128)(2,1)} %bitcast.81), channel_id=1, source_target_pairs={{0,128},{64,192},{128,0},{192,64},{256,384},{320,448},{384,256},{4... | collective-permute-start | bytes 786440 | tf_op jit(solution)/shard_map/ppermute | solution.py:490
  50.4 6.6 %copy-start.8 = (bf16[128,1024]{1,0:T(8,128)(2,1)}, bf16[128,1024]{1,0:T(8,128)(2,1)S(1)}, u32[]{:S(2)}) copy-start(bf16[128,1024]{1,0:T(8,128)(2,1)S(1)} %collective-permute-done.1.tok_b) | copy-start | bytes 786436
  50.5 7.8 %collective-permute-start.4 = (bf16[3,128,1024]{2,1,0:T(8,128)(2,1)S(1)}, bf16[3,128,1024]{2,1,0:T(8,128)(2,1)S(1)}, u32[]{:S(2)}, u32[]{:S(2)}) collective-permute-start(bf16[3,128,1024]{2,1,0:T(8,128)(2,1)S(1)} %maximum_add_fusion), channel_id=1, source_target_pairs={{0,64},{64,0},{128,192},{192,128},{256,320},{320,256},{384,448},{4... | collective-permute-start | bytes 2359304 | tf_op jit(solution)/shard_map/ppermute | solution.py:505
  54.8 3.4 %collective-permute-start.3 = (bf16[128,1024]{1,0:T(8,128)(2,1)S(1)}, bf16[128,1024]{1,0:T(8,128)(2,1)S(1)}, u32[]{:S(2)}, u32[]{:S(2)}) collective-permute-start(bf16[128,1024]{1,0:T(8,128)(2,1)S(1)} %bitcast.82), channel_id=1, source_target_pairs={{0,64},{64,0},{128,192},{192,128},{256,320},{320,256},{384,448},{4... | collective-permute-start | bytes 786440 | tf_op jit(solution)/shard_map/ppermute | solution.py:489
  56.8 1.5 copy-start.18
  56.8 1.5 copy-start.20
  56.8 1.5 copy-start.22
  57.0 20.7 %copy-start.1 = (bf16[4,128,1024]{2,1,0:T(8,128)(2,1)}, bf16[4,128,1024]{2,1,0:T(8,128)(2,1)S(1)}, u32[]{:S(2)}) copy-start(bf16[4,128,1024]{2,1,0:T(8,128)(2,1)S(1)} %pad_maximum_fusion.half_ref) | copy-start | bytes 3145732
  58.3 2.5 %copy-start.10 = (bf16[3,128,1024]{2,1,0:T(8,128)(2,1)}, bf16[3,128,1024]{2,1,0:T(8,128)(2,1)S(1)}, u32[]{:S(2)}) copy-start(bf16[3,128,1024]{2,1,0:T(8,128)(2,1)S(1)} %collective-permute-done.4.other_ref) | copy-start | bytes 2359300
  60.7 10.0 %copy-start.25 = (bf16[32,32,128]{2,1,0:T(8,128)(2,1)}, bf16[32,32,128]{2,1,0:T(8,128)(2,1)S(1)}, u32[]{:S(2)}) copy-start(bf16[32,32,128]{2,1,0:T(8,128)(2,1)S(1)} %get-tuple-element.26.q_ref) | copy-start | bytes 786436
  60.7 10.1 %copy-start.43 = (bf16[512]{0:T(512)(128)(2,1)S(1)}, bf16[512]{0:T(512)(128)(2,1)}, u32[]{:S(2)}) copy-start(bf16[512]{0:T(512)(128)(2,1)} %param.26) | copy-start | bytes 3076
  60.8 10.8 %copy-start.33 = (bf16[2,2,384,128]{3,2,1,0:T(8,128)(2,1)S(1)}, bf16[2,2,384,128]{3,2,1,0:T(8,128)(2,1)}, u32[]{:S(2)}) copy-start(bf16[2,2,384,128]{3,2,1,0:T(8,128)(2,1)} %param.32) | copy-start | bytes 1179652
  60.8 16.2 %copy-start.36 = (bf16[128,1024]{1,0:T(8,128)(2,1)S(1)}, bf16[128,1024]{1,0:T(8,128)(2,1)}, u32[]{:S(2)}) copy-start(bf16[128,1024]{1,0:T(8,128)(2,1)} %param.21) | copy-start | bytes 786436
  60.8 38.3 %all-to-all-start = ((bf16[32,4,32,128]{3,2,1,0:T(8,128)(2,1)}), bf16[32,4,32,128]{3,2,1,0:T(8,128)(2,1)}, u32[]{:S(2)}, u32[]{:S(2)}) async-start(bf16[32,4,32,128]{3,2,1,0:T(8,128)(2,1)} %bitcast.11), calls=%async_computation | async-start | bytes 2097152 | tf_op jit(solution)/shard_map/all_to_all | solution.py:531
  70.7 113.1 %all-gather.5.cloned.1.call-start = ((), (), s32[]{:S(2)}) async-start(), calls=%async_computation.4 | async-start | bytes 2359296 | tf_op jit(solution)/shard_map/all_gather | solution.py:513
  72.4 25.6 %collective-permute-start.5 = (bf16[1536,128]{1,0:T(8,128)(2,1)}, bf16[1536,128]{1,0:T(8,128)(2,1)}, u32[]{:S(2)}, u32[]{:S(2)}) collective-permute-start(bf16[1536,128]{1,0:T(8,128)(2,1)} %bitcast.14), channel_id=1, source_target_pairs={{0,32},{1,33},{2,34},{3,35},{4,36},{5,37},{6,38},{7,39},{8,40},{9,... | collective-permute-start | bytes 1179656 | tf_op jit(solution)/shard_map/ppermute | solution.py:510
  77.7 1.2 copy-start.6
  77.7 1.6 copy-start.7
  79.5 41.5 %copy-start = (bf16[2,2064,256]{2,1,0:T(8,128)(2,1)}, bf16[2,2064,256]{2,1,0:T(8,128)(2,1)S(1)}, u32[]{:S(2)}) copy-start(bf16[2,2064,256]{2,1,0:T(8,128)(2,1)S(1)} %shard_map.196.after_ref.w0) | copy-start | bytes 6340612
  79.5 19.6 %copy-start.32 = (s32[4]{0:T(128)S(1)}, s32[4]{0:T(128)}, u32[]{:S(2)}) copy-start(s32[4]{0:T(128)} %get-tuple-element.20.lens) | copy-start | bytes 52
  79.5 104.4 %collective-permute-start.8 = (bf16[2,2064,256]{2,1,0:T(8,128)(2,1)S(1)}, bf16[2,2064,256]{2,1,0:T(8,128)(2,1)}, u32[]{:S(2)}, u32[]{:S(2)}) collective-permute-start(bf16[2,2064,256]{2,1,0:T(8,128)(2,1)S(1)} %shard_map.196.after_ref.w0), channel_id=1, source_target_pairs={{0,64},{64,0},{128,192},{192,128},{256,320},{320,256},{384,448},{4... | collective-permute-start | bytes 6340616 | tf_op jit(solution)/shard_map/ppermute | solution.py:515
  108.2 63.8 %all-to-all-start.1 = ((bf16[32,9,16,128]{3,2,1,0:T(8,128)(2,1)}), bf16[32,9,16,128]{3,2,1,0:T(8,128)(2,1)S(1)}, u32[]{:S(2)}, u32[]{:S(2)}) async-start(bf16[32,9,16,128]{3,2,1,0:T(8,128)(2,1)} %copy-done.3), calls=%async_computation.1 | async-start | bytes 2359296 | tf_op jit(solution)/shard_map/all_to_all | solution.py:557
  120.9 7.0 %copy-start.35 = (bf16[1024,3,128]{2,0,1:T(8,128)(2,1)S(1)}, bf16[1024,3,128]{2,0,1:T(8,128)(2,1)}, u32[]{:S(2)}) copy-start(bf16[1024,3,128]{2,0,1:T(8,128)(2,1)} %param.20) | copy-start | bytes 2359300
  121.1 7.3 %copy-start.11 = (bf16[3,128,1024]{2,1,0:T(8,128)(2,1)S(1)}, bf16[3,128,1024]{2,1,0:T(8,128)(2,1)}, u32[]{:S(2)}) copy-start(bf16[3,128,1024]{2,1,0:T(8,128)(2,1)} %copy-done.10) | copy-start | bytes 2359300
  121.1 27.4 %collective-permute-start.9 = (bf16[2064,256]{1,0:T(8,128)(2,1)S(1)}, bf16[2064,256]{1,0:T(8,128)(2,1)}, u32[]{:S(2)}, u32[]{:S(2)}) collective-permute-start(bf16[2064,256]{1,0:T(8,128)(2,1)S(1)} %get-tuple-element.35), channel_id=1, source_target_pairs={{0,128},{1,129},{2,130},{3,131},{4,132},{5,133},{6,134},{7,135},{8... | collective-permute-start | bytes 3170312 | tf_op jit(solution)/shard_map/ppermute | solution.py:552
  123.2 5.6 %copy-start.37 = (bf16[512,128]{1,0:T(8,128)(2,1)S(1)}, bf16[512,128]{1,0:T(8,128)(2,1)}, u32[]{:S(2)}) copy-start(bf16[512,128]{1,0:T(8,128)(2,1)} %fusion.10) | copy-start | bytes 393220
  123.2 28.9 %collective-permute-start.10 = (bf16[2064,256]{1,0:T(8,128)(2,1)S(1)}, bf16[2064,256]{1,0:T(8,128)(2,1)}, u32[]{:S(2)}, u32[]{:S(2)}) collective-permute-start(bf16[2064,256]{1,0:T(8,128)(2,1)S(1)} %get-tuple-element.34), channel_id=1, source_target_pairs={{0,416},{1,417},{2,418},{3,419},{4,420},{5,421},{6,422},{7,423},{8... | collective-permute-start | bytes 3170312 | tf_op jit(solution)/shard_map/ppermute | solution.py:552
  148.5 35.4 %collective-permute-start.11 = (bf16[2064,256]{1,0:T(8,128)(2,1)}, bf16[2064,256]{1,0:T(8,128)(2,1)}, u32[]{:S(2)}, u32[]{:S(2)}) collective-permute-start(bf16[2064,256]{1,0:T(8,128)(2,1)} %collective-permute-done.9.w2), channel_id=1, source_target_pairs={{0,64},{64,0},{128,192},{192,128},{256,320},{320,256},{384,448},{4... | collective-permute-start | bytes 3170312 | tf_op jit(solution)/shard_map/ppermute | solution.py:555
  152.1 31.8 %collective-permute-start.12 = (bf16[2064,256]{1,0:T(8,128)(2,1)}, bf16[2064,256]{1,0:T(8,128)(2,1)}, u32[]{:S(2)}, u32[]{:S(2)}) collective-permute-start(bf16[2064,256]{1,0:T(8,128)(2,1)} %collective-permute-done.10.w3), channel_id=1, source_target_pairs={{0,64},{64,0},{128,192},{192,128},{256,320},{320,256},{384,448},{4... | collective-permute-start | bytes 3170312 | tf_op jit(solution)/shard_map/ppermute | solution.py:555
  155.0 1.6 copy-start.24
  172.0 1.0 copy-start.13
  173.1 1.0 copy-start.15
  178.8 4.7 %copy-start.38 = (bf16[1024]{0:T(1024)(128)(2,1)S(1)}, bf16[1024]{0:T(1024)(128)(2,1)}, u32[]{:S(2)}) copy-start(bf16[1024]{0:T(1024)(128)(2,1)} %param.23) | copy-start | bytes 6148
  178.8 4.7 %copy-start.39 = (bf16[1024]{0:T(1024)(128)(2,1)S(1)}, bf16[1024]{0:T(1024)(128)(2,1)}, u32[]{:S(2)}) copy-start(bf16[1024]{0:T(1024)(128)(2,1)} %param.24) | copy-start | bytes 6148
  178.8 4.8 %copy-start.40 = (bf16[1024]{0:T(1024)(128)(2,1)S(1)}, bf16[1024]{0:T(1024)(128)(2,1)}, u32[]{:S(2)}) copy-start(bf16[1024]{0:T(1024)(128)(2,1)} %param.28) | copy-start | bytes 6148
  178.8 4.8 %copy-start.41 = (bf16[1024]{0:T(1024)(128)(2,1)S(1)}, bf16[1024]{0:T(1024)(128)(2,1)}, u32[]{:S(2)}) copy-start(bf16[1024]{0:T(1024)(128)(2,1)} %param.29) | copy-start | bytes 6148
  178.8 4.8 %copy-start.42 = (bf16[1024]{0:T(1024)(128)(2,1)S(1)}, bf16[1024]{0:T(1024)(128)(2,1)}, u32[]{:S(2)}) copy-start(bf16[1024]{0:T(1024)(128)(2,1)} %param.30) | copy-start | bytes 6148
  178.8 18.5 %copy-start.9 = (bf16[128,1024]{1,0:T(8,128)(2,1)S(1)}, bf16[128,1024]{1,0:T(8,128)(2,1)}, u32[]{:S(2)}) copy-start(bf16[128,1024]{1,0:T(8,128)(2,1)} %copy-done.8) | copy-start | bytes 786436
  178.8 18.5 %all-to-all-start.2 = ((bf16[8,256,128]{2,1,0:T(8,128)(2,1)}), bf16[8,256,128]{2,1,0:T(8,128)(2,1)S(1)}, u32[]{:S(2)}, u32[]{:S(2)}) async-start(bf16[8,256,128]{2,1,0:T(8,128)(2,1)} %bitcast.69), calls=%async_computation.2 | async-start | bytes 1048576 | tf_op jit(solution)/shard_map/all_to_all | solution.py:565
  183.8 23.9 %copy-start.5 = (bf16[1024,128]{1,0:T(8,128)(2,1)S(1)}, bf16[1024,128]{1,0:T(8,128)(2,1)}, u32[]{:S(2)}) copy-start(bf16[1024,128]{1,0:T(8,128)(2,1)} %maximum_convert_fusion.1) | copy-start | bytes 786436
  205.8 15.7 %collective-permute-start.13 = (bf16[128,1024]{1,0:T(8,128)(2,1)S(1)}, bf16[128,1024]{1,0:T(8,128)(2,1)S(1)}, u32[]{:S(2)}, u32[]{:S(2)}) collective-permute-start(bf16[128,1024]{1,0:T(8,128)(2,1)S(1)} %get-tuple-element.31), channel_id=1, source_target_pairs={{0,256},{64,320},{128,384},{192,448},{256,0},{320,64},{384,128},{4... | collective-permute-start | bytes 786440 | tf_op jit(solution)/shard_map/ppermute | solution.py:570
  (15 other events, 11.3 us)
Sparse Core Ops, SparseCore 0:
  35.3 95.0 all-gather.2
  132.5 46.2 all-gather.4

commit v6 on v5

--- a/solution.py
+++ b/solution.py
@@ -55,93 +55,96 @@
     return jnp.where(lane < HD, first, second)
 
 
-def table_kernel(
-    coords, leaf_of, parent, place, length, dst_b, dst_l, pos, lens, members, valid, chunk_tenant, used, tenant_of, count
-):
+DST_B, DST_L, POS, LENS, USED, ROOT_LEN, PLACE, TENANT, MEMBERS, VALID, COUNT, CHUNK_TENANT, TABLE = (
+    0, 32, 64, 96, 100, 104, 112, 128, 160, 208, 256, 264, 288,
+)
+
+
+def table_kernel(coords, leaf_of, parent, place, length, root_len, out):
     my_z, my_x, my_y, blk = (coords[i] for i in range(4))
     reqs = leaf_of.shape[0]
     req_dev = reqs // N_BLK
-    tenants = count.shape[0]
+    tenants = root_len.shape[0]
+    seats = (reqs // CHUNK + tenants - 1) * CHUNK
 
     def slot_index(slot):
-        owner = slot // 2
-        return (owner % PEERS) * SLOTS + ((owner // PEERS) ^ my_z) * 2 + slot % 2
+        owner = slot >> 1
+        return (owner & (PEERS - 1)) * SLOTS + (((owner // PEERS) ^ my_z) << 1) + (slot & 1)
 
     for t in range(tenants):
-        count[t] = 0
+        out[COUNT + t] = 0
+        out[ROOT_LEN + t] = root_len[t]
+    out[PLACE] = my_z
+    out[PLACE + 1] = my_x
 
     def first_pass(r, _):
         leaf = leaf_of[r]
         branch = parent[leaf]
         tenant = parent[branch]
-        dst_b[r] = slot_index(place[branch])
-        dst_l[r] = slot_index(place[leaf])
+        out[DST_B + r] = slot_index(place[branch])
+        out[DST_L + r] = slot_index(place[leaf])
         rel = (r // req_dev) ^ blk
-        pos[r] = ((rel % 2) * (N_BLK // 2) + rel // 2) * req_dev + r % req_dev
-        tenant_of[r] = tenant
-        count[tenant] = count[tenant] + 1
-        return 0
-
-    lax.fori_loop(0, reqs, first_pass, 0)
+        out[POS + r] = ((rel & 1) * (N_BLK // 2) + (rel >> 1)) * req_dev + (r & (req_dev - 1))
+        out[TENANT + r] = tenant
+        out[COUNT + tenant] = out[COUNT + tenant] + 1
+        return 0
+
+    lax.fori_loop(0, reqs, first_pass, 0, unroll=4)
 
     def clear(i, _):
-        members[i] = 0
-        valid[i] = 0
-        return 0
-
-    lax.fori_loop(0, members.shape[0], clear, 0)
+        out[MEMBERS + i] = 0
+        out[VALID + i] = 0
+        return 0
+
+    lax.fori_loop(0, seats, clear, 0, unroll=4)
     end = 0
     for t in range(tenants):
-        chunks = (count[t] + CHUNK - 1) // CHUNK
+        chunks = (out[COUNT + t] + CHUNK - 1) // CHUNK
 
         def name(c, _, t=t):
-            chunk_tenant[c] = t
+            out[CHUNK_TENANT + c] = t
             return 0
 
         lax.fori_loop(end, end + chunks, name, 0)
-        count[t] = end * CHUNK
+        out[COUNT + t] = end * CHUNK
         end = end + chunks
-    used[0] = end
+    out[USED] = end
 
     def second_pass(r, _):
-        tenant = tenant_of[r]
-        seat = count[tenant]
-        count[tenant] = seat + 1
-        members[seat] = pos[r]
-        valid[seat] = 1
-        return 0
-
-    lax.fori_loop(0, reqs, second_pass, 0)
+        tenant = out[TENANT + r]
+        seat = out[COUNT + tenant]
+        out[COUNT + tenant] = seat + 1
+        out[MEMBERS + seat] = out[POS + r]
+        out[VALID + seat] = 1
+        return 0
+
+    lax.fori_loop(0, reqs, second_pass, 0, unroll=4)
 
     def node(n, _):
         slot = place[n]
-        owner = slot // 2
-
-        @pl.when(owner % PEERS == my_x * NY + my_y)
+        owner = slot >> 1
+
+        @pl.when((owner & (PEERS - 1)) == my_x * NY + my_y)
         def _():
-            lens[((owner // PEERS) ^ my_z) * 2 + slot % 2] = length[n]
-
-        return 0
-
-    lax.fori_loop(0, place.shape[0], node, 0)
-
-
-def make_tables(coords, leaf_of, parent, place, length, tenants):
-    reqs = leaf_of.shape[0]
-    max_chunks = reqs // CHUNK + tenants - 1
+            out[LENS + (((owner // PEERS) ^ my_z) << 1) + (slot & 1)] = length[n]
+
+        return 0
+
+    lax.fori_loop(0, place.shape[0], node, 0, unroll=4)
+
+
+def make_tables(coords, leaf_of, parent, place, length, root_len):
     smem = pl.BlockSpec(memory_space=pltpu.SMEM)
-    sizes = (reqs, reqs, reqs, SLOTS, max_chunks * CHUNK, max_chunks * CHUNK, max_chunks, 1)
     return pl.pallas_call(
         table_kernel,
-        out_shape=tuple(jax.ShapeDtypeStruct((n,), I32) for n in sizes),
-        in_specs=[smem] * 5,
-        out_specs=(smem,) * len(sizes),
-        scratch_shapes=[pltpu.SMEM((reqs,), I32), pltpu.SMEM((tenants,), I32)],
+        out_shape=jax.ShapeDtypeStruct((TABLE,), I32),
+        in_specs=[smem] * 6,
+        out_specs=smem,
         cost_estimate=pl.CostEstimate(flops=1 << 20, bytes_accessed=1 << 12, transcendentals=0),
-    )(coords, leaf_of, parent, place, length)
-
-
-def query_kernel(pos, dst_b, dst_l, half_ref, near_ref, other_ref, w_ref, after_ref, q_ref, out_ref):
+    )(coords, leaf_of, parent, place, length, root_len)
+
+
+def query_kernel(tab, half_ref, near_ref, other_ref, w_ref, after_ref, q_ref, out_ref):
     del after_ref
     reqs, suf, cols = q_ref.shape
     out_ref[...] = jnp.zeros_like(out_ref)
@@ -155,16 +158,16 @@
         at += count
 
     def body(r, _):
-        tile = q_ref[pos[r]]
-        out_ref[dst_b[r]] = tile
-        out_ref[dst_l[r]] = tile
+        tile = q_ref[tab[POS + r]]
+        out_ref[tab[DST_B + r]] = tile
+        out_ref[tab[DST_L + r]] = tile
         return 0
 
     lax.fori_loop(0, reqs, body, 0, unroll=2)
 
 
-def query_and_route(pos, dst_b, dst_l, half, near, other, w, suf, after):
-    reqs = pos.shape[0]
+def query_and_route(tab, half, near, other, w, suf, after):
+    reqs = (half.size + near.size + other.size) // (suf * half.shape[-1])
     vmem = pl.BlockSpec(memory_space=pltpu.VMEM)
     return pl.pallas_call(
         query_kernel,
@@ -172,13 +175,13 @@
             jax.ShapeDtypeStruct((reqs, suf, LANES), BF16),
             jax.ShapeDtypeStruct((PEERS * SLOTS, suf, LANES), BF16),
         ),
-        in_specs=[pl.BlockSpec(memory_space=pltpu.SMEM)] * 3
+        in_specs=[pl.BlockSpec(memory_space=pltpu.SMEM)]
         + [vmem] * 4
         + [pl.BlockSpec(memory_space=pl.ANY)],
         out_specs=(vmem, vmem),
         compiler_params=pltpu.CompilerParams(vmem_limit_bytes=24 << 20),
         cost_estimate=pl.CostEstimate(flops=1 << 28, bytes_accessed=4 << 20, transcendentals=0),
-    )(pos, dst_b, dst_l, half, near, other, w, after)
+    )(tab, half, near, other, w, after)
 
 
 def pack_kernel(up_ref, down_ref, bias_ref, after_ref, out_ref):
@@ -209,7 +212,7 @@
     )(up, down, bias.reshape(1, units), after)
 
 
-def node_kernel(lens, q_ref, cache_ref, after_ref, out_ref):
+def node_kernel(tab, q_ref, cache_ref, after_ref, out_ref):
     del after_ref
     peers, slots, suf, _ = q_ref.shape
     group = 4
@@ -221,7 +224,7 @@
         keys = both_heads(cache_ref[slot // 2, 0, slot % 2])
         values = cache_ref[slot // 2, 1, slot % 2]
         values = jnp.concatenate([both_heads(values), both_heads(jnp.ones_like(values))], axis=1)
-        keep = lax.broadcasted_iota(I32, (1, node_max), 1) < lens[slot]
+        keep = lax.broadcasted_iota(I32, (1, node_max), 1) < tab[LENS + slot]
         lane = lax.broadcasted_iota(I32, (group, HALF, LANES), 2)
         piece = lane % (HD // 2) - 3 * slot
         for g in range(peers // group):
@@ -254,7 +257,7 @@
     lax.fori_loop(0, slots, one_slot, 0)
 
 
-def node_attention(lens, queries, caches, after):
+def node_attention(tab, queries, caches, after):
     peers, slots, suf, _ = queries.shape
     vmem = pl.BlockSpec(memory_space=pltpu.VMEM)
     return pl.pallas_call(
@@ -271,20 +274,18 @@
         cost_estimate=pl.CostEstimate(
             flops=2 << 30, bytes_accessed=4 << 20, transcendentals=4 << 20
         ),
-    )(lens, queries, caches, after)
-
-
-def root_kernel(
-    used, members, valid, chunk_tenant, root_len, coords, q_ref, k_ref, v_ref, root_ref, out_ref, mass_ref
-):
+    )(tab, queries, caches, after)
+
+
+def root_kernel(tab, q_ref, k_ref, v_ref, root_ref, out_ref, mass_ref):
     suf = q_ref.shape[1]
     rows = CHUNK * suf
-    root_rows = NY * NZ * NX * root_ref.shape[5]
     per = root_ref.shape[5]
+    root_rows = NY * NZ * NX * per
 
     def body(c, _):
-        tenant = chunk_tenant[c]
-        where_ = [members[c * CHUNK + j] for j in range(CHUNK)]
+        tenant = tab[CHUNK_TENANT + c]
+        where_ = [tab[MEMBERS + c * CHUNK + j] for j in range(CHUNK)]
         q = both_heads(jnp.concatenate([q_ref[w] for w in where_], axis=0))
         own_k = jnp.concatenate([k_ref[w] for w in where_], axis=0)
         own_v = jnp.concatenate([v_ref[w] for w in where_], axis=0)
@@ -292,12 +293,11 @@
         values = root_ref[:, :, :, 1, tenant].reshape(root_rows, LANES)
         n = lax.broadcasted_iota(I32, (1, root_rows), 1)
         row = n % per
-        z = ((n // per) % NZ) ^ coords[0]
-        x_side = (n // (per * NZ)) % 2
-        y = (n // (per * NZ * 2)) % NY
-        x = (n // (per * NZ * 2 * NY) * 2 + coords[1]) ^ x_side
+        z = ((n // per) % NZ) ^ tab[PLACE]
+        x = (n // (per * NZ)) % NX
+        y = n // (per * NZ * NX)
         place = ((z * NX + x) * NY + y) * per + row
-        scores = jnp.where(place < root_len[tenant], dot_nt(q, keys), NEG)
+        scores = jnp.where(place < tab[ROOT_LEN + tenant], dot_nt(q, keys), NEG)
         own_row = (lax.broadcasted_iota(I32, (2 * rows, rows), 0) % rows) // suf
         own_col = lax.broadcasted_iota(I32, (2 * rows, rows), 1) // suf
         own = jnp.where(own_row == own_col, dot_nt(q, own_k), NEG)
@@ -314,33 +314,33 @@
         mass = by_head(peak + jnp.log(total))
         for j in range(CHUNK):
 
-            @pl.when(valid[c * CHUNK + j] > 0)
+            @pl.when(tab[VALID + c * CHUNK + j] > 0)
             def _(j=j):
                 out_ref[where_[j]] = out[j * suf : (j + 1) * suf]
                 mass_ref[where_[j]] = mass[j * suf : (j + 1) * suf]
 
         return 0
 
-    lax.fori_loop(0, used[0], body, 0)
-
-
-def root_attention(used, members, valid, chunk_tenant, root_len, coords, q, k, v, roots):
+    lax.fori_loop(0, tab[USED], body, 0)
+
+
+def root_attention(tab, q, k, v, roots):
     reqs, suf, _ = q.shape
     shape = jax.ShapeDtypeStruct((reqs, suf, LANES), F32)
     vmem = pl.BlockSpec(memory_space=pltpu.VMEM)
     return pl.pallas_call(
         root_kernel,
         out_shape=(shape, shape),
-        in_specs=[pl.BlockSpec(memory_space=pltpu.SMEM)] * 6 + [vmem] * 4,
+        in_specs=[pl.BlockSpec(memory_space=pltpu.SMEM)] + [vmem] * 4,
         out_specs=(vmem, vmem),
         compiler_params=pltpu.CompilerParams(vmem_limit_bytes=40 << 20),
         cost_estimate=pl.CostEstimate(
             flops=4 << 30, bytes_accessed=4 << 20, transcendentals=4 << 20
         ),
-    )(used, members, valid, chunk_tenant, root_len, coords, q, k, v, roots)
-
-
-def merge_kernel(pos, dst_b, dst_l, back_ref, out_ref, mass_ref, send_ref, node_mass):
+    )(tab, q, k, v, roots)
+
+
+def merge_kernel(tab, back_ref, out_ref, mass_ref, send_ref, node_mass):
     reqs, suf, _ = out_ref.shape
     per_block = reqs // N_BLK
     src = lax.broadcasted_iota(I32, (LANES, LANES), 0)
@@ -354,12 +354,12 @@
             node_mass[:, s, g] = dot_nn(packed, pick).reshape(PEERS, HALF, LANES)
 
     def body(r, _):
-        here = pos[r]
+        here = tab[POS + r]
         outs = [out_ref[here]]
         masses = [mass_ref[here]]
-        for table in (dst_b, dst_l):
-            peer = table[r] // SLOTS
-            slot = table[r] % SLOTS
+        for first in (DST_B, DST_L):
+            peer = tab[first + r] // SLOTS
+            slot = tab[first + r] % SLOTS
             outs.append(back_ref[peer, pl.ds(2 * slot, 2)].astype(F32).reshape(suf, LANES))
             masses.append(node_mass[peer, slot].reshape(suf, LANES))
         top = jnp.maximum(jnp.maximum(masses[0], masses[1]), masses[2])
@@ -375,20 +375,20 @@
     lax.fori_loop(0, reqs, body, 0, unroll=2)
 
 
-def merge(pos, dst_b, dst_l, back, out, mass):
+def merge(tab, back, out, mass):
     reqs, suf, _ = out.shape
     vmem = pl.BlockSpec(memory_space=pltpu.VMEM)
     return pl.pallas_call(
         merge_kernel,
         out_shape=jax.ShapeDtypeStruct((N_BLK, 2, reqs // N_BLK, suf, LANES), BF16),
-        in_specs=[pl.BlockSpec(memory_space=pltpu.SMEM)] * 3 + [vmem] * 3,
+        in_specs=[pl.BlockSpec(memory_space=pltpu.SMEM)] + [vmem] * 3,
         out_specs=vmem,
         scratch_shapes=[pltpu.VMEM((PEERS, SLOTS, 2, HALF, LANES), F32)],
         compiler_params=pltpu.CompilerParams(vmem_limit_bytes=30 << 20),
         cost_estimate=pl.CostEstimate(
             flops=1 << 27, bytes_accessed=4 << 20, transcendentals=1 << 20
         ),
-    )(pos, dst_b, dst_l, back, out, mass)
+    )(tab, back, out, mass)
 
 
 def rows_norm(values, gain, shift):
@@ -481,9 +481,7 @@
         return jnp.minimum(jnp.abs(flat[:1, :1]), 0)
 
     coords = jnp.stack([my_z, my_x, my_y, blk]).astype(I32)
-    dst_b, dst_l, pos, lens, members, valid, chunk_tenant, used = make_tables(
-        coords, req_leaf, node_parent, node_place, node_len, tenants
-    )
+    tab = make_tables(coords, req_leaf, node_parent, node_place, node_len, root_len)
 
     tok = tokens.reshape(own_rows, width)
     near = lax.ppermute(tok, "blk", swap)
@@ -493,18 +491,18 @@
     n_owner = NX * NY * NZ
     roots = root_cache.reshape(-1, LANES)
     roots = jnp.stack([roots, lax.ppermute(roots, "owner", xor_pairs(n_owner, NX * NY))])
-    roots = jnp.stack([roots, lax.ppermute(roots, "owner", xor_pairs(n_owner, NY))])
-    roots = roots + zero_after(last_come)
-    groups = [
-        [(z * NX + parity + 2 * i) * NY + y for i in range(NX // 2) for y in range(NY)]
-        for z in range(NZ)
-        for parity in range(2)
-    ]
-    roots = lax.all_gather(roots, "owner", axis=0, tiled=False, axis_index_groups=groups)
-    planned = zero_after(jnp.broadcast_to(pos[None, :1], (1, 1)).astype(BF16))
+    x_groups = [[(z * NX + x) * NY + y for x in range(NX)] for z in range(NZ) for y in range(NY)]
+    y_groups = [[g * NY + y for y in range(NY)] for g in range(NZ * NX)]
+    roots = lax.all_gather(roots, "owner", axis=0, tiled=False, axis_index_groups=x_groups)
+    tables_made = jnp.minimum(jnp.abs(tab[:1]), 0).astype(BF16)
+    planned = zero_after(roots)
+    roots = roots + tables_made
+    for came in half + [near]:
+        roots = roots + zero_after(came)
+    roots = lax.all_gather(roots, "owner", axis=0, tiled=False, axis_index_groups=y_groups)
     other = lax.ppermute(jnp.stack(half) + planned, "blk", swap)
     half = jnp.stack([tok] + half)
-    roots = roots.reshape(NX // 2 * NY, 2, NZ, 2, tenants, root_per, LANES)
+    roots = roots.reshape(NY, NX, NZ, 2, tenants, root_per, LANES)
 
     node_rows = node_cache.reshape(-1, LANES) + zero_after(last_come)
     node_far = lax.ppermute(node_rows, "owner", xor_pairs(n_owner, NX * NY))
@@ -514,7 +512,7 @@
     packs = pack_weights(w_up, w_down, b_up, last_come)
     pack_side = lax.ppermute(packs, "blk", swap)
 
-    q, outgoing = query_and_route(pos, dst_b, dst_l, half, near, other, w_qkv[:, 0], suf, last_come)
+    q, outgoing = query_and_route(tab, half, near, other, w_qkv[:, 0], suf, last_come)
     outgoing = outgoing.reshape(PEERS, SLOTS, suf, cols)
 
     def project(which):
@@ -538,7 +536,7 @@
     new_caches = jnp.stack([k_new, v_new]).reshape(2, N_BLK, req_dev, suf, cols)
     new_caches = jnp.take(new_caches, order, axis=1).reshape(2, reqs, suf, cols)
 
-    answers = node_attention(lens, incoming, caches, packs)
+    answers = node_attention(tab, incoming, caches, packs)
     z_chips = NZ * n_own
 
     def to_neighbour(step):
@@ -552,16 +550,13 @@
         return lax.ppermute(sent, ("blk", "owner"), pairs)
 
     pack_next = [to_neighbour(1), to_neighbour(-1)]
-    pack_last = [lax.ppermute(part, "blk", swap) for part in pack_next]
-    parts = [packs, pack_side] + pack_next + pack_last
     back = lax.all_to_all(
         answers, "owner", split_axis=0, concat_axis=0, axis_index_groups=groups, tiled=True
     )
-    parity = jnp.stack([my_z, my_x % 2]).astype(I32)
-    out, mass = root_attention(
-        used, members, valid, chunk_tenant, root_len, parity, q, k_new, v_new, roots
-    )
-    send = merge(pos, dst_b, dst_l, back, out, mass)
+    out, mass = root_attention(tab, q, k_new, v_new, roots)
+    send = merge(tab, back, out, mass)
+    pack_last = [lax.ppermute(part + zero_after(mass.reshape(-1, LANES)).astype(BF16), "blk", swap) for part in pack_next]
+    parts = [packs, pack_side] + pack_next + pack_last
     attn = lax.all_to_all(
         send.reshape(N_BLK, 2 * own_rows, cols), "blk", split_axis=0, concat_axis=0, tiled=True
     )

time: 231 us -> 245 us (1.061)
  waiting for transfers between devices: 68.9 us -> 57.9 us
  blocking collectives: 0 us -> 9.71 us
  other arithmetic: 9.32 us -> 16.1 us
  matrix products: 3.99 us -> 8.57 us
  between operations: 16.4 us -> 20.2 us
  Pallas kernels: 36 us -> 33.1 us
    all_to_all x1, waiting for transfers between devices: 0.01 us -> 10.5 us  [on_device(): lax.all_to_all(outgoing, 'owner', split_axis=0, concat_axis=0, axis_index...]
    all_gather x0 -> x1, blocking collectives: none -> 9.71 us  [on_device(): lax.all_gather(roots, 'owner', axis=0, tiled=False, axis_index_groups=x_g...]
    ppermute x2, waiting for transfers between devices: 18.6 us -> 9.62 us  [to_neighbour(): return lax.ppermute(sent, ('blk', 'owner'), pairs)]
    ppermute x1, waiting for transfers between devices: 15.9 us -> 9.33 us  [on_device(): node_far = lax.ppermute(node_rows, 'owner', xor_pairs(n_owner, NX * NY))]
    add x1 -> x3, other arithmetic: 0.66 us -> 5.35 us  [the longest x2 4.58 us: on_device(): part + zero_after(mass.reshape(-1, LANES)).astype(BF16)]
    dot_general x6, matrix products: 3.99 us -> 8.57 us  [project(): jnp.dot(part.reshape(-1, width), w, preferred_element_type=F32)]
    ppermute x1, starting transfers between devices: 1.92 us -> 6.34 us  [on_device(): near = lax.ppermute(tok, 'blk', swap)]
    ppermute x3 -> x2, starting transfers between devices: 8.8 us -> 12.5 us  [on_device(): lax.ppermute(part + zero_after(mass.reshape(-1, LANES)).astype(BF16), 'bl...]
  transfers between devices with their start and end apart: 19 -> 18, of which waited for: 8 -> 8; matrix products, arithmetic and copies ran while one was open for 6% -> 12% of each run, Pallas kernels for 12% -> 11%
where the time goes in v6:
time: 245 us; the launch traced here: 243 us
  starting transfers between devices  76.8 us (31%)
  waiting for transfers between devices  57.9 us (24%)
  Pallas kernels  33.1 us (14%)
  local copies, waits for them, and re-layouts  20.5 us (8%)
  between operations  20.2 us (8%)
  other arithmetic  16.1 us (7%)
  blocking collectives  9.71 us (4%)
  matrix products  8.57 us (3%)
    all_to_all x1, waiting for transfers between devices, on_device(): lax.all_to_all(send.reshape(N_BLK, 2 * own_rows, cols), 'blk', split_axis...  13.4 us
    unnamed x80, local copies, waits for them, and re-layouts  13.1 us
    ppermute x3, starting transfers between devices, on_device(): lax.ppermute(tok, 'blk', xor_pairs(N_BLK, 2 * k))  12.6 us
    ppermute x2, starting transfers between devices, on_device(): lax.ppermute(part + zero_after(mass.reshape(-1, LANES)).astype(BF16), 'bl...  12.5 us
    ppermute x1, waiting for transfers between devices, on_device(): lax.ppermute(down_far, 'blk', xor_pairs(N_BLK, N_BLK // 2)).astype(F32)  12.1 us
    all_to_all x1, waiting for transfers between devices, on_device(): lax.all_to_all(outgoing, 'owner', split_axis=0, concat_axis=0, axis_index...  10.5 us
    all_gather x1, blocking collectives, on_device(): lax.all_gather(roots, 'owner', axis=0, tiled=False, axis_index_groups=x_g...  9.71 us
    ppermute x2, waiting for transfers between devices, to_neighbour(): return lax.ppermute(sent, ('blk', 'owner'), pairs)  9.62 us
  transfers between devices with their start and end apart: 18, of which 8 were waited for; matrix products, arithmetic and copies ran while one was open for 12% of the time, Pallas kernels for 11%

profile of v6, /device:TPU:1, one launch (start us, length us, event | category | flops | bytes accessed | tf_op | source)
XLA Modules:
  0.0 242.9 jit_solution(15260541507251601445)
XLA Ops:
  7.2 8.4 %collective-permute-start.2 = (bf16[128,1024]{1,0:T(8,128)(2,1)}, bf16[128,1024]{1,0:T(8,128)(2,1)S(1)}, u32[]{:S(2)}, u32[]{:S(2)}) collective-permute-start(bf16[128,1024]{1,0:T(8,128)(2,1)} %bitcast.83), channel_id=1, source_target_pairs={{0,384},{64,448},{128,256},{192,320},{256,128},{320,192},{384,0},{... | collective-permute-start | bytes 786440 | tf_op jit(solution)/shard_map/ppermute | solution.py:488
  15.7 1.9 collective-permute-start.1
  17.6 2.2 collective-permute-start
  19.8 6.3 %collective-permute-start.3 = (bf16[128,1024]{1,0:T(8,128)(2,1)}, bf16[128,1024]{1,0:T(8,128)(2,1)S(1)}, u32[]{:S(2)}, u32[]{:S(2)}) collective-permute-start(bf16[128,1024]{1,0:T(8,128)(2,1)} %bitcast.86), channel_id=1, source_target_pairs={{0,64},{64,0},{128,192},{192,128},{256,320},{320,256},{384,448},{4... | collective-permute-start | bytes 786440 | tf_op jit(solution)/shard_map/ppermute | solution.py:487
  26.1 5.3 %collective-permute-start.4 = (bf16[128,128]{1,0:T(8,128)(2,1)}, bf16[128,128]{1,0:T(8,128)(2,1)S(1)}, u32[]{:S(2)}, u32[]{:S(2)}) collective-permute-start(bf16[128,128]{1,0:T(8,128)(2,1)} %bitcast.97), channel_id=1, source_target_pairs={{0,32},{1,33},{2,34},{3,35},{4,36},{5,37},{6,38},{7,39},{8,40},{9,... | collective-permute-start | bytes 98312 | tf_op jit(solution)/shard_map/ppermute | solution.py:493
  32.1 3.9 %shard_map.194.tab = s32[288]{0:T(512)} custom-call(s32[4]{0:T(128)} %pad_add_fusion.coords, s32[32]{0:T(128)} %leaf_of.1, s32[128]{0:T(128)} %parent.1, s32[128]{0:T(128)} %place.1, s32[128]{0:T(128)} %length.1, s32[4]{0:T(128)} %root_len.1), custom_call_target="tpu_custom_call" | custom-call | flops 1048576 | bytes 4096 | tf_op jit(solution)/shard_map/pallas_call | solution.py:138
  36.0 1.2 slice.42
  37.8 2.2 collective-permute-done.4
  40.8 9.7 %all-gather = bf16[8,128,128]{2,1,0:T(8,128)(2,1)S(1)} all-gather(bf16[2,128,128]{2,1,0:T(8,128)(2,1)S(1)} %pad_maximum_fusion.3), channel_id=2, replica_groups={{0,8,16,24},{1,9,17,25},{2,10,18,26},{3,11,19,27},{4,12,20,28},{5,13,21..., dimensions={0}, use_global_device_ids=true | all-gather | bytes 327680 | tf_op jit(solution)/shard_map/all_gather | solution.py:496
  57.4 7.0 %collective-permute-start.5 = (bf16[3,128,1024]{2,1,0:T(8,128)(2,1)S(1)}, bf16[3,128,1024]{2,1,0:T(8,128)(2,1)S(1)}, u32[]{:S(2)}, u32[]{:S(2)}) collective-permute-start(bf16[3,128,1024]{2,1,0:T(8,128)(2,1)S(1)} %maximum_add_fusion), channel_id=1, source_target_pairs={{0,64},{64,0},{128,192},{192,128},{256,320},{320,256},{384,448},{4... | collective-permute-start | bytes 2359304 | tf_op jit(solution)/shard_map/ppermute | solution.py:503
  64.4 1.0 slice_bitcast_fusion.w_ref
  66.3 2.4 %shard_map.195 = (bf16[32,32,128]{2,1,0:T(8,128)(2,1)S(1)}, bf16[128,32,128]{2,1,0:T(8,128)(2,1)}) custom-call(s32[288]{0:T(512)S(1)} %copy-done.20, bf16[4,128,1024]{2,1,0:T(8,128)(2,1)S(1)} %pad_maximum_fusion.half_ref, bf16[128,1024]{1,0:T(8,128)(2,1)S(1)} %collective-permute-done.3.near_ref, bf16[3,128,1024]{2,1,0:T(8,128)(2,1)S(1)} %collective-permute-done.5.other_ref, ...), custom_call_target="tpu_custom_call" | custom-call | flops 268435456 | bytes 4194304 | tf_op jit(solution)/shard_map/pallas_call | solution.py:172
  69.4 9.0 %all-to-all-start = ((bf16[32,4,32,128]{3,2,1,0:T(8,128)(2,1)}), bf16[32,4,32,128]{3,2,1,0:T(8,128)(2,1)}, u32[]{:S(2)}, u32[]{:S(2)}) async-start(bf16[32,4,32,128]{3,2,1,0:T(8,128)(2,1)} %bitcast.15), calls=%async_computation | async-start | bytes 2097152 | tf_op jit(solution)/shard_map/all_to_all | solution.py:529
  79.4 1.9 collective-permute-start.6
  81.3 1.2 copy-done.7
  82.6 1.2 copy-done.8
  84.0 2.6 %collective-permute-start.7 = (bf16[2,2064,256]{2,1,0:T(8,128)(2,1)S(1)}, bf16[2,2064,256]{2,1,0:T(8,128)(2,1)}, u32[]{:S(2)}, u32[]{:S(2)}) collective-permute-start(bf16[2,2064,256]{2,1,0:T(8,128)(2,1)S(1)} %shard_map.196.after_ref.w0), channel_id=1, source_target_pairs={{0,64},{64,0},{128,192},{192,128},{256,320},{320,256},{384,448},{4... | collective-permute-start | bytes 6340616 | tf_op jit(solution)/shard_map/ppermute | solution.py:513
  87.3 1.9 fusion.8
  89.2 1.1 fusion.30
  90.3 1.1 fusion.10
  92.3 1.1 fusion.4
  93.4 9.3 %collective-permute-done.6 = bf16[1536,128]{1,0:T(8,128)(2,1)} collective-permute-done((bf16[1536,128]{1,0:T(8,128)(2,1)}, bf16[1536,128]{1,0:T(8,128)(2,1)}, u32[]{:S(2)}, u32[]{:S(2)}) %collective-permute-start.6) | collective-permute-done | bytes 393248 | tf_op jit(solution)/shard_map/ppermute | solution.py:508
  102.7 2.0 pad_maximum_fusion.1.cache_ref
  104.7 10.5 %all-to-all-done.q_ref = bf16[32,4,32,128]{3,2,1,0:T(8,128)(2,1)} async-done(((bf16[32,4,32,128]{3,2,1,0:T(8,128)(2,1)}), bf16[32,4,32,128]{3,2,1,0:T(8,128)(2,1)}, u32[]{:S(2)}, u32[]{:S(2)}) %all-to-all-start) | async-done | bytes 1048608 | tf_op jit(solution)/shard_map/all_to_all | solution.py:529
  115.1 1.1 copy-done.11
  116.3 8.1 %shard_map.197 = bf16[32,9,16,128]{3,2,1,0:T(8,128)(2,1)S(1)} custom-call(s32[288]{0:T(512)S(1)} %copy-done.20, bf16[32,4,32,128]{3,2,1,0:T(8,128)(2,1)} %all-to-all-done.q_ref, bf16[2,2,2,384,128]{4,3,2,1,0:T(8,128)(2,1)S(1)} %copy-done.11, bf16[2,2064,256]{2,1,0:T(8,128)(2,1)S(1)} %shard_map.196.after_ref.w0), custom_call_target="tpu_custom_call" | custom-call | flops 2147483648 | bytes 4194304 | tf_op jit(solution)/shard_map/pallas_call | solution.py:263
  125.7 1.5 add_bitcast_fusion
  127.2 1.9 collective-permute-start.9
  129.1 2.0 fusion.6
  131.1 7.8 %all-to-all-start.1 = ((bf16[32,9,16,128]{3,2,1,0:T(8,128)(2,1)}), bf16[32,9,16,128]{3,2,1,0:T(8,128)(2,1)S(1)}, u32[]{:S(2)}, u32[]{:S(2)}) async-start(bf16[32,9,16,128]{3,2,1,0:T(8,128)(2,1)} %copy-done.4), calls=%async_computation.1 | async-start | bytes 2359296 | tf_op jit(solution)/shard_map/all_to_all | solution.py:553
  139.0 1.6 fusion
  141.4 3.4 %collective-permute-start.8 = (bf16[2064,256]{1,0:T(8,128)(2,1)}, bf16[2064,256]{1,0:T(8,128)(2,1)}, u32[]{:S(2)}, u32[]{:S(2)}) collective-permute-start(bf16[2064,256]{1,0:T(8,128)(2,1)} %get-tuple-element.19), channel_id=1, source_target_pairs={{0,128},{1,129},{2,130},{3,131},{4,132},{5,133},{6,134},{7,135},{8... | collective-permute-start | bytes 3170312 | tf_op jit(solution)/shard_map/ppermute | solution.py:550
  146.4 1.6 copy-done.23
  149.0 8.9 %shard_map.198 = (f32[32,32,128]{2,1,0:T(8,128)S(1)}, f32[32,32,128]{2,1,0:T(8,128)S(1)}) custom-call(s32[288]{0:T(512)S(1)} %copy-done.21, bf16[32,32,128]{2,1,0:T(8,128)(2,1)S(1)} %copy-done.25, bf16[32,32,128]{2,1,0:T(8,128)(2,1)S(1)} %bitcast.74, bf16[32,32,128]{2,1,0:T(8,128)(2,1)S(1)} %bitcast.76, bf16[8,4,2,2,4,16,128]{6,5,4,3,2,1,0:T(8,128)(2,1)S(1)} %bitcast.89), custom_call_target="tpu_custom_call" | custom-call | flops 4294967296 | bytes 4194304 | tf_op jit(solution)/shard_map/pallas_call | solution.py:331
  159.2 8.2 %collective-permute-done.9.w3 = bf16[2064,256]{1,0:T(8,128)(2,1)} collective-permute-done((bf16[2064,256]{1,0:T(8,128)(2,1)}, bf16[2064,256]{1,0:T(8,128)(2,1)}, u32[]{:S(2)}, u32[]{:S(2)}) %collective-permute-start.9) | collective-permute-done | bytes 1056800 | tf_op jit(solution)/shard_map/ppermute | solution.py:550
  167.4 2.3 broadcast_add_fusion
  169.7 9.3 %collective-permute-start.11 = (bf16[2064,256]{1,0:T(8,128)(2,1)}, bf16[2064,256]{1,0:T(8,128)(2,1)}, u32[]{:S(2)}, u32[]{:S(2)}) collective-permute-start(bf16[2064,256]{1,0:T(8,128)(2,1)} %broadcast_add_fusion), channel_id=1, source_target_pairs={{0,64},{64,0},{128,192},{192,128},{256,320},{320,256},{384,448},{4... | collective-permute-start | bytes 3170312 | tf_op jit(solution)/shard_map/ppermute | solution.py:558
  179.0 1.4 collective-permute-done.8.w2
  180.4 2.3 broadcast_add_fusion.1
  182.7 3.2 %collective-permute-start.10 = (bf16[2064,256]{1,0:T(8,128)(2,1)}, bf16[2064,256]{1,0:T(8,128)(2,1)}, u32[]{:S(2)}, u32[]{:S(2)}) collective-permute-start(bf16[2064,256]{1,0:T(8,128)(2,1)} %broadcast_add_fusion.1), channel_id=1, source_target_pairs={{0,64},{64,0},{128,192},{192,128},{256,320},{320,256},{384,448},{4... | collective-permute-start | bytes 3170312 | tf_op jit(solution)/shard_map/ppermute | solution.py:558
  185.9 1.0 copy-done.15
  186.9 1.0 copy-done.17
  188.6 2.1 shard_map.199
  191.5 4.6 %all-to-all-start.2 = ((bf16[8,256,128]{2,1,0:T(8,128)(2,1)}), bf16[8,256,128]{2,1,0:T(8,128)(2,1)S(1)}, u32[]{:S(2)}, u32[]{:S(2)}) async-start(bf16[8,256,128]{2,1,0:T(8,128)(2,1)} %bitcast.72), calls=%async_computation.2 | async-start | bytes 1048576 | tf_op jit(solution)/shard_map/all_to_all | solution.py:560
  197.2 13.4 %all-to-all-done.2.attn_ref = bf16[8,256,128]{2,1,0:T(8,128)(2,1)S(1)} async-done(((bf16[8,256,128]{2,1,0:T(8,128)(2,1)}), bf16[8,256,128]{2,1,0:T(8,128)(2,1)S(1)}, u32[]{:S(2)}, u32[]{:S(2)}) %all-to-all-start.2) | async-done | bytes 524320 | tf_op jit(solution)/shard_map/all_to_all | solution.py:560
  211.6 7.5 %shard_map.200 = (bf16[128,1024]{1,0:T(8,128)(2,1)S(1)}, f32[128,1024]{1,0:T(8,128)S(1)}, bf16[128,1024]{1,0:T(8,128)(2,1)S(1)}) custom-call(bf16[8,256,128]{2,1,0:T(8,128)(2,1)S(1)} %all-to-all-done.2.attn_ref, bf16[1024,1024]{1,0:T(8,128)(2,1)} %all-gather.5.cloned.1.call-done.w_out_ref, bf16[128,1024]{1,0:T(8,128)(2,1)S(1)} %bitcast.88, ...), custom_call_target="tpu_custom_call" | custom-call | flops 3221225472 | bytes 12582912 | tf_op jit(solution)/shard_map/pallas_call | solution.py:427
  219.1 1.9 collective-permute-start.12
  222.7 12.1 %collective-permute-done.12 = bf16[128,1024]{1,0:T(8,128)(2,1)S(1)} collective-permute-done((bf16[128,1024]{1,0:T(8,128)(2,1)S(1)}, bf16[128,1024]{1,0:T(8,128)(2,1)S(1)}, u32[]{:S(2)}, u32[]{:S(2)}) %collective-permute-start.12) | collective-permute-done | bytes 262176 | tf_op jit(solution)/shard_map/ppermute | solution.py:565
  (129 shorter events, 19.9 us)
Async XLA Ops:
  7.2 137.6 %all-gather.7.cloned.1.call-start = ((), (), s32[]{:S(2)}) async-start(), calls=%async_computation.4 | async-start | bytes 2359296 | tf_op jit(solution)/shard_map/all_gather | solution.py:502
  7.2 43.3 %collective-permute-start.2 = (bf16[128,1024]{1,0:T(8,128)(2,1)}, bf16[128,1024]{1,0:T(8,128)(2,1)S(1)}, u32[]{:S(2)}, u32[]{:S(2)}) collective-permute-start(bf16[128,1024]{1,0:T(8,128)(2,1)} %bitcast.83), channel_id=1, source_target_pairs={{0,384},{64,448},{128,256},{192,320},{256,128},{320,192},{384,0},{... | collective-permute-start | bytes 786440 | tf_op jit(solution)/shard_map/ppermute | solution.py:488
  15.7 37.3 %collective-permute-start.1 = (bf16[128,1024]{1,0:T(8,128)(2,1)}, bf16[128,1024]{1,0:T(8,128)(2,1)S(1)}, u32[]{:S(2)}, u32[]{:S(2)}) collective-permute-start(bf16[128,1024]{1,0:T(8,128)(2,1)} %bitcast.84), channel_id=1, source_target_pairs={{0,256},{64,320},{128,384},{192,448},{256,0},{320,64},{384,128},{4... | collective-permute-start | bytes 786440 | tf_op jit(solution)/shard_map/ppermute | solution.py:488
  17.6 36.6 %collective-permute-start = (bf16[128,1024]{1,0:T(8,128)(2,1)}, bf16[128,1024]{1,0:T(8,128)(2,1)S(1)}, u32[]{:S(2)}, u32[]{:S(2)}) collective-permute-start(bf16[128,1024]{1,0:T(8,128)(2,1)} %bitcast.85), channel_id=1, source_target_pairs={{0,128},{64,192},{128,0},{192,64},{256,384},{320,448},{384,256},{4... | collective-permute-start | bytes 786440 | tf_op jit(solution)/shard_map/ppermute | solution.py:488
  19.8 31.9 %collective-permute-start.3 = (bf16[128,1024]{1,0:T(8,128)(2,1)}, bf16[128,1024]{1,0:T(8,128)(2,1)S(1)}, u32[]{:S(2)}, u32[]{:S(2)}) collective-permute-start(bf16[128,1024]{1,0:T(8,128)(2,1)} %bitcast.86), channel_id=1, source_target_pairs={{0,64},{64,0},{128,192},{192,128},{256,320},{320,256},{384,448},{4... | collective-permute-start | bytes 786440 | tf_op jit(solution)/shard_map/ppermute | solution.py:487
  26.1 13.9 %collective-permute-start.4 = (bf16[128,128]{1,0:T(8,128)(2,1)}, bf16[128,128]{1,0:T(8,128)(2,1)S(1)}, u32[]{:S(2)}, u32[]{:S(2)}) collective-permute-start(bf16[128,128]{1,0:T(8,128)(2,1)} %bitcast.97), channel_id=1, source_target_pairs={{0,32},{1,33},{2,34},{3,35},{4,36},{5,37},{6,38},{7,39},{8,40},{9,... | collective-permute-start | bytes 98312 | tf_op jit(solution)/shard_map/ppermute | solution.py:493
  51.7 17.0 %copy-start.1 = (bf16[128,1024]{1,0:T(8,128)(2,1)}, bf16[128,1024]{1,0:T(8,128)(2,1)S(1)}, u32[]{:S(2)}) copy-start(bf16[128,1024]{1,0:T(8,128)(2,1)S(1)} %collective-permute-done.3.near_ref) | copy-start | bytes 786436
  52.9 12.4 %copy-start.9 = (bf16[128,1024]{1,0:T(8,128)(2,1)}, bf16[128,1024]{1,0:T(8,128)(2,1)S(1)}, u32[]{:S(2)}) copy-start(bf16[128,1024]{1,0:T(8,128)(2,1)S(1)} %collective-permute-done.1.tok_b) | copy-start | bytes 786436
  56.1 9.3 %copy-start.18 = (bf16[4,32,1024]{2,1,0:T(8,128)(2,1)S(1)}, bf16[4,32,1024]{2,1,0:T(8,128)(2,1)}, u32[]{:S(2)}) copy-start(bf16[4,32,1024]{2,1,0:T(8,128)(2,1)} %param.19) | copy-start | bytes 786436
  57.4 8.9 %collective-permute-start.5 = (bf16[3,128,1024]{2,1,0:T(8,128)(2,1)S(1)}, bf16[3,128,1024]{2,1,0:T(8,128)(2,1)S(1)}, u32[]{:S(2)}, u32[]{:S(2)}) collective-permute-start(bf16[3,128,1024]{2,1,0:T(8,128)(2,1)S(1)} %maximum_add_fusion), channel_id=1, source_target_pairs={{0,64},{64,0},{128,192},{192,128},{256,320},{320,256},{384,448},{4... | collective-permute-start | bytes 2359304 | tf_op jit(solution)/shard_map/ppermute | solution.py:503
  66.2 3.2 %copy-start.12 = (bf16[3,128,1024]{2,1,0:T(8,128)(2,1)}, bf16[3,128,1024]{2,1,0:T(8,128)(2,1)S(1)}, u32[]{:S(2)}) copy-start(bf16[3,128,1024]{2,1,0:T(8,128)(2,1)S(1)} %collective-permute-done.5.other_ref) | copy-start | bytes 2359300
  69.4 9.2 %copy-start.39 = (bf16[512]{0:T(512)(128)(2,1)S(1)}, bf16[512]{0:T(512)(128)(2,1)}, u32[]{:S(2)}) copy-start(bf16[512]{0:T(512)(128)(2,1)} %param.26) | copy-start | bytes 3076
  69.4 9.2 %copy-start.26 = (bf16[2,2,384,128]{3,2,1,0:T(8,128)(2,1)S(1)}, bf16[2,2,384,128]{3,2,1,0:T(8,128)(2,1)}, u32[]{:S(2)}) copy-start(bf16[2,2,384,128]{3,2,1,0:T(8,128)(2,1)} %param.32) | copy-start | bytes 1179652
  69.4 45.7 %all-to-all-start = ((bf16[32,4,32,128]{3,2,1,0:T(8,128)(2,1)}), bf16[32,4,32,128]{3,2,1,0:T(8,128)(2,1)}, u32[]{:S(2)}, u32[]{:S(2)}) async-start(bf16[32,4,32,128]{3,2,1,0:T(8,128)(2,1)} %bitcast.15), calls=%async_computation | async-start | bytes 2097152 | tf_op jit(solution)/shard_map/all_to_all | solution.py:529
  78.4 118.8 %all-gather.5.cloned.1.call-start = ((), (), s32[]{:S(2)}) async-start(), calls=%async_computation.3 | async-start | bytes 2359296 | tf_op jit(solution)/shard_map/all_gather | solution.py:511
  79.4 23.3 %collective-permute-start.6 = (bf16[1536,128]{1,0:T(8,128)(2,1)}, bf16[1536,128]{1,0:T(8,128)(2,1)}, u32[]{:S(2)}, u32[]{:S(2)}) collective-permute-start(bf16[1536,128]{1,0:T(8,128)(2,1)} %bitcast.18), channel_id=1, source_target_pairs={{0,32},{1,33},{2,34},{3,35},{4,36},{5,37},{6,38},{7,39},{8,40},{9,... | collective-permute-start | bytes 1179656 | tf_op jit(solution)/shard_map/ppermute | solution.py:508
  81.3 1.2 copy-start.7
  82.6 1.2 copy-start.8
  83.8 2.7 %copy-start.28 = (bf16[128,1024]{1,0:T(8,128)(2,1)S(1)}, bf16[128,1024]{1,0:T(8,128)(2,1)}, u32[]{:S(2)}) copy-start(bf16[128,1024]{1,0:T(8,128)(2,1)} %param.21) | copy-start | bytes 786436
  83.9 41.7 %copy-start = (bf16[2,2064,256]{2,1,0:T(8,128)(2,1)}, bf16[2,2064,256]{2,1,0:T(8,128)(2,1)S(1)}, u32[]{:S(2)}) copy-start(bf16[2,2064,256]{2,1,0:T(8,128)(2,1)S(1)} %shard_map.196.after_ref.w0) | copy-start | bytes 6340612
  84.0 113.2 %collective-permute-start.7 = (bf16[2,2064,256]{2,1,0:T(8,128)(2,1)S(1)}, bf16[2,2064,256]{2,1,0:T(8,128)(2,1)}, u32[]{:S(2)}, u32[]{:S(2)}) collective-permute-start(bf16[2,2064,256]{2,1,0:T(8,128)(2,1)S(1)} %shard_map.196.after_ref.w0), channel_id=1, source_target_pairs={{0,64},{64,0},{128,192},{192,128},{256,320},{320,256},{384,448},{4... | collective-permute-start | bytes 6340616 | tf_op jit(solution)/shard_map/ppermute | solution.py:513
  87.3 3.0 %copy-start.27 = (bf16[1024,3,128]{2,0,1:T(8,128)(2,1)S(1)}, bf16[1024,3,128]{2,0,1:T(8,128)(2,1)}, u32[]{:S(2)}) copy-start(bf16[1024,3,128]{2,0,1:T(8,128)(2,1)} %param.20) | copy-start | bytes 2359300
  89.2 2.2 copy-start.2
  115.1 1.1 copy-start.11
  124.4 4.7 %copy-start.4 = (bf16[32,9,16,128]{3,2,1,0:T(8,128)(2,1)}, bf16[32,9,16,128]{3,2,1,0:T(8,128)(2,1)S(1)}, u32[]{:S(2)}) copy-start(bf16[32,9,16,128]{3,2,1,0:T(8,128)(2,1)S(1)} %shard_map.197) | copy-start | bytes 3538948
  125.6 3.5 %copy-start.13 = (bf16[3,128,1024]{2,1,0:T(8,128)(2,1)S(1)}, bf16[3,128,1024]{2,1,0:T(8,128)(2,1)}, u32[]{:S(2)}) copy-start(bf16[3,128,1024]{2,1,0:T(8,128)(2,1)} %copy-done.12) | copy-start | bytes 2359300
  127.2 40.2 %collective-permute-start.9 = (bf16[2064,256]{1,0:T(8,128)(2,1)}, bf16[2064,256]{1,0:T(8,128)(2,1)}, u32[]{:S(2)}, u32[]{:S(2)}) collective-permute-start(bf16[2064,256]{1,0:T(8,128)(2,1)} %get-tuple-element.18), channel_id=1, source_target_pairs={{0,416},{1,417},{2,418},{3,419},{4,420},{5,421},{6,422},{7,423},{8... | collective-permute-start | bytes 3170312 | tf_op jit(solution)/shard_map/ppermute | solution.py:550
  131.1 54.8 %all-to-all-start.1 = ((bf16[32,9,16,128]{3,2,1,0:T(8,128)(2,1)}), bf16[32,9,16,128]{3,2,1,0:T(8,128)(2,1)S(1)}, u32[]{:S(2)}, u32[]{:S(2)}) async-start(bf16[32,9,16,128]{3,2,1,0:T(8,128)(2,1)} %copy-done.4), calls=%async_computation.1 | async-start | bytes 2359296 | tf_op jit(solution)/shard_map/all_to_all | solution.py:553
  138.9 1.7 copy-start.29
  138.9 1.7 copy-start.32
  138.9 1.7 copy-start.33
  138.9 1.7 copy-start.30
  138.9 1.7 copy-start.31
  141.4 39.0 %collective-permute-start.8 = (bf16[2064,256]{1,0:T(8,128)(2,1)}, bf16[2064,256]{1,0:T(8,128)(2,1)}, u32[]{:S(2)}, u32[]{:S(2)}) collective-permute-start(bf16[2064,256]{1,0:T(8,128)(2,1)} %get-tuple-element.19), channel_id=1, source_target_pairs={{0,128},{1,129},{2,130},{3,131},{4,132},{5,133},{6,134},{7,135},{8... | collective-permute-start | bytes 3170312 | tf_op jit(solution)/shard_map/ppermute | solution.py:550
  146.4 1.6 copy-start.23
  157.9 11.8 %copy-start.14 = (f32[32,32,128]{2,1,0:T(8,128)}, f32[32,32,128]{2,1,0:T(8,128)S(1)}, u32[]{:S(2)}) copy-start(f32[32,32,128]{2,1,0:T(8,128)S(1)} %get-tuple-element.11.out_ref) | copy-start | bytes 1572868
  157.9 11.7 %copy-start.16 = (f32[32,32,128]{2,1,0:T(8,128)}, f32[32,32,128]{2,1,0:T(8,128)S(1)}, u32[]{:S(2)}) copy-start(f32[32,32,128]{2,1,0:T(8,128)S(1)} %get-tuple-element.12.mass_ref) | copy-start | bytes 1572868
  169.7 27.6 %collective-permute-start.11 = (bf16[2064,256]{1,0:T(8,128)(2,1)}, bf16[2064,256]{1,0:T(8,128)(2,1)}, u32[]{:S(2)}, u32[]{:S(2)}) collective-permute-start(bf16[2064,256]{1,0:T(8,128)(2,1)} %broadcast_add_fusion), channel_id=1, source_target_pairs={{0,64},{64,0},{128,192},{192,128},{256,320},{320,256},{384,448},{4... | collective-permute-start | bytes 3170312 | tf_op jit(solution)/shard_map/ppermute | solution.py:558
  182.7 14.6 %collective-permute-start.10 = (bf16[2064,256]{1,0:T(8,128)(2,1)}, bf16[2064,256]{1,0:T(8,128)(2,1)}, u32[]{:S(2)}, u32[]{:S(2)}) collective-permute-start(bf16[2064,256]{1,0:T(8,128)(2,1)} %broadcast_add_fusion.1), channel_id=1, source_target_pairs={{0,64},{64,0},{128,192},{192,128},{256,320},{320,256},{384,448},{4... | collective-permute-start | bytes 3170312 | tf_op jit(solution)/shard_map/ppermute | solution.py:558
  191.5 5.3 %copy-start.34 = (bf16[1024]{0:T(1024)(128)(2,1)S(1)}, bf16[1024]{0:T(1024)(128)(2,1)}, u32[]{:S(2)}) copy-start(bf16[1024]{0:T(1024)(128)(2,1)} %param.23) | copy-start | bytes 6148
  191.5 5.3 %copy-start.35 = (bf16[1024]{0:T(1024)(128)(2,1)S(1)}, bf16[1024]{0:T(1024)(128)(2,1)}, u32[]{:S(2)}) copy-start(bf16[1024]{0:T(1024)(128)(2,1)} %param.24) | copy-start | bytes 6148
  191.5 5.4 %copy-start.36 = (bf16[1024]{0:T(1024)(128)(2,1)S(1)}, bf16[1024]{0:T(1024)(128)(2,1)}, u32[]{:S(2)}) copy-start(bf16[1024]{0:T(1024)(128)(2,1)} %param.28) | copy-start | bytes 6148
  191.5 5.4 %copy-start.37 = (bf16[1024]{0:T(1024)(128)(2,1)S(1)}, bf16[1024]{0:T(1024)(128)(2,1)}, u32[]{:S(2)}) copy-start(bf16[1024]{0:T(1024)(128)(2,1)} %param.29) | copy-start | bytes 6148
  191.5 5.4 %copy-start.38 = (bf16[1024]{0:T(1024)(128)(2,1)S(1)}, bf16[1024]{0:T(1024)(128)(2,1)}, u32[]{:S(2)}) copy-start(bf16[1024]{0:T(1024)(128)(2,1)} %param.30) | copy-start | bytes 6148
  191.5 19.1 %copy-start.10 = (bf16[128,1024]{1,0:T(8,128)(2,1)S(1)}, bf16[128,1024]{1,0:T(8,128)(2,1)}, u32[]{:S(2)}) copy-start(bf16[128,1024]{1,0:T(8,128)(2,1)} %copy-done.9) | copy-start | bytes 786436
  191.5 19.1 %all-to-all-start.2 = ((bf16[8,256,128]{2,1,0:T(8,128)(2,1)}), bf16[8,256,128]{2,1,0:T(8,128)(2,1)S(1)}, u32[]{:S(2)}, u32[]{:S(2)}) async-start(bf16[8,256,128]{2,1,0:T(8,128)(2,1)} %bitcast.72), calls=%async_computation.2 | async-start | bytes 1048576 | tf_op jit(solution)/shard_map/all_to_all | solution.py:560
  197.2 23.9 %copy-start.6 = (bf16[1024,128]{1,0:T(8,128)(2,1)S(1)}, bf16[1024,128]{1,0:T(8,128)(2,1)}, u32[]{:S(2)}) copy-start(bf16[1024,128]{1,0:T(8,128)(2,1)} %maximum_convert_fusion.1) | copy-start | bytes 786436
  219.1 15.7 %collective-permute-start.12 = (bf16[128,1024]{1,0:T(8,128)(2,1)S(1)}, bf16[128,1024]{1,0:T(8,128)(2,1)S(1)}, u32[]{:S(2)}, u32[]{:S(2)}) collective-permute-start(bf16[128,1024]{1,0:T(8,128)(2,1)S(1)} %get-tuple-element.15), channel_id=1, source_target_pairs={{0,256},{64,320},{128,384},{192,448},{256,0},{320,64},{384,128},{4... | collective-permute-start | bytes 786440 | tf_op jit(solution)/shard_map/ppermute | solution.py:565
  (10 other events, 8.7 us)
Sparse Core Ops, SparseCore 0:
  56.2 60.8 all-gather.6
  119.2 54.7 all-gather.4

commit v7 on v6

--- a/solution.py
+++ b/solution.py
@@ -294,8 +294,8 @@
         n = lax.broadcasted_iota(I32, (1, root_rows), 1)
         row = n % per
         z = ((n // per) % NZ) ^ tab[PLACE]
-        x = (n // (per * NZ)) % NX
-        y = n // (per * NZ * NX)
+        y = (n // (per * NZ)) % NY
+        x = n // (per * NZ * NY)
         place = ((z * NX + x) * NY + y) * per + row
         scores = jnp.where(place < tab[ROOT_LEN + tenant], dot_nt(q, keys), NEG)
         own_row = (lax.broadcasted_iota(I32, (2 * rows, rows), 0) % rows) // suf
@@ -389,6 +389,23 @@
             flops=1 << 27, bytes_accessed=4 << 20, transcendentals=1 << 20
         ),
     )(tab, back, out, mass)
+
+
+def after_kernel(*refs):
+    del refs
+
+
+def after(arrays, value):
+    keep = pl.BlockSpec(memory_space=pl.ANY)
+    return list(
+        pl.pallas_call(
+            after_kernel,
+            out_shape=tuple(jax.ShapeDtypeStruct(a.shape, a.dtype) for a in arrays),
+            in_specs=[keep] * (len(arrays) + 1),
+            out_specs=(keep,) * len(arrays),
+            input_output_aliases={i: i for i in range(len(arrays))},
+        )(*arrays, value)
+    )
 
 
 def rows_norm(values, gain, shift):
@@ -491,18 +508,14 @@
     n_owner = NX * NY * NZ
     roots = root_cache.reshape(-1, LANES)
     roots = jnp.stack([roots, lax.ppermute(roots, "owner", xor_pairs(n_owner, NX * NY))])
-    x_groups = [[(z * NX + x) * NY + y for x in range(NX)] for z in range(NZ) for y in range(NY)]
-    y_groups = [[g * NY + y for y in range(NY)] for g in range(NZ * NX)]
-    roots = lax.all_gather(roots, "owner", axis=0, tiled=False, axis_index_groups=x_groups)
-    tables_made = jnp.minimum(jnp.abs(tab[:1]), 0).astype(BF16)
-    planned = zero_after(roots)
-    roots = roots + tables_made
+    groups = [[z * PEERS + p for p in range(PEERS)] for z in range(NZ)]
+    roots = roots + jnp.minimum(jnp.abs(tab[:1]), 0).astype(BF16)
     for came in half + [near]:
         roots = roots + zero_after(came)
-    roots = lax.all_gather(roots, "owner", axis=0, tiled=False, axis_index_groups=y_groups)
-    other = lax.ppermute(jnp.stack(half) + planned, "blk", swap)
+    roots = lax.all_gather(roots, "owner", axis=0, tiled=False, axis_index_groups=groups)
+    other = lax.ppermute(jnp.stack(half), "blk", swap)
     half = jnp.stack([tok] + half)
-    roots = roots.reshape(NY, NX, NZ, 2, tenants, root_per, LANES)
+    roots = roots.reshape(NX, NY, NZ, 2, tenants, root_per, LANES)
 
     node_rows = node_cache.reshape(-1, LANES) + zero_after(last_come)
     node_far = lax.ppermute(node_rows, "owner", xor_pairs(n_owner, NX * NY))
@@ -525,7 +538,6 @@
         )
         return out.astype(BF16).reshape(reqs, suf, cols)
 
-    groups = [[z * PEERS + p for p in range(PEERS)] for z in range(NZ)]
     incoming = lax.all_to_all(
         outgoing, "owner", split_axis=0, concat_axis=0, axis_index_groups=groups, tiled=True
     )
@@ -555,7 +567,8 @@
     )
     out, mass = root_attention(tab, q, k_new, v_new, roots)
     send = merge(tab, back, out, mass)
-    pack_last = [lax.ppermute(part + zero_after(mass.reshape(-1, LANES)).astype(BF16), "blk", swap) for part in pack_next]
+    pack_next = after(pack_next, mass)
+    pack_last = [lax.ppermute(part, "blk", swap) for part in pack_next]
     parts = [packs, pack_side] + pack_next + pack_last
     attn = lax.all_to_all(
         send.reshape(N_BLK, 2 * own_rows, cols), "blk", split_axis=0, concat_axis=0, tiled=True

time: 245 us -> 230 us (0.939)
  blocking collectives: 9.71 us -> 0 us
  other arithmetic: 16.1 us -> 9.33 us
  waiting for transfers between devices: 57.9 us -> 60.9 us
  matrix products: 8.57 us -> 5.96 us
    all_gather x1, waiting for transfers between devices: 0.02 us -> 18.2 us  [on_device(): lax.all_gather(roots, 'owner', axis=0, tiled=False, axis_index_groups=gro...]
    all_gather x1, waiting for transfers between devices: 0.02 us -> 13.9 us  [on_device(): lax.all_gather(w_out + zero_after(last_come), 'blk', axis=0, tiled=True)]
    all_to_all x1, waiting for transfers between devices: 10.5 us -> 0.01 us  [on_device(): lax.all_to_all(outgoing, 'owner', split_axis=0, concat_axis=0, axis_index...]
    ppermute x3, starting transfers between devices: 19.5 us -> 9.3 us  [the longest x2 6.54 us: on_device(): pack_last = [lax.ppermute(part, 'blk', swap) for part in pack_next]]
    all_gather x1 -> x0, blocking collectives: 9.71 us -> none  [on_device(): lax.all_gather(roots, 'owner', axis=0, tiled=False, axis_index_groups=x_g...]
    ppermute x2, waiting for transfers between devices: 9.62 us -> 0.01 us  [to_neighbour(): return lax.ppermute(sent, ('blk', 'owner'), pairs)]
    all_to_all x1, waiting for transfers between devices: 13.4 us -> 5.59 us  [on_device(): lax.all_to_all(send.reshape(N_BLK, 2 * own_rows, cols), 'blk', split_axis...]
    ppermute x1, starting transfers between devices: 1.91 us -> 8.18 us  [on_device(): node_far = lax.ppermute(node_rows, 'owner', xor_pairs(n_owner, NX * NY))]
  transfers between devices with their start and end apart: 18 -> 18, of which waited for: 8 -> 6; matrix products, arithmetic and copies ran while one was open for 12% -> 9% of each run, Pallas kernels for 11% -> 11%
where the time goes in v7:
time: 230 us; the launch traced here: 228 us
  starting transfers between devices  79.1 us (34%)
  waiting for transfers between devices  60.9 us (26%)
  Pallas kernels  33.2 us (14%)
  local copies, waits for them, and re-layouts  20.7 us (9%)
  between operations  18.8 us (8%)
  other arithmetic  9.33 us (4%)
  matrix products  5.96 us (3%)
    all_gather x1, waiting for transfers between devices, on_device(): lax.all_gather(roots, 'owner', axis=0, tiled=False, axis_index_groups=gro...  18.2 us
    ppermute x3, starting transfers between devices, on_device(): lax.ppermute(tok, 'blk', xor_pairs(N_BLK, 2 * k))  15.5 us
    all_gather x1, waiting for transfers between devices, on_device(): lax.all_gather(w_out + zero_after(last_come), 'blk', axis=0, tiled=True)  13.9 us
    unnamed x70, local copies, waits for them, and re-layouts  13.7 us
    ppermute x1, waiting for transfers between devices, on_device(): lax.ppermute(down_far, 'blk', xor_pairs(N_BLK, N_BLK // 2)).astype(F32)  12.7 us
    all_to_all x1, starting transfers between devices, on_device(): lax.all_to_all(outgoing, 'owner', split_axis=0, concat_axis=0, axis_index...  9.94 us
    ppermute x1, waiting for transfers between devices, on_device(): node_far = lax.ppermute(node_rows, 'owner', xor_pairs(n_owner, NX * NY))  9.65 us
    pallas_call x1, Pallas kernels, root_attention(): pl.pallas_call(root_kernel, out_shape=(shape, shape), in_specs=[pl.BlockS...  8.92 us
  transfers between devices with their start and end apart: 18, of which 6 were waited for; matrix products, arithmetic and copies ran while one was open for 9% of the time, Pallas kernels for 11%

profile of v7, /device:TPU:1, one launch (start us, length us, event | category | flops | bytes accessed | tf_op | source)
XLA Modules:
  0.0 228.0 jit_solution(7952978179230302559)
XLA Ops:
  7.2 8.4 %collective-permute-start.2 = (bf16[128,1024]{1,0:T(8,128)(2,1)}, bf16[128,1024]{1,0:T(8,128)(2,1)S(1)}, u32[]{:S(2)}, u32[]{:S(2)}) collective-permute-start(bf16[128,1024]{1,0:T(8,128)(2,1)} %bitcast.77), channel_id=1, source_target_pairs={{0,384},{64,448},{128,256},{192,320},{256,128},{320,192},{384,0},{... | collective-permute-start | bytes 786440 | tf_op jit(solution)/shard_map/ppermute | solution.py:505
  15.7 2.9 %collective-permute-start.3 = (bf16[128,1024]{1,0:T(8,128)(2,1)}, bf16[128,1024]{1,0:T(8,128)(2,1)S(1)}, u32[]{:S(2)}, u32[]{:S(2)}) collective-permute-start(bf16[128,1024]{1,0:T(8,128)(2,1)} %bitcast.78), channel_id=1, source_target_pairs={{0,64},{64,0},{128,192},{192,128},{256,320},{320,256},{384,448},{4... | collective-permute-start | bytes 786440 | tf_op jit(solution)/shard_map/ppermute | solution.py:504
  18.5 1.9 collective-permute-start.1
  20.5 5.1 %collective-permute-start = (bf16[128,1024]{1,0:T(8,128)(2,1)}, bf16[128,1024]{1,0:T(8,128)(2,1)S(1)}, u32[]{:S(2)}, u32[]{:S(2)}) collective-permute-start(bf16[128,1024]{1,0:T(8,128)(2,1)} %bitcast.80), channel_id=1, source_target_pairs={{0,128},{64,192},{128,0},{192,64},{256,384},{320,448},{384,256},{4... | collective-permute-start | bytes 786440 | tf_op jit(solution)/shard_map/ppermute | solution.py:505
  25.6 5.3 %collective-permute-start.6 = (bf16[128,128]{1,0:T(8,128)(2,1)}, bf16[128,128]{1,0:T(8,128)(2,1)S(1)}, u32[]{:S(2)}, u32[]{:S(2)}) collective-permute-start(bf16[128,128]{1,0:T(8,128)(2,1)} %bitcast.89), channel_id=1, source_target_pairs={{0,32},{1,33},{2,34},{3,35},{4,36},{5,37},{6,38},{7,39},{8,40},{9,... | collective-permute-start | bytes 98312 | tf_op jit(solution)/shard_map/ppermute | solution.py:510
  31.5 3.9 %shard_map.194.tab = s32[288]{0:T(512)} custom-call(s32[4]{0:T(128)} %pad_add_fusion.coords, s32[32]{0:T(128)} %leaf_of.1, s32[128]{0:T(128)} %parent.1, s32[128]{0:T(128)} %place.1, s32[128]{0:T(128)} %length.1, s32[4]{0:T(128)} %root_len.1), custom_call_target="tpu_custom_call" | custom-call | flops 1048576 | bytes 4096 | tf_op jit(solution)/shard_map/pallas_call | solution.py:138
  35.4 1.1 slice.34
  42.0 1.4 fusion.21
  43.6 2.8 %collective-permute-start.4 = (bf16[3,128,1024]{2,1,0:T(8,128)(2,1)S(1)}, bf16[3,128,1024]{2,1,0:T(8,128)(2,1)S(1)}, u32[]{:S(2)}, u32[]{:S(2)}) collective-permute-start(bf16[3,128,1024]{2,1,0:T(8,128)(2,1)S(1)} %pad_maximum_fusion.1), channel_id=1, source_target_pairs={{0,64},{64,0},{128,192},{192,128},{256,320},{320,256},{384,448},{4... | collective-permute-start | bytes 2359304 | tf_op jit(solution)/shard_map/ppermute | solution.py:516
  46.3 1.0 slice_bitcast_fusion.w_ref
  48.2 2.5 %shard_map.195 = (bf16[32,32,128]{2,1,0:T(8,128)(2,1)S(1)}, bf16[128,32,128]{2,1,0:T(8,128)(2,1)}) custom-call(s32[288]{0:T(512)S(1)} %copy-done.19, bf16[4,128,1024]{2,1,0:T(8,128)(2,1)S(1)} %pad_maximum_fusion.half_ref, bf16[128,1024]{1,0:T(8,128)(2,1)S(1)} %collective-permute-done.3.near_ref, bf16[3,128,1024]{2,1,0:T(8,128)(2,1)S(1)} %collective-permute-done.4.other_ref, ...), custom_call_target="tpu_custom_call" | custom-call | flops 268435456 | bytes 4194304 | tf_op jit(solution)/shard_map/pallas_call | solution.py:172
  50.7 9.9 %all-to-all-start = ((bf16[32,4,32,128]{3,2,1,0:T(8,128)(2,1)}), bf16[32,4,32,128]{3,2,1,0:T(8,128)(2,1)}, u32[]{:S(2)}, u32[]{:S(2)}) async-start(bf16[32,4,32,128]{3,2,1,0:T(8,128)(2,1)} %bitcast.10), calls=%async_computation | async-start | bytes 2097152 | tf_op jit(solution)/shard_map/all_to_all | solution.py:541
  61.6 8.2 %collective-permute-start.5 = (bf16[1536,128]{1,0:T(8,128)(2,1)}, bf16[1536,128]{1,0:T(8,128)(2,1)}, u32[]{:S(2)}, u32[]{:S(2)}) collective-permute-start(bf16[1536,128]{1,0:T(8,128)(2,1)} %bitcast.13), channel_id=1, source_target_pairs={{0,32},{1,33},{2,34},{3,35},{4,36},{5,37},{6,38},{7,39},{8,40},{9,... | collective-permute-start | bytes 1179656 | tf_op jit(solution)/shard_map/ppermute | solution.py:521
  69.8 1.2 copy-done.9
  71.1 1.2 copy-done.10
  72.4 2.8 %collective-permute-start.7 = (bf16[2,2064,256]{2,1,0:T(8,128)(2,1)S(1)}, bf16[2,2064,256]{2,1,0:T(8,128)(2,1)}, u32[]{:S(2)}, u32[]{:S(2)}) collective-permute-start(bf16[2,2064,256]{2,1,0:T(8,128)(2,1)S(1)} %shard_map.196.after_ref.w0), channel_id=1, source_target_pairs={{0,64},{64,0},{128,192},{192,128},{256,320},{320,256},{384,448},{4... | collective-permute-start | bytes 6340616 | tf_op jit(solution)/shard_map/ppermute | solution.py:526
  76.1 1.8 fusion.8
  77.9 9.6 %collective-permute-done.5 = bf16[1536,128]{1,0:T(8,128)(2,1)} collective-permute-done((bf16[1536,128]{1,0:T(8,128)(2,1)}, bf16[1536,128]{1,0:T(8,128)(2,1)}, u32[]{:S(2)}, u32[]{:S(2)}) %collective-permute-start.5) | collective-permute-done | bytes 393248 | tf_op jit(solution)/shard_map/ppermute | solution.py:521
  87.5 1.1 pad_maximum_fusion.2.cache_ref
  88.6 8.1 %shard_map.197 = bf16[32,9,16,128]{3,2,1,0:T(8,128)(2,1)S(1)} custom-call(s32[288]{0:T(512)S(1)} %copy-done.19, bf16[32,4,32,128]{3,2,1,0:T(8,128)(2,1)} %all-to-all-done.q_ref, bf16[2,2,2,384,128]{4,3,2,1,0:T(8,128)(2,1)S(1)} %pad_maximum_fusion.2.cache_ref, bf16[2,2064,256]{2,1,0:T(8,128)(2,1)S(1)} %shard_map.196.after_ref.w0), custom_call_target="tpu_custom_call" | custom-call | flops 2147483648 | bytes 4194304 | tf_op jit(solution)/shard_map/pallas_call | solution.py:263
  96.8 1.0 copy-done.6
  97.7 8.8 %all-to-all-start.1 = ((bf16[32,9,16,128]{3,2,1,0:T(8,128)(2,1)}), bf16[32,9,16,128]{3,2,1,0:T(8,128)(2,1)S(1)}, u32[]{:S(2)}, u32[]{:S(2)}) async-start(bf16[32,9,16,128]{3,2,1,0:T(8,128)(2,1)} %copy-done.6), calls=%async_computation.1 | async-start | bytes 2359296 | tf_op jit(solution)/shard_map/all_to_all | solution.py:565
  106.6 1.3 fusion.2
  107.9 1.7 fusion.10
  110.1 1.2 slice.45
  112.0 1.5 add_bitcast_fusion
  113.4 2.0 collective-permute-start.8
  115.5 6.2 %collective-permute-start.9 = (bf16[2064,256]{1,0:T(8,128)(2,1)}, bf16[2064,256]{1,0:T(8,128)(2,1)}, u32[]{:S(2)}, u32[]{:S(2)}) collective-permute-start(bf16[2064,256]{1,0:T(8,128)(2,1)} %get-tuple-element.22), channel_id=1, source_target_pairs={{0,416},{1,417},{2,418},{3,419},{4,420},{5,421},{6,422},{7,423},{8... | collective-permute-start | bytes 3170312 | tf_op jit(solution)/shard_map/ppermute | solution.py:562
  123.2 18.2 %all-gather.3.cloned.1.call-done = bf16[32,2,128,128]{3,2,1,0:T(8,128)(2,1)} async-done(((bf16[1,2,128,128]{3,2,1,0:T(8,128)(2,1)}), bf16[32,2,128,128]{3,2,1,0:T(8,128)(2,1)}) %all-gather.3.cloned.1.call-update) | async-done | bytes 2097168 | tf_op jit(solution)/shard_map/all_gather | solution.py:515
  141.5 0.9 copy-done.7
  143.0 1.6 copy-done.22
  144.6 0.9 copy-done.24
  145.6 8.9 %shard_map.198 = (f32[32,32,128]{2,1,0:T(8,128)S(1)}, f32[32,32,128]{2,1,0:T(8,128)S(1)}) custom-call(s32[288]{0:T(512)S(1)} %copy-done.20, bf16[32,32,128]{2,1,0:T(8,128)(2,1)S(1)} %copy-done.24, bf16[32,32,128]{2,1,0:T(8,128)(2,1)S(1)} %bitcast.69, bf16[32,32,128]{2,1,0:T(8,128)(2,1)S(1)} %bitcast.71, bf16[4,8,2,2,4,16,128]{6,5,4,3,2,1,0:T(8,128)(2,1)S(1)} %bitcast.83), custom_call_target="tpu_custom_call" | custom-call | flops 4294967296 | bytes 4194304 | tf_op jit(solution)/shard_map/pallas_call | solution.py:331
  154.5 0.8 copy-done.3
  156.1 4.6 %collective-permute-start.10 = (bf16[2064,256]{1,0:T(8,128)(2,1)}, bf16[2064,256]{1,0:T(8,128)(2,1)}, u32[]{:S(2)}, u32[]{:S(2)}) collective-permute-start(bf16[2064,256]{1,0:T(8,128)(2,1)} %get-tuple-element.15.w2), channel_id=1, source_target_pairs={{0,64},{64,0},{128,192},{192,128},{256,320},{320,256},{384,448},{4... | collective-permute-start | bytes 3170312 | tf_op jit(solution)/shard_map/ppermute | solution.py:571
  160.8 1.9 collective-permute-start.11
  162.7 1.0 copy-done.4
  163.8 1.0 copy-done.16
  165.4 2.1 shard_map.199
  168.3 6.2 %all-to-all-start.2 = ((bf16[8,256,128]{2,1,0:T(8,128)(2,1)}), bf16[8,256,128]{2,1,0:T(8,128)(2,1)S(1)}, u32[]{:S(2)}, u32[]{:S(2)}) async-start(bf16[8,256,128]{2,1,0:T(8,128)(2,1)} %bitcast.67), calls=%async_computation.2 | async-start | bytes 1048576 | tf_op jit(solution)/shard_map/all_to_all | solution.py:573
  175.5 13.9 %all-gather.5.cloned.1.call-done.w_out_ref = bf16[1024,1024]{1,0:T(8,128)(2,1)} async-done(((bf16[128,1024]{1,0:T(8,128)(2,1)}), bf16[1024,1024]{1,0:T(8,128)(2,1)}) %all-gather.5.cloned.1.call-update) | async-done | bytes 2097168 | tf_op jit(solution)/shard_map/all_gather | solution.py:524
  189.5 5.6 %all-to-all-done.2.attn_ref = bf16[8,256,128]{2,1,0:T(8,128)(2,1)S(1)} async-done(((bf16[8,256,128]{2,1,0:T(8,128)(2,1)}), bf16[8,256,128]{2,1,0:T(8,128)(2,1)S(1)}, u32[]{:S(2)}, u32[]{:S(2)}) %all-to-all-start.2) | async-done | bytes 524320 | tf_op jit(solution)/shard_map/all_to_all | solution.py:573
  195.1 0.9 copy-done.18
  196.0 7.5 %shard_map.201 = (bf16[128,1024]{1,0:T(8,128)(2,1)S(1)}, f32[128,1024]{1,0:T(8,128)S(1)}, bf16[128,1024]{1,0:T(8,128)(2,1)S(1)}) custom-call(bf16[8,256,128]{2,1,0:T(8,128)(2,1)S(1)} %all-to-all-done.2.attn_ref, bf16[1024,1024]{1,0:T(8,128)(2,1)} %all-gather.5.cloned.1.call-done.w_out_ref, bf16[128,1024]{1,0:T(8,128)(2,1)S(1)} %bitcast.82, ...), custom_call_target="tpu_custom_call" | custom-call | flops 3221225472 | bytes 12582912 | tf_op jit(solution)/shard_map/pallas_call | solution.py:444
  203.6 1.9 collective-permute-start.12
  206.3 0.9 broadcast_select_fusion
  207.2 12.7 %collective-permute-done.12 = bf16[128,1024]{1,0:T(8,128)(2,1)S(1)} collective-permute-done((bf16[128,1024]{1,0:T(8,128)(2,1)S(1)}, bf16[128,1024]{1,0:T(8,128)(2,1)S(1)}, u32[]{:S(2)}, u32[]{:S(2)}) %collective-permute-start.12) | collective-permute-done | bytes 262176 | tf_op jit(solution)/shard_map/ppermute | solution.py:578
  220.3 0.9 add_convert_fusion
  (114 shorter events, 12.4 us)
Async XLA Ops:
  7.2 134.3 %all-gather.3.cloned.1.call-start = ((), (), s32[]{:S(2)}) async-start(), calls=%async_computation.3 | async-start | bytes 2162688 | tf_op jit(solution)/shard_map/all_gather | solution.py:515
  7.2 30.0 %collective-permute-start.2 = (bf16[128,1024]{1,0:T(8,128)(2,1)}, bf16[128,1024]{1,0:T(8,128)(2,1)S(1)}, u32[]{:S(2)}, u32[]{:S(2)}) collective-permute-start(bf16[128,1024]{1,0:T(8,128)(2,1)} %bitcast.77), channel_id=1, source_target_pairs={{0,384},{64,448},{128,256},{192,320},{256,128},{320,192},{384,0},{... | collective-permute-start | bytes 786440 | tf_op jit(solution)/shard_map/ppermute | solution.py:505
  15.7 22.7 %collective-permute-start.3 = (bf16[128,1024]{1,0:T(8,128)(2,1)}, bf16[128,1024]{1,0:T(8,128)(2,1)S(1)}, u32[]{:S(2)}, u32[]{:S(2)}) collective-permute-start(bf16[128,1024]{1,0:T(8,128)(2,1)} %bitcast.78), channel_id=1, source_target_pairs={{0,64},{64,0},{128,192},{192,128},{256,320},{320,256},{384,448},{4... | collective-permute-start | bytes 786440 | tf_op jit(solution)/shard_map/ppermute | solution.py:504
  18.5 21.0 %collective-permute-start.1 = (bf16[128,1024]{1,0:T(8,128)(2,1)}, bf16[128,1024]{1,0:T(8,128)(2,1)S(1)}, u32[]{:S(2)}, u32[]{:S(2)}) collective-permute-start(bf16[128,1024]{1,0:T(8,128)(2,1)} %bitcast.79), channel_id=1, source_target_pairs={{0,256},{64,320},{128,384},{192,448},{256,0},{320,64},{384,128},{4... | collective-permute-start | bytes 786440 | tf_op jit(solution)/shard_map/ppermute | solution.py:505
  20.5 20.4 %collective-permute-start = (bf16[128,1024]{1,0:T(8,128)(2,1)}, bf16[128,1024]{1,0:T(8,128)(2,1)S(1)}, u32[]{:S(2)}, u32[]{:S(2)}) collective-permute-start(bf16[128,1024]{1,0:T(8,128)(2,1)} %bitcast.80), channel_id=1, source_target_pairs={{0,128},{64,192},{128,0},{192,64},{256,384},{320,448},{384,256},{4... | collective-permute-start | bytes 786440 | tf_op jit(solution)/shard_map/ppermute | solution.py:505
  25.6 16.4 %collective-permute-start.6 = (bf16[128,128]{1,0:T(8,128)(2,1)}, bf16[128,128]{1,0:T(8,128)(2,1)S(1)}, u32[]{:S(2)}, u32[]{:S(2)}) collective-permute-start(bf16[128,128]{1,0:T(8,128)(2,1)} %bitcast.89), channel_id=1, source_target_pairs={{0,32},{1,33},{2,34},{3,35},{4,36},{5,37},{6,38},{7,39},{8,40},{9,... | collective-permute-start | bytes 98312 | tf_op jit(solution)/shard_map/ppermute | solution.py:510
  39.6 7.7 %copy-start.11 = (bf16[128,1024]{1,0:T(8,128)(2,1)}, bf16[128,1024]{1,0:T(8,128)(2,1)S(1)}, u32[]{:S(2)}) copy-start(bf16[128,1024]{1,0:T(8,128)(2,1)S(1)} %collective-permute-done.1.tok_b) | copy-start | bytes 786436
  43.4 3.9 %copy-start.17 = (bf16[4,32,1024]{2,1,0:T(8,128)(2,1)S(1)}, bf16[4,32,1024]{2,1,0:T(8,128)(2,1)}, u32[]{:S(2)}) copy-start(bf16[4,32,1024]{2,1,0:T(8,128)(2,1)} %param.19) | copy-start | bytes 786436
  43.6 4.7 %collective-permute-start.4 = (bf16[3,128,1024]{2,1,0:T(8,128)(2,1)S(1)}, bf16[3,128,1024]{2,1,0:T(8,128)(2,1)S(1)}, u32[]{:S(2)}, u32[]{:S(2)}) collective-permute-start(bf16[3,128,1024]{2,1,0:T(8,128)(2,1)S(1)} %pad_maximum_fusion.1), channel_id=1, source_target_pairs={{0,64},{64,0},{128,192},{192,128},{256,320},{320,256},{384,448},{4... | collective-permute-start | bytes 2359304 | tf_op jit(solution)/shard_map/ppermute | solution.py:516
  47.3 0.9 copy-start.19
  47.5 3.2 %copy-start.1 = (bf16[4,128,1024]{2,1,0:T(8,128)(2,1)}, bf16[4,128,1024]{2,1,0:T(8,128)(2,1)S(1)}, u32[]{:S(2)}) copy-start(bf16[4,128,1024]{2,1,0:T(8,128)(2,1)S(1)} %pad_maximum_fusion.half_ref) | copy-start | bytes 3145732
  48.2 2.5 %copy-start.13 = (bf16[3,128,1024]{2,1,0:T(8,128)(2,1)}, bf16[3,128,1024]{2,1,0:T(8,128)(2,1)S(1)}, u32[]{:S(2)}) copy-start(bf16[3,128,1024]{2,1,0:T(8,128)(2,1)S(1)} %collective-permute-done.4.other_ref) | copy-start | bytes 2359300
  50.7 10.0 %copy-start.23 = (bf16[32,32,128]{2,1,0:T(8,128)(2,1)}, bf16[32,32,128]{2,1,0:T(8,128)(2,1)S(1)}, u32[]{:S(2)}) copy-start(bf16[32,32,128]{2,1,0:T(8,128)(2,1)S(1)} %get-tuple-element.12.q_ref) | copy-start | bytes 786436
  50.7 10.1 %copy-start.34 = (bf16[512]{0:T(512)(128)(2,1)S(1)}, bf16[512]{0:T(512)(128)(2,1)}, u32[]{:S(2)}) copy-start(bf16[512]{0:T(512)(128)(2,1)} %param.26) | copy-start | bytes 3076
  50.7 10.1 %copy-start.25 = (bf16[2,2,384,128]{3,2,1,0:T(8,128)(2,1)S(1)}, bf16[2,2,384,128]{3,2,1,0:T(8,128)(2,1)}, u32[]{:S(2)}) copy-start(bf16[2,2,384,128]{3,2,1,0:T(8,128)(2,1)} %param.32) | copy-start | bytes 1179652
  50.7 37.9 %all-to-all-start = ((bf16[32,4,32,128]{3,2,1,0:T(8,128)(2,1)}), bf16[32,4,32,128]{3,2,1,0:T(8,128)(2,1)}, u32[]{:S(2)}, u32[]{:S(2)}) async-start(bf16[32,4,32,128]{3,2,1,0:T(8,128)(2,1)} %bitcast.10), calls=%async_computation | async-start | bytes 2097152 | tf_op jit(solution)/shard_map/all_to_all | solution.py:541
  60.7 128.8 %all-gather.5.cloned.1.call-start = ((), (), s32[]{:S(2)}) async-start(), calls=%async_computation.4 | async-start | bytes 2359296 | tf_op jit(solution)/shard_map/all_gather | solution.py:524
  61.6 25.9 %collective-permute-start.5 = (bf16[1536,128]{1,0:T(8,128)(2,1)}, bf16[1536,128]{1,0:T(8,128)(2,1)}, u32[]{:S(2)}, u32[]{:S(2)}) collective-permute-start(bf16[1536,128]{1,0:T(8,128)(2,1)} %bitcast.13), channel_id=1, source_target_pairs={{0,32},{1,33},{2,34},{3,35},{4,36},{5,37},{6,38},{7,39},{8,40},{9,... | collective-permute-start | bytes 1179656 | tf_op jit(solution)/shard_map/ppermute | solution.py:521
  69.8 1.2 copy-start.9
  71.1 1.2 copy-start.10
  72.3 3.0 %copy-start.27 = (bf16[128,1024]{1,0:T(8,128)(2,1)S(1)}, bf16[128,1024]{1,0:T(8,128)(2,1)}, u32[]{:S(2)}) copy-start(bf16[128,1024]{1,0:T(8,128)(2,1)} %param.21) | copy-start | bytes 786436
  72.4 39.5 %copy-start = (bf16[2,2064,256]{2,1,0:T(8,128)(2,1)}, bf16[2,2064,256]{2,1,0:T(8,128)(2,1)S(1)}, u32[]{:S(2)}) copy-start(bf16[2,2064,256]{2,1,0:T(8,128)(2,1)S(1)} %shard_map.196.after_ref.w0) | copy-start | bytes 6340612
  72.4 103.1 %collective-permute-start.7 = (bf16[2,2064,256]{2,1,0:T(8,128)(2,1)S(1)}, bf16[2,2064,256]{2,1,0:T(8,128)(2,1)}, u32[]{:S(2)}, u32[]{:S(2)}) collective-permute-start(bf16[2,2064,256]{2,1,0:T(8,128)(2,1)S(1)} %shard_map.196.after_ref.w0), channel_id=1, source_target_pairs={{0,64},{64,0},{128,192},{192,128},{256,320},{320,256},{384,448},{4... | collective-permute-start | bytes 6340616 | tf_op jit(solution)/shard_map/ppermute | solution.py:526
  96.7 1.0 copy-start.6
  97.7 65.0 %all-to-all-start.1 = ((bf16[32,9,16,128]{3,2,1,0:T(8,128)(2,1)}), bf16[32,9,16,128]{3,2,1,0:T(8,128)(2,1)S(1)}, u32[]{:S(2)}, u32[]{:S(2)}) async-start(bf16[32,9,16,128]{3,2,1,0:T(8,128)(2,1)} %copy-done.6), calls=%async_computation.1 | async-start | bytes 2359296 | tf_op jit(solution)/shard_map/all_to_all | solution.py:565
  106.6 3.0 %copy-start.2 = (bf16[4,128,1024]{2,1,0:T(8,128)(2,1)S(1)}, bf16[4,128,1024]{2,1,0:T(8,128)(2,1)}, u32[]{:S(2)}) copy-start(bf16[4,128,1024]{2,1,0:T(8,128)(2,1)} %copy-done.1) | copy-start | bytes 3145732
  106.6 3.0 %copy-start.26 = (bf16[1024,3,128]{2,0,1:T(8,128)(2,1)S(1)}, bf16[1024,3,128]{2,0,1:T(8,128)(2,1)}, u32[]{:S(2)}) copy-start(bf16[1024,3,128]{2,0,1:T(8,128)(2,1)} %param.20) | copy-start | bytes 2359300
  111.9 9.7 %copy-start.14 = (bf16[3,128,1024]{2,1,0:T(8,128)(2,1)S(1)}, bf16[3,128,1024]{2,1,0:T(8,128)(2,1)}, u32[]{:S(2)}) copy-start(bf16[3,128,1024]{2,1,0:T(8,128)(2,1)} %copy-done.13) | copy-start | bytes 2359300
  113.4 8.7 %copy-start.28 = (bf16[128,128]{1,0:T(8,128)(2,1)S(1)}, bf16[128,128]{1,0:T(8,128)(2,1)}, u32[]{:S(2)}) copy-start(bf16[128,128]{1,0:T(8,128)(2,1)} %fusion.8) | copy-start | bytes 98308
  113.4 42.7 %collective-permute-start.8 = (bf16[2064,256]{1,0:T(8,128)(2,1)}, bf16[2064,256]{1,0:T(8,128)(2,1)}, u32[]{:S(2)}, u32[]{:S(2)}) collective-permute-start(bf16[2064,256]{1,0:T(8,128)(2,1)} %get-tuple-element.23), channel_id=1, source_target_pairs={{0,128},{1,129},{2,130},{3,131},{4,132},{5,133},{6,134},{7,135},{8... | collective-permute-start | bytes 3170312 | tf_op jit(solution)/shard_map/ppermute | solution.py:562
  115.5 40.7 %collective-permute-start.9 = (bf16[2064,256]{1,0:T(8,128)(2,1)}, bf16[2064,256]{1,0:T(8,128)(2,1)}, u32[]{:S(2)}, u32[]{:S(2)}) collective-permute-start(bf16[2064,256]{1,0:T(8,128)(2,1)} %get-tuple-element.22), channel_id=1, source_target_pairs={{0,416},{1,417},{2,418},{3,419},{4,420},{5,421},{6,422},{7,423},{8... | collective-permute-start | bytes 3170312 | tf_op jit(solution)/shard_map/ppermute | solution.py:562
  141.5 0.9 copy-start.7
  143.0 1.6 copy-start.22
  144.6 0.9 copy-start.24
  156.1 33.3 %collective-permute-start.10 = (bf16[2064,256]{1,0:T(8,128)(2,1)}, bf16[2064,256]{1,0:T(8,128)(2,1)}, u32[]{:S(2)}, u32[]{:S(2)}) collective-permute-start(bf16[2064,256]{1,0:T(8,128)(2,1)} %get-tuple-element.15.w2), channel_id=1, source_target_pairs={{0,64},{64,0},{128,192},{192,128},{256,320},{320,256},{384,448},{4... | collective-permute-start | bytes 3170312 | tf_op jit(solution)/shard_map/ppermute | solution.py:571
  160.8 28.7 %collective-permute-start.11 = (bf16[2064,256]{1,0:T(8,128)(2,1)}, bf16[2064,256]{1,0:T(8,128)(2,1)}, u32[]{:S(2)}, u32[]{:S(2)}) collective-permute-start(bf16[2064,256]{1,0:T(8,128)(2,1)} %get-tuple-element.16.w3), channel_id=1, source_target_pairs={{0,64},{64,0},{128,192},{192,128},{256,320},{320,256},{384,448},{4... | collective-permute-start | bytes 3170312 | tf_op jit(solution)/shard_map/ppermute | solution.py:571
  162.7 1.0 copy-start.4
  163.8 1.0 copy-start.16
  168.3 6.9 %copy-start.29 = (bf16[1024]{0:T(1024)(128)(2,1)S(1)}, bf16[1024]{0:T(1024)(128)(2,1)}, u32[]{:S(2)}) copy-start(bf16[1024]{0:T(1024)(128)(2,1)} %param.23) | copy-start | bytes 6148
  168.3 6.9 %copy-start.30 = (bf16[1024]{0:T(1024)(128)(2,1)S(1)}, bf16[1024]{0:T(1024)(128)(2,1)}, u32[]{:S(2)}) copy-start(bf16[1024]{0:T(1024)(128)(2,1)} %param.24) | copy-start | bytes 6148
  168.3 6.9 %copy-start.31 = (bf16[1024]{0:T(1024)(128)(2,1)S(1)}, bf16[1024]{0:T(1024)(128)(2,1)}, u32[]{:S(2)}) copy-start(bf16[1024]{0:T(1024)(128)(2,1)} %param.28) | copy-start | bytes 6148
  168.3 6.9 %copy-start.32 = (bf16[1024]{0:T(1024)(128)(2,1)S(1)}, bf16[1024]{0:T(1024)(128)(2,1)}, u32[]{:S(2)}) copy-start(bf16[1024]{0:T(1024)(128)(2,1)} %param.29) | copy-start | bytes 6148
  168.3 7.0 %copy-start.33 = (bf16[1024]{0:T(1024)(128)(2,1)S(1)}, bf16[1024]{0:T(1024)(128)(2,1)}, u32[]{:S(2)}) copy-start(bf16[1024]{0:T(1024)(128)(2,1)} %param.30) | copy-start | bytes 6148
  168.3 26.8 %copy-start.12 = (bf16[128,1024]{1,0:T(8,128)(2,1)S(1)}, bf16[128,1024]{1,0:T(8,128)(2,1)}, u32[]{:S(2)}) copy-start(bf16[128,1024]{1,0:T(8,128)(2,1)} %copy-done.11) | copy-start | bytes 786436
  168.3 26.8 %all-to-all-start.2 = ((bf16[8,256,128]{2,1,0:T(8,128)(2,1)}), bf16[8,256,128]{2,1,0:T(8,128)(2,1)S(1)}, u32[]{:S(2)}, u32[]{:S(2)}) async-start(bf16[8,256,128]{2,1,0:T(8,128)(2,1)} %bitcast.67), calls=%async_computation.2 | async-start | bytes 1048576 | tf_op jit(solution)/shard_map/all_to_all | solution.py:573
  175.5 30.0 %copy-start.8 = (bf16[1024,128]{1,0:T(8,128)(2,1)S(1)}, bf16[1024,128]{1,0:T(8,128)(2,1)}, u32[]{:S(2)}) copy-start(bf16[1024,128]{1,0:T(8,128)(2,1)} %maximum_convert_fusion.1) | copy-start | bytes 786436
  195.1 1.0 copy-start.18
  203.6 16.3 %collective-permute-start.12 = (bf16[128,1024]{1,0:T(8,128)(2,1)S(1)}, bf16[128,1024]{1,0:T(8,128)(2,1)S(1)}, u32[]{:S(2)}, u32[]{:S(2)}) collective-permute-start(bf16[128,1024]{1,0:T(8,128)(2,1)S(1)} %get-tuple-element.19), channel_id=1, source_target_pairs={{0,256},{64,320},{128,384},{192,448},{256,0},{320,64},{384,128},{4... | collective-permute-start | bytes 786440 | tf_op jit(solution)/shard_map/ppermute | solution.py:578
  (5 other events, 3.7 us)
Sparse Core Ops, SparseCore 0:
  43.6 97.8 all-gather.2
  143.5 45.9 all-gather.4

commit v8 on v7

--- a/solution.py
+++ b/solution.py
@@ -294,8 +294,8 @@
         n = lax.broadcasted_iota(I32, (1, root_rows), 1)
         row = n % per
         z = ((n // per) % NZ) ^ tab[PLACE]
-        y = (n // (per * NZ)) % NY
-        x = n // (per * NZ * NY)
+        x = ((n // (per * NZ)) % NX) ^ tab[PLACE + 1]
+        y = n // (per * NZ * NX)
         place = ((z * NX + x) * NY + y) * per + row
         scores = jnp.where(place < tab[ROOT_LEN + tenant], dot_nt(q, keys), NEG)
         own_row = (lax.broadcasted_iota(I32, (2 * rows, rows), 0) % rows) // suf
@@ -508,14 +508,18 @@
     n_owner = NX * NY * NZ
     roots = root_cache.reshape(-1, LANES)
     roots = jnp.stack([roots, lax.ppermute(roots, "owner", xor_pairs(n_owner, NX * NY))])
-    groups = [[z * PEERS + p for p in range(PEERS)] for z in range(NZ)]
+    roots = jnp.stack(
+        [roots] + [lax.ppermute(roots, "owner", xor_pairs(n_owner, k * NY)) for k in range(1, NX)]
+    )
     roots = roots + jnp.minimum(jnp.abs(tab[:1]), 0).astype(BF16)
     for came in half + [near]:
         roots = roots + zero_after(came)
-    roots = lax.all_gather(roots, "owner", axis=0, tiled=False, axis_index_groups=groups)
+    y_groups = [[g * NY + y for y in range(NY)] for g in range(NZ * NX)]
+    roots = lax.all_gather(roots, "owner", axis=0, tiled=False, axis_index_groups=y_groups)
+    groups = [[z * PEERS + p for p in range(PEERS)] for z in range(NZ)]
     other = lax.ppermute(jnp.stack(half), "blk", swap)
     half = jnp.stack([tok] + half)
-    roots = roots.reshape(NX, NY, NZ, 2, tenants, root_per, LANES)
+    roots = roots.reshape(NY, NX, NZ, 2, tenants, root_per, LANES)
 
     node_rows = node_cache.reshape(-1, LANES) + zero_after(last_come)
     node_far = lax.ppermute(node_rows, "owner", xor_pairs(n_owner, NX * NY))

time: 230 us -> 246 us (1.070)
  waiting for transfers between devices: 60.9 us -> 78.7 us
    ppermute x2, waiting for transfers between devices: 0.01 us -> 18.4 us  [to_neighbour(): return lax.ppermute(sent, ('blk', 'owner'), pairs)]
    all_gather x1, waiting for transfers between devices: 18.2 us -> 0.01 us  [on_device(): lax.all_gather(roots, 'owner', axis=0, tiled=False, axis_index_groups=y_g...]
    all_gather x1, waiting for transfers between devices: 13.9 us -> 0.02 us  [on_device(): lax.all_gather(w_out + zero_after(last_come), 'blk', axis=0, tiled=True)]
    ppermute x0 -> x3, starting transfers between devices: none -> 9.58 us  [on_device(): lax.ppermute(roots, 'owner', xor_pairs(n_owner, k * NY))]
    all_to_all x1, waiting for transfers between devices: 0.01 us -> 9.34 us  [on_device(): lax.all_to_all(outgoing, 'owner', split_axis=0, concat_axis=0, axis_index...]
    ppermute x1, waiting for transfers between devices: 0.01 us -> 9 us  [on_device(): lax.ppermute(roots, 'owner', xor_pairs(n_owner, NX * NY))]
    all_to_all x1, waiting for transfers between devices: 5.59 us -> 13.4 us  [on_device(): lax.all_to_all(send.reshape(N_BLK, 2 * own_rows, cols), 'blk', split_axis...]
    ppermute x1, starting transfers between devices: 8.18 us -> 1.91 us  [on_device(): node_far = lax.ppermute(node_rows, 'owner', xor_pairs(n_owner, NX * NY))]
  transfers between devices with their start and end apart: 18 -> 21, of which waited for: 6 -> 8; matrix products, arithmetic and copies ran while one was open for 9% -> 8% of each run, Pallas kernels for 11% -> 11%
where the time goes in v8:
time: 246 us; the launch traced here: 244 us
  waiting for transfers between devices  78.7 us (32%)
  starting transfers between devices  77.4 us (31%)
  Pallas kernels  33.2 us (13%)
  local copies, waits for them, and re-layouts  20.6 us (8%)
  between operations  18.8 us (8%)
  other arithmetic  9.54 us (4%)
  matrix products  5.95 us (2%)
    ppermute x2, waiting for transfers between devices, to_neighbour(): return lax.ppermute(sent, ('blk', 'owner'), pairs)  18.4 us
    ppermute x1, waiting for transfers between devices, on_device(): node_far = lax.ppermute(node_rows, 'owner', xor_pairs(n_owner, NX * NY))  15.7 us
    ppermute x3, starting transfers between devices, on_device(): lax.ppermute(tok, 'blk', xor_pairs(N_BLK, 2 * k))  15.5 us
    unnamed x70, local copies, waits for them, and re-layouts  13.7 us
    all_to_all x1, waiting for transfers between devices, on_device(): lax.all_to_all(send.reshape(N_BLK, 2 * own_rows, cols), 'blk', split_axis...  13.4 us
    ppermute x1, waiting for transfers between devices, on_device(): lax.ppermute(down_far, 'blk', xor_pairs(N_BLK, N_BLK // 2)).astype(F32)  12.1 us
    all_to_all x1, starting transfers between devices, on_device(): lax.all_to_all(outgoing, 'owner', split_axis=0, concat_axis=0, axis_index...  9.68 us
    ppermute x3, starting transfers between devices, on_device(): lax.ppermute(roots, 'owner', xor_pairs(n_owner, k * NY))  9.58 us
  transfers between devices with their start and end apart: 21, of which 8 were waited for; matrix products, arithmetic and copies ran while one was open for 8% of the time, Pallas kernels for 11%

profile of v8, /device:TPU:1, one launch (start us, length us, event | category | flops | bytes accessed | tf_op | source)
XLA Modules:
  0.0 244.3 jit_solution(13399807684139535484)
XLA Ops:
  7.2 8.4 %collective-permute-start.2 = (bf16[128,1024]{1,0:T(8,128)(2,1)}, bf16[128,1024]{1,0:T(8,128)(2,1)S(1)}, u32[]{:S(2)}, u32[]{:S(2)}) collective-permute-start(bf16[128,1024]{1,0:T(8,128)(2,1)} %bitcast.82), channel_id=1, source_target_pairs={{0,384},{64,448},{128,256},{192,320},{256,128},{320,192},{384,0},{... | collective-permute-start | bytes 786440 | tf_op jit(solution)/shard_map/ppermute | solution.py:505
  15.7 2.9 %collective-permute-start.3 = (bf16[128,1024]{1,0:T(8,128)(2,1)}, bf16[128,1024]{1,0:T(8,128)(2,1)S(1)}, u32[]{:S(2)}, u32[]{:S(2)}) collective-permute-start(bf16[128,1024]{1,0:T(8,128)(2,1)} %bitcast.83), channel_id=1, source_target_pairs={{0,64},{64,0},{128,192},{192,128},{256,320},{320,256},{384,448},{4... | collective-permute-start | bytes 786440 | tf_op jit(solution)/shard_map/ppermute | solution.py:504
  18.5 1.9 collective-permute-start.1
  20.5 5.1 %collective-permute-start = (bf16[128,1024]{1,0:T(8,128)(2,1)}, bf16[128,1024]{1,0:T(8,128)(2,1)S(1)}, u32[]{:S(2)}, u32[]{:S(2)}) collective-permute-start(bf16[128,1024]{1,0:T(8,128)(2,1)} %bitcast.85), channel_id=1, source_target_pairs={{0,128},{64,192},{128,0},{192,64},{256,384},{320,448},{384,256},{4... | collective-permute-start | bytes 786440 | tf_op jit(solution)/shard_map/ppermute | solution.py:505
  25.6 5.3 %collective-permute-start.6 = (bf16[128,128]{1,0:T(8,128)(2,1)}, bf16[128,128]{1,0:T(8,128)(2,1)S(1)}, u32[]{:S(2)}, u32[]{:S(2)}) collective-permute-start(bf16[128,128]{1,0:T(8,128)(2,1)} %bitcast.97), channel_id=1, source_target_pairs={{0,32},{1,33},{2,34},{3,35},{4,36},{5,37},{6,38},{7,39},{8,40},{9,... | collective-permute-start | bytes 98312 | tf_op jit(solution)/shard_map/ppermute | solution.py:510
  30.9 9.0 %collective-permute-done.6 = bf16[128,128]{1,0:T(8,128)(2,1)S(1)} collective-permute-done((bf16[128,128]{1,0:T(8,128)(2,1)}, bf16[128,128]{1,0:T(8,128)(2,1)S(1)}, u32[]{:S(2)}, u32[]{:S(2)}) %collective-permute-start.6) | collective-permute-done | bytes 32800 | tf_op jit(solution)/shard_map/ppermute | solution.py:510
  40.7 3.1 %collective-permute-start.7 = (bf16[2,128,128]{2,1,0:T(8,128)(2,1)S(1)}, bf16[2,128,128]{2,1,0:T(8,128)(2,1)S(1)}, u32[]{:S(2)}, u32[]{:S(2)}) collective-permute-start(bf16[2,128,128]{2,1,0:T(8,128)(2,1)S(1)} %get-tuple-element.25), channel_id=1, source_target_pairs={{0,8},{1,9},{2,10},{3,11},{4,12},{5,13},{6,14},{7,15},{8,0},{9,1},... | collective-permute-start | bytes 196616 | tf_op jit(solution)/shard_map/ppermute | solution.py:512
  43.8 4.4 %collective-permute-start.8 = (bf16[2,128,128]{2,1,0:T(8,128)(2,1)S(1)}, bf16[2,128,128]{2,1,0:T(8,128)(2,1)S(1)}, u32[]{:S(2)}, u32[]{:S(2)}) collective-permute-start(bf16[2,128,128]{2,1,0:T(8,128)(2,1)S(1)} %get-tuple-element.25), channel_id=1, source_target_pairs={{0,16},{1,17},{2,18},{3,19},{4,20},{5,21},{6,22},{7,23},{8,24},{9,... | collective-permute-start | bytes 196616 | tf_op jit(solution)/shard_map/ppermute | solution.py:512
  48.2 2.1 collective-permute-start.9
  50.9 3.9 %shard_map.194.tab = s32[288]{0:T(512)} custom-call(s32[4]{0:T(128)} %pad_add_fusion.coords, s32[32]{0:T(128)} %leaf_of.1, s32[128]{0:T(128)} %parent.1, s32[128]{0:T(128)} %place.1, s32[128]{0:T(128)} %length.1, s32[4]{0:T(128)} %root_len.1), custom_call_target="tpu_custom_call" | custom-call | flops 1048576 | bytes 4096 | tf_op jit(solution)/shard_map/pallas_call | solution.py:138
  54.8 1.1 slice.34
  62.3 4.7 %collective-permute-start.4 = (bf16[3,128,1024]{2,1,0:T(8,128)(2,1)S(1)}, bf16[3,128,1024]{2,1,0:T(8,128)(2,1)S(1)}, u32[]{:S(2)}, u32[]{:S(2)}) collective-permute-start(bf16[3,128,1024]{2,1,0:T(8,128)(2,1)S(1)} %pad_maximum_fusion.1), channel_id=1, source_target_pairs={{0,64},{64,0},{128,192},{192,128},{256,320},{320,256},{384,448},{4... | collective-permute-start | bytes 2359304 | tf_op jit(solution)/shard_map/ppermute | solution.py:520
  67.0 1.0 slice_bitcast_fusion.w_ref
  68.9 2.5 %shard_map.195 = (bf16[32,32,128]{2,1,0:T(8,128)(2,1)S(1)}, bf16[128,32,128]{2,1,0:T(8,128)(2,1)}) custom-call(s32[288]{0:T(512)S(1)} %copy-done.19, bf16[4,128,1024]{2,1,0:T(8,128)(2,1)S(1)} %pad_maximum_fusion.half_ref, bf16[128,1024]{1,0:T(8,128)(2,1)S(1)} %collective-permute-done.3.near_ref, bf16[3,128,1024]{2,1,0:T(8,128)(2,1)S(1)} %collective-permute-done.4.other_ref, ...), custom_call_target="tpu_custom_call" | custom-call | flops 268435456 | bytes 4194304 | tf_op jit(solution)/shard_map/pallas_call | solution.py:172
  71.4 9.7 %all-to-all-start = ((bf16[32,4,32,128]{3,2,1,0:T(8,128)(2,1)}), bf16[32,4,32,128]{3,2,1,0:T(8,128)(2,1)}, u32[]{:S(2)}, u32[]{:S(2)}) async-start(bf16[32,4,32,128]{3,2,1,0:T(8,128)(2,1)} %bitcast.10), calls=%async_computation | async-start | bytes 2097152 | tf_op jit(solution)/shard_map/all_to_all | solution.py:545
  82.0 1.9 collective-permute-start.5
  84.0 1.2 copy-done.9
  85.2 1.2 copy-done.10
  86.6 2.6 %collective-permute-start.10 = (bf16[2,2064,256]{2,1,0:T(8,128)(2,1)S(1)}, bf16[2,2064,256]{2,1,0:T(8,128)(2,1)}, u32[]{:S(2)}, u32[]{:S(2)}) collective-permute-start(bf16[2,2064,256]{2,1,0:T(8,128)(2,1)S(1)} %shard_map.196.after_ref.w0), channel_id=1, source_target_pairs={{0,64},{64,0},{128,192},{192,128},{256,320},{320,256},{384,448},{4... | collective-permute-start | bytes 6340616 | tf_op jit(solution)/shard_map/ppermute | solution.py:530
  89.9 1.8 fusion.12
  91.7 15.7 %collective-permute-done.5 = bf16[1536,128]{1,0:T(8,128)(2,1)} collective-permute-done((bf16[1536,128]{1,0:T(8,128)(2,1)}, bf16[1536,128]{1,0:T(8,128)(2,1)}, u32[]{:S(2)}, u32[]{:S(2)}) %collective-permute-start.5) | collective-permute-done | bytes 393248 | tf_op jit(solution)/shard_map/ppermute | solution.py:525
  107.5 1.1 pad_maximum_fusion.2.cache_ref
  108.5 9.3 %all-to-all-done.q_ref = bf16[32,4,32,128]{3,2,1,0:T(8,128)(2,1)} async-done(((bf16[32,4,32,128]{3,2,1,0:T(8,128)(2,1)}), bf16[32,4,32,128]{3,2,1,0:T(8,128)(2,1)}, u32[]{:S(2)}, u32[]{:S(2)}) %all-to-all-start) | async-done | bytes 1048608 | tf_op jit(solution)/shard_map/all_to_all | solution.py:545
  117.9 8.1 %shard_map.197 = bf16[32,9,16,128]{3,2,1,0:T(8,128)(2,1)S(1)} custom-call(s32[288]{0:T(512)S(1)} %copy-done.19, bf16[32,4,32,128]{3,2,1,0:T(8,128)(2,1)} %all-to-all-done.q_ref, bf16[2,2,2,384,128]{4,3,2,1,0:T(8,128)(2,1)S(1)} %pad_maximum_fusion.2.cache_ref, bf16[2,2064,256]{2,1,0:T(8,128)(2,1)S(1)} %shard_map.196.after_ref.w0), custom_call_target="tpu_custom_call" | custom-call | flops 2147483648 | bytes 4194304 | tf_op jit(solution)/shard_map/pallas_call | solution.py:263
  126.0 1.0 copy-done.6
  127.0 7.5 %all-to-all-start.1 = ((bf16[32,9,16,128]{3,2,1,0:T(8,128)(2,1)}), bf16[32,9,16,128]{3,2,1,0:T(8,128)(2,1)S(1)}, u32[]{:S(2)}, u32[]{:S(2)}) async-start(bf16[32,9,16,128]{3,2,1,0:T(8,128)(2,1)} %copy-done.6), calls=%async_computation.1 | async-start | bytes 2359296 | tf_op jit(solution)/shard_map/all_to_all | solution.py:569
  134.5 1.3 fusion.6
  135.8 1.7 fusion.14
  138.0 1.2 slice.45
  139.9 1.5 add_bitcast_fusion
  141.3 2.0 collective-permute-start.11
  143.4 4.6 %collective-permute-start.12 = (bf16[2064,256]{1,0:T(8,128)(2,1)}, bf16[2064,256]{1,0:T(8,128)(2,1)}, u32[]{:S(2)}, u32[]{:S(2)}) collective-permute-start(bf16[2064,256]{1,0:T(8,128)(2,1)} %get-tuple-element.22), channel_id=1, source_target_pairs={{0,416},{1,417},{2,418},{3,419},{4,420},{5,421},{6,422},{7,423},{8... | collective-permute-start | bytes 3170312 | tf_op jit(solution)/shard_map/ppermute | solution.py:566
  149.5 0.9 copy-done.7
  151.1 1.6 copy-done.22
  152.7 0.9 copy-done.24
  153.6 8.9 %shard_map.198 = (f32[32,32,128]{2,1,0:T(8,128)S(1)}, f32[32,32,128]{2,1,0:T(8,128)S(1)}) custom-call(s32[288]{0:T(512)S(1)} %copy-done.20, bf16[32,32,128]{2,1,0:T(8,128)(2,1)S(1)} %copy-done.24, bf16[32,32,128]{2,1,0:T(8,128)(2,1)S(1)} %bitcast.74, bf16[32,32,128]{2,1,0:T(8,128)(2,1)S(1)} %bitcast.76, bf16[8,4,2,2,4,16,128]{6,5,4,3,2,1,0:T(8,128)(2,1)S(1)} %bitcast.88), custom_call_target="tpu_custom_call" | custom-call | flops 4294967296 | bytes 4194304 | tf_op jit(solution)/shard_map/pallas_call | solution.py:331
  164.2 17.6 %collective-permute-done.11.refs_0_ = bf16[2064,256]{1,0:T(8,128)(2,1)} collective-permute-done((bf16[2064,256]{1,0:T(8,128)(2,1)}, bf16[2064,256]{1,0:T(8,128)(2,1)}, u32[]{:S(2)}, u32[]{:S(2)}) %collective-permute-start.11) | collective-permute-done | bytes 1056800 | tf_op jit(solution)/shard_map/ppermute | solution.py:566
  182.6 3.3 %collective-permute-start.13 = (bf16[2064,256]{1,0:T(8,128)(2,1)}, bf16[2064,256]{1,0:T(8,128)(2,1)}, u32[]{:S(2)}, u32[]{:S(2)}) collective-permute-start(bf16[2064,256]{1,0:T(8,128)(2,1)} %get-tuple-element.15.w2), channel_id=1, source_target_pairs={{0,64},{64,0},{128,192},{192,128},{256,320},{320,256},{384,448},{4... | collective-permute-start | bytes 3170312 | tf_op jit(solution)/shard_map/ppermute | solution.py:575
  185.9 1.9 collective-permute-start.14
  187.8 1.0 copy-done.4
  188.9 1.0 copy-done.16
  190.5 2.1 shard_map.199
  193.4 4.1 %all-to-all-start.2 = ((bf16[8,256,128]{2,1,0:T(8,128)(2,1)}), bf16[8,256,128]{2,1,0:T(8,128)(2,1)S(1)}, u32[]{:S(2)}, u32[]{:S(2)}) async-start(bf16[8,256,128]{2,1,0:T(8,128)(2,1)} %bitcast.72), calls=%async_computation.2 | async-start | bytes 1048576 | tf_op jit(solution)/shard_map/all_to_all | solution.py:577
  198.6 13.4 %all-to-all-done.2.attn_ref = bf16[8,256,128]{2,1,0:T(8,128)(2,1)S(1)} async-done(((bf16[8,256,128]{2,1,0:T(8,128)(2,1)}), bf16[8,256,128]{2,1,0:T(8,128)(2,1)S(1)}, u32[]{:S(2)}, u32[]{:S(2)}) %all-to-all-start.2) | async-done | bytes 524320 | tf_op jit(solution)/shard_map/all_to_all | solution.py:577
  212.0 0.9 copy-done.18
  212.9 7.5 %shard_map.201 = (bf16[128,1024]{1,0:T(8,128)(2,1)S(1)}, f32[128,1024]{1,0:T(8,128)S(1)}, bf16[128,1024]{1,0:T(8,128)(2,1)S(1)}) custom-call(bf16[8,256,128]{2,1,0:T(8,128)(2,1)S(1)} %all-to-all-done.2.attn_ref, bf16[1024,1024]{1,0:T(8,128)(2,1)} %all-gather.5.cloned.1.call-done.w_out_ref, bf16[128,1024]{1,0:T(8,128)(2,1)S(1)} %bitcast.87, ...), custom_call_target="tpu_custom_call" | custom-call | flops 3221225472 | bytes 12582912 | tf_op jit(solution)/shard_map/pallas_call | solution.py:444
  220.5 1.9 collective-permute-start.15
  224.1 12.1 %collective-permute-done.15 = bf16[128,1024]{1,0:T(8,128)(2,1)S(1)} collective-permute-done((bf16[128,1024]{1,0:T(8,128)(2,1)S(1)}, bf16[128,1024]{1,0:T(8,128)(2,1)S(1)}, u32[]{:S(2)}, u32[]{:S(2)}) %collective-permute-start.15) | collective-permute-done | bytes 262176 | tf_op jit(solution)/shard_map/ppermute | solution.py:582
  (121 shorter events, 17.4 us)
Async XLA Ops:
  7.2 142.3 %all-gather.3.cloned.1.call-start = ((), (), s32[]{:S(2)}) async-start(), calls=%async_computation.3 | async-start | bytes 2359296 | tf_op jit(solution)/shard_map/all_gather | solution.py:518
  7.2 36.6 %collective-permute-start.2 = (bf16[128,1024]{1,0:T(8,128)(2,1)}, bf16[128,1024]{1,0:T(8,128)(2,1)S(1)}, u32[]{:S(2)}, u32[]{:S(2)}) collective-permute-start(bf16[128,1024]{1,0:T(8,128)(2,1)} %bitcast.82), channel_id=1, source_target_pairs={{0,384},{64,448},{128,256},{192,320},{256,128},{320,192},{384,0},{... | collective-permute-start | bytes 786440 | tf_op jit(solution)/shard_map/ppermute | solution.py:505
  15.7 32.5 %collective-permute-start.3 = (bf16[128,1024]{1,0:T(8,128)(2,1)}, bf16[128,1024]{1,0:T(8,128)(2,1)S(1)}, u32[]{:S(2)}, u32[]{:S(2)}) collective-permute-start(bf16[128,1024]{1,0:T(8,128)(2,1)} %bitcast.83), channel_id=1, source_target_pairs={{0,64},{64,0},{128,192},{192,128},{256,320},{320,256},{384,448},{4... | collective-permute-start | bytes 786440 | tf_op jit(solution)/shard_map/ppermute | solution.py:504
  18.5 40.5 %collective-permute-start.1 = (bf16[128,1024]{1,0:T(8,128)(2,1)}, bf16[128,1024]{1,0:T(8,128)(2,1)S(1)}, u32[]{:S(2)}, u32[]{:S(2)}) collective-permute-start(bf16[128,1024]{1,0:T(8,128)(2,1)} %bitcast.84), channel_id=1, source_target_pairs={{0,256},{64,320},{128,384},{192,448},{256,0},{320,64},{384,128},{4... | collective-permute-start | bytes 786440 | tf_op jit(solution)/shard_map/ppermute | solution.py:505
  20.5 39.8 %collective-permute-start = (bf16[128,1024]{1,0:T(8,128)(2,1)}, bf16[128,1024]{1,0:T(8,128)(2,1)S(1)}, u32[]{:S(2)}, u32[]{:S(2)}) collective-permute-start(bf16[128,1024]{1,0:T(8,128)(2,1)} %bitcast.85), channel_id=1, source_target_pairs={{0,128},{64,192},{128,0},{192,64},{256,384},{320,448},{384,256},{4... | collective-permute-start | bytes 786440 | tf_op jit(solution)/shard_map/ppermute | solution.py:505
  25.6 14.3 %collective-permute-start.6 = (bf16[128,128]{1,0:T(8,128)(2,1)}, bf16[128,128]{1,0:T(8,128)(2,1)S(1)}, u32[]{:S(2)}, u32[]{:S(2)}) collective-permute-start(bf16[128,128]{1,0:T(8,128)(2,1)} %bitcast.97), channel_id=1, source_target_pairs={{0,32},{1,33},{2,34},{3,35},{4,36},{5,37},{6,38},{7,39},{8,40},{9,... | collective-permute-start | bytes 98312 | tf_op jit(solution)/shard_map/ppermute | solution.py:510
  40.7 20.6 %collective-permute-start.7 = (bf16[2,128,128]{2,1,0:T(8,128)(2,1)S(1)}, bf16[2,128,128]{2,1,0:T(8,128)(2,1)S(1)}, u32[]{:S(2)}, u32[]{:S(2)}) collective-permute-start(bf16[2,128,128]{2,1,0:T(8,128)(2,1)S(1)} %get-tuple-element.25), channel_id=1, source_target_pairs={{0,8},{1,9},{2,10},{3,11},{4,12},{5,13},{6,14},{7,15},{8,0},{9,1},... | collective-permute-start | bytes 196616 | tf_op jit(solution)/shard_map/ppermute | solution.py:512
  43.8 17.5 %collective-permute-start.8 = (bf16[2,128,128]{2,1,0:T(8,128)(2,1)S(1)}, bf16[2,128,128]{2,1,0:T(8,128)(2,1)S(1)}, u32[]{:S(2)}, u32[]{:S(2)}) collective-permute-start(bf16[2,128,128]{2,1,0:T(8,128)(2,1)S(1)} %get-tuple-element.25), channel_id=1, source_target_pairs={{0,16},{1,17},{2,18},{3,19},{4,20},{5,21},{6,22},{7,23},{8,24},{9,... | collective-permute-start | bytes 196616 | tf_op jit(solution)/shard_map/ppermute | solution.py:512
  48.2 13.1 %collective-permute-start.9 = (bf16[2,128,128]{2,1,0:T(8,128)(2,1)S(1)}, bf16[2,128,128]{2,1,0:T(8,128)(2,1)S(1)}, u32[]{:S(2)}, u32[]{:S(2)}) collective-permute-start(bf16[2,128,128]{2,1,0:T(8,128)(2,1)S(1)} %get-tuple-element.25), channel_id=1, source_target_pairs={{0,24},{1,25},{2,26},{3,27},{4,28},{5,29},{6,30},{7,31},{8,16},{9,... | collective-permute-start | bytes 196616 | tf_op jit(solution)/shard_map/ppermute | solution.py:512
  59.0 9.0 %copy-start.11 = (bf16[128,1024]{1,0:T(8,128)(2,1)}, bf16[128,1024]{1,0:T(8,128)(2,1)S(1)}, u32[]{:S(2)}) copy-start(bf16[128,1024]{1,0:T(8,128)(2,1)S(1)} %collective-permute-done.1.tok_b) | copy-start | bytes 786436
  62.1 5.8 %copy-start.17 = (bf16[4,32,1024]{2,1,0:T(8,128)(2,1)S(1)}, bf16[4,32,1024]{2,1,0:T(8,128)(2,1)}, u32[]{:S(2)}) copy-start(bf16[4,32,1024]{2,1,0:T(8,128)(2,1)} %param.19) | copy-start | bytes 786436
  62.3 6.6 %collective-permute-start.4 = (bf16[3,128,1024]{2,1,0:T(8,128)(2,1)S(1)}, bf16[3,128,1024]{2,1,0:T(8,128)(2,1)S(1)}, u32[]{:S(2)}, u32[]{:S(2)}) collective-permute-start(bf16[3,128,1024]{2,1,0:T(8,128)(2,1)S(1)} %pad_maximum_fusion.1), channel_id=1, source_target_pairs={{0,64},{64,0},{128,192},{192,128},{256,320},{320,256},{384,448},{4... | collective-permute-start | bytes 2359304 | tf_op jit(solution)/shard_map/ppermute | solution.py:520
  68.1 3.2 %copy-start.1 = (bf16[4,128,1024]{2,1,0:T(8,128)(2,1)}, bf16[4,128,1024]{2,1,0:T(8,128)(2,1)S(1)}, u32[]{:S(2)}) copy-start(bf16[4,128,1024]{2,1,0:T(8,128)(2,1)S(1)} %pad_maximum_fusion.half_ref) | copy-start | bytes 3145732
  68.9 2.5 %copy-start.13 = (bf16[3,128,1024]{2,1,0:T(8,128)(2,1)}, bf16[3,128,1024]{2,1,0:T(8,128)(2,1)S(1)}, u32[]{:S(2)}) copy-start(bf16[3,128,1024]{2,1,0:T(8,128)(2,1)S(1)} %collective-permute-done.4.other_ref) | copy-start | bytes 2359300
  71.4 9.8 %copy-start.23 = (bf16[32,32,128]{2,1,0:T(8,128)(2,1)}, bf16[32,32,128]{2,1,0:T(8,128)(2,1)S(1)}, u32[]{:S(2)}) copy-start(bf16[32,32,128]{2,1,0:T(8,128)(2,1)S(1)} %get-tuple-element.12.q_ref) | copy-start | bytes 786436
  71.4 9.9 %copy-start.34 = (bf16[512]{0:T(512)(128)(2,1)S(1)}, bf16[512]{0:T(512)(128)(2,1)}, u32[]{:S(2)}) copy-start(bf16[512]{0:T(512)(128)(2,1)} %param.26) | copy-start | bytes 3076
  71.4 9.9 %copy-start.25 = (bf16[2,2,384,128]{3,2,1,0:T(8,128)(2,1)S(1)}, bf16[2,2,384,128]{3,2,1,0:T(8,128)(2,1)}, u32[]{:S(2)}) copy-start(bf16[2,2,384,128]{3,2,1,0:T(8,128)(2,1)} %param.32) | copy-start | bytes 1179652
  71.4 46.5 %all-to-all-start = ((bf16[32,4,32,128]{3,2,1,0:T(8,128)(2,1)}), bf16[32,4,32,128]{3,2,1,0:T(8,128)(2,1)}, u32[]{:S(2)}, u32[]{:S(2)}) async-start(bf16[32,4,32,128]{3,2,1,0:T(8,128)(2,1)} %bitcast.10), calls=%async_computation | async-start | bytes 2097152 | tf_op jit(solution)/shard_map/all_to_all | solution.py:545
  81.1 117.5 %all-gather.5.cloned.1.call-start = ((), (), s32[]{:S(2)}) async-start(), calls=%async_computation.4 | async-start | bytes 2359296 | tf_op jit(solution)/shard_map/all_gather | solution.py:528
  82.0 25.4 %collective-permute-start.5 = (bf16[1536,128]{1,0:T(8,128)(2,1)}, bf16[1536,128]{1,0:T(8,128)(2,1)}, u32[]{:S(2)}, u32[]{:S(2)}) collective-permute-start(bf16[1536,128]{1,0:T(8,128)(2,1)} %bitcast.13), channel_id=1, source_target_pairs={{0,32},{1,33},{2,34},{3,35},{4,36},{5,37},{6,38},{7,39},{8,40},{9,... | collective-permute-start | bytes 1179656 | tf_op jit(solution)/shard_map/ppermute | solution.py:525
  84.0 1.2 copy-start.9
  85.2 1.2 copy-start.10
  86.4 2.7 %copy-start.27 = (bf16[128,1024]{1,0:T(8,128)(2,1)S(1)}, bf16[128,1024]{1,0:T(8,128)(2,1)}, u32[]{:S(2)}) copy-start(bf16[128,1024]{1,0:T(8,128)(2,1)} %param.21) | copy-start | bytes 786436
  86.6 53.3 %copy-start = (bf16[2,2064,256]{2,1,0:T(8,128)(2,1)}, bf16[2,2064,256]{2,1,0:T(8,128)(2,1)S(1)}, u32[]{:S(2)}) copy-start(bf16[2,2064,256]{2,1,0:T(8,128)(2,1)S(1)} %shard_map.196.after_ref.w0) | copy-start | bytes 6340612
  86.6 112.0 %collective-permute-start.10 = (bf16[2,2064,256]{2,1,0:T(8,128)(2,1)S(1)}, bf16[2,2064,256]{2,1,0:T(8,128)(2,1)}, u32[]{:S(2)}, u32[]{:S(2)}) collective-permute-start(bf16[2,2064,256]{2,1,0:T(8,128)(2,1)S(1)} %shard_map.196.after_ref.w0), channel_id=1, source_target_pairs={{0,64},{64,0},{128,192},{192,128},{256,320},{320,256},{384,448},{4... | collective-permute-start | bytes 6340616 | tf_op jit(solution)/shard_map/ppermute | solution.py:530
  126.0 1.0 copy-start.6
  127.0 60.8 %all-to-all-start.1 = ((bf16[32,9,16,128]{3,2,1,0:T(8,128)(2,1)}), bf16[32,9,16,128]{3,2,1,0:T(8,128)(2,1)S(1)}, u32[]{:S(2)}, u32[]{:S(2)}) async-start(bf16[32,9,16,128]{3,2,1,0:T(8,128)(2,1)} %copy-done.6), calls=%async_computation.1 | async-start | bytes 2359296 | tf_op jit(solution)/shard_map/all_to_all | solution.py:569
  134.5 3.0 %copy-start.2 = (bf16[4,128,1024]{2,1,0:T(8,128)(2,1)S(1)}, bf16[4,128,1024]{2,1,0:T(8,128)(2,1)}, u32[]{:S(2)}) copy-start(bf16[4,128,1024]{2,1,0:T(8,128)(2,1)} %copy-done.1) | copy-start | bytes 3145732
  134.5 3.0 %copy-start.26 = (bf16[1024,3,128]{2,0,1:T(8,128)(2,1)S(1)}, bf16[1024,3,128]{2,0,1:T(8,128)(2,1)}, u32[]{:S(2)}) copy-start(bf16[1024,3,128]{2,0,1:T(8,128)(2,1)} %param.20) | copy-start | bytes 2359300
  139.8 8.1 %copy-start.14 = (bf16[3,128,1024]{2,1,0:T(8,128)(2,1)S(1)}, bf16[3,128,1024]{2,1,0:T(8,128)(2,1)}, u32[]{:S(2)}) copy-start(bf16[3,128,1024]{2,1,0:T(8,128)(2,1)} %copy-done.13) | copy-start | bytes 2359300
  141.3 7.0 %copy-start.28 = (bf16[128,128]{1,0:T(8,128)(2,1)S(1)}, bf16[128,128]{1,0:T(8,128)(2,1)}, u32[]{:S(2)}) copy-start(bf16[128,128]{1,0:T(8,128)(2,1)} %fusion.12) | copy-start | bytes 98308
  141.3 40.4 %collective-permute-start.11 = (bf16[2064,256]{1,0:T(8,128)(2,1)}, bf16[2064,256]{1,0:T(8,128)(2,1)}, u32[]{:S(2)}, u32[]{:S(2)}) collective-permute-start(bf16[2064,256]{1,0:T(8,128)(2,1)} %get-tuple-element.23), channel_id=1, source_target_pairs={{0,128},{1,129},{2,130},{3,131},{4,132},{5,133},{6,134},{7,135},{8... | collective-permute-start | bytes 3170312 | tf_op jit(solution)/shard_map/ppermute | solution.py:566
  143.4 39.2 %collective-permute-start.12 = (bf16[2064,256]{1,0:T(8,128)(2,1)}, bf16[2064,256]{1,0:T(8,128)(2,1)}, u32[]{:S(2)}, u32[]{:S(2)}) collective-permute-start(bf16[2064,256]{1,0:T(8,128)(2,1)} %get-tuple-element.22), channel_id=1, source_target_pairs={{0,416},{1,417},{2,418},{3,419},{4,420},{5,421},{6,422},{7,423},{8... | collective-permute-start | bytes 3170312 | tf_op jit(solution)/shard_map/ppermute | solution.py:566
  149.5 1.0 copy-start.7
  151.1 1.6 copy-start.22
  182.6 16.0 %collective-permute-start.13 = (bf16[2064,256]{1,0:T(8,128)(2,1)}, bf16[2064,256]{1,0:T(8,128)(2,1)}, u32[]{:S(2)}, u32[]{:S(2)}) collective-permute-start(bf16[2064,256]{1,0:T(8,128)(2,1)} %get-tuple-element.15.w2), channel_id=1, source_target_pairs={{0,64},{64,0},{128,192},{192,128},{256,320},{320,256},{384,448},{4... | collective-permute-start | bytes 3170312 | tf_op jit(solution)/shard_map/ppermute | solution.py:575
  185.9 12.7 %collective-permute-start.14 = (bf16[2064,256]{1,0:T(8,128)(2,1)}, bf16[2064,256]{1,0:T(8,128)(2,1)}, u32[]{:S(2)}, u32[]{:S(2)}) collective-permute-start(bf16[2064,256]{1,0:T(8,128)(2,1)} %get-tuple-element.16.w3), channel_id=1, source_target_pairs={{0,64},{64,0},{128,192},{192,128},{256,320},{320,256},{384,448},{4... | collective-permute-start | bytes 3170312 | tf_op jit(solution)/shard_map/ppermute | solution.py:575
  187.8 1.0 copy-start.4
  188.9 1.0 copy-start.16
  193.4 4.8 %copy-start.29 = (bf16[1024]{0:T(1024)(128)(2,1)S(1)}, bf16[1024]{0:T(1024)(128)(2,1)}, u32[]{:S(2)}) copy-start(bf16[1024]{0:T(1024)(128)(2,1)} %param.23) | copy-start | bytes 6148
  193.4 4.8 %copy-start.30 = (bf16[1024]{0:T(1024)(128)(2,1)S(1)}, bf16[1024]{0:T(1024)(128)(2,1)}, u32[]{:S(2)}) copy-start(bf16[1024]{0:T(1024)(128)(2,1)} %param.24) | copy-start | bytes 6148
  193.4 4.8 %copy-start.31 = (bf16[1024]{0:T(1024)(128)(2,1)S(1)}, bf16[1024]{0:T(1024)(128)(2,1)}, u32[]{:S(2)}) copy-start(bf16[1024]{0:T(1024)(128)(2,1)} %param.28) | copy-start | bytes 6148
  193.4 4.8 %copy-start.32 = (bf16[1024]{0:T(1024)(128)(2,1)S(1)}, bf16[1024]{0:T(1024)(128)(2,1)}, u32[]{:S(2)}) copy-start(bf16[1024]{0:T(1024)(128)(2,1)} %param.29) | copy-start | bytes 6148
  193.4 4.9 %copy-start.33 = (bf16[1024]{0:T(1024)(128)(2,1)S(1)}, bf16[1024]{0:T(1024)(128)(2,1)}, u32[]{:S(2)}) copy-start(bf16[1024]{0:T(1024)(128)(2,1)} %param.30) | copy-start | bytes 6148
  193.4 18.6 %copy-start.12 = (bf16[128,1024]{1,0:T(8,128)(2,1)S(1)}, bf16[128,1024]{1,0:T(8,128)(2,1)}, u32[]{:S(2)}) copy-start(bf16[128,1024]{1,0:T(8,128)(2,1)} %copy-done.11) | copy-start | bytes 786436
  193.4 18.6 %all-to-all-start.2 = ((bf16[8,256,128]{2,1,0:T(8,128)(2,1)}), bf16[8,256,128]{2,1,0:T(8,128)(2,1)S(1)}, u32[]{:S(2)}, u32[]{:S(2)}) async-start(bf16[8,256,128]{2,1,0:T(8,128)(2,1)} %bitcast.72), calls=%async_computation.2 | async-start | bytes 1048576 | tf_op jit(solution)/shard_map/all_to_all | solution.py:577
  198.5 23.9 %copy-start.8 = (bf16[1024,128]{1,0:T(8,128)(2,1)S(1)}, bf16[1024,128]{1,0:T(8,128)(2,1)}, u32[]{:S(2)}) copy-start(bf16[1024,128]{1,0:T(8,128)(2,1)} %maximum_convert_fusion.1) | copy-start | bytes 786436
  220.5 15.7 %collective-permute-start.15 = (bf16[128,1024]{1,0:T(8,128)(2,1)S(1)}, bf16[128,1024]{1,0:T(8,128)(2,1)S(1)}, u32[]{:S(2)}, u32[]{:S(2)}) collective-permute-start(bf16[128,1024]{1,0:T(8,128)(2,1)S(1)} %get-tuple-element.19), channel_id=1, source_target_pairs={{0,256},{64,320},{128,384},{192,448},{256,0},{320,64},{384,128},{4... | collective-permute-start | bytes 786440 | tf_op jit(solution)/shard_map/ppermute | solution.py:582
  (8 other events, 6.5 us)
Sparse Core Ops, SparseCore 0:
  62.3 58.4 all-gather.2
  122.8 50.8 all-gather.4

commit v9 on v7

--- a/solution.py
+++ b/solution.py
@@ -76,6 +76,7 @@
         out[ROOT_LEN + t] = root_len[t]
     out[PLACE] = my_z
     out[PLACE + 1] = my_x
+    out[PLACE + 2] = blk
 
     def first_pass(r, _):
         leaf = leaf_of[r]
@@ -384,7 +385,7 @@
         in_specs=[pl.BlockSpec(memory_space=pltpu.SMEM)] + [vmem] * 3,
         out_specs=vmem,
         scratch_shapes=[pltpu.VMEM((PEERS, SLOTS, 2, HALF, LANES), F32)],
-        compiler_params=pltpu.CompilerParams(vmem_limit_bytes=30 << 20),
+        compiler_params=pltpu.CompilerParams(vmem_limit_bytes=16 << 20),
         cost_estimate=pl.CostEstimate(
             flops=1 << 27, bytes_accessed=4 << 20, transcendentals=1 << 20
         ),
@@ -414,13 +415,18 @@
     return center * lax.rsqrt(spread + EPS) * gain + shift
 
 
-def feed_kernel(attn_ref, w_out_ref, tok_a, tok_b, vec_ref, w0, w1, w2, w3, w4, w5, norm_ref, own_ref, far_ref):
-    rows = tok_a.shape[0]
-    width = tok_a.shape[1]
-    attn = jnp.concatenate([attn_ref[h] for h in range(N_BLK)], axis=1)
+def feed_kernel(
+    tab, attn_ref, half_ref, other_ref, tok_a, tok_b, vec_ref, w0, w1, w2, w3, w4, w5, norm_ref, own_ref, far_ref
+):
+    rows, width = tok_a.shape
+    blk = tab[PLACE + 2]
+    proj = jnp.zeros((2 * rows, width), F32)
+    for core, ref in enumerate((half_ref, other_ref)):
+        parts = [attn_ref[blk ^ (2 * k + core)] for k in range(N_BLK // 2)]
+        proj = proj + dot_nn(jnp.concatenate(parts, axis=1), ref[...].reshape(-1, width))
     tok = jnp.concatenate([tok_a[...], tok_b[...]], axis=0).astype(F32)
     vec = vec_ref[...].astype(F32)
-    mixed = tok + dot_nn(attn, w_out_ref[...]) + vec[0:1]
+    mixed = tok + proj + vec[0:1]
     norm = rows_norm(mixed, vec[1:2], vec[2:3]).astype(BF16)
     norm_ref[...] = norm[:rows]
     total = jnp.zeros((2 * rows, width), F32)
@@ -438,7 +444,7 @@
     far_ref[...] = total[rows:].astype(BF16)
 
 
-def feed_forward(attn, w_out, tok_a, tok_b, vectors, packs):
+def feed_forward(tab, attn, out_half, out_other, tok_a, tok_b, vectors, packs):
     rows, width = tok_a.shape
     vmem = pl.BlockSpec(memory_space=pltpu.VMEM)
     return pl.pallas_call(
@@ -448,13 +454,13 @@
             jax.ShapeDtypeStruct((rows, width), F32),
             jax.ShapeDtypeStruct((rows, width), BF16),
         ),
-        in_specs=[vmem] * (5 + len(packs)),
+        in_specs=[pl.BlockSpec(memory_space=pltpu.SMEM)] + [vmem] * (6 + len(packs)),
         out_specs=(vmem, vmem, vmem),
         compiler_params=pltpu.CompilerParams(vmem_limit_bytes=48 << 20),
         cost_estimate=pl.CostEstimate(
             flops=3 << 30, bytes_accessed=12 << 20, transcendentals=1 << 20
         ),
-    )(attn, w_out, tok_a, tok_b, vectors, *packs)
+    )(tab, attn, out_half, out_other, tok_a, tok_b, vectors, *packs)
 
 
 def on_device(
@@ -521,7 +527,6 @@
     node_far = lax.ppermute(node_rows, "owner", xor_pairs(n_owner, NX * NY))
     caches = jnp.stack([node_rows, node_far]).reshape(NZ, 2, 2, node_max, LANES)
 
-    w_out_all = lax.all_gather(w_out + zero_after(last_come), "blk", axis=0, tiled=True)
     packs = pack_weights(w_up, w_down, b_up, last_come)
     pack_side = lax.ppermute(packs, "blk", swap)
 
@@ -562,11 +567,17 @@
         return lax.ppermute(sent, ("blk", "owner"), pairs)
 
     pack_next = [to_neighbour(1), to_neighbour(-1)]
+    w_out_sent = w_out + zero_after(answers.reshape(-1, LANES))
+    out_half = [
+        lax.ppermute(w_out_sent, "blk", xor_pairs(N_BLK, 2 * k)) for k in range(1, n_own)
+    ]
     back = lax.all_to_all(
         answers, "owner", split_axis=0, concat_axis=0, axis_index_groups=groups, tiled=True
     )
     out, mass = root_attention(tab, q, k_new, v_new, roots)
     send = merge(tab, back, out, mass)
+    out_half = jnp.stack([w_out] + out_half)
+    out_other = lax.ppermute(out_half, "blk", swap)
     pack_next = after(pack_next, mass)
     pack_last = [lax.ppermute(part, "blk", swap) for part in pack_next]
     parts = [packs, pack_side] + pack_next + pack_last
@@ -574,7 +585,7 @@
         send.reshape(N_BLK, 2 * own_rows, cols), "blk", split_axis=0, concat_axis=0, tiled=True
     )
     vectors = jnp.stack([b_out, gain1, shift1])
-    own_norm, down, down_far = feed_forward(attn, w_out_all, tok, tok_far, vectors, parts)
+    own_norm, down, down_far = feed_forward(tab, attn, out_half, out_other, tok, tok_far, vectors, parts)
     total = down + lax.ppermute(down_far, "blk", xor_pairs(N_BLK, N_BLK // 2)).astype(F32)
     result = layer_norm(
         own_norm.astype(F32) + total + b_down.astype(F32), gain2, shift2

time: 230 us -> 249 us (1.083)
  waiting for transfers between devices: 60.9 us -> 71.3 us
  starting transfers between devices: 79.1 us -> 85.9 us
  local copies, waits for them, and re-layouts: 20.7 us -> 23.3 us
    all_gather x1, waiting for transfers between devices: 18.2 us -> 0.02 us  [on_device(): lax.all_gather(roots, 'owner', axis=0, tiled=False, axis_index_groups=gro...]
    ppermute x3, waiting for transfers between devices: 0.01 us -> 17.1 us  [on_device(): lax.ppermute(tok, 'blk', xor_pairs(N_BLK, 2 * k))]
    all_gather x1 -> x0, waiting for transfers between devices: 13.9 us -> none  [on_device(): lax.all_gather(w_out + zero_after(last_come), 'blk', axis=0, tiled=True)]
    ppermute x2, waiting for transfers between devices: 0.01 us -> 12.7 us  [to_neighbour(): return lax.ppermute(sent, ('blk', 'owner'), pairs)]
    ppermute x0 -> x4, starting transfers between devices: none -> 11.4 us  [the longest x3 9.02 us: on_device(): lax.ppermute(w_out_sent, 'blk', xor_pairs(N_BLK, 2 * k))]
    all_to_all x1, waiting for transfers between devices: 5.59 us -> 13.2 us  [on_device(): lax.all_to_all(send.reshape(N_BLK, 2 * own_rows, cols), 'blk', split_axis...]
    ppermute x1, starting transfers between devices: 8.18 us -> 1.92 us  [on_device(): node_far = lax.ppermute(node_rows, 'owner', xor_pairs(n_owner, NX * NY))]
    ppermute x2, starting transfers between devices: 6.54 us -> 12.4 us  [on_device(): pack_last = [lax.ppermute(part, 'blk', swap) for part in pack_next]]
  transfers between devices with their start and end apart: 18 -> 21, of which waited for: 6 -> 7; matrix products, arithmetic and copies ran while one was open for 9% -> 8% of each run, Pallas kernels for 11% -> 10%
where the time goes in v9:
time: 249 us; the launch traced here: 247 us
  starting transfers between devices  85.9 us (34%)
  waiting for transfers between devices  71.3 us (29%)
  Pallas kernels  33.2 us (13%)
  local copies, waits for them, and re-layouts  23.3 us (9%)
  between operations  19 us (8%)
  other arithmetic  10.5 us (4%)
  matrix products  3.99 us (2%)
    ppermute x3, waiting for transfers between devices, on_device(): lax.ppermute(tok, 'blk', xor_pairs(N_BLK, 2 * k))  17.1 us
    unnamed x86, local copies, waits for them, and re-layouts  16.2 us
    all_to_all x1, waiting for transfers between devices, on_device(): lax.all_to_all(send.reshape(N_BLK, 2 * own_rows, cols), 'blk', split_axis...  13.2 us
    ppermute x2, waiting for transfers between devices, to_neighbour(): return lax.ppermute(sent, ('blk', 'owner'), pairs)  12.7 us
    ppermute x3, starting transfers between devices, on_device(): lax.ppermute(tok, 'blk', xor_pairs(N_BLK, 2 * k))  12.7 us
    ppermute x2, starting transfers between devices, on_device(): pack_last = [lax.ppermute(part, 'blk', swap) for part in pack_next]  12.4 us
    ppermute x1, waiting for transfers between devices, on_device(): lax.ppermute(down_far, 'blk', xor_pairs(N_BLK, N_BLK // 2)).astype(F32)  12.2 us
    ppermute x1, waiting for transfers between devices, on_device(): node_far = lax.ppermute(node_rows, 'owner', xor_pairs(n_owner, NX * NY))  10.2 us
  transfers between devices with their start and end apart: 21, of which 7 were waited for; matrix products, arithmetic and copies ran while one was open for 8% of the time, Pallas kernels for 10%

profile of v9, /device:TPU:1, one launch (start us, length us, event | category | flops | bytes accessed | tf_op | source)
XLA Modules:
  0.0 247.1 jit_solution(11022821333793999882)
XLA Ops:
  7.2 8.6 %collective-permute-start.2 = (bf16[128,1024]{1,0:T(8,128)(2,1)}, bf16[128,1024]{1,0:T(8,128)(2,1)S(1)}, u32[]{:S(2)}, u32[]{:S(2)}) collective-permute-start(bf16[128,1024]{1,0:T(8,128)(2,1)} %bitcast.81), channel_id=1, source_target_pairs={{0,384},{64,448},{128,256},{192,320},{256,128},{320,192},{384,0},{... | collective-permute-start | bytes 786440 | tf_op jit(solution)/shard_map/ppermute | solution.py:511
  15.8 1.9 collective-permute-start.1
  17.7 2.2 collective-permute-start
  20.0 1.2 collective-permute-done.2.after_ref
  21.2 15.9 %collective-permute-done.1.tok_b = bf16[128,1024]{1,0:T(8,128)(2,1)S(1)} collective-permute-done((bf16[128,1024]{1,0:T(8,128)(2,1)}, bf16[128,1024]{1,0:T(8,128)(2,1)S(1)}, u32[]{:S(2)}, u32[]{:S(2)}) %collective-permute-start.1) | collective-permute-done | bytes 262176 | tf_op jit(solution)/shard_map/ppermute | solution.py:511
  37.1 1.0 pad_maximum_fusion.2
  38.1 3.1 %collective-permute-start.4 = (bf16[3,128,1024]{2,1,0:T(8,128)(2,1)}, bf16[3,128,1024]{2,1,0:T(8,128)(2,1)S(1)}, u32[]{:S(2)}, u32[]{:S(2)}) collective-permute-start(bf16[3,128,1024]{2,1,0:T(8,128)(2,1)} %pad_maximum_fusion.2), channel_id=1, source_target_pairs={{0,64},{64,0},{128,192},{192,128},{256,320},{320,256},{384,448},{4... | collective-permute-start | bytes 2359304 | tf_op jit(solution)/shard_map/ppermute | solution.py:522
  41.2 1.9 collective-permute-start.3
  43.1 9.1 %collective-permute-start.6 = (bf16[128,128]{1,0:T(8,128)(2,1)S(1)}, bf16[128,128]{1,0:T(8,128)(2,1)S(1)}, u32[]{:S(2)}, u32[]{:S(2)}) collective-permute-start(bf16[128,128]{1,0:T(8,128)(2,1)S(1)} %bitcast.96), channel_id=1, source_target_pairs={{0,32},{1,33},{2,34},{3,35},{4,36},{5,37},{6,38},{7,39},{8,40},{9,... | collective-permute-start | bytes 98312 | tf_op jit(solution)/shard_map/ppermute | solution.py:516
  52.9 3.9 %shard_map.194.tab = s32[288]{0:T(512)} custom-call(s32[4]{0:T(128)} %pad_add_fusion.coords, s32[32]{0:T(128)} %leaf_of.1, s32[128]{0:T(128)} %parent.1, s32[128]{0:T(128)} %place.1, s32[128]{0:T(128)} %length.1, s32[4]{0:T(128)} %root_len.1), custom_call_target="tpu_custom_call" | custom-call | flops 1048576 | bytes 4096 | tf_op jit(solution)/shard_map/pallas_call | solution.py:139
  56.8 1.2 slice.34
  64.2 1.0 slice_bitcast_fusion.w_ref
  65.9 2.5 %shard_map.195 = (bf16[32,32,128]{2,1,0:T(8,128)(2,1)S(1)}, bf16[128,32,128]{2,1,0:T(8,128)(2,1)}) custom-call(s32[288]{0:T(512)S(1)} %copy-done.20, bf16[4,128,1024]{2,1,0:T(8,128)(2,1)S(1)} %pad_maximum_fusion.half_ref, bf16[128,1024]{1,0:T(8,128)(2,1)S(1)} %collective-permute-done.3.near_ref, bf16[3,128,1024]{2,1,0:T(8,128)(2,1)S(1)} %collective-permute-done.4.other_ref, ...), custom_call_target="tpu_custom_call" | custom-call | flops 268435456 | bytes 4194304 | tf_op jit(solution)/shard_map/pallas_call | solution.py:173
  68.4 9.9 %all-to-all-start = ((bf16[32,4,32,128]{3,2,1,0:T(8,128)(2,1)}), bf16[32,4,32,128]{3,2,1,0:T(8,128)(2,1)}, u32[]{:S(2)}, u32[]{:S(2)}) async-start(bf16[32,4,32,128]{3,2,1,0:T(8,128)(2,1)} %bitcast.10), calls=%async_computation | async-start | bytes 2097152 | tf_op jit(solution)/shard_map/all_to_all | solution.py:546
  78.6 1.9 collective-permute-start.5
  80.5 1.2 copy-done.9
  81.7 1.2 copy-done.10
  83.1 3.2 %collective-permute-start.11 = (bf16[2,2064,256]{2,1,0:T(8,128)(2,1)S(1)}, bf16[2,2064,256]{2,1,0:T(8,128)(2,1)}, u32[]{:S(2)}, u32[]{:S(2)}) collective-permute-start(bf16[2,2064,256]{2,1,0:T(8,128)(2,1)S(1)} %shard_map.196.after_ref.w0), channel_id=1, source_target_pairs={{0,64},{64,0},{128,192},{192,128},{256,320},{320,256},{384,448},{4... | collective-permute-start | bytes 6340616 | tf_op jit(solution)/shard_map/ppermute | solution.py:531
  86.4 1.1 fusion.10
  88.4 1.1 fusion.4
  89.5 10.2 %collective-permute-done.5 = bf16[1536,128]{1,0:T(8,128)(2,1)S(1)} collective-permute-done((bf16[1536,128]{1,0:T(8,128)(2,1)S(1)}, bf16[1536,128]{1,0:T(8,128)(2,1)S(1)}, u32[]{:S(2)}, u32[]{:S(2)}) %collective-permute-start.5) | collective-permute-done | bytes 393248 | tf_op jit(solution)/shard_map/ppermute | solution.py:527
  100.6 5.6 %all-to-all-done.q_ref = bf16[32,4,32,128]{3,2,1,0:T(8,128)(2,1)} async-done(((bf16[32,4,32,128]{3,2,1,0:T(8,128)(2,1)}), bf16[32,4,32,128]{3,2,1,0:T(8,128)(2,1)}, u32[]{:S(2)}, u32[]{:S(2)}) %all-to-all-start) | async-done | bytes 1048608 | tf_op jit(solution)/shard_map/all_to_all | solution.py:546
  106.3 1.1 copy-done.13
  108.1 8.1 %shard_map.197 = bf16[32,9,16,128]{3,2,1,0:T(8,128)(2,1)S(1)} custom-call(s32[288]{0:T(512)S(1)} %copy-done.21, bf16[32,4,32,128]{3,2,1,0:T(8,128)(2,1)} %all-to-all-done.q_ref, bf16[2,2,2,384,128]{4,3,2,1,0:T(8,128)(2,1)S(1)} %copy-done.13, bf16[2,2064,256]{2,1,0:T(8,128)(2,1)S(1)} %shard_map.196.after_ref.w0), custom_call_target="tpu_custom_call" | custom-call | flops 2147483648 | bytes 4194304 | tf_op jit(solution)/shard_map/pallas_call | solution.py:264
  116.2 1.1 copy-done.6
  117.3 7.8 %all-to-all-start.1 = ((bf16[32,9,16,128]{3,2,1,0:T(8,128)(2,1)}), bf16[32,9,16,128]{3,2,1,0:T(8,128)(2,1)S(1)}, u32[]{:S(2)}, u32[]{:S(2)}) async-start(bf16[32,9,16,128]{3,2,1,0:T(8,128)(2,1)} %copy-done.6), calls=%async_computation.1 | async-start | bytes 2359296 | tf_op jit(solution)/shard_map/all_to_all | solution.py:574
  125.1 1.2 slice.45
  127.0 1.1 add_bitcast_fusion
  128.1 1.9 collective-permute-start.12
  130.7 4.7 %collective-permute-start.13 = (bf16[2064,256]{1,0:T(8,128)(2,1)}, bf16[2064,256]{1,0:T(8,128)(2,1)}, u32[]{:S(2)}, u32[]{:S(2)}) collective-permute-start(bf16[2064,256]{1,0:T(8,128)(2,1)} %get-tuple-element.22), channel_id=1, source_target_pairs={{0,416},{1,417},{2,418},{3,419},{4,420},{5,421},{6,422},{7,423},{8... | collective-permute-start | bytes 3170312 | tf_op jit(solution)/shard_map/ppermute | solution.py:567
  137.3 1.9 collective-permute-start.7
  139.2 2.8 %collective-permute-start.8 = (bf16[128,1024]{1,0:T(8,128)(2,1)}, bf16[128,1024]{1,0:T(8,128)(2,1)}, u32[]{:S(2)}, u32[]{:S(2)}) collective-permute-start(bf16[128,1024]{1,0:T(8,128)(2,1)} %broadcast_add_fusion.1), channel_id=1, source_target_pairs={{0,256},{64,320},{128,384},{192,448},{256,0},{320,64},{384,128},{4... | collective-permute-start | bytes 786440 | tf_op jit(solution)/shard_map/ppermute | solution.py:572
  142.1 12.7 %collective-permute-done.12.refs_0_ = bf16[2064,256]{1,0:T(8,128)(2,1)} collective-permute-done((bf16[2064,256]{1,0:T(8,128)(2,1)S(1)}, bf16[2064,256]{1,0:T(8,128)(2,1)}, u32[]{:S(2)}, u32[]{:S(2)}) %collective-permute-start.12) | collective-permute-done | bytes 1056800 | tf_op jit(solution)/shard_map/ppermute | solution.py:567
  154.8 4.3 %collective-permute-start.9 = (bf16[128,1024]{1,0:T(8,128)(2,1)}, bf16[128,1024]{1,0:T(8,128)(2,1)}, u32[]{:S(2)}, u32[]{:S(2)}) collective-permute-start(bf16[128,1024]{1,0:T(8,128)(2,1)} %broadcast_add_fusion.1), channel_id=1, source_target_pairs={{0,384},{64,448},{128,256},{192,320},{256,128},{320,192},{384,0},{... | collective-permute-start | bytes 786440 | tf_op jit(solution)/shard_map/ppermute | solution.py:572
  160.7 1.6 copy-done.25
  163.2 8.9 %shard_map.198 = (f32[32,32,128]{2,1,0:T(8,128)S(1)}, f32[32,32,128]{2,1,0:T(8,128)S(1)}) custom-call(s32[288]{0:T(512)S(1)} %copy-done.22, bf16[32,32,128]{2,1,0:T(8,128)(2,1)S(1)} %copy-done.27, bf16[32,32,128]{2,1,0:T(8,128)(2,1)S(1)} %bitcast.73, bf16[32,32,128]{2,1,0:T(8,128)(2,1)S(1)} %bitcast.75, bf16[4,8,2,2,4,16,128]{6,5,4,3,2,1,0:T(8,128)(2,1)S(1)} %bitcast.87), custom_call_target="tpu_custom_call" | custom-call | flops 4294967296 | bytes 4194304 | tf_op jit(solution)/shard_map/pallas_call | solution.py:332
  173.8 10.5 %collective-permute-start.14 = (bf16[2064,256]{1,0:T(8,128)(2,1)}, bf16[2064,256]{1,0:T(8,128)(2,1)}, u32[]{:S(2)}, u32[]{:S(2)}) collective-permute-start(bf16[2064,256]{1,0:T(8,128)(2,1)} %get-tuple-element.15.w2), channel_id=1, source_target_pairs={{0,64},{64,0},{128,192},{192,128},{256,320},{320,256},{384,448},{4... | collective-permute-start | bytes 3170312 | tf_op jit(solution)/shard_map/ppermute | solution.py:582
  184.3 1.9 collective-permute-start.15
  186.2 2.3 pad_maximum_fusion.1.half_ref
  188.5 2.4 collective-permute-start.10
  190.9 1.0 copy-done.4
  192.0 1.0 copy-done.17
  193.7 2.1 shard_map.199
  196.6 3.8 %all-to-all-start.2 = ((bf16[8,256,128]{2,1,0:T(8,128)(2,1)}), bf16[8,256,128]{2,1,0:T(8,128)(2,1)S(1)}, u32[]{:S(2)}, u32[]{:S(2)}) async-start(bf16[8,256,128]{2,1,0:T(8,128)(2,1)} %bitcast.71), calls=%async_computation.2 | async-start | bytes 1048576 | tf_op jit(solution)/shard_map/all_to_all | solution.py:584
  201.5 13.2 %all-to-all-done.2.attn_ref = bf16[8,256,128]{2,1,0:T(8,128)(2,1)S(1)} async-done(((bf16[8,256,128]{2,1,0:T(8,128)(2,1)}), bf16[8,256,128]{2,1,0:T(8,128)(2,1)S(1)}, u32[]{:S(2)}, u32[]{:S(2)}) %all-to-all-start.2) | async-done | bytes 524320 | tf_op jit(solution)/shard_map/all_to_all | solution.py:584
  215.6 7.5 %shard_map.201 = (bf16[128,1024]{1,0:T(8,128)(2,1)S(1)}, f32[128,1024]{1,0:T(8,128)S(1)}, bf16[128,1024]{1,0:T(8,128)(2,1)S(1)}) custom-call(s32[288]{0:T(512)S(1)} %copy-done.24, bf16[8,256,128]{2,1,0:T(8,128)(2,1)S(1)} %all-to-all-done.2.attn_ref, bf16[4,128,1024]{2,1,0:T(8,128)(2,1)} %pad_maximum_fusion.1.half_ref, ...), custom_call_target="tpu_custom_call" | custom-call | flops 3221225472 | bytes 12582912 | tf_op jit(solution)/shard_map/pallas_call | solution.py:450
  223.2 1.9 collective-permute-start.16
  226.8 12.2 %collective-permute-done.16 = bf16[128,1024]{1,0:T(8,128)(2,1)S(1)} collective-permute-done((bf16[128,1024]{1,0:T(8,128)(2,1)S(1)}, bf16[128,1024]{1,0:T(8,128)(2,1)S(1)}, u32[]{:S(2)}, u32[]{:S(2)}) %collective-permute-start.16) | collective-permute-done | bytes 262176 | tf_op jit(solution)/shard_map/ppermute | solution.py:589
  (136 shorter events, 19.8 us)
Async XLA Ops:
  7.2 34.0 %copy-start.18 = (bf16[4,32,1024]{2,1,0:T(8,128)(2,1)S(1)}, bf16[4,32,1024]{2,1,0:T(8,128)(2,1)}, u32[]{:S(2)}) copy-start(bf16[4,32,1024]{2,1,0:T(8,128)(2,1)} %param.19) | copy-start | bytes 786436
  7.2 36.0 %copy-start.36 = (bf16[2,4,16,128]{3,2,1,0:T(8,128)(2,1)S(1)}, bf16[2,4,16,128]{3,2,1,0:T(8,128)(2,1)}, u32[]{:S(2)}) copy-start(bf16[2,4,16,128]{3,2,1,0:T(8,128)(2,1)} %param.31) | copy-start | bytes 98308
  7.2 151.9 %all-gather.2.cloned.1.call-start = ((), (), s32[]{:S(2)}) async-start(), calls=%async_computation.3 | async-start | bytes 2162688 | tf_op jit(solution)/shard_map/all_gather | solution.py:521
  7.2 13.9 %collective-permute-start.2 = (bf16[128,1024]{1,0:T(8,128)(2,1)}, bf16[128,1024]{1,0:T(8,128)(2,1)S(1)}, u32[]{:S(2)}, u32[]{:S(2)}) collective-permute-start(bf16[128,1024]{1,0:T(8,128)(2,1)} %bitcast.81), channel_id=1, source_target_pairs={{0,384},{64,448},{128,256},{192,320},{256,128},{320,192},{384,0},{... | collective-permute-start | bytes 786440 | tf_op jit(solution)/shard_map/ppermute | solution.py:511
  15.8 21.3 %collective-permute-start.1 = (bf16[128,1024]{1,0:T(8,128)(2,1)}, bf16[128,1024]{1,0:T(8,128)(2,1)S(1)}, u32[]{:S(2)}, u32[]{:S(2)}) collective-permute-start(bf16[128,1024]{1,0:T(8,128)(2,1)} %bitcast.82), channel_id=1, source_target_pairs={{0,256},{64,320},{128,384},{192,448},{256,0},{320,64},{384,128},{4... | collective-permute-start | bytes 786440 | tf_op jit(solution)/shard_map/ppermute | solution.py:511
  17.7 19.3 %collective-permute-start = (bf16[128,1024]{1,0:T(8,128)(2,1)}, bf16[128,1024]{1,0:T(8,128)(2,1)S(1)}, u32[]{:S(2)}, u32[]{:S(2)}) collective-permute-start(bf16[128,1024]{1,0:T(8,128)(2,1)} %bitcast.83), channel_id=1, source_target_pairs={{0,128},{64,192},{128,0},{192,64},{256,384},{320,448},{384,256},{4... | collective-permute-start | bytes 786440 | tf_op jit(solution)/shard_map/ppermute | solution.py:511
  37.1 28.1 %copy-start.11 = (bf16[128,1024]{1,0:T(8,128)(2,1)}, bf16[128,1024]{1,0:T(8,128)(2,1)S(1)}, u32[]{:S(2)}) copy-start(bf16[128,1024]{1,0:T(8,128)(2,1)S(1)} %collective-permute-done.1.tok_b) | copy-start | bytes 786436
  38.1 27.3 %collective-permute-start.4 = (bf16[3,128,1024]{2,1,0:T(8,128)(2,1)}, bf16[3,128,1024]{2,1,0:T(8,128)(2,1)S(1)}, u32[]{:S(2)}, u32[]{:S(2)}) collective-permute-start(bf16[3,128,1024]{2,1,0:T(8,128)(2,1)} %pad_maximum_fusion.2), channel_id=1, source_target_pairs={{0,64},{64,0},{128,192},{192,128},{256,320},{320,256},{384,448},{4... | collective-permute-start | bytes 2359304 | tf_op jit(solution)/shard_map/ppermute | solution.py:522
  41.2 18.7 %collective-permute-start.3 = (bf16[128,1024]{1,0:T(8,128)(2,1)S(1)}, bf16[128,1024]{1,0:T(8,128)(2,1)S(1)}, u32[]{:S(2)}, u32[]{:S(2)}) collective-permute-start(bf16[128,1024]{1,0:T(8,128)(2,1)S(1)} %bitcast.84), channel_id=1, source_target_pairs={{0,64},{64,0},{128,192},{192,128},{256,320},{320,256},{384,448},{4... | collective-permute-start | bytes 786440 | tf_op jit(solution)/shard_map/ppermute | solution.py:510
  43.1 20.4 %collective-permute-start.6 = (bf16[128,128]{1,0:T(8,128)(2,1)S(1)}, bf16[128,128]{1,0:T(8,128)(2,1)S(1)}, u32[]{:S(2)}, u32[]{:S(2)}) collective-permute-start(bf16[128,128]{1,0:T(8,128)(2,1)S(1)} %bitcast.96), channel_id=1, source_target_pairs={{0,32},{1,33},{2,34},{3,35},{4,36},{5,37},{6,38},{7,39},{8,40},{9,... | collective-permute-start | bytes 98312 | tf_op jit(solution)/shard_map/ppermute | solution.py:516
  59.9 5.5 %copy-start.1 = (bf16[128,1024]{1,0:T(8,128)(2,1)}, bf16[128,1024]{1,0:T(8,128)(2,1)S(1)}, u32[]{:S(2)}) copy-start(bf16[128,1024]{1,0:T(8,128)(2,1)S(1)} %collective-permute-done.3.near_ref) | copy-start | bytes 786436
  65.9 2.5 %copy-start.14 = (bf16[3,128,1024]{2,1,0:T(8,128)(2,1)}, bf16[3,128,1024]{2,1,0:T(8,128)(2,1)S(1)}, u32[]{:S(2)}) copy-start(bf16[3,128,1024]{2,1,0:T(8,128)(2,1)S(1)} %collective-permute-done.4.other_ref) | copy-start | bytes 2359300
  68.4 10.0 %copy-start.26 = (bf16[32,32,128]{2,1,0:T(8,128)(2,1)}, bf16[32,32,128]{2,1,0:T(8,128)(2,1)S(1)}, u32[]{:S(2)}) copy-start(bf16[32,32,128]{2,1,0:T(8,128)(2,1)S(1)} %get-tuple-element.12.q_ref) | copy-start | bytes 786436
  68.4 10.1 %copy-start.42 = (bf16[512]{0:T(512)(128)(2,1)S(1)}, bf16[512]{0:T(512)(128)(2,1)}, u32[]{:S(2)}) copy-start(bf16[512]{0:T(512)(128)(2,1)} %param.26) | copy-start | bytes 3076
  68.4 10.1 %copy-start.28 = (bf16[2,2,384,128]{3,2,1,0:T(8,128)(2,1)S(1)}, bf16[2,2,384,128]{3,2,1,0:T(8,128)(2,1)}, u32[]{:S(2)}) copy-start(bf16[2,2,384,128]{3,2,1,0:T(8,128)(2,1)} %param.32) | copy-start | bytes 1179652
  68.4 37.8 %all-to-all-start = ((bf16[32,4,32,128]{3,2,1,0:T(8,128)(2,1)}), bf16[32,4,32,128]{3,2,1,0:T(8,128)(2,1)}, u32[]{:S(2)}, u32[]{:S(2)}) async-start(bf16[32,4,32,128]{3,2,1,0:T(8,128)(2,1)} %bitcast.10), calls=%async_computation | async-start | bytes 2097152 | tf_op jit(solution)/shard_map/all_to_all | solution.py:546
  78.6 21.1 %collective-permute-start.5 = (bf16[1536,128]{1,0:T(8,128)(2,1)S(1)}, bf16[1536,128]{1,0:T(8,128)(2,1)S(1)}, u32[]{:S(2)}, u32[]{:S(2)}) collective-permute-start(bf16[1536,128]{1,0:T(8,128)(2,1)S(1)} %bitcast.94), channel_id=1, source_target_pairs={{0,32},{1,33},{2,34},{3,35},{4,36},{5,37},{6,38},{7,39},{8,40},{9,... | collective-permute-start | bytes 1179656 | tf_op jit(solution)/shard_map/ppermute | solution.py:527
  83.0 3.4 %copy-start.29 = (bf16[2,2,384,128]{3,2,1,0:T(8,128)(2,1)S(1)}, bf16[2,2,384,128]{3,2,1,0:T(8,128)(2,1)}, u32[]{:S(2)}) copy-start(bf16[2,2,384,128]{3,2,1,0:T(8,128)(2,1)} %param.32) | copy-start | bytes 1179652
  83.0 3.5 %copy-start.31 = (bf16[1024,3,128]{2,0,1:T(8,128)(2,1)S(1)}, bf16[1024,3,128]{2,0,1:T(8,128)(2,1)}, u32[]{:S(2)}) copy-start(bf16[1024,3,128]{2,0,1:T(8,128)(2,1)} %param.20) | copy-start | bytes 2359300
  83.1 43.8 %copy-start = (bf16[2,2064,256]{2,1,0:T(8,128)(2,1)}, bf16[2,2064,256]{2,1,0:T(8,128)(2,1)S(1)}, u32[]{:S(2)}) copy-start(bf16[2,2064,256]{2,1,0:T(8,128)(2,1)S(1)} %shard_map.196.after_ref.w0) | copy-start | bytes 6340612
  83.1 4.4 %copy-start.2 = (bf16[128,1024]{1,0:T(8,128)(2,1)S(1)}, bf16[128,1024]{1,0:T(8,128)(2,1)}, u32[]{:S(2)}) copy-start(bf16[128,1024]{1,0:T(8,128)(2,1)} %copy-done.1) | copy-start | bytes 786436
  83.1 118.3 %collective-permute-start.11 = (bf16[2,2064,256]{2,1,0:T(8,128)(2,1)S(1)}, bf16[2,2064,256]{2,1,0:T(8,128)(2,1)}, u32[]{:S(2)}, u32[]{:S(2)}) collective-permute-start(bf16[2,2064,256]{2,1,0:T(8,128)(2,1)S(1)} %shard_map.196.after_ref.w0), channel_id=1, source_target_pairs={{0,64},{64,0},{128,192},{192,128},{256,320},{320,256},{384,448},{4... | collective-permute-start | bytes 6340616 | tf_op jit(solution)/shard_map/ppermute | solution.py:531
  117.3 73.6 %all-to-all-start.1 = ((bf16[32,9,16,128]{3,2,1,0:T(8,128)(2,1)}), bf16[32,9,16,128]{3,2,1,0:T(8,128)(2,1)S(1)}, u32[]{:S(2)}, u32[]{:S(2)}) async-start(bf16[32,9,16,128]{3,2,1,0:T(8,128)(2,1)} %copy-done.6), calls=%async_computation.1 | async-start | bytes 2359296 | tf_op jit(solution)/shard_map/all_to_all | solution.py:574
  127.0 3.1 %copy-start.32 = (bf16[1024,3,128]{2,0,1:T(8,128)(2,1)S(1)}, bf16[1024,3,128]{2,0,1:T(8,128)(2,1)}, u32[]{:S(2)}) copy-start(bf16[1024,3,128]{2,0,1:T(8,128)(2,1)} %param.20) | copy-start | bytes 2359300
  127.0 3.3 %copy-start.15 = (bf16[3,128,1024]{2,1,0:T(8,128)(2,1)S(1)}, bf16[3,128,1024]{2,1,0:T(8,128)(2,1)}, u32[]{:S(2)}) copy-start(bf16[3,128,1024]{2,1,0:T(8,128)(2,1)} %copy-done.14) | copy-start | bytes 2359300
  128.1 26.7 %collective-permute-start.12 = (bf16[2064,256]{1,0:T(8,128)(2,1)S(1)}, bf16[2064,256]{1,0:T(8,128)(2,1)}, u32[]{:S(2)}, u32[]{:S(2)}) collective-permute-start(bf16[2064,256]{1,0:T(8,128)(2,1)S(1)} %get-tuple-element.23), channel_id=1, source_target_pairs={{0,128},{1,129},{2,130},{3,131},{4,132},{5,133},{6,134},{7,135},{8... | collective-permute-start | bytes 3170312 | tf_op jit(solution)/shard_map/ppermute | solution.py:567
  130.3 5.5 %copy-start.33 = (bf16[128,128]{1,0:T(8,128)(2,1)S(1)}, bf16[128,128]{1,0:T(8,128)(2,1)}, u32[]{:S(2)}) copy-start(bf16[128,128]{1,0:T(8,128)(2,1)} %fusion.8) | copy-start | bytes 98308
  130.3 5.5 %copy-start.35 = (bf16[512,128]{1,0:T(8,128)(2,1)S(1)}, bf16[512,128]{1,0:T(8,128)(2,1)}, u32[]{:S(2)}) copy-start(bf16[512,128]{1,0:T(8,128)(2,1)} %fusion.10) | copy-start | bytes 393220
  130.7 5.2 %copy-start.34 = (bf16[512,128]{1,0:T(8,128)(2,1)S(1)}, bf16[512,128]{1,0:T(8,128)(2,1)}, u32[]{:S(2)}) copy-start(bf16[512,128]{1,0:T(8,128)(2,1)} %fusion.4) | copy-start | bytes 393220
  130.7 5.9 %copy-start.30 = (bf16[128,1024]{1,0:T(8,128)(2,1)S(1)}, bf16[128,1024]{1,0:T(8,128)(2,1)}, u32[]{:S(2)}) copy-start(bf16[128,1024]{1,0:T(8,128)(2,1)} %param.21) | copy-start | bytes 786436
  130.7 43.1 %collective-permute-start.13 = (bf16[2064,256]{1,0:T(8,128)(2,1)}, bf16[2064,256]{1,0:T(8,128)(2,1)}, u32[]{:S(2)}, u32[]{:S(2)}) collective-permute-start(bf16[2064,256]{1,0:T(8,128)(2,1)} %get-tuple-element.22), channel_id=1, source_target_pairs={{0,416},{1,417},{2,418},{3,419},{4,420},{5,421},{6,422},{7,423},{8... | collective-permute-start | bytes 3170312 | tf_op jit(solution)/shard_map/ppermute | solution.py:567
  137.3 47.0 %collective-permute-start.7 = (bf16[128,1024]{1,0:T(8,128)(2,1)}, bf16[128,1024]{1,0:T(8,128)(2,1)}, u32[]{:S(2)}, u32[]{:S(2)}) collective-permute-start(bf16[128,1024]{1,0:T(8,128)(2,1)} %broadcast_add_fusion.1), channel_id=1, source_target_pairs={{0,128},{64,192},{128,0},{192,64},{256,384},{320,448},{384,256},{4... | collective-permute-start | bytes 786440 | tf_op jit(solution)/shard_map/ppermute | solution.py:572
  139.2 47.0 %collective-permute-start.8 = (bf16[128,1024]{1,0:T(8,128)(2,1)}, bf16[128,1024]{1,0:T(8,128)(2,1)}, u32[]{:S(2)}, u32[]{:S(2)}) collective-permute-start(bf16[128,1024]{1,0:T(8,128)(2,1)} %broadcast_add_fusion.1), channel_id=1, source_target_pairs={{0,256},{64,320},{128,384},{192,448},{256,0},{320,64},{384,128},{4... | collective-permute-start | bytes 786440 | tf_op jit(solution)/shard_map/ppermute | solution.py:572
  154.8 31.5 %collective-permute-start.9 = (bf16[128,1024]{1,0:T(8,128)(2,1)}, bf16[128,1024]{1,0:T(8,128)(2,1)}, u32[]{:S(2)}, u32[]{:S(2)}) collective-permute-start(bf16[128,1024]{1,0:T(8,128)(2,1)} %broadcast_add_fusion.1), channel_id=1, source_target_pairs={{0,384},{64,448},{128,256},{192,320},{256,128},{320,192},{384,0},{... | collective-permute-start | bytes 786440 | tf_op jit(solution)/shard_map/ppermute | solution.py:572
  160.7 1.6 copy-start.25
  173.8 27.7 %collective-permute-start.14 = (bf16[2064,256]{1,0:T(8,128)(2,1)}, bf16[2064,256]{1,0:T(8,128)(2,1)}, u32[]{:S(2)}, u32[]{:S(2)}) collective-permute-start(bf16[2064,256]{1,0:T(8,128)(2,1)} %get-tuple-element.15.w2), channel_id=1, source_target_pairs={{0,64},{64,0},{128,192},{192,128},{256,320},{320,256},{384,448},{4... | collective-permute-start | bytes 3170312 | tf_op jit(solution)/shard_map/ppermute | solution.py:582
  184.3 17.2 %collective-permute-start.15 = (bf16[2064,256]{1,0:T(8,128)(2,1)}, bf16[2064,256]{1,0:T(8,128)(2,1)}, u32[]{:S(2)}, u32[]{:S(2)}) collective-permute-start(bf16[2064,256]{1,0:T(8,128)(2,1)} %get-tuple-element.16.w3), channel_id=1, source_target_pairs={{0,64},{64,0},{128,192},{192,128},{256,320},{320,256},{384,448},{4... | collective-permute-start | bytes 3170312 | tf_op jit(solution)/shard_map/ppermute | solution.py:582
  188.5 12.9 %collective-permute-start.10 = (bf16[4,128,1024]{2,1,0:T(8,128)(2,1)}, bf16[4,128,1024]{2,1,0:T(8,128)(2,1)}, u32[]{:S(2)}, u32[]{:S(2)}) collective-permute-start(bf16[4,128,1024]{2,1,0:T(8,128)(2,1)} %pad_maximum_fusion.1.half_ref), channel_id=1, source_target_pairs={{0,64},{64,0},{128,192},{192,128},{256,320},{320,256},{384,448},{4... | collective-permute-start | bytes 3145736 | tf_op jit(solution)/shard_map/ppermute | solution.py:580
  196.5 4.5 %copy-start.37 = (bf16[1024]{0:T(1024)(128)(2,1)S(1)}, bf16[1024]{0:T(1024)(128)(2,1)}, u32[]{:S(2)}) copy-start(bf16[1024]{0:T(1024)(128)(2,1)} %param.22) | copy-start | bytes 6148
  196.5 4.5 %copy-start.38 = (bf16[1024]{0:T(1024)(128)(2,1)S(1)}, bf16[1024]{0:T(1024)(128)(2,1)}, u32[]{:S(2)}) copy-start(bf16[1024]{0:T(1024)(128)(2,1)} %param.23) | copy-start | bytes 6148
  196.6 4.5 %copy-start.39 = (bf16[1024]{0:T(1024)(128)(2,1)S(1)}, bf16[1024]{0:T(1024)(128)(2,1)}, u32[]{:S(2)}) copy-start(bf16[1024]{0:T(1024)(128)(2,1)} %param.28) | copy-start | bytes 6148
  196.6 4.6 %copy-start.40 = (bf16[1024]{0:T(1024)(128)(2,1)S(1)}, bf16[1024]{0:T(1024)(128)(2,1)}, u32[]{:S(2)}) copy-start(bf16[1024]{0:T(1024)(128)(2,1)} %param.29) | copy-start | bytes 6148
  196.6 4.6 %copy-start.41 = (bf16[1024]{0:T(1024)(128)(2,1)S(1)}, bf16[1024]{0:T(1024)(128)(2,1)}, u32[]{:S(2)}) copy-start(bf16[1024]{0:T(1024)(128)(2,1)} %param.30) | copy-start | bytes 6148
  196.6 18.1 %copy-start.12 = (bf16[128,1024]{1,0:T(8,128)(2,1)S(1)}, bf16[128,1024]{1,0:T(8,128)(2,1)}, u32[]{:S(2)}) copy-start(bf16[128,1024]{1,0:T(8,128)(2,1)} %copy-done.11) | copy-start | bytes 786436
  196.6 18.1 %copy-start.24 = (s32[288]{0:T(512)S(1)}, s32[288]{0:T(512)}, u32[]{:S(2)}) copy-start(s32[288]{0:T(512)} %shard_map.194.tab) | copy-start | bytes 3460
  196.6 18.1 %all-to-all-start.2 = ((bf16[8,256,128]{2,1,0:T(8,128)(2,1)}), bf16[8,256,128]{2,1,0:T(8,128)(2,1)S(1)}, u32[]{:S(2)}, u32[]{:S(2)}) async-start(bf16[8,256,128]{2,1,0:T(8,128)(2,1)} %bitcast.71), calls=%async_computation.2 | async-start | bytes 1048576 | tf_op jit(solution)/shard_map/all_to_all | solution.py:584
  201.4 23.7 %copy-start.8 = (bf16[1024,128]{1,0:T(8,128)(2,1)S(1)}, bf16[1024,128]{1,0:T(8,128)(2,1)}, u32[]{:S(2)}) copy-start(bf16[1024,128]{1,0:T(8,128)(2,1)} %maximum_convert_fusion.1) | copy-start | bytes 786436
  223.2 15.9 %collective-permute-start.16 = (bf16[128,1024]{1,0:T(8,128)(2,1)S(1)}, bf16[128,1024]{1,0:T(8,128)(2,1)S(1)}, u32[]{:S(2)}, u32[]{:S(2)}) collective-permute-start(bf16[128,1024]{1,0:T(8,128)(2,1)S(1)} %get-tuple-element.19), channel_id=1, source_target_pairs={{0,256},{64,320},{128,384},{192,448},{256,0},{320,64},{384,128},{4... | collective-permute-start | bytes 786440 | tf_op jit(solution)/shard_map/ppermute | solution.py:589
  (16 other events, 14.7 us)
Sparse Core Ops, SparseCore 0:
  64.4 87.9 all-gather.1

commit v10 on v9

--- a/solution.py
+++ b/solution.py
@@ -518,8 +518,9 @@
     roots = roots + jnp.minimum(jnp.abs(tab[:1]), 0).astype(BF16)
     for came in half + [near]:
         roots = roots + zero_after(came)
+    planned = zero_after(roots)
     roots = lax.all_gather(roots, "owner", axis=0, tiled=False, axis_index_groups=groups)
-    other = lax.ppermute(jnp.stack(half), "blk", swap)
+    other = lax.ppermute(jnp.stack(half) + planned, "blk", swap)
     half = jnp.stack([tok] + half)
     roots = roots.reshape(NX, NY, NZ, 2, tenants, root_per, LANES)
 

time: 249 us -> 233 us (0.936)
  waiting for transfers between devices: 71.3 us -> 48.1 us
  starting transfers between devices: 85.9 us -> 91.3 us
    ppermute x3, waiting for transfers between devices: 17.1 us -> 0.01 us  [on_device(): lax.ppermute(tok, 'blk', xor_pairs(N_BLK, 2 * k))]
    ppermute x1, starting transfers between devices: 1.92 us -> 7.99 us  [on_device(): node_far = lax.ppermute(node_rows, 'owner', xor_pairs(n_owner, NX * NY))]
    all_to_all x1, waiting for transfers between devices: 5.64 us -> 0.66 us  [on_device(): lax.all_to_all(outgoing, 'owner', split_axis=0, concat_axis=0, axis_index...]
    ppermute x1, starting transfers between devices: 9.1 us -> 5.26 us  [on_device(): lax.ppermute(roots, 'owner', xor_pairs(n_owner, NX * NY))]
    ppermute x3, starting transfers between devices: 12.7 us -> 15.5 us  [on_device(): lax.ppermute(tok, 'blk', xor_pairs(N_BLK, 2 * k))]
    ppermute x2, starting transfers between devices: 6.61 us -> 9.17 us  [to_neighbour(): return lax.ppermute(sent, ('blk', 'owner'), pairs)]
  transfers between devices with their start and end apart: 21 -> 21, of which waited for: 7 -> 6; matrix products, arithmetic and copies ran while one was open for 8% -> 8% of each run, Pallas kernels for 10% -> 11%
where the time goes in v10:
time: 233 us; the launch traced here: 231 us
  starting transfers between devices  91.3 us (39%)
  waiting for transfers between devices  48.1 us (21%)
  Pallas kernels  33.3 us (14%)
  local copies, waits for them, and re-layouts  23.5 us (10%)
  between operations  19.6 us (8%)
  other arithmetic  11.4 us (5%)
  matrix products  3.99 us (2%)
    unnamed x86, local copies, waits for them, and re-layouts  15.9 us
    ppermute x3, starting transfers between devices, on_device(): lax.ppermute(tok, 'blk', xor_pairs(N_BLK, 2 * k))  15.5 us
    all_to_all x1, waiting for transfers between devices, on_device(): lax.all_to_all(send.reshape(N_BLK, 2 * own_rows, cols), 'blk', split_axis...  13.2 us
    ppermute x2, waiting for transfers between devices, to_neighbour(): return lax.ppermute(sent, ('blk', 'owner'), pairs)  12.5 us
    ppermute x1, waiting for transfers between devices, on_device(): lax.ppermute(down_far, 'blk', xor_pairs(N_BLK, N_BLK // 2)).astype(F32)  12.2 us
    ppermute x2, starting transfers between devices, on_device(): pack_last = [lax.ppermute(part, 'blk', swap) for part in pack_next]  11.7 us
    all_to_all x1, starting transfers between devices, on_device(): lax.all_to_all(outgoing, 'owner', split_axis=0, concat_axis=0, axis_index...  9.95 us
    ppermute x2, starting transfers between devices, to_neighbour(): return lax.ppermute(sent, ('blk', 'owner'), pairs)  9.17 us
  transfers between devices with their start and end apart: 21, of which 6 were waited for; matrix products, arithmetic and copies ran while one was open for 8% of the time, Pallas kernels for 11%

profile of v10, /device:TPU:1, one launch (start us, length us, event | category | flops | bytes accessed | tf_op | source)
XLA Modules:
  0.0 231.3 jit_solution(11895681979196446657)
XLA Ops:
  7.2 8.4 %collective-permute-start.2 = (bf16[128,1024]{1,0:T(8,128)(2,1)}, bf16[128,1024]{1,0:T(8,128)(2,1)S(1)}, u32[]{:S(2)}, u32[]{:S(2)}) collective-permute-start(bf16[128,1024]{1,0:T(8,128)(2,1)} %bitcast.85), channel_id=1, source_target_pairs={{0,384},{64,448},{128,256},{192,320},{256,128},{320,192},{384,0},{... | collective-permute-start | bytes 786440 | tf_op jit(solution)/shard_map/ppermute | solution.py:511
  15.7 2.9 %collective-permute-start.3 = (bf16[128,1024]{1,0:T(8,128)(2,1)}, bf16[128,1024]{1,0:T(8,128)(2,1)S(1)}, u32[]{:S(2)}, u32[]{:S(2)}) collective-permute-start(bf16[128,1024]{1,0:T(8,128)(2,1)} %bitcast.86), channel_id=1, source_target_pairs={{0,64},{64,0},{128,192},{192,128},{256,320},{320,256},{384,448},{4... | collective-permute-start | bytes 786440 | tf_op jit(solution)/shard_map/ppermute | solution.py:510
  18.6 1.9 collective-permute-start.1
  20.5 5.1 %collective-permute-start = (bf16[128,1024]{1,0:T(8,128)(2,1)}, bf16[128,1024]{1,0:T(8,128)(2,1)S(1)}, u32[]{:S(2)}, u32[]{:S(2)}) collective-permute-start(bf16[128,1024]{1,0:T(8,128)(2,1)} %bitcast.88), channel_id=1, source_target_pairs={{0,128},{64,192},{128,0},{192,64},{256,384},{320,448},{384,256},{4... | collective-permute-start | bytes 786440 | tf_op jit(solution)/shard_map/ppermute | solution.py:511
  25.6 5.3 %collective-permute-start.4 = (bf16[128,128]{1,0:T(8,128)(2,1)}, bf16[128,128]{1,0:T(8,128)(2,1)S(1)}, u32[]{:S(2)}, u32[]{:S(2)}) collective-permute-start(bf16[128,128]{1,0:T(8,128)(2,1)} %bitcast.100), channel_id=1, source_target_pairs={{0,32},{1,33},{2,34},{3,35},{4,36},{5,37},{6,38},{7,39},{8,40},{9,... | collective-permute-start | bytes 98312 | tf_op jit(solution)/shard_map/ppermute | solution.py:516
  31.6 3.9 %shard_map.194.tab = s32[288]{0:T(512)} custom-call(s32[4]{0:T(128)} %pad_add_fusion.coords, s32[32]{0:T(128)} %leaf_of.1, s32[128]{0:T(128)} %parent.1, s32[128]{0:T(128)} %place.1, s32[128]{0:T(128)} %length.1, s32[4]{0:T(128)} %root_len.1), custom_call_target="tpu_custom_call" | custom-call | flops 1048576 | bytes 4096 | tf_op jit(solution)/shard_map/pallas_call | solution.py:139
  35.5 1.2 slice.33
  44.3 1.0 maximum_add_fusion
  45.2 2.7 %collective-permute-start.5 = (bf16[3,128,1024]{2,1,0:T(8,128)(2,1)}, bf16[3,128,1024]{2,1,0:T(8,128)(2,1)S(1)}, u32[]{:S(2)}, u32[]{:S(2)}) collective-permute-start(bf16[3,128,1024]{2,1,0:T(8,128)(2,1)} %maximum_add_fusion), channel_id=1, source_target_pairs={{0,64},{64,0},{128,192},{192,128},{256,320},{320,256},{384,448},{4... | collective-permute-start | bytes 2359304 | tf_op jit(solution)/shard_map/ppermute | solution.py:523
  48.7 1.0 slice_bitcast_fusion.w_ref
  50.3 2.5 %shard_map.195 = (bf16[32,32,128]{2,1,0:T(8,128)(2,1)S(1)}, bf16[128,32,128]{2,1,0:T(8,128)(2,1)}) custom-call(s32[288]{0:T(512)S(1)} %copy-done.20, bf16[4,128,1024]{2,1,0:T(8,128)(2,1)S(1)} %pad_maximum_fusion.half_ref, bf16[128,1024]{1,0:T(8,128)(2,1)S(1)} %collective-permute-done.3.near_ref, bf16[3,128,1024]{2,1,0:T(8,128)(2,1)S(1)} %collective-permute-done.5.other_ref, ...), custom_call_target="tpu_custom_call" | custom-call | flops 268435456 | bytes 4194304 | tf_op jit(solution)/shard_map/pallas_call | solution.py:173
  52.9 9.9 %all-to-all-start = ((bf16[32,4,32,128]{3,2,1,0:T(8,128)(2,1)}), bf16[32,4,32,128]{3,2,1,0:T(8,128)(2,1)}, u32[]{:S(2)}, u32[]{:S(2)}) async-start(bf16[32,4,32,128]{3,2,1,0:T(8,128)(2,1)} %bitcast.20), calls=%async_computation | async-start | bytes 2097152 | tf_op jit(solution)/shard_map/all_to_all | solution.py:547
  63.0 8.0 %collective-permute-start.6 = (bf16[1536,128]{1,0:T(8,128)(2,1)S(1)}, bf16[1536,128]{1,0:T(8,128)(2,1)S(1)}, u32[]{:S(2)}, u32[]{:S(2)}) collective-permute-start(bf16[1536,128]{1,0:T(8,128)(2,1)S(1)} %bitcast.98), channel_id=1, source_target_pairs={{0,32},{1,33},{2,34},{3,35},{4,36},{5,37},{6,38},{7,39},{8,40},{9,... | collective-permute-start | bytes 1179656 | tf_op jit(solution)/shard_map/ppermute | solution.py:528
  71.0 1.2 copy-done.9
  72.2 1.2 copy-done.10
  73.6 2.9 %collective-permute-start.11 = (bf16[2,2064,256]{2,1,0:T(8,128)(2,1)S(1)}, bf16[2,2064,256]{2,1,0:T(8,128)(2,1)}, u32[]{:S(2)}, u32[]{:S(2)}) collective-permute-start(bf16[2,2064,256]{2,1,0:T(8,128)(2,1)S(1)} %shard_map.196.after_ref.w0), channel_id=1, source_target_pairs={{0,64},{64,0},{128,192},{192,128},{256,320},{320,256},{384,448},{4... | collective-permute-start | bytes 6340616 | tf_op jit(solution)/shard_map/ppermute | solution.py:532
  76.6 1.1 fusion.10
  78.5 1.1 fusion.4
  79.6 9.1 %collective-permute-done.6 = bf16[1536,128]{1,0:T(8,128)(2,1)S(1)} collective-permute-done((bf16[1536,128]{1,0:T(8,128)(2,1)S(1)}, bf16[1536,128]{1,0:T(8,128)(2,1)S(1)}, u32[]{:S(2)}, u32[]{:S(2)}) %collective-permute-start.6) | collective-permute-done | bytes 393248 | tf_op jit(solution)/shard_map/ppermute | solution.py:528
  90.3 1.1 copy-done.13
  92.1 8.1 %shard_map.197 = bf16[32,9,16,128]{3,2,1,0:T(8,128)(2,1)S(1)} custom-call(s32[288]{0:T(512)S(1)} %copy-done.21, bf16[32,4,32,128]{3,2,1,0:T(8,128)(2,1)} %all-to-all-done.q_ref, bf16[2,2,2,384,128]{4,3,2,1,0:T(8,128)(2,1)S(1)} %copy-done.13, bf16[2,2064,256]{2,1,0:T(8,128)(2,1)S(1)} %shard_map.196.after_ref.w0), custom_call_target="tpu_custom_call" | custom-call | flops 2147483648 | bytes 4194304 | tf_op jit(solution)/shard_map/pallas_call | solution.py:264
  100.3 1.1 copy-done.6
  101.3 8.1 %all-to-all-start.1 = ((bf16[32,9,16,128]{3,2,1,0:T(8,128)(2,1)}), bf16[32,9,16,128]{3,2,1,0:T(8,128)(2,1)S(1)}, u32[]{:S(2)}, u32[]{:S(2)}) async-start(bf16[32,9,16,128]{3,2,1,0:T(8,128)(2,1)} %copy-done.6), calls=%async_computation.1 | async-start | bytes 2359296 | tf_op jit(solution)/shard_map/all_to_all | solution.py:575
  109.4 1.2 slice.50
  111.3 1.1 add_bitcast_fusion
  112.4 2.4 %collective-permute-start.12 = (bf16[2064,256]{1,0:T(8,128)(2,1)S(1)}, bf16[2064,256]{1,0:T(8,128)(2,1)}, u32[]{:S(2)}, u32[]{:S(2)}) collective-permute-start(bf16[2064,256]{1,0:T(8,128)(2,1)S(1)} %get-tuple-element.23), channel_id=1, source_target_pairs={{0,128},{1,129},{2,130},{3,131},{4,132},{5,133},{6,134},{7,135},{8... | collective-permute-start | bytes 3170312 | tf_op jit(solution)/shard_map/ppermute | solution.py:568
  115.5 6.8 %collective-permute-start.13 = (bf16[2064,256]{1,0:T(8,128)(2,1)}, bf16[2064,256]{1,0:T(8,128)(2,1)}, u32[]{:S(2)}, u32[]{:S(2)}) collective-permute-start(bf16[2064,256]{1,0:T(8,128)(2,1)} %get-tuple-element.22), channel_id=1, source_target_pairs={{0,416},{1,417},{2,418},{3,419},{4,420},{5,421},{6,422},{7,423},{8... | collective-permute-start | bytes 3170312 | tf_op jit(solution)/shard_map/ppermute | solution.py:568
  124.2 1.9 collective-permute-start.7
  126.1 3.3 %collective-permute-start.8 = (bf16[128,1024]{1,0:T(8,128)(2,1)}, bf16[128,1024]{1,0:T(8,128)(2,1)}, u32[]{:S(2)}, u32[]{:S(2)}) collective-permute-start(bf16[128,1024]{1,0:T(8,128)(2,1)} %broadcast_add_fusion.1), channel_id=1, source_target_pairs={{0,256},{64,320},{128,384},{192,448},{256,0},{320,64},{384,128},{4... | collective-permute-start | bytes 786440 | tf_op jit(solution)/shard_map/ppermute | solution.py:573
  129.4 12.5 %collective-permute-done.12.refs_0_ = bf16[2064,256]{1,0:T(8,128)(2,1)} collective-permute-done((bf16[2064,256]{1,0:T(8,128)(2,1)S(1)}, bf16[2064,256]{1,0:T(8,128)(2,1)}, u32[]{:S(2)}, u32[]{:S(2)}) %collective-permute-start.12) | collective-permute-done | bytes 1056800 | tf_op jit(solution)/shard_map/ppermute | solution.py:568
  141.9 1.9 collective-permute-start.9
  143.9 0.9 copy-done.7
  145.5 1.6 copy-done.25
  147.1 0.9 copy-done.27
  148.1 8.9 %shard_map.198 = (f32[32,32,128]{2,1,0:T(8,128)S(1)}, f32[32,32,128]{2,1,0:T(8,128)S(1)}) custom-call(s32[288]{0:T(512)S(1)} %copy-done.22, bf16[32,32,128]{2,1,0:T(8,128)(2,1)S(1)} %copy-done.27, bf16[32,32,128]{2,1,0:T(8,128)(2,1)S(1)} %bitcast.77, bf16[32,32,128]{2,1,0:T(8,128)(2,1)S(1)} %bitcast.79, bf16[4,8,2,2,4,16,128]{6,5,4,3,2,1,0:T(8,128)(2,1)S(1)} %bitcast.91), custom_call_target="tpu_custom_call" | custom-call | flops 4294967296 | bytes 4194304 | tf_op jit(solution)/shard_map/pallas_call | solution.py:332
  158.6 9.8 %collective-permute-start.14 = (bf16[2064,256]{1,0:T(8,128)(2,1)}, bf16[2064,256]{1,0:T(8,128)(2,1)}, u32[]{:S(2)}, u32[]{:S(2)}) collective-permute-start(bf16[2064,256]{1,0:T(8,128)(2,1)} %get-tuple-element.15.w2), channel_id=1, source_target_pairs={{0,64},{64,0},{128,192},{192,128},{256,320},{320,256},{384,448},{4... | collective-permute-start | bytes 3170312 | tf_op jit(solution)/shard_map/ppermute | solution.py:583
  168.4 1.9 collective-permute-start.15
  170.3 2.3 pad_maximum_fusion.1.half_ref
  172.6 2.4 %collective-permute-start.10 = (bf16[4,128,1024]{2,1,0:T(8,128)(2,1)}, bf16[4,128,1024]{2,1,0:T(8,128)(2,1)}, u32[]{:S(2)}, u32[]{:S(2)}) collective-permute-start(bf16[4,128,1024]{2,1,0:T(8,128)(2,1)} %pad_maximum_fusion.1.half_ref), channel_id=1, source_target_pairs={{0,64},{64,0},{128,192},{192,128},{256,320},{320,256},{384,448},{4... | collective-permute-start | bytes 3145736 | tf_op jit(solution)/shard_map/ppermute | solution.py:581
  175.0 1.0 copy-done.4
  176.1 1.0 copy-done.17
  177.8 2.1 shard_map.199
  180.7 3.8 %all-to-all-start.2 = ((bf16[8,256,128]{2,1,0:T(8,128)(2,1)}), bf16[8,256,128]{2,1,0:T(8,128)(2,1)S(1)}, u32[]{:S(2)}, u32[]{:S(2)}) async-start(bf16[8,256,128]{2,1,0:T(8,128)(2,1)} %bitcast.75), calls=%async_computation.2 | async-start | bytes 1048576 | tf_op jit(solution)/shard_map/all_to_all | solution.py:585
  185.6 13.2 %all-to-all-done.2.attn_ref = bf16[8,256,128]{2,1,0:T(8,128)(2,1)S(1)} async-done(((bf16[8,256,128]{2,1,0:T(8,128)(2,1)}), bf16[8,256,128]{2,1,0:T(8,128)(2,1)S(1)}, u32[]{:S(2)}, u32[]{:S(2)}) %all-to-all-start.2) | async-done | bytes 524320 | tf_op jit(solution)/shard_map/all_to_all | solution.py:585
  198.8 0.9 copy-done.19
  199.7 7.5 %shard_map.201 = (bf16[128,1024]{1,0:T(8,128)(2,1)S(1)}, f32[128,1024]{1,0:T(8,128)S(1)}, bf16[128,1024]{1,0:T(8,128)(2,1)S(1)}) custom-call(s32[288]{0:T(512)S(1)} %copy-done.24, bf16[8,256,128]{2,1,0:T(8,128)(2,1)S(1)} %all-to-all-done.2.attn_ref, bf16[4,128,1024]{2,1,0:T(8,128)(2,1)} %pad_maximum_fusion.1.half_ref, ...), custom_call_target="tpu_custom_call" | custom-call | flops 3221225472 | bytes 12582912 | tf_op jit(solution)/shard_map/pallas_call | solution.py:450
  207.3 1.9 collective-permute-start.16
  210.9 12.2 %collective-permute-done.16 = bf16[128,1024]{1,0:T(8,128)(2,1)S(1)} collective-permute-done((bf16[128,1024]{1,0:T(8,128)(2,1)S(1)}, bf16[128,1024]{1,0:T(8,128)(2,1)S(1)}, u32[]{:S(2)}, u32[]{:S(2)}) %collective-permute-start.16) | collective-permute-done | bytes 262176 | tf_op jit(solution)/shard_map/ppermute | solution.py:590
  (138 shorter events, 19.0 us)
Async XLA Ops:
  7.2 40.8 %copy-start.36 = (bf16[2,4,16,128]{3,2,1,0:T(8,128)(2,1)S(1)}, bf16[2,4,16,128]{3,2,1,0:T(8,128)(2,1)}, u32[]{:S(2)}) copy-start(bf16[2,4,16,128]{3,2,1,0:T(8,128)(2,1)} %param.31) | copy-start | bytes 98308
  7.2 136.7 %all-gather.2.cloned.1.call-start = ((), (), s32[]{:S(2)}) async-start(), calls=%async_computation.3 | async-start | bytes 2162688 | tf_op jit(solution)/shard_map/all_gather | solution.py:522
  7.2 30.1 %collective-permute-start.2 = (bf16[128,1024]{1,0:T(8,128)(2,1)}, bf16[128,1024]{1,0:T(8,128)(2,1)S(1)}, u32[]{:S(2)}, u32[]{:S(2)}) collective-permute-start(bf16[128,1024]{1,0:T(8,128)(2,1)} %bitcast.85), channel_id=1, source_target_pairs={{0,384},{64,448},{128,256},{192,320},{256,128},{320,192},{384,0},{... | collective-permute-start | bytes 786440 | tf_op jit(solution)/shard_map/ppermute | solution.py:511
  15.7 22.9 %collective-permute-start.3 = (bf16[128,1024]{1,0:T(8,128)(2,1)}, bf16[128,1024]{1,0:T(8,128)(2,1)S(1)}, u32[]{:S(2)}, u32[]{:S(2)}) collective-permute-start(bf16[128,1024]{1,0:T(8,128)(2,1)} %bitcast.86), channel_id=1, source_target_pairs={{0,64},{64,0},{128,192},{192,128},{256,320},{320,256},{384,448},{4... | collective-permute-start | bytes 786440 | tf_op jit(solution)/shard_map/ppermute | solution.py:510
  18.6 21.2 %collective-permute-start.1 = (bf16[128,1024]{1,0:T(8,128)(2,1)}, bf16[128,1024]{1,0:T(8,128)(2,1)S(1)}, u32[]{:S(2)}, u32[]{:S(2)}) collective-permute-start(bf16[128,1024]{1,0:T(8,128)(2,1)} %bitcast.87), channel_id=1, source_target_pairs={{0,256},{64,320},{128,384},{192,448},{256,0},{320,64},{384,128},{4... | collective-permute-start | bytes 786440 | tf_op jit(solution)/shard_map/ppermute | solution.py:511
  20.5 20.6 %collective-permute-start = (bf16[128,1024]{1,0:T(8,128)(2,1)}, bf16[128,1024]{1,0:T(8,128)(2,1)S(1)}, u32[]{:S(2)}, u32[]{:S(2)}) collective-permute-start(bf16[128,1024]{1,0:T(8,128)(2,1)} %bitcast.88), channel_id=1, source_target_pairs={{0,128},{64,192},{128,0},{192,64},{256,384},{320,448},{384,256},{4... | collective-permute-start | bytes 786440 | tf_op jit(solution)/shard_map/ppermute | solution.py:511
  25.6 16.7 %collective-permute-start.4 = (bf16[128,128]{1,0:T(8,128)(2,1)}, bf16[128,128]{1,0:T(8,128)(2,1)S(1)}, u32[]{:S(2)}, u32[]{:S(2)}) collective-permute-start(bf16[128,128]{1,0:T(8,128)(2,1)} %bitcast.100), channel_id=1, source_target_pairs={{0,32},{1,33},{2,34},{3,35},{4,36},{5,37},{6,38},{7,39},{8,40},{9,... | collective-permute-start | bytes 98312 | tf_op jit(solution)/shard_map/ppermute | solution.py:516
  38.5 11.5 %copy-start.1 = (bf16[128,1024]{1,0:T(8,128)(2,1)}, bf16[128,1024]{1,0:T(8,128)(2,1)S(1)}, u32[]{:S(2)}) copy-start(bf16[128,1024]{1,0:T(8,128)(2,1)S(1)} %collective-permute-done.3.near_ref) | copy-start | bytes 786436
  39.8 9.8 %copy-start.11 = (bf16[128,1024]{1,0:T(8,128)(2,1)}, bf16[128,1024]{1,0:T(8,128)(2,1)S(1)}, u32[]{:S(2)}) copy-start(bf16[128,1024]{1,0:T(8,128)(2,1)S(1)} %collective-permute-done.1.tok_b) | copy-start | bytes 786436
  44.2 5.4 %copy-start.18 = (bf16[4,32,1024]{2,1,0:T(8,128)(2,1)S(1)}, bf16[4,32,1024]{2,1,0:T(8,128)(2,1)}, u32[]{:S(2)}) copy-start(bf16[4,32,1024]{2,1,0:T(8,128)(2,1)} %param.19) | copy-start | bytes 786436
  45.2 4.9 %collective-permute-start.5 = (bf16[3,128,1024]{2,1,0:T(8,128)(2,1)}, bf16[3,128,1024]{2,1,0:T(8,128)(2,1)S(1)}, u32[]{:S(2)}, u32[]{:S(2)}) collective-permute-start(bf16[3,128,1024]{2,1,0:T(8,128)(2,1)} %maximum_add_fusion), channel_id=1, source_target_pairs={{0,64},{64,0},{128,192},{192,128},{256,320},{320,256},{384,448},{4... | collective-permute-start | bytes 2359304 | tf_op jit(solution)/shard_map/ppermute | solution.py:523
  50.3 2.5 %copy-start.14 = (bf16[3,128,1024]{2,1,0:T(8,128)(2,1)}, bf16[3,128,1024]{2,1,0:T(8,128)(2,1)S(1)}, u32[]{:S(2)}) copy-start(bf16[3,128,1024]{2,1,0:T(8,128)(2,1)S(1)} %collective-permute-done.5.other_ref) | copy-start | bytes 2359300
  52.8 10.0 %copy-start.26 = (bf16[32,32,128]{2,1,0:T(8,128)(2,1)}, bf16[32,32,128]{2,1,0:T(8,128)(2,1)S(1)}, u32[]{:S(2)}) copy-start(bf16[32,32,128]{2,1,0:T(8,128)(2,1)S(1)} %get-tuple-element.12.q_ref) | copy-start | bytes 786436
  52.8 10.1 %copy-start.42 = (bf16[512]{0:T(512)(128)(2,1)S(1)}, bf16[512]{0:T(512)(128)(2,1)}, u32[]{:S(2)}) copy-start(bf16[512]{0:T(512)(128)(2,1)} %param.26) | copy-start | bytes 3076
  52.8 10.1 %copy-start.28 = (bf16[2,2,384,128]{3,2,1,0:T(8,128)(2,1)S(1)}, bf16[2,2,384,128]{3,2,1,0:T(8,128)(2,1)}, u32[]{:S(2)}) copy-start(bf16[2,2,384,128]{3,2,1,0:T(8,128)(2,1)} %param.32) | copy-start | bytes 1179652
  52.9 37.5 %all-to-all-start = ((bf16[32,4,32,128]{3,2,1,0:T(8,128)(2,1)}), bf16[32,4,32,128]{3,2,1,0:T(8,128)(2,1)}, u32[]{:S(2)}, u32[]{:S(2)}) async-start(bf16[32,4,32,128]{3,2,1,0:T(8,128)(2,1)} %bitcast.20), calls=%async_computation | async-start | bytes 2097152 | tf_op jit(solution)/shard_map/all_to_all | solution.py:547
  63.0 25.7 %collective-permute-start.6 = (bf16[1536,128]{1,0:T(8,128)(2,1)S(1)}, bf16[1536,128]{1,0:T(8,128)(2,1)S(1)}, u32[]{:S(2)}, u32[]{:S(2)}) collective-permute-start(bf16[1536,128]{1,0:T(8,128)(2,1)S(1)} %bitcast.98), channel_id=1, source_target_pairs={{0,32},{1,33},{2,34},{3,35},{4,36},{5,37},{6,38},{7,39},{8,40},{9,... | collective-permute-start | bytes 1179656 | tf_op jit(solution)/shard_map/ppermute | solution.py:528
  73.4 3.1 %copy-start.29 = (bf16[2,2,384,128]{3,2,1,0:T(8,128)(2,1)S(1)}, bf16[2,2,384,128]{3,2,1,0:T(8,128)(2,1)}, u32[]{:S(2)}) copy-start(bf16[2,2,384,128]{3,2,1,0:T(8,128)(2,1)} %param.32) | copy-start | bytes 1179652
  73.4 3.1 %copy-start.31 = (bf16[1024,3,128]{2,0,1:T(8,128)(2,1)S(1)}, bf16[1024,3,128]{2,0,1:T(8,128)(2,1)}, u32[]{:S(2)}) copy-start(bf16[1024,3,128]{2,0,1:T(8,128)(2,1)} %param.20) | copy-start | bytes 2359300
  73.6 37.7 %copy-start = (bf16[2,2064,256]{2,1,0:T(8,128)(2,1)}, bf16[2,2064,256]{2,1,0:T(8,128)(2,1)S(1)}, u32[]{:S(2)}) copy-start(bf16[2,2064,256]{2,1,0:T(8,128)(2,1)S(1)} %shard_map.196.after_ref.w0) | copy-start | bytes 6340612
  73.6 4.1 %copy-start.2 = (bf16[128,1024]{1,0:T(8,128)(2,1)S(1)}, bf16[128,1024]{1,0:T(8,128)(2,1)}, u32[]{:S(2)}) copy-start(bf16[128,1024]{1,0:T(8,128)(2,1)} %copy-done.1) | copy-start | bytes 786436
  73.6 111.9 %collective-permute-start.11 = (bf16[2,2064,256]{2,1,0:T(8,128)(2,1)S(1)}, bf16[2,2064,256]{2,1,0:T(8,128)(2,1)}, u32[]{:S(2)}, u32[]{:S(2)}) collective-permute-start(bf16[2,2064,256]{2,1,0:T(8,128)(2,1)S(1)} %shard_map.196.after_ref.w0), channel_id=1, source_target_pairs={{0,64},{64,0},{128,192},{192,128},{256,320},{320,256},{384,448},{4... | collective-permute-start | bytes 6340616 | tf_op jit(solution)/shard_map/ppermute | solution.py:532
  101.3 73.7 %all-to-all-start.1 = ((bf16[32,9,16,128]{3,2,1,0:T(8,128)(2,1)}), bf16[32,9,16,128]{3,2,1,0:T(8,128)(2,1)S(1)}, u32[]{:S(2)}, u32[]{:S(2)}) async-start(bf16[32,9,16,128]{3,2,1,0:T(8,128)(2,1)} %copy-done.6), calls=%async_computation.1 | async-start | bytes 2359296 | tf_op jit(solution)/shard_map/all_to_all | solution.py:575
  111.3 3.5 %copy-start.32 = (bf16[1024,3,128]{2,0,1:T(8,128)(2,1)S(1)}, bf16[1024,3,128]{2,0,1:T(8,128)(2,1)}, u32[]{:S(2)}) copy-start(bf16[1024,3,128]{2,0,1:T(8,128)(2,1)} %param.20) | copy-start | bytes 2359300
  111.3 3.8 %copy-start.15 = (bf16[3,128,1024]{2,1,0:T(8,128)(2,1)S(1)}, bf16[3,128,1024]{2,1,0:T(8,128)(2,1)}, u32[]{:S(2)}) copy-start(bf16[3,128,1024]{2,1,0:T(8,128)(2,1)} %copy-done.14) | copy-start | bytes 2359300
  112.4 29.5 %collective-permute-start.12 = (bf16[2064,256]{1,0:T(8,128)(2,1)S(1)}, bf16[2064,256]{1,0:T(8,128)(2,1)}, u32[]{:S(2)}, u32[]{:S(2)}) collective-permute-start(bf16[2064,256]{1,0:T(8,128)(2,1)S(1)} %get-tuple-element.23), channel_id=1, source_target_pairs={{0,128},{1,129},{2,130},{3,131},{4,132},{5,133},{6,134},{7,135},{8... | collective-permute-start | bytes 3170312 | tf_op jit(solution)/shard_map/ppermute | solution.py:568
  115.1 7.6 %copy-start.33 = (bf16[128,128]{1,0:T(8,128)(2,1)S(1)}, bf16[128,128]{1,0:T(8,128)(2,1)}, u32[]{:S(2)}) copy-start(bf16[128,128]{1,0:T(8,128)(2,1)} %fusion.8) | copy-start | bytes 98308
  115.1 7.6 %copy-start.35 = (bf16[512,128]{1,0:T(8,128)(2,1)S(1)}, bf16[512,128]{1,0:T(8,128)(2,1)}, u32[]{:S(2)}) copy-start(bf16[512,128]{1,0:T(8,128)(2,1)} %fusion.10) | copy-start | bytes 393220
  115.5 7.2 %copy-start.34 = (bf16[512,128]{1,0:T(8,128)(2,1)S(1)}, bf16[512,128]{1,0:T(8,128)(2,1)}, u32[]{:S(2)}) copy-start(bf16[512,128]{1,0:T(8,128)(2,1)} %fusion.4) | copy-start | bytes 393220
  115.5 8.0 %copy-start.30 = (bf16[128,1024]{1,0:T(8,128)(2,1)S(1)}, bf16[128,1024]{1,0:T(8,128)(2,1)}, u32[]{:S(2)}) copy-start(bf16[128,1024]{1,0:T(8,128)(2,1)} %param.21) | copy-start | bytes 786436
  115.5 43.1 %collective-permute-start.13 = (bf16[2064,256]{1,0:T(8,128)(2,1)}, bf16[2064,256]{1,0:T(8,128)(2,1)}, u32[]{:S(2)}, u32[]{:S(2)}) collective-permute-start(bf16[2064,256]{1,0:T(8,128)(2,1)} %get-tuple-element.22), channel_id=1, source_target_pairs={{0,416},{1,417},{2,418},{3,419},{4,420},{5,421},{6,422},{7,423},{8... | collective-permute-start | bytes 3170312 | tf_op jit(solution)/shard_map/ppermute | solution.py:568
  124.2 44.2 %collective-permute-start.7 = (bf16[128,1024]{1,0:T(8,128)(2,1)}, bf16[128,1024]{1,0:T(8,128)(2,1)}, u32[]{:S(2)}, u32[]{:S(2)}) collective-permute-start(bf16[128,1024]{1,0:T(8,128)(2,1)} %broadcast_add_fusion.1), channel_id=1, source_target_pairs={{0,128},{64,192},{128,0},{192,64},{256,384},{320,448},{384,256},{4... | collective-permute-start | bytes 786440 | tf_op jit(solution)/shard_map/ppermute | solution.py:573
  126.1 44.2 %collective-permute-start.8 = (bf16[128,1024]{1,0:T(8,128)(2,1)}, bf16[128,1024]{1,0:T(8,128)(2,1)}, u32[]{:S(2)}, u32[]{:S(2)}) collective-permute-start(bf16[128,1024]{1,0:T(8,128)(2,1)} %broadcast_add_fusion.1), channel_id=1, source_target_pairs={{0,256},{64,320},{128,384},{192,448},{256,0},{320,64},{384,128},{4... | collective-permute-start | bytes 786440 | tf_op jit(solution)/shard_map/ppermute | solution.py:573
  141.9 28.4 %collective-permute-start.9 = (bf16[128,1024]{1,0:T(8,128)(2,1)}, bf16[128,1024]{1,0:T(8,128)(2,1)}, u32[]{:S(2)}, u32[]{:S(2)}) collective-permute-start(bf16[128,1024]{1,0:T(8,128)(2,1)} %broadcast_add_fusion.1), channel_id=1, source_target_pairs={{0,384},{64,448},{128,256},{192,320},{256,128},{320,192},{384,0},{... | collective-permute-start | bytes 786440 | tf_op jit(solution)/shard_map/ppermute | solution.py:573
  145.5 1.6 copy-start.25
  158.6 26.9 %collective-permute-start.14 = (bf16[2064,256]{1,0:T(8,128)(2,1)}, bf16[2064,256]{1,0:T(8,128)(2,1)}, u32[]{:S(2)}, u32[]{:S(2)}) collective-permute-start(bf16[2064,256]{1,0:T(8,128)(2,1)} %get-tuple-element.15.w2), channel_id=1, source_target_pairs={{0,64},{64,0},{128,192},{192,128},{256,320},{320,256},{384,448},{4... | collective-permute-start | bytes 3170312 | tf_op jit(solution)/shard_map/ppermute | solution.py:583
  168.4 17.2 %collective-permute-start.15 = (bf16[2064,256]{1,0:T(8,128)(2,1)}, bf16[2064,256]{1,0:T(8,128)(2,1)}, u32[]{:S(2)}, u32[]{:S(2)}) collective-permute-start(bf16[2064,256]{1,0:T(8,128)(2,1)} %get-tuple-element.16.w3), channel_id=1, source_target_pairs={{0,64},{64,0},{128,192},{192,128},{256,320},{320,256},{384,448},{4... | collective-permute-start | bytes 3170312 | tf_op jit(solution)/shard_map/ppermute | solution.py:583
  172.6 12.9 %collective-permute-start.10 = (bf16[4,128,1024]{2,1,0:T(8,128)(2,1)}, bf16[4,128,1024]{2,1,0:T(8,128)(2,1)}, u32[]{:S(2)}, u32[]{:S(2)}) collective-permute-start(bf16[4,128,1024]{2,1,0:T(8,128)(2,1)} %pad_maximum_fusion.1.half_ref), channel_id=1, source_target_pairs={{0,64},{64,0},{128,192},{192,128},{256,320},{320,256},{384,448},{4... | collective-permute-start | bytes 3145736 | tf_op jit(solution)/shard_map/ppermute | solution.py:581
  180.6 4.5 %copy-start.37 = (bf16[1024]{0:T(1024)(128)(2,1)S(1)}, bf16[1024]{0:T(1024)(128)(2,1)}, u32[]{:S(2)}) copy-start(bf16[1024]{0:T(1024)(128)(2,1)} %param.23) | copy-start | bytes 6148
  180.6 4.5 %copy-start.38 = (bf16[1024]{0:T(1024)(128)(2,1)S(1)}, bf16[1024]{0:T(1024)(128)(2,1)}, u32[]{:S(2)}) copy-start(bf16[1024]{0:T(1024)(128)(2,1)} %param.24) | copy-start | bytes 6148
  180.7 4.5 %copy-start.39 = (bf16[1024]{0:T(1024)(128)(2,1)S(1)}, bf16[1024]{0:T(1024)(128)(2,1)}, u32[]{:S(2)}) copy-start(bf16[1024]{0:T(1024)(128)(2,1)} %param.28) | copy-start | bytes 6148
  180.7 4.6 %copy-start.40 = (bf16[1024]{0:T(1024)(128)(2,1)S(1)}, bf16[1024]{0:T(1024)(128)(2,1)}, u32[]{:S(2)}) copy-start(bf16[1024]{0:T(1024)(128)(2,1)} %param.29) | copy-start | bytes 6148
  180.7 4.6 %copy-start.41 = (bf16[1024]{0:T(1024)(128)(2,1)S(1)}, bf16[1024]{0:T(1024)(128)(2,1)}, u32[]{:S(2)}) copy-start(bf16[1024]{0:T(1024)(128)(2,1)} %param.30) | copy-start | bytes 6148
  180.7 18.1 %copy-start.12 = (bf16[128,1024]{1,0:T(8,128)(2,1)S(1)}, bf16[128,1024]{1,0:T(8,128)(2,1)}, u32[]{:S(2)}) copy-start(bf16[128,1024]{1,0:T(8,128)(2,1)} %copy-done.11) | copy-start | bytes 786436
  180.7 18.1 %copy-start.24 = (s32[288]{0:T(512)S(1)}, s32[288]{0:T(512)}, u32[]{:S(2)}) copy-start(s32[288]{0:T(512)} %shard_map.194.tab) | copy-start | bytes 3460
  180.7 18.1 %all-to-all-start.2 = ((bf16[8,256,128]{2,1,0:T(8,128)(2,1)}), bf16[8,256,128]{2,1,0:T(8,128)(2,1)S(1)}, u32[]{:S(2)}, u32[]{:S(2)}) async-start(bf16[8,256,128]{2,1,0:T(8,128)(2,1)} %bitcast.75), calls=%async_computation.2 | async-start | bytes 1048576 | tf_op jit(solution)/shard_map/all_to_all | solution.py:585
  185.5 23.7 %copy-start.8 = (bf16[1024,128]{1,0:T(8,128)(2,1)S(1)}, bf16[1024,128]{1,0:T(8,128)(2,1)}, u32[]{:S(2)}) copy-start(bf16[1024,128]{1,0:T(8,128)(2,1)} %maximum_convert_fusion.1) | copy-start | bytes 786436
  207.3 15.9 %collective-permute-start.16 = (bf16[128,1024]{1,0:T(8,128)(2,1)S(1)}, bf16[128,1024]{1,0:T(8,128)(2,1)S(1)}, u32[]{:S(2)}, u32[]{:S(2)}) collective-permute-start(bf16[128,1024]{1,0:T(8,128)(2,1)S(1)} %get-tuple-element.19), channel_id=1, source_target_pairs={{0,256},{64,320},{128,384},{192,448},{256,0},{320,64},{384,128},{4... | collective-permute-start | bytes 786440 | tf_op jit(solution)/shard_map/ppermute | solution.py:590
  (16 other events, 14.7 us)
Sparse Core Ops, SparseCore 0:
  48.8 94.7 all-gather.1
